TPU v7x, 256 devices: a whole 4x4x8 slice. The times are simulated.
256 devices in a mesh: dp: 2 (over z_hi), layer: 4 (over y), feat: 32 (over z_lo, x, core).
Axes of the slice: x: 4, y: 4, z: 8 (z_hi: 2, z_lo: 4; z = z_hi * 4 + z_lo), core: 2. Of those that a mesh axis runs over, the one named last changes fastest.
Arguments:
- resid: bfloat16 [4, 1024, 2304], P('layer', 'dp'), may hold values from -6 to 6
- enc_weight: bfloat16 [4, 2304, 16384], P('layer', None, 'feat'), may hold values from -0.125 to 0.125
- enc_bias: float32 [4, 16384], P('layer', 'feat'), may hold values from -3 to 3
- dec_weight: bfloat16 [4, 4, 16384, 2304], P('layer', None, 'feat', 'dp'), may hold values from -0.09375 to 0.09375
- dec_bias: float32 [4, 2304], P('layer', ('dp', 'feat')), may hold values from -3 to 3
- lengths: int32 [8], P('dp'), may hold values from 32 to 128, as said below
Outputs:
- recon: bfloat16 [4, 1024, 2304], P('layer', None, ('dp', 'feat'))
Inputs may be any that keep to these rules, and one draw needn't show every extreme that they name: `lengths`: the first sequence has length 128.
All inputs are finite; a program needn't handle non-finite values.
Results may differ from a plain program's by a relative error of at most 0.0047.
Values may be sent and summed in bfloat16 or wider, within the bound.
No kernel may reach another device: no remote copies, remote signals or barrier semaphores. Data moves between devices by JAX's collectives and lax.ppermute only.
A program may use at most 64 MiB of HBM per device.

v0:
```python
import jax
import jax.numpy as jnp
from jax import lax
from jax.sharding import PartitionSpec as P

SEQ = 128


def joined_along(blocks, dim):
    lengths = list(blocks.shape[1:])
    lengths[dim] *= blocks.shape[0]
    return jnp.moveaxis(blocks, 0, dim).reshape(lengths)


def copy_for_each(array, axis):
    copies = jnp.broadcast_to(array, (lax.axis_size(axis), *array.shape))
    return lax.all_to_all(copies, axis, split_axis=0, concat_axis=0, tiled=True)


def gather_directly(array, axis, dim):
    return joined_along(copy_for_each(array, axis), dim)


def passed_along(array, axis, by):
    size = lax.axis_size(axis)
    pairs = [(i, i + by) for i in range(size) if 0 <= i + by < size]
    return lax.ppermute(array, axis, pairs)


def per_device(resid, enc_weight, enc_bias, dec_weight, dec_bias, lengths):
    valid = (jnp.arange(SEQ)[None, :] < lengths[:, None]).reshape(-1).astype(jnp.float32)
    pre = jnp.dot(resid[0], enc_weight[0], preferred_element_type=jnp.float32) + enc_bias[0]
    acts = (jax.nn.relu(pre) * valid[:, None]).astype(jnp.bfloat16)
    target = lax.axis_index("layer")
    decoders = dec_weight[0]
    all_rows = gather_directly(acts, "dp", 0)
    pieces = None
    pieces = [(all_rows, target)]
    current = all_rows
    for step in range(1, lax.axis_size("layer")):
        current = passed_along(current, "layer", 1)
        pieces.append((current, target - step))
    width = decoders.shape[2] // lax.axis_size("feat")
    carry = jnp.zeros((lax.axis_size("feat") * width, all_rows.shape[0]), jnp.float32)
    for block, source in pieces:

        def apply_cols(inner, block=block, source=source):
            matrix = lax.dynamic_index_in_dim(decoders, jnp.maximum(source, 0), 0, keepdims=False)
            return inner + jnp.einsum(
                "fc,rf->cr", matrix, block, preferred_element_type=jnp.float32
            )

        carry = lax.cond((source >= 0) & (source <= target), apply_cols, lambda inner: inner, carry)
    summed = lax.psum_scatter(carry, "feat", scatter_dimension=0, tiled=True).T
    return (summed + dec_bias[0][None, :]).astype(jnp.bfloat16)[None]


def solution(mesh):
    in_specs = (
        P("layer", "dp", None),
        P("layer", None, "feat"),
        P("layer", "feat"),
        P("layer", None, "feat", "dp"),
        P("layer", ("dp", "feat")),
        P("dp"),
    )
    out_specs = P("layer", None, ("dp", "feat"))
    return jax.shard_map(
        per_device, mesh=mesh, in_specs=in_specs, out_specs=out_specs, check_vma=False
    )
```

profile of v0, /device:TPU:24, one launch (start us, length us, event | category | flops | bytes accessed | tf_op | source)
XLA Modules:
  0.0 209.5 jit_solution(115609807708806828)
XLA Ops:
  0.0 0.9 convert_bitcast_fusion
  0.9 0.8 copy-done
  1.7 3.0 %fusion.32 = bf16[512,512]{1,0:T(8,128)(2,1)S(1)} fusion(bf16[1,2304,512]{2,1,0:T(8,128)(2,1)S(1)} %copy-done, bf16[1,512,2304]{2,1,0:T(8,128)(2,1)} %param.14, f32[512]{0:T(512)S(1)} %convert_bitcast_fusion, f32[512]{0:T(512)} %bitcast.58), kind=kOutput, calls=%fused_computation.22 | convolution fusion | flops 1209008128 | bytes 5246976 | tf_op jit(solution)/shard_map/dot_general | solution.py:32
  4.8 36.1 %all_to_all.5 = bf16[2,512,512]{2,1,0:T(8,128)(2,1)S(1)} all-to-all(bf16[2,512,512]{2,1,0:T(8,128)(2,1)S(1)} %broadcast_in_dim.12), channel_id=1, replica_groups=mesh['dp'=2,'layer'=4,'feat'=32] {'dp'}, dimensions={0} | all-to-all | bytes 2097152 | tf_op jit(solution)/shard_map/all_to_all | solution.py:17
  41.0 1.3 collective-permute-start
  42.2 22.0 %collective-permute-done = bf16[1024,512]{1,0:T(8,128)(2,1)S(1)} collective-permute-done((bf16[1024,512]{1,0:T(8,128)(2,1)S(1)}, bf16[1024,512]{1,0:T(8,128)(2,1)S(1)}, u32[]{:S(2)}, u32[]{:S(2)}) %collective-permute-start) | collective-permute-done | bytes 1048608 | tf_op jit(solution)/shard_map/ppermute | solution.py:27
  64.3 1.3 collective-permute-start.1
  65.6 22.2 %collective-permute-done.1 = bf16[1024,512]{1,0:T(8,128)(2,1)} collective-permute-done((bf16[1024,512]{1,0:T(8,128)(2,1)S(1)}, bf16[1024,512]{1,0:T(8,128)(2,1)}, u32[]{:S(2)}, u32[]{:S(2)}) %collective-permute-start.1) | collective-permute-done | bytes 1048608 | tf_op jit(solution)/shard_map/ppermute | solution.py:27
  87.8 1.3 collective-permute-start.2
  89.1 5.2 %conditional.4 = (f32[1152,1024]{1,0:T(8,128)}) conditional(s32[]{:T(128)} %convert_element_type.34, () %tuple.29, (s32[]{:T(128)}, bf16[4,512,1152]{2,1,0:T(8,128)(2,1)}, bf16[1024,512]{1,0:T(8,128)(2,1)}) %tuple.47), branch_computations={%region_0.1_spmd, %region_1.2_spmd} | conditional | flops 1207959552 | bytes 6946840 | solution.py:53
  89.1 5.2 %fusion.1 = f32[1152,1024]{1,0:T(8,128)} fusion(bf16[1024,512]{1,0:T(8,128)(2,1)} %get-tuple-element.52, bf16[4,512,1152]{2,1,0:T(8,128)(2,1)} %get-tuple-element.50, s32[]{:T(128)S(6)} %max.14), kind=kOutput, calls=%fused_computation | convolution fusion | flops 1207959552 | bytes 6946820 | tf_op jit(solution)/shard_map/cond/branch_1_fun/fc,rf->cr/dot_general | solution.py:49
  94.2 6.6 %conditional.5 = (f32[1152,1024]{1,0:T(8,128)}) conditional(s32[]{:T(128)} %convert_element_type.33, f32[1152,1024]{1,0:T(8,128)} %get-tuple-element.65, (s32[]{:T(128)}, bf16[4,512,1152]{2,1,0:T(8,128)(2,1)}, bf16[1024,512]{1,0:T(8,128)(2,1)}, f32[1152,1024]{1,0:T(8,128)}) %tuple.46), branch_computations={%region_2.3_spmd, %region_3.4_spmd} | conditional | flops 1209139200 | bytes 11665432 | solution.py:53
  94.2 6.6 %convolution_add_fusion = f32[1152,1024]{1,0:T(8,128)} fusion(f32[1152,1024]{1,0:T(8,128)} %get-tuple-element.53, bf16[1024,512]{1,0:T(8,128)(2,1)} %get-tuple-element.56, bf16[4,512,1152]{2,1,0:T(8,128)(2,1)} %get-tuple-element.54, s32[]{:T(128)S(6)} %max.15), kind=kOutput, calls=%fused_computation.4 | convolution fusion | flops 1209139200 | bytes 11665412 | tf_op jit(solution)/shard_map/cond/branch_1_fun/fc,rf->cr/dot_general | solution.py:49
  100.8 6.6 %conditional.6 = (f32[1152,1024]{1,0:T(8,128)}) conditional(s32[]{:T(128)} %convert_element_type.32, f32[1152,1024]{1,0:T(8,128)} %get-tuple-element.66, (s32[]{:T(128)}, bf16[4,512,1152]{2,1,0:T(8,128)(2,1)}, bf16[1024,512]{1,0:T(8,128)(2,1)}, f32[1152,1024]{1,0:T(8,128)}) %tuple.44), branch_computations={%region_4.5_spmd, %region_5.6_spmd} | conditional | flops 1209139200 | bytes 11665432 | solution.py:53
  100.8 6.6 %convolution_add_fusion.1 = f32[1152,1024]{1,0:T(8,128)} fusion(f32[1152,1024]{1,0:T(8,128)} %get-tuple-element.57, bf16[1024,512]{1,0:T(8,128)(2,1)} %get-tuple-element.60, bf16[4,512,1152]{2,1,0:T(8,128)(2,1)} %get-tuple-element.58, s32[]{:T(128)S(6)} %max.16), kind=kOutput, calls=%fused_computation.8 | convolution fusion | flops 1209139200 | bytes 11665412 | tf_op jit(solution)/shard_map/cond/branch_1_fun/fc,rf->cr/dot_general | solution.py:49
  107.4 6.3 %conditional.7 = (f32[1152,1024]{1,0:T(8,128)}) conditional(s32[]{:T(128)} %convert_element_type.31, f32[1152,1024]{1,0:T(8,128)} %get-tuple-element.67, (s32[]{:T(128)}, bf16[4,512,1152]{2,1,0:T(8,128)(2,1)}, bf16[1024,512]{1,0:T(8,128)(2,1)S(1)}, f32[1152,1024]{1,0:T(8,128)}) %tuple.45), branch_computations={%region_6.7_spmd, %region_7.8_spmd} | conditional | flops 1209139200 | bytes 11665432 | solution.py:53
  107.4 6.3 %convolution_add_fusion.2 = f32[1152,1024]{1,0:T(8,128)} fusion(f32[1152,1024]{1,0:T(8,128)} %get-tuple-element.61, bf16[1024,512]{1,0:T(8,128)(2,1)S(1)} %get-tuple-element.64, bf16[4,512,1152]{2,1,0:T(8,128)(2,1)} %get-tuple-element.62, s32[]{:T(128)S(6)} %max.17), kind=kOutput, calls=%fused_computation.12 | convolution fusion | flops 1209139200 | bytes 11665412 | tf_op jit(solution)/shard_map/cond/branch_1_fun/fc,rf->cr/dot_general | solution.py:49
  113.7 84.5 %fusion = f32[40,1024]{1,0:T(8,128)S(1)} fusion(f32[1152,1024]{1,0:T(8,128)} %get-tuple-element.68), kind=kCustom, calls=%all-reduce-scatter | all-reduce-scatter fusion | flops 1310721 | bytes 4883456
  198.2 1.3 collective-permute-start.3
  199.5 1.3 collective-permute-start.4
  200.8 2.0 collective-permute-start.5
  202.8 1.3 collective-permute-start.6
  206.4 2.4 %concatenate = f32[164,1024]{1,0:T(8,128)S(1)} concatenate(f32[4,1024]{1,0:T(4,128)S(1)} %collective-permute-done.6, f32[40,1024]{1,0:T(8,128)} %collective-permute-done.5, f32[40,1024]{1,0:T(8,128)} %copy-done.3, f32[40,1024]{1,0:T(8,128)S(1)} %collective-permute-done.3, f32[40,1024]{1,0:T(8,128)S(1)} %fusion), dimensions={0} | concatenate | bytes 1343488
  208.8 0.7 fusion.38
  (19 shorter events, 1.8 us)
Async XLA Ops:
  0.0 1.7 copy-start
  40.9 46.8 %copy-start.2 = (bf16[2,512,512]{2,1,0:T(8,128)(2,1)}, bf16[2,512,512]{2,1,0:T(8,128)(2,1)S(1)}, u32[]{:S(2)}) copy-start(bf16[2,512,512]{2,1,0:T(8,128)(2,1)S(1)} %all_to_all.5) | copy-start | bytes 3145732
  41.0 23.3 %collective-permute-start = (bf16[1024,512]{1,0:T(8,128)(2,1)S(1)}, bf16[1024,512]{1,0:T(8,128)(2,1)S(1)}, u32[]{:S(2)}, u32[]{:S(2)}) collective-permute-start(bf16[1024,512]{1,0:T(8,128)(2,1)S(1)} %bitcast.55), channel_id=1, source_target_pairs={{0,32},{32,64},{64,96},{1,33},{33,65},{65,97},{2,34},{34,66},{66,9... | collective-permute-start | bytes 3145736 | tf_op jit(solution)/shard_map/ppermute | solution.py:27
  64.3 1.3 copy-start.1
  64.3 23.5 %collective-permute-start.1 = (bf16[1024,512]{1,0:T(8,128)(2,1)S(1)}, bf16[1024,512]{1,0:T(8,128)(2,1)}, u32[]{:S(2)}, u32[]{:S(2)}) collective-permute-start(bf16[1024,512]{1,0:T(8,128)(2,1)S(1)} %collective-permute-done), channel_id=1, source_target_pairs={{0,32},{32,64},{64,96},{1,33},{33,65},{65,97},{2,34},{34,66},{66,9... | collective-permute-start | bytes 3145736 | tf_op jit(solution)/shard_map/ppermute | solution.py:27
  87.8 19.7 %collective-permute-start.2 = (bf16[1024,512]{1,0:T(8,128)(2,1)}, bf16[1024,512]{1,0:T(8,128)(2,1)S(1)}, u32[]{:S(2)}, u32[]{:S(2)}) collective-permute-start(bf16[1024,512]{1,0:T(8,128)(2,1)} %collective-permute-done.1), channel_id=1, source_target_pairs={{0,32},{32,64},{64,96},{1,33},{33,65},{65,97},{2,34},{34,66},{66,9... | collective-permute-start | bytes 3145736 | tf_op jit(solution)/shard_map/ppermute | solution.py:27
  113.7 90.4 %copy-start.5 = (u32[256]{0:T(256)S(1)}, u32[256]{0:T(256)}, u32[]{:S(2)}) copy-start(u32[256]{0:T(256)} %constant.51) | copy-start | bytes 3076
  113.7 95.1 %copy-start.4 = (f32[1,36]{1,0:T(1,128)S(1)}, f32[1,36]{1,0:T(1,128)}, u32[]{:S(2)}) copy-start(f32[1,36]{1,0:T(1,128)} %param.18) | copy-start | bytes 436
  198.2 7.5 %collective-permute-start.3 = (f32[40,1024]{1,0:T(8,128)S(1)}, f32[40,1024]{1,0:T(8,128)S(1)}, u32[]{:S(2)}, u32[]{:S(2)}) collective-permute-start(f32[40,1024]{1,0:T(8,128)S(1)} %fusion), channel_id=1, source_target_pairs={{0,1},{1,2},{2,3},{3,4},{4,5},{5,6},{6,7},{7,8},{8,9},{9,10},{10,1... | collective-permute-start | bytes 491528
  199.5 6.2 %collective-permute-start.4 = (f32[40,1024]{1,0:T(8,128)S(1)}, f32[40,1024]{1,0:T(8,128)S(1)}, u32[]{:S(2)}, u32[]{:S(2)}) collective-permute-start(f32[40,1024]{1,0:T(8,128)S(1)} %fusion), channel_id=1, source_target_pairs={{0,2},{1,3},{2,4},{3,5},{4,6},{5,7},{6,8},{7,9},{8,10},{9,11},{10,... | collective-permute-start | bytes 491528
  200.8 5.6 %collective-permute-start.5 = (f32[40,1024]{1,0:T(8,128)S(1)}, f32[40,1024]{1,0:T(8,128)}, u32[]{:S(2)}, u32[]{:S(2)}) collective-permute-start(f32[40,1024]{1,0:T(8,128)S(1)} %fusion), channel_id=1, source_target_pairs={{0,3},{1,4},{2,5},{3,6},{4,7},{5,8},{6,9},{7,10},{8,11},{9,12},{10... | collective-permute-start | bytes 491528
  202.8 2.9 %collective-permute-start.6 = (f32[4,1024]{1,0:T(4,128)S(1)}, f32[4,1024]{1,0:T(4,128)S(1)}, u32[]{:S(2)}, u32[]{:S(2)}) collective-permute-start(f32[4,1024]{1,0:T(4,128)S(1)} %slice), channel_id=1, source_target_pairs={{0,4},{1,5},{2,6},{3,7},{4,8},{5,9},{6,10},{7,11},{8,12},{9,13},{1... | collective-permute-start | bytes 49160
  205.7 0.7 copy-start.3
where the time goes:
time: 213 us; the launch traced here: 210 us
  blocking collectives  121 us (57%)
  waiting for transfers between devices  44.6 us (21%)
  matrix products  27.7 us (13%)
  starting transfers between devices  9.69 us (5%)
  local copies, waits for them, and re-layouts  4.53 us (2%)
    unnamed x1, blocking collectives  84.5 us
    ppermute x3, waiting for transfers between devices, passed_along(): return lax.ppermute(array, axis, pairs)  44.2 us
    all_to_all x1, blocking collectives, copy_for_each(): return lax.all_to_all(copies, axis, split_axis=0, concat_axis=0, tiled=True)  36.1 us
    dot_general x4, matrix products, apply_cols(): jnp.einsum('fc,rf->cr', matrix, block, preferred_element_type=jnp.float32)  24.6 us
    unnamed x4, starting transfers between devices  5.85 us
    unnamed x15, local copies, waits for them, and re-layouts  4.46 us
  transfers between devices with their start and end apart: 7, of which 3 were waited for; matrix products, arithmetic and copies ran while one was open for 9% of the time, Pallas kernels for 0%

commit v1 on v0

v1 whole, which is shorter than its diff:
```python
import jax
import jax.numpy as jnp
from jax import lax
from jax.sharding import PartitionSpec as P

SEQ = 128
BF = jnp.bfloat16
F32 = jnp.float32


def feat_groups():
    at = lambda z, x, c: z * 8 + x * 2 + c
    along_x = [[at(z, x, c) for x in range(4)] for z in range(4) for c in range(2)]
    along_z = [[at(z, x, c) for z in range(4)] for x in range(4) for c in range(2)]
    return along_x, along_z


def layer_exchange(acts, target):
    half = acts.shape[0] // 2
    up = lax.ppermute(acts, "layer", [(0, 1), (1, 2), (2, 3)])
    down = lax.ppermute(acts, "layer", [(0, 3), (1, 0)])
    far_up = lax.ppermute(up[:half], "layer", [(1, 2), (2, 3)])
    far_down = lax.ppermute(down[half:], "layer", [(3, 2), (0, 3)])
    return up, jnp.where(target == 3, down, 0), jnp.concatenate([far_up, far_down])


def partial_recon(blocks, decoders, target):
    total = None
    for back, block in blocks:
        matrix = lax.dynamic_index_in_dim(decoders, jnp.maximum(target - back, 0), 0, keepdims=False)
        halves = block.reshape(2, block.shape[0] // 2, block.shape[1])
        term = jnp.einsum("fc,grf->gcr", matrix, halves, preferred_element_type=F32)
        total = term if total is None else total + term
    return total


def reduce_features(total, core):
    along_x, along_z = feat_groups()
    partner = [(i, i ^ 1) for i in range(32)]
    away = lax.dynamic_index_in_dim(total, 1 - core, 0, keepdims=False).astype(BF)
    kept = lax.dynamic_index_in_dim(total, core, 0, keepdims=False)
    chip = kept + lax.ppermute(away, "feat", partner).astype(F32)
    rows = chip.shape[1]
    pieces = chip.astype(BF).reshape(4, 4, 72, rows).transpose(1, 0, 2, 3)
    pieces = lax.all_to_all(pieces, "feat", 0, 0, tiled=True, axis_index_groups=along_x)
    pieces = pieces.astype(F32).sum(0).astype(BF)
    pieces = lax.all_to_all(pieces, "feat", 0, 0, tiled=True, axis_index_groups=along_z)
    return pieces.astype(F32).sum(0)


def per_device(resid, enc_weight, enc_bias, dec_weight, dec_bias, lengths):
    target = lax.axis_index("layer")
    core = lax.axis_index("feat") % 2
    valid = (jnp.arange(SEQ)[None, :] < lengths[:, None]).reshape(-1).astype(F32)
    pre = jnp.dot(resid[0], enc_weight[0], preferred_element_type=F32) + enc_bias[0]
    own = (jax.nn.relu(pre) * valid[:, None]).astype(BF)
    other = lax.ppermute(own, "dp", [(0, 1), (1, 0)])
    decoders = dec_weight[0]
    sums = []
    for acts in (own, other):
        one, three, two = layer_exchange(acts, target)
        blocks = [(0, acts), (1, one), (3, three), (2, two)]
        sums.append(reduce_features(partial_recon(blocks, decoders, target), core))
    both = jnp.stack(sums)
    partner = [(i, i ^ 1) for i in range(32)]
    low, high = both[:, :36], both[:, 36:]
    kept = jnp.where(core == 0, low, high)
    came = lax.ppermute(jnp.where(core == 0, high, low), "feat", partner)
    halves = jnp.where(core == 0, jnp.concatenate([kept, came], 2), jnp.concatenate([came, kept], 2))
    halves = jnp.where(lax.axis_index("dp") == 0, halves, halves[::-1])
    out = jnp.concatenate([halves[0], halves[1]], 1) + dec_bias[0][:, None]
    return out.T.astype(BF)[None]


def solution(mesh):
    in_specs = (
        P("layer", "dp", None),
        P("layer", None, "feat"),
        P("layer", "feat"),
        P("layer", None, "feat", "dp"),
        P("layer", ("dp", "feat")),
        P("dp"),
    )
    out_specs = P("layer", None, ("dp", "feat"))
    return jax.shard_map(
        per_device, mesh=mesh, in_specs=in_specs, out_specs=out_specs, check_vma=False
    )
```

time: 213 us -> 127 us (0.60); the launches traced: 210 us -> 126 us
  blocking collectives: 121 us -> 0 us
  starting transfers between devices: 9.69 us -> 44.7 us
  matrix products: 27.7 us -> 13.3 us
  waiting for transfers between devices: 44.6 us -> 53.9 us
  other arithmetic: 1.59 us -> 6.28 us
  local copies, waits for them, and re-layouts: 4.53 us -> 7.39 us
    unnamed x1 -> x0, blocking collectives: 84.5 us -> none
    all_to_all x1 -> x0, blocking collectives: 36.1 us -> none  [copy_for_each(): return lax.all_to_all(copies, axis, split_axis=0, concat_axis=0, tiled=True)]
    all_to_all x0 -> x4, waiting for transfers between devices: none -> 26.6 us  [the longest x2 15.5 us: reduce_features(): lax.all_to_all(pieces, 'feat', 0, 0, tiled=True, axis_index_groups=along_x)]
    all_to_all x0 -> x4, starting transfers between devices: none -> 24.1 us  [the longest x2 16.4 us: reduce_features(): lax.all_to_all(pieces, 'feat', 0, 0, tiled=True, axis_index_groups=along_z)]
    ppermute x3 -> x12, waiting for transfers between devices: 44.2 us -> 27.3 us  [the longest x2 13.9 us: layer_exchange(): up = lax.ppermute(acts, 'layer', [(0, 1), (1, 2), (2, 3)])]
    ppermute x3 -> x12, starting transfers between devices: 3.84 us -> 20.5 us  [the longest x1 7.28 us: per_device(): other = lax.ppermute(own, 'dp', [(0, 1), (1, 0)])]
    dot_general x5 -> x9, matrix products: 27.7 us -> 13.3 us  [the longest x8 9.42 us: partial_recon(): term = jnp.einsum('fc,grf->gcr', matrix, halves, preferred_element_type=F32)]
    unnamed x4 -> x0, starting transfers between devices: 5.85 us -> none
  transfers between devices with their start and end apart: 7 -> 16, of which waited for: 3 -> 12; matrix products, arithmetic and copies ran while one was open for 9% -> 15% of each run, Pallas kernels for 0% -> 0%
where the time goes in v1:
time: 127 us; the launch traced here: 126 us
  waiting for transfers between devices  53.9 us (42%)
  starting transfers between devices  44.7 us (35%)
  matrix products  13.3 us (10%)
  local copies, waits for them, and re-layouts  7.39 us (6%)
  other arithmetic  6.28 us (5%)
    all_to_all x2, starting transfers between devices, reduce_features(): lax.all_to_all(pieces, 'feat', 0, 0, tiled=True, axis_index_groups=along_z)  16.4 us
    all_to_all x2, waiting for transfers between devices, reduce_features(): lax.all_to_all(pieces, 'feat', 0, 0, tiled=True, axis_index_groups=along_x)  15.5 us
    ppermute x2, waiting for transfers between devices, layer_exchange(): up = lax.ppermute(acts, 'layer', [(0, 1), (1, 2), (2, 3)])  13.9 us
    all_to_all x2, waiting for transfers between devices, reduce_features(): lax.all_to_all(pieces, 'feat', 0, 0, tiled=True, axis_index_groups=along_z)  11.1 us
    dot_general x8, matrix products, partial_recon(): term = jnp.einsum('fc,grf->gcr', matrix, halves, preferred_element_type=F32)  9.42 us
    all_to_all x2, starting transfers between devices, reduce_features(): lax.all_to_all(pieces, 'feat', 0, 0, tiled=True, axis_index_groups=along_x)  7.77 us
    ppermute x1, starting transfers between devices, per_device(): other = lax.ppermute(own, 'dp', [(0, 1), (1, 0)])  7.28 us
    ppermute x2, starting transfers between devices, layer_exchange(): far_down = lax.ppermute(down[half:], 'layer', [(3, 2), (0, 3)])  5.34 us
  transfers between devices with their start and end apart: 16, of which 12 were waited for; matrix products, arithmetic and copies ran while one was open for 15% of the time, Pallas kernels for 0%

profile of v1, /device:TPU:24, one launch (start us, length us, event | category | flops | bytes accessed | tf_op | source)
XLA Modules:
  0.0 125.9 jit_solution(2744395343724289529)
XLA Ops:
  1.7 3.9 %fusion.20 = bf16[512,512]{1,0:T(8,128)(2,1)} fusion(bf16[1,2304,512]{2,1,0:T(8,128)(2,1)S(1)} %copy-done, bf16[1,512,2304]{2,1,0:T(8,128)(2,1)} %param.6, f32[512]{0:T(512)S(1)} %convert_bitcast_fusion, f32[512]{0:T(512)} %bitcast.117), kind=kOutput, calls=%fused_computation.12 | convolution fusion | flops 1209008128 | bytes 5246976 | tf_op jit(solution)/shard_map/dot_general | solution.py:55
  8.1 7.3 %collective-permute-start.5 = (bf16[512,512]{1,0:T(8,128)(2,1)}, bf16[512,512]{1,0:T(8,128)(2,1)}, u32[]{:S(2)}, u32[]{:S(2)}) collective-permute-start(bf16[512,512]{1,0:T(8,128)(2,1)} %fusion.20), channel_id=1, source_target_pairs={{0,128},{128,0},{1,129},{129,1},{2,130},{130,2},{3,131},{131,3},{4... | collective-permute-start | bytes 1572872 | tf_op jit(solution)/shard_map/ppermute | solution.py:57
  15.4 2.4 %fusion.37 = f32[2,256,1152]{2,1,0:T(8,128)S(1)} fusion(bf16[2,256,512]{2,1,0:T(8,128)(2,1)} %bitcast.4, bf16[1,4,512,1152]{3,2,1,0:T(8,128)(2,1)} %param.9, s32[]{:T(128)S(6)} %max.26), kind=kOutput, calls=%fused_computation.27 | convolution fusion | flops 603979776 | bytes 4063236 | tf_op jit(solution)/shard_map/fc,grf->gcr/dot_general | solution.py:32
  17.8 3.5 %collective-permute-done = bf16[512,512]{1,0:T(8,128)(2,1)S(1)} collective-permute-done((bf16[512,512]{1,0:T(8,128)(2,1)}, bf16[512,512]{1,0:T(8,128)(2,1)S(1)}, u32[]{:S(2)}, u32[]{:S(2)}) %collective-permute-start) | collective-permute-done | bytes 524320 | tf_op jit(solution)/shard_map/ppermute | solution.py:20
  23.8 3.4 %collective-permute-start.3 = (bf16[256,512]{1,0:T(8,128)(2,1)S(1)}, bf16[256,512]{1,0:T(8,128)(2,1)S(1)}, u32[]{:S(2)}, u32[]{:S(2)}) collective-permute-start(bf16[256,512]{1,0:T(8,128)(2,1)S(1)} %slice.33), channel_id=1, source_target_pairs={{96,64},{0,96},{97,65},{1,97},{98,66},{2,98},{99,67},{3,99},{100,6... | collective-permute-start | bytes 786440 | tf_op jit(solution)/shard_map/ppermute | solution.py:23
  28.1 1.8 %collective-permute-done.5 = bf16[512,512]{1,0:T(8,128)(2,1)} collective-permute-done((bf16[512,512]{1,0:T(8,128)(2,1)}, bf16[512,512]{1,0:T(8,128)(2,1)}, u32[]{:S(2)}, u32[]{:S(2)}) %collective-permute-start.5) | collective-permute-done | bytes 524320 | tf_op jit(solution)/shard_map/ppermute | solution.py:57
  29.9 1.9 %fusion.35 = f32[2,256,1152]{2,1,0:T(8,128)S(1)} fusion(bf16[2,256,512]{2,1,0:T(8,128)(2,1)} %bitcast.23, bf16[1,4,512,1152]{3,2,1,0:T(8,128)(2,1)S(1)} %copy-done.1, s32[]{:T(128)S(6)} %max.26), kind=kOutput, calls=%fused_computation.25 | convolution fusion | flops 603979776 | bytes 4063236 | tf_op jit(solution)/shard_map/fc,grf->gcr/dot_general | solution.py:32
  36.4 10.4 %collective-permute-done.6 = bf16[512,512]{1,0:T(8,128)(2,1)S(1)} collective-permute-done((bf16[512,512]{1,0:T(8,128)(2,1)}, bf16[512,512]{1,0:T(8,128)(2,1)S(1)}, u32[]{:S(2)}, u32[]{:S(2)}) %collective-permute-start.6) | collective-permute-done | bytes 524320 | tf_op jit(solution)/shard_map/ppermute | solution.py:20
  48.1 2.6 %collective-permute-done.7 = bf16[512,512]{1,0:T(8,128)(2,1)S(1)} collective-permute-done((bf16[512,512]{1,0:T(8,128)(2,1)}, bf16[512,512]{1,0:T(8,128)(2,1)S(1)}, u32[]{:S(2)}, u32[]{:S(2)}) %collective-permute-start.7) | collective-permute-done | bytes 524320 | tf_op jit(solution)/shard_map/ppermute | solution.py:21
  50.8 2.0 %collective-permute-start.9 = (bf16[256,512]{1,0:T(8,128)(2,1)S(1)}, bf16[256,512]{1,0:T(8,128)(2,1)S(1)}, u32[]{:S(2)}, u32[]{:S(2)}) collective-permute-start(bf16[256,512]{1,0:T(8,128)(2,1)S(1)} %slice.35), channel_id=1, source_target_pairs={{96,64},{0,96},{97,65},{1,97},{98,66},{2,98},{99,67},{3,99},{100,6... | collective-permute-start | bytes 786440 | tf_op jit(solution)/shard_map/ppermute | solution.py:23
  53.6 1.5 %collective-permute-done.8 = bf16[256,512]{1,0:T(8,128)(2,1)S(1)} collective-permute-done((bf16[256,512]{1,0:T(8,128)(2,1)S(1)}, bf16[256,512]{1,0:T(8,128)(2,1)S(1)}, u32[]{:S(2)}, u32[]{:S(2)}) %collective-permute-start.8) | collective-permute-done | bytes 262176 | tf_op jit(solution)/shard_map/ppermute | solution.py:22
  55.2 5.1 %collective-permute-done.9 = bf16[256,512]{1,0:T(8,128)(2,1)S(1)} collective-permute-done((bf16[256,512]{1,0:T(8,128)(2,1)S(1)}, bf16[256,512]{1,0:T(8,128)(2,1)S(1)}, u32[]{:S(2)}, u32[]{:S(2)}) %collective-permute-start.9) | collective-permute-done | bytes 262176 | tf_op jit(solution)/shard_map/ppermute | solution.py:23
  62.0 1.4 %copy-done.3 = f32[2,256,1152]{2,1,0:T(8,128)} copy-done((f32[2,256,1152]{2,1,0:T(8,128)}, f32[2,256,1152]{2,1,0:T(8,128)S(1)}, u32[]{:S(2)}) %copy-start.3) | copy-done | bytes 2359320
  64.3 1.4 %fusion.26 = bf16[1152,256]{0,1:T(8,128)(2,1)S(1)} fusion(bf16[1152,256]{0,1:T(8,128)(2,1)S(1)} %collective-permute-done.4, f32[2,256,1152]{2,1,0:T(8,128)} %copy-done.2, s32[]{:T(128)S(6)} %select_n.69), kind=kLoop, calls=%fused_computation.16 | loop fusion | flops 884736 | bytes 2359300 | tf_op jit(solution)/shard_map/convert_element_type | solution.py:44
  66.8 4.3 %all-to-all-start = ((bf16[4,4,72,256]{3,2,1,0:T(8,128)(2,1)}), bf16[4,4,72,256]{3,2,1,0:T(8,128)(2,1)S(1)}, u32[]{:S(2)}, u32[]{:S(2)}) async-start(bf16[4,4,72,256]{3,2,1,0:T(8,128)(2,1)} %copy.14), calls=%async_computation | async-start | bytes 1179648 | tf_op jit(solution)/shard_map/all_to_all | solution.py:45
  71.1 1.6 %fusion.25 = bf16[1152,256]{0,1:T(8,128)(2,1)S(1)} fusion(bf16[1152,256]{0,1:T(8,128)(2,1)} %collective-permute-done.10, f32[2,256,1152]{2,1,0:T(8,128)} %copy-done.3, s32[]{:T(128)S(6)} %select_n.69), kind=kLoop, calls=%fused_computation.14 | loop fusion | flops 884736 | bytes 2359300 | tf_op jit(solution)/shard_map/convert_element_type | solution.py:44
  73.7 1.9 %copy.16 = bf16[4,4,72,256]{3,2,1,0:T(8,128)(2,1)} copy(bf16[4,4,72,256]{3,2,0,1:T(8,128)(2,1)} %bitcast.107) | data formatting | bytes 1179648 | tf_op jit(solution)/shard_map/transpose | solution.py:44
  75.7 6.3 %all-to-all-done = bf16[4,4,72,256]{3,2,1,0:T(8,128)(2,1)S(1)} async-done(((bf16[4,4,72,256]{3,2,1,0:T(8,128)(2,1)}), bf16[4,4,72,256]{3,2,1,0:T(8,128)(2,1)S(1)}, u32[]{:S(2)}, u32[]{:S(2)}) %all-to-all-start) | async-done | bytes 589856 | tf_op jit(solution)/shard_map/all_to_all | solution.py:45
  82.0 3.5 %all-to-all-start.2 = ((bf16[4,4,72,256]{3,2,1,0:T(8,128)(2,1)}), bf16[4,4,72,256]{3,2,1,0:T(8,128)(2,1)S(1)}, u32[]{:S(2)}, u32[]{:S(2)}) async-start(bf16[4,4,72,256]{3,2,1,0:T(8,128)(2,1)} %copy.16), calls=%async_computation.2 | async-start | bytes 1179648 | tf_op jit(solution)/shard_map/all_to_all | solution.py:45
  86.2 9.2 %all-to-all-done.2 = bf16[4,4,72,256]{3,2,1,0:T(8,128)(2,1)S(1)} async-done(((bf16[4,4,72,256]{3,2,1,0:T(8,128)(2,1)}), bf16[4,4,72,256]{3,2,1,0:T(8,128)(2,1)S(1)}, u32[]{:S(2)}, u32[]{:S(2)}) %all-to-all-start.2) | async-done | bytes 589856 | tf_op jit(solution)/shard_map/all_to_all | solution.py:45
  95.4 13.0 %all-to-all-start.1 = ((bf16[4,72,256]{2,1,0:T(8,128)(2,1)}), bf16[4,72,256]{2,1,0:T(8,128)(2,1)S(1)}, u32[]{:S(2)}, u32[]{:S(2)}) async-start(bf16[4,72,256]{2,1,0:T(8,128)(2,1)} %reduce_sum.42), calls=%async_computation.1 | async-start | bytes 294912 | tf_op jit(solution)/shard_map/all_to_all | solution.py:47
  109.2 5.2 %all-to-all-done.1 = bf16[4,72,256]{2,1,0:T(8,128)(2,1)S(1)} async-done(((bf16[4,72,256]{2,1,0:T(8,128)(2,1)}), bf16[4,72,256]{2,1,0:T(8,128)(2,1)S(1)}, u32[]{:S(2)}, u32[]{:S(2)}) %all-to-all-start.1) | async-done | bytes 147488 | tf_op jit(solution)/shard_map/all_to_all | solution.py:47
  114.4 3.3 %all-to-all-start.3 = ((bf16[4,72,256]{2,1,0:T(8,128)(2,1)}), bf16[4,72,256]{2,1,0:T(8,128)(2,1)S(1)}, u32[]{:S(2)}, u32[]{:S(2)}) async-start(bf16[4,72,256]{2,1,0:T(8,128)(2,1)} %reduce_sum.44), calls=%async_computation.3 | async-start | bytes 294912 | tf_op jit(solution)/shard_map/all_to_all | solution.py:47
  117.8 5.9 %all-to-all-done.3 = bf16[4,72,256]{2,1,0:T(8,128)(2,1)S(1)} async-done(((bf16[4,72,256]{2,1,0:T(8,128)(2,1)}), bf16[4,72,256]{2,1,0:T(8,128)(2,1)S(1)}, u32[]{:S(2)}, u32[]{:S(2)}) %all-to-all-start.3) | async-done | bytes 147488 | tf_op jit(solution)/shard_map/all_to_all | solution.py:47
  (53 shorter events, 22.9 us)
Async XLA Ops:
  0.0 1.7 %copy-start = (bf16[1,2304,512]{2,1,0:T(8,128)(2,1)S(1)}, bf16[1,2304,512]{2,1,0:T(8,128)(2,1)}, u32[]{:S(2)}) copy-start(bf16[1,2304,512]{2,1,0:T(8,128)(2,1)} %param.7) | copy-start | bytes 7077892
  5.5 15.8 %collective-permute-start = (bf16[512,512]{1,0:T(8,128)(2,1)}, bf16[512,512]{1,0:T(8,128)(2,1)S(1)}, u32[]{:S(2)}, u32[]{:S(2)}) collective-permute-start(bf16[512,512]{1,0:T(8,128)(2,1)} %fusion.20), channel_id=1, source_target_pairs={{0,32},{32,64},{64,96},{1,33},{33,65},{65,97},{2,34},{34,66},{66,9... | collective-permute-start | bytes 1572872 | tf_op jit(solution)/shard_map/ppermute | solution.py:20
  6.8 17.0 %collective-permute-start.1 = (bf16[512,512]{1,0:T(8,128)(2,1)}, bf16[512,512]{1,0:T(8,128)(2,1)S(1)}, u32[]{:S(2)}, u32[]{:S(2)}) collective-permute-start(bf16[512,512]{1,0:T(8,128)(2,1)} %fusion.20), channel_id=1, source_target_pairs={{0,96},{32,0},{1,97},{33,1},{2,98},{34,2},{3,99},{35,3},{4,100},{3... | collective-permute-start | bytes 1572872 | tf_op jit(solution)/shard_map/ppermute | solution.py:21
  8.1 21.8 %collective-permute-start.5 = (bf16[512,512]{1,0:T(8,128)(2,1)}, bf16[512,512]{1,0:T(8,128)(2,1)}, u32[]{:S(2)}, u32[]{:S(2)}) collective-permute-start(bf16[512,512]{1,0:T(8,128)(2,1)} %fusion.20), channel_id=1, source_target_pairs={{0,128},{128,0},{1,129},{129,1},{2,130},{130,2},{3,131},{131,3},{4... | collective-permute-start | bytes 1572872 | tf_op jit(solution)/shard_map/ppermute | solution.py:57
  15.4 11.8 %copy-start.1 = (bf16[1,4,512,1152]{3,2,1,0:T(8,128)(2,1)S(1)}, bf16[1,4,512,1152]{3,2,1,0:T(8,128)(2,1)}, u32[]{:S(2)}) copy-start(bf16[1,4,512,1152]{3,2,1,0:T(8,128)(2,1)} %param.9) | copy-start | bytes 14155780
  21.3 13.1 %collective-permute-start.2 = (bf16[256,512]{1,0:T(8,128)(2,1)S(1)}, bf16[256,512]{1,0:T(8,128)(2,1)S(1)}, u32[]{:S(2)}, u32[]{:S(2)}) collective-permute-start(bf16[256,512]{1,0:T(8,128)(2,1)S(1)} %slice.32), channel_id=1, source_target_pairs={{32,64},{64,96},{33,65},{65,97},{34,66},{66,98},{35,67},{67,99},{3... | collective-permute-start | bytes 786440 | tf_op jit(solution)/shard_map/ppermute | solution.py:22
  23.8 10.6 %collective-permute-start.3 = (bf16[256,512]{1,0:T(8,128)(2,1)S(1)}, bf16[256,512]{1,0:T(8,128)(2,1)S(1)}, u32[]{:S(2)}, u32[]{:S(2)}) collective-permute-start(bf16[256,512]{1,0:T(8,128)(2,1)S(1)} %slice.33), channel_id=1, source_target_pairs={{96,64},{0,96},{97,65},{1,97},{98,66},{2,98},{99,67},{3,99},{100,6... | collective-permute-start | bytes 786440 | tf_op jit(solution)/shard_map/ppermute | solution.py:23
  31.8 15.0 %collective-permute-start.6 = (bf16[512,512]{1,0:T(8,128)(2,1)}, bf16[512,512]{1,0:T(8,128)(2,1)S(1)}, u32[]{:S(2)}, u32[]{:S(2)}) collective-permute-start(bf16[512,512]{1,0:T(8,128)(2,1)} %collective-permute-done.5), channel_id=1, source_target_pairs={{0,32},{32,64},{64,96},{1,33},{33,65},{65,97},{2,34},{34,66},{66,9... | collective-permute-start | bytes 1572872 | tf_op jit(solution)/shard_map/ppermute | solution.py:20
  33.1 17.7 %collective-permute-start.7 = (bf16[512,512]{1,0:T(8,128)(2,1)}, bf16[512,512]{1,0:T(8,128)(2,1)S(1)}, u32[]{:S(2)}, u32[]{:S(2)}) collective-permute-start(bf16[512,512]{1,0:T(8,128)(2,1)} %collective-permute-done.5), channel_id=1, source_target_pairs={{0,96},{32,0},{1,97},{33,1},{2,98},{34,2},{3,99},{35,3},{4,100},{3... | collective-permute-start | bytes 1572872 | tf_op jit(solution)/shard_map/ppermute | solution.py:21
  36.2 17.4 %copy-start.2 = (f32[2,256,1152]{2,1,0:T(8,128)}, f32[2,256,1152]{2,1,0:T(8,128)S(1)}, u32[]{:S(2)}) copy-start(f32[2,256,1152]{2,1,0:T(8,128)S(1)} %fusion) | copy-start | bytes 7077892
  36.3 28.0 %collective-permute-start.4 = (bf16[1152,256]{0,1:T(8,128)(2,1)S(1)}, bf16[1152,256]{0,1:T(8,128)(2,1)S(1)}, u32[]{:S(2)}, u32[]{:S(2)}) collective-permute-start(bf16[1152,256]{0,1:T(8,128)(2,1)S(1)} %fusion.47), channel_id=1, source_target_pairs={{0,1},{1,0},{2,3},{3,2},{4,5},{5,4},{6,7},{7,6},{8,9},{9,8},{10,11... | collective-permute-start | bytes 1769480 | tf_op jit(solution)/shard_map/ppermute | solution.py:42
  46.8 8.3 %collective-permute-start.8 = (bf16[256,512]{1,0:T(8,128)(2,1)S(1)}, bf16[256,512]{1,0:T(8,128)(2,1)S(1)}, u32[]{:S(2)}, u32[]{:S(2)}) collective-permute-start(bf16[256,512]{1,0:T(8,128)(2,1)S(1)} %slice.34), channel_id=1, source_target_pairs={{32,64},{64,96},{33,65},{65,97},{34,66},{66,98},{35,67},{67,99},{3... | collective-permute-start | bytes 786440 | tf_op jit(solution)/shard_map/ppermute | solution.py:22
  50.8 9.5 %collective-permute-start.9 = (bf16[256,512]{1,0:T(8,128)(2,1)S(1)}, bf16[256,512]{1,0:T(8,128)(2,1)S(1)}, u32[]{:S(2)}, u32[]{:S(2)}) collective-permute-start(bf16[256,512]{1,0:T(8,128)(2,1)S(1)} %slice.35), channel_id=1, source_target_pairs={{96,64},{0,96},{97,65},{1,97},{98,66},{2,98},{99,67},{3,99},{100,6... | collective-permute-start | bytes 786440 | tf_op jit(solution)/shard_map/ppermute | solution.py:23
  62.0 1.4 %copy-start.3 = (f32[2,256,1152]{2,1,0:T(8,128)}, f32[2,256,1152]{2,1,0:T(8,128)S(1)}, u32[]{:S(2)}) copy-start(f32[2,256,1152]{2,1,0:T(8,128)S(1)} %fusion.1) | copy-start | bytes 7077892
  64.3 6.8 %collective-permute-start.10 = (bf16[1152,256]{0,1:T(8,128)(2,1)}, bf16[1152,256]{0,1:T(8,128)(2,1)}, u32[]{:S(2)}, u32[]{:S(2)}) collective-permute-start(bf16[1152,256]{0,1:T(8,128)(2,1)} %fusion.48), channel_id=1, source_target_pairs={{0,1},{1,0},{2,3},{3,2},{4,5},{5,4},{6,7},{7,6},{8,9},{9,8},{10,11... | collective-permute-start | bytes 1769480 | tf_op jit(solution)/shard_map/ppermute | solution.py:42
  66.8 15.1 %all-to-all-start = ((bf16[4,4,72,256]{3,2,1,0:T(8,128)(2,1)}), bf16[4,4,72,256]{3,2,1,0:T(8,128)(2,1)S(1)}, u32[]{:S(2)}, u32[]{:S(2)}) async-start(bf16[4,4,72,256]{3,2,1,0:T(8,128)(2,1)} %copy.14), calls=%async_computation | async-start | bytes 1179648 | tf_op jit(solution)/shard_map/all_to_all | solution.py:45
  75.7 49.5 %copy-start.4 = (f32[1,36]{1,0:T(1,128)S(1)}, f32[1,36]{1,0:T(1,128)}, u32[]{:S(2)}) copy-start(f32[1,36]{1,0:T(1,128)} %param.10) | copy-start | bytes 436
  82.0 13.4 %all-to-all-start.2 = ((bf16[4,4,72,256]{3,2,1,0:T(8,128)(2,1)}), bf16[4,4,72,256]{3,2,1,0:T(8,128)(2,1)S(1)}, u32[]{:S(2)}, u32[]{:S(2)}) async-start(bf16[4,4,72,256]{3,2,1,0:T(8,128)(2,1)} %copy.16), calls=%async_computation.2 | async-start | bytes 1179648 | tf_op jit(solution)/shard_map/all_to_all | solution.py:45
  95.4 19.0 %all-to-all-start.1 = ((bf16[4,72,256]{2,1,0:T(8,128)(2,1)}), bf16[4,72,256]{2,1,0:T(8,128)(2,1)S(1)}, u32[]{:S(2)}, u32[]{:S(2)}) async-start(bf16[4,72,256]{2,1,0:T(8,128)(2,1)} %reduce_sum.42), calls=%async_computation.1 | async-start | bytes 294912 | tf_op jit(solution)/shard_map/all_to_all | solution.py:47
  114.4 9.3 %all-to-all-start.3 = ((bf16[4,72,256]{2,1,0:T(8,128)(2,1)}), bf16[4,72,256]{2,1,0:T(8,128)(2,1)S(1)}, u32[]{:S(2)}, u32[]{:S(2)}) async-start(bf16[4,72,256]{2,1,0:T(8,128)(2,1)} %reduce_sum.44), calls=%async_computation.3 | async-start | bytes 294912 | tf_op jit(solution)/shard_map/all_to_all | solution.py:47
  123.7 1.4 %collective-permute-start.11 = (f32[2,36,256]{2,1,0:T(8,128)S(1)}, f32[2,36,256]{2,1,0:T(8,128)S(1)}, u32[]{:S(2)}, u32[]{:S(2)}) collective-permute-start(f32[2,36,256]{2,1,0:T(8,128)S(1)} %get-tuple-element.8), channel_id=1, source_target_pairs={{0,1},{1,0},{2,3},{3,2},{4,5},{5,4},{6,7},{7,6},{8,9},{9,8},{10,11... | collective-permute-start | bytes 221192 | tf_op jit(solution)/shard_map/ppermute | solution.py:68

commit v2 on v0

v2 whole, which is shorter than its diff:
```python
import functools

import jax
import jax.numpy as jnp
from jax import lax
from jax.experimental import pallas as pl
from jax.experimental.pallas import tpu as pltpu
from jax.sharding import PartitionSpec as P

SEQ = 128
BF = jnp.bfloat16
F32 = jnp.float32

NX, NZ = 4, 4
PARTNER = [(i, i ^ 1) for i in range(32)]


def feat_at(z, x, c):
    return z * 8 + x * 2 + c


def x_pairs(by):
    return [
        (feat_at(z, x, c), feat_at(z, (x + by) % NX, c))
        for z in range(NZ) for x in range(NX) for c in range(2)
    ]


ZC_GROUPS = [[feat_at(z, x, c) for z in range(NZ) for c in range(2)] for x in range(NX)]


def whole(shape):
    return pl.BlockSpec(shape, lambda *_: (0,) * len(shape))


def encode_kernel(at_ref, len_ref, resid_ref, weight_ref, bias_ref, keep_ref, send_ref, total):
    step = pl.program_id(0)
    term = jnp.dot(resid_ref[0], weight_ref[0], preferred_element_type=F32)

    @pl.when(step == 0)
    def _():
        total[...] = term

    @pl.when(step > 0)
    def _():
        total[...] += term

    @pl.when(step == pl.num_programs(0) - 1)
    def _():
        core = at_ref[0]
        for ref, half in ((keep_ref, core), (send_ref, 1 - core)):
            for s in range(2):
                seq = half * 2 + s
                pre = total[pl.ds(pl.multiple_of(seq * SEQ, SEQ), SEQ), :] + bias_ref[...]
                row = lax.broadcasted_iota(jnp.int32, pre.shape, 0)
                acts = jnp.where(row < len_ref[seq], jnp.maximum(pre, 0.0), 0.0)
                ref[s * SEQ : (s + 1) * SEQ, :] = acts.astype(BF)


def encode(at, lengths, resid, weight, bias):
    rows, depth = resid.shape[1:]
    feats = weight.shape[2]
    tile = 384
    half = jax.ShapeDtypeStruct((rows // 2, feats), BF)
    return pl.pallas_call(
        encode_kernel,
        out_shape=(half, half),
        grid_spec=pltpu.PrefetchScalarGridSpec(
            num_scalar_prefetch=2,
            grid=(depth // tile,),
            in_specs=[
                pl.BlockSpec((1, rows, tile), lambda k, *_: (0, 0, k)),
                pl.BlockSpec((1, tile, feats), lambda k, *_: (0, k, 0)),
                whole((1, feats)),
            ],
            out_specs=(whole(half.shape), whole(half.shape)),
            scratch_shapes=[pltpu.VMEM((rows, feats), F32)],
        ),
        cost_estimate=pl.CostEstimate(
            flops=2 * rows * depth * feats, bytes_accessed=2 * depth * (rows + feats), transcendentals=0
        ),
        name="encode",
    )(at, lengths, resid, weight, bias)


TILE = 384


def weight_specs(back):
    at = lambda n, at_ref: (0, jnp.maximum(at_ref[1] - back, 0), 0, n)
    return [pl.BlockSpec((1, 1, 512, TILE), at)] * 2


def add_terms(backs, at_ref, refs, total_ref):
    for i, back in enumerate(backs):
        mine, theirs, w_mine, w_theirs = refs[4 * i : 4 * i + 4]

        def add(mine=mine, theirs=theirs, w_mine=w_mine, w_theirs=w_theirs):
            term = jnp.dot(mine[...], w_mine[0, 0], preferred_element_type=F32)
            term += jnp.dot(theirs[...], w_theirs[0, 0], preferred_element_type=F32)
            total_ref[...] += term

        if back:
            pl.when(at_ref[1] >= back)(add)
        else:
            add()


def partial_kernel(backs, has_base, at_ref, *refs):
    total_ref = refs[-1]
    if has_base:
        total_ref[...] = refs[0][...]
        refs = refs[1:]
    else:
        total_ref[...] = jnp.zeros_like(total_ref)
    add_terms(backs, at_ref, refs, total_ref)


def term_operands(terms, w_mine, w_theirs):
    specs, operands = [], []
    for back, (mine, theirs) in terms:
        for array, index in (mine, theirs):
            if array.ndim == 3:
                specs.append(pl.BlockSpec((pl.Squeezed(), *array.shape[1:]), lambda n, *_, i=index: (i, 0, 0)))
            else:
                specs.append(whole(array.shape))
            operands.append(array)
        specs += weight_specs(back)
        operands += [w_mine, w_theirs]
    return specs, operands


def cost(terms, rows):
    n = 2 * len(terms)
    return pl.CostEstimate(
        flops=2 * n * rows * 512 * 1152, bytes_accessed=n * 512 * 1152 * 2 + rows * 1152 * 8, transcendentals=0
    )


def partial(at, terms, w_mine, w_theirs, base=None):
    rows, cols = terms[0][1][0][0].shape[-2], w_mine.shape[3]
    specs, operands = term_operands(terms, w_mine, w_theirs)
    tile = pl.BlockSpec((rows, TILE), lambda n, *_: (0, n))
    if base is not None:
        specs, operands = [tile] + specs, [base] + operands
    return pl.pallas_call(
        functools.partial(partial_kernel, [b for b, _ in terms], base is not None),
        out_shape=jax.ShapeDtypeStruct((rows, cols), F32),
        grid_spec=pltpu.PrefetchScalarGridSpec(
            num_scalar_prefetch=1, grid=(cols // TILE,), in_specs=specs, out_specs=tile
        ),
        cost_estimate=cost(terms, rows),
        name="partial",
    )(at, *operands)


def last_kernel(backs, at_ref, base_ref, *refs):
    turned, total_ref = refs[-2:]
    self_ref, *away = refs[-6:-2]
    n = pl.program_id(0)
    total_ref[...] = base_ref[...]
    add_terms(backs, at_ref, refs, total_ref)
    turned[pl.ds(pl.multiple_of(n * TILE, TILE), TILE), :] = total_ref[...].T

    @pl.when(n == pl.num_programs(0) - 1)
    def _():
        for by in range(NX):
            owner = lax.rem(at_ref[2] + by, NX)
            for z in range(NZ):
                piece = turned[pl.ds(pl.multiple_of((z * NX + owner) * 72, 8), 72), :]
                if by == 0:
                    self_ref[z] = piece
                else:
                    away[by - 1][z] = piece.astype(BF)


def last(at, base, terms, w_mine, w_theirs):
    rows, cols = base.shape
    specs, operands = term_operands(terms, w_mine, w_theirs)
    tile = pl.BlockSpec((rows, TILE), lambda n, *_: (0, n))
    piece = (NZ, cols // (NX * NZ), rows)
    return pl.pallas_call(
        functools.partial(last_kernel, [b for b, _ in terms]),
        out_shape=[jax.ShapeDtypeStruct(piece, F32)] + [jax.ShapeDtypeStruct(piece, BF)] * 3,
        grid_spec=pltpu.PrefetchScalarGridSpec(
            num_scalar_prefetch=1,
            grid=(cols // TILE,),
            in_specs=[tile] + specs,
            out_specs=[whole(piece)] * 4,
            scratch_shapes=[pltpu.VMEM((cols, rows), F32), pltpu.VMEM((rows, TILE), F32)],
        ),
        cost_estimate=cost(terms, rows),
        name="last",
    )(at, base, *operands)


def x_sum_kernel(self_ref, a_ref, b_ref, c_ref, out_ref):
    for z in range(NZ):
        total = self_ref[z] + a_ref[z].astype(F32) + b_ref[z].astype(F32) + c_ref[z].astype(F32)
        total = total.astype(BF)
        out_ref[2 * z] = total[:36]
        out_ref[2 * z + 1] = total[36:]


def reduce_features(pieces):
    kept, *away = pieces
    came = [lax.ppermute(piece, "feat", x_pairs(by + 1)) for by, piece in enumerate(away)]
    rows = kept.shape[2]
    chips = pl.pallas_call(
        x_sum_kernel, out_shape=jax.ShapeDtypeStruct((2 * NZ, 36, rows), BF), name="x_sum"
    )(kept, *came)
    return lax.all_to_all(chips, "feat", 0, 0, tiled=True, axis_index_groups=ZC_GROUPS)


def final_kernel(at_ref, own_ref, other_ref, bias_ref, out_ref):
    for ref, flip in ((own_ref, 0), (other_ref, 1)):
        for c in range(2):
            total = bias_ref[...]
            for z in range(NZ):
                total = total + ref[2 * z + c].astype(F32)
            total = total.astype(BF)
            for dp in range(2):

                @pl.when(at_ref[3] == dp)
                def _(total=total, start=((dp + flip) % 2) * 512 + c * 256):
                    out_ref[:, start : start + 256] = total


def finish(at, own, other, bias):
    return pl.pallas_call(
        final_kernel,
        out_shape=jax.ShapeDtypeStruct((36, 1024), BF),
        grid_spec=pltpu.PrefetchScalarGridSpec(
            num_scalar_prefetch=1,
            grid=(1,),
            in_specs=[whole(own.shape), whole(other.shape), whole(bias.shape)],
            out_specs=whole((36, 1024)),
        ),
        name="finish",
    )(at, own, other, bias)


def per_device(resid, enc_weight, enc_bias, dec_weight, dec_bias, lengths):
    target, feat, dp = lax.axis_index("layer"), lax.axis_index("feat"), lax.axis_index("dp")
    at = jnp.stack([feat % 2, target, feat // 2 % NX, dp]).astype(jnp.int32)
    theirs_w = lax.ppermute(dec_weight, "feat", PARTNER)
    keep, send = encode(at, lengths, resid, enc_weight, enc_bias)
    across = lambda flip: [(d * 32 + f, (1 - d) * 32 + (f ^ flip)) for d in range(2) for f in range(32)]
    other_mine = lax.ppermute(keep, ("dp", "feat"), across(0))
    other_theirs = lax.ppermute(send, ("dp", "feat"), across(1))
    own_theirs = lax.ppermute(send, "feat", PARTNER)
    results = []
    for mine, theirs in ((keep, own_theirs), (other_mine, other_theirs)):
        acts = jnp.stack([mine, theirs])
        up = lax.ppermute(acts, "layer", [(0, 1), (1, 2), (2, 3)])
        down = lax.ppermute(acts, "layer", [(0, 3), (1, 0)])
        far_up = lax.ppermute(up[0], "layer", [(1, 2), (2, 3)])
        far_down = lax.ppermute(down[1], "layer", [(3, 2), (0, 3)])
        total = partial(at, [(0, ((acts, 0), (acts, 1)))], dec_weight, theirs_w)
        total = partial(
            at,
            [(1, ((up, 0), (up, 1))), (3, ((down, 0), (down, 1)))],
            dec_weight, theirs_w, total,
        )
        pieces = last(at, total, [(2, ((far_up, 0), (far_down, 0)))], dec_weight, theirs_w)
        results.append(reduce_features(pieces))
    out = finish(at, *results, dec_bias.reshape(36, 1))
    return out.T[None]


def solution(mesh):
    in_specs = (
        P("layer", "dp", None),
        P("layer", None, "feat"),
        P("layer", "feat"),
        P("layer", None, "feat", "dp"),
        P("layer", ("dp", "feat")),
        P("dp"),
    )
    out_specs = P("layer", None, ("dp", "feat"))
    return jax.shard_map(
        per_device, mesh=mesh, in_specs=in_specs, out_specs=out_specs, check_vma=False
    )
```

time: 213 us -> 152 us (0.71)
  blocking collectives: 121 us -> 0 us
  Pallas kernels: 0 us -> 48.7 us
  starting transfers between devices: 9.69 us -> 49.5 us
  matrix products: 27.7 us -> 0 us
    unnamed x1 -> x0, blocking collectives: 84.5 us -> none
    pallas_call x0 -> x10, Pallas kernels: none -> 48.7 us  [the longest x4 23.7 us: partial(): pl.pallas_call(functools.partial(partial_kernel, [b for b, _ in terms], b...]
    all_to_all x1 -> x0, blocking collectives: 36.1 us -> none  [copy_for_each(): return lax.all_to_all(copies, axis, split_axis=0, concat_axis=0, tiled=True)]
    ppermute x3 -> x18, starting transfers between devices: 3.84 us -> 32.9 us  [the longest x6 9.77 us: reduce_features(): lax.ppermute(piece, 'feat', x_pairs(by + 1))]
    dot_general x5 -> x0, matrix products: 27.7 us -> none  [the longest x4 24.6 us: apply_cols(): jnp.einsum('fc,rf->cr', matrix, block, preferred_element_type=jnp.float32)]
    all_to_all x0 -> x2, starting transfers between devices: none -> 16.6 us  [reduce_features(): lax.all_to_all(chips, 'feat', 0, 0, tiled=True, axis_index_groups=ZC_GROUPS)]
    ppermute x3 -> x18, waiting for transfers between devices: 44.2 us -> 37.4 us  [the longest x2 13.8 us: per_device(): up = lax.ppermute(acts, 'layer', [(0, 1), (1, 2), (2, 3)])]
    all_to_all x0 -> x2, waiting for transfers between devices: none -> 6.47 us  [reduce_features(): lax.all_to_all(chips, 'feat', 0, 0, tiled=True, axis_index_groups=ZC_GROUPS)]
  transfers between devices with their start and end apart: 7 -> 20, of which waited for: 3 -> 10; matrix products, arithmetic and copies ran while one was open for 9% -> 4% of each run, Pallas kernels for 0% -> 31%
where the time goes in v2:
time: 152 us; the launch traced here: 150 us
  starting transfers between devices  49.5 us (33%)
  Pallas kernels  48.7 us (32%)
  waiting for transfers between devices  43.9 us (29%)
  local copies, waits for them, and re-layouts  6.56 us (4%)
  other arithmetic  1.63 us (1%)
    pallas_call x4, Pallas kernels, partial(): pl.pallas_call(functools.partial(partial_kernel, [b for b, _ in terms], b...  23.7 us
    all_to_all x2, starting transfers between devices, reduce_features(): lax.all_to_all(chips, 'feat', 0, 0, tiled=True, axis_index_groups=ZC_GROUPS)  16.6 us
    ppermute x2, waiting for transfers between devices, per_device(): up = lax.ppermute(acts, 'layer', [(0, 1), (1, 2), (2, 3)])  13.8 us
    pallas_call x2, Pallas kernels, last(): pl.pallas_call(functools.partial(last_kernel, [b for b, _ in terms]), out...  11.4 us
    ppermute x6, starting transfers between devices, reduce_features(): lax.ppermute(piece, 'feat', x_pairs(by + 1))  9.77 us
    ppermute x1, waiting for transfers between devices, per_device(): other_mine = lax.ppermute(keep, ('dp', 'feat'), across(0))  8.39 us
    ppermute x2, starting transfers between devices, per_device(): far_down = lax.ppermute(down[1], 'layer', [(3, 2), (0, 3)])  8.03 us
    ppermute x6, waiting for transfers between devices, reduce_features(): lax.ppermute(piece, 'feat', x_pairs(by + 1))  7.31 us
  transfers between devices with their start and end apart: 20, of which 10 were waited for; matrix products, arithmetic and copies ran while one was open for 4% of the time, Pallas kernels for 31%

profile of v2, /device:TPU:24, one launch (start us, length us, event | category | flops | bytes accessed | tf_op | source)
XLA Modules:
  0.0 150.5 jit_solution(4704121712778746833)
XLA Ops:
  0.6 7.2 %encode.1 = (bf16[256,512]{1,0:T(8,128)(2,1)}, bf16[256,512]{1,0:T(8,128)(2,1)}) custom-call(s32[4]{0:T(128)} %pad_add_fusion.at_ref, s32[4]{0:T(128)} %len_ref.1, bf16[1,512,2304]{2,1,0:T(8,128)(2,1)} %resid_ref.1, bf16[1,2304,512]{2,1,0:T(8,128)(2,1)} %weight_ref.1, f32[1,512]{1,0:T(1,128)} %bias_ref.1), custom_call_target="tpu_custom_call" | custom-call | flops 1207959552 | bytes 4718592 | tf_op jit(solution)/shard_map/encode/pallas_call | solution.py:65
  7.8 7.2 %collective-permute-start.9 = (bf16[256,512]{1,0:T(8,128)(2,1)}, bf16[256,512]{1,0:T(8,128)(2,1)S(1)}, u32[]{:S(2)}, u32[]{:S(2)}) collective-permute-start(bf16[256,512]{1,0:T(8,128)(2,1)} %get-tuple-element.15), channel_id=1, source_target_pairs={{0,128},{1,129},{2,130},{3,131},{4,132},{5,133},{6,134},{7,135},{8... | collective-permute-start | bytes 786440 | tf_op jit(solution)/shard_map/ppermute | solution.py:249
  15.1 8.4 %collective-permute-done.9 = bf16[256,512]{1,0:T(8,128)(2,1)S(1)} collective-permute-done((bf16[256,512]{1,0:T(8,128)(2,1)}, bf16[256,512]{1,0:T(8,128)(2,1)S(1)}, u32[]{:S(2)}, u32[]{:S(2)}) %collective-permute-start.9) | collective-permute-done | bytes 262176 | tf_op jit(solution)/shard_map/ppermute | solution.py:249
  23.5 6.4 %collective-permute-done.10 = bf16[256,512]{1,0:T(8,128)(2,1)S(1)} collective-permute-done((bf16[256,512]{1,0:T(8,128)(2,1)}, bf16[256,512]{1,0:T(8,128)(2,1)S(1)}, u32[]{:S(2)}, u32[]{:S(2)}) %collective-permute-start.10) | collective-permute-done | bytes 262176 | tf_op jit(solution)/shard_map/ppermute | solution.py:250
  36.7 9.9 %collective-permute-done.11.refs_1_.refs_2_ = bf16[2,256,512]{2,1,0:T(8,128)(2,1)S(1)} collective-permute-done((bf16[2,256,512]{2,1,0:T(8,128)(2,1)S(1)}, bf16[2,256,512]{2,1,0:T(8,128)(2,1)S(1)}, u32[]{:S(2)}, u32[]{:S(2)}) %collective-permute-start.11) | collective-permute-done | bytes 524320 | tf_op jit(solution)/shard_map/ppermute | solution.py:255
  50.0 4.0 %collective-permute-start.14 = (bf16[256,512]{1,0:T(8,128)(2,1)}, bf16[256,512]{1,0:T(8,128)(2,1)}, u32[]{:S(2)}, u32[]{:S(2)}) collective-permute-start(bf16[256,512]{1,0:T(8,128)(2,1)} %slice_bitcast_fusion), channel_id=1, source_target_pairs={{96,64},{0,96},{97,65},{1,97},{98,66},{2,98},{99,67},{3,99},{100,6... | collective-permute-start | bytes 786440 | tf_op jit(solution)/shard_map/ppermute | solution.py:258
  54.0 3.8 %collective-permute-done.2.refs_1_.refs_2_ = bf16[2,256,512]{2,1,0:T(8,128)(2,1)S(1)} collective-permute-done((bf16[2,256,512]{2,1,0:T(8,128)(2,1)S(1)}, bf16[2,256,512]{2,1,0:T(8,128)(2,1)S(1)}, u32[]{:S(2)}, u32[]{:S(2)}) %collective-permute-start.2) | collective-permute-done | bytes 524320 | tf_op jit(solution)/shard_map/ppermute | solution.py:255
  61.2 4.0 %collective-permute-start.5 = (bf16[256,512]{1,0:T(8,128)(2,1)}, bf16[256,512]{1,0:T(8,128)(2,1)}, u32[]{:S(2)}, u32[]{:S(2)}) collective-permute-start(bf16[256,512]{1,0:T(8,128)(2,1)} %slice_bitcast_fusion.2), channel_id=1, source_target_pairs={{96,64},{0,96},{97,65},{1,97},{98,66},{2,98},{99,67},{3,99},{100,6... | collective-permute-start | bytes 786440 | tf_op jit(solution)/shard_map/ppermute | solution.py:258
  65.3 4.9 %partial.6.refs_0_ = f32[256,1152]{1,0:T(8,128)} custom-call(s32[4]{0:T(128)} %pad_add_fusion.at_ref, bf16[2,256,512]{2,1,0:T(8,128)(2,1)} %copy-done.1, bf16[2,256,512]{2,1,0:T(8,128)(2,1)} %copy-done.1, bf16[1,4,512,1152]{3,2,1,0:T(8,128)(2,1)} %refs_2_.7, bf16[1,4,512,1152]{3,2,1,0:T(8,128)(2,1)} %collective-permute-done.1.refs_3_.refs_4_.refs_8_), custom_call_target="tpu_custom_call" | custom-call | flops 603979776 | bytes 4718592 | tf_op jit(solution)/shard_map/partial/pallas_call | solution.py:146
  70.2 7.0 %partial.7.base_ref = f32[256,1152]{1,0:T(8,128)} custom-call(s32[4]{0:T(128)} %pad_add_fusion.at_ref, f32[256,1152]{1,0:T(8,128)} %partial.6.refs_0_, bf16[2,256,512]{2,1,0:T(8,128)(2,1)} %copy-done.4, bf16[2,256,512]{2,1,0:T(8,128)(2,1)} %copy-done.4, bf16[1,4,512,1152]{3,2,1,0:T(8,128)(2,1)} %refs_2_.7, ...), custom_call_target="tpu_custom_call" | custom-call | flops 1207959552 | bytes 7077888 | tf_op jit(solution)/shard_map/partial/pallas_call | solution.py:146
  77.2 5.7 %last.3 = (f32[4,72,256]{2,1,0:T(8,128)}, bf16[4,72,256]{2,1,0:T(8,128)(2,1)}, bf16[4,72,256]{2,1,0:T(8,128)(2,1)}, bf16[4,72,256]{2,1,0:T(8,128)(2,1)}) custom-call(s32[4]{0:T(128)} %pad_add_fusion.at_ref, f32[256,1152]{1,0:T(8,128)} %partial.7.base_ref, bf16[256,512]{1,0:T(8,128)(2,1)} %collective-permute-done.13.refs_0_, ...), custom_call_target="tpu_custom_call" | custom-call | flops 603979776 | bytes 4718592 | tf_op jit(solution)/shard_map/last/pallas_call | solution.py:182
  82.9 1.5 collective-permute-start.15
  84.4 2.8 %collective-permute-start.16 = (bf16[4,72,256]{2,1,0:T(8,128)(2,1)}, bf16[4,72,256]{2,1,0:T(8,128)(2,1)S(1)}, u32[]{:S(2)}, u32[]{:S(2)}) collective-permute-start(bf16[4,72,256]{2,1,0:T(8,128)(2,1)} %get-tuple-element.23), channel_id=1, source_target_pairs={{0,4},{1,5},{2,6},{3,7},{4,0},{5,1},{6,2},{7,3},{8,12},{9,13},{10,... | collective-permute-start | bytes 442376 | tf_op jit(solution)/shard_map/ppermute | solution.py:207
  88.5 4.9 %partial.4.refs_0_ = f32[256,1152]{1,0:T(8,128)} custom-call(s32[4]{0:T(128)} %pad_add_fusion.at_ref, bf16[2,256,512]{2,1,0:T(8,128)(2,1)} %copy-done, bf16[2,256,512]{2,1,0:T(8,128)(2,1)} %copy-done, bf16[1,4,512,1152]{3,2,1,0:T(8,128)(2,1)} %refs_2_.7, bf16[1,4,512,1152]{3,2,1,0:T(8,128)(2,1)} %collective-permute-done.1.refs_3_.refs_4_.refs_8_), custom_call_target="tpu_custom_call" | custom-call | flops 603979776 | bytes 4718592 | tf_op jit(solution)/shard_map/partial/pallas_call | solution.py:146
  94.2 1.9 %x_sum.3 = bf16[8,36,256]{2,1,0:T(8,128)(2,1)} custom-call(f32[4,72,256]{2,1,0:T(8,128)} %get-tuple-element.21.self_ref, bf16[4,72,256]{2,1,0:T(8,128)(2,1)} %copy-done.9, bf16[4,72,256]{2,1,0:T(8,128)(2,1)} %copy-done.11, bf16[4,72,256]{2,1,0:T(8,128)(2,1)} %copy-done.13), custom_call_target="tpu_custom_call" | custom-call | tf_op jit(solution)/shard_map/x_sum/pallas_call | solution.py:209
  96.1 11.9 %all-to-all-start.1 = ((bf16[8,36,256]{2,1,0:T(8,128)(2,1)}), bf16[8,36,256]{2,1,0:T(8,128)(2,1)S(1)}, u32[]{:S(2)}, u32[]{:S(2)}) async-start(bf16[8,36,256]{2,1,0:T(8,128)(2,1)} %x_sum.3), calls=%async_computation.1 | async-start | bytes 327680 | tf_op jit(solution)/shard_map/all_to_all | solution.py:212
  108.0 6.9 %partial.5.base_ref = f32[256,1152]{1,0:T(8,128)} custom-call(s32[4]{0:T(128)} %pad_add_fusion.at_ref, f32[256,1152]{1,0:T(8,128)} %partial.4.refs_0_, bf16[2,256,512]{2,1,0:T(8,128)(2,1)} %copy-done.2, bf16[2,256,512]{2,1,0:T(8,128)(2,1)} %copy-done.2, bf16[1,4,512,1152]{3,2,1,0:T(8,128)(2,1)} %refs_2_.7, ...), custom_call_target="tpu_custom_call" | custom-call | flops 1207959552 | bytes 7077888 | tf_op jit(solution)/shard_map/partial/pallas_call | solution.py:146
  115.6 5.7 %last.2 = (f32[4,72,256]{2,1,0:T(8,128)}, bf16[4,72,256]{2,1,0:T(8,128)(2,1)}, bf16[4,72,256]{2,1,0:T(8,128)(2,1)}, bf16[4,72,256]{2,1,0:T(8,128)(2,1)}) custom-call(s32[4]{0:T(128)} %pad_add_fusion.at_ref, f32[256,1152]{1,0:T(8,128)} %partial.5.base_ref, bf16[256,512]{1,0:T(8,128)(2,1)} %copy-done.8, bf16[256,512]{1,0:T(8,128)(2,1)} %collective-permute-done.5.refs_1_, ...), custom_call_target="tpu_custom_call" | custom-call | flops 603979776 | bytes 4718592 | tf_op jit(solution)/shard_map/last/pallas_call | solution.py:182
  121.9 2.4 %collective-permute-start.7 = (bf16[4,72,256]{2,1,0:T(8,128)(2,1)}, bf16[4,72,256]{2,1,0:T(8,128)(2,1)S(1)}, u32[]{:S(2)}, u32[]{:S(2)}) collective-permute-start(bf16[4,72,256]{2,1,0:T(8,128)(2,1)} %get-tuple-element.19), channel_id=1, source_target_pairs={{0,4},{1,5},{2,6},{3,7},{4,0},{5,1},{6,2},{7,3},{8,12},{9,13},{10,... | collective-permute-start | bytes 442376 | tf_op jit(solution)/shard_map/ppermute | solution.py:207
  125.5 6.7 %collective-permute-done.6.a_ref = bf16[4,72,256]{2,1,0:T(8,128)(2,1)S(1)} collective-permute-done((bf16[4,72,256]{2,1,0:T(8,128)(2,1)}, bf16[4,72,256]{2,1,0:T(8,128)(2,1)S(1)}, u32[]{:S(2)}, u32[]{:S(2)}) %collective-permute-start.6) | collective-permute-done | bytes 147488 | tf_op jit(solution)/shard_map/ppermute | solution.py:207
  133.4 1.9 %x_sum.2 = bf16[8,36,256]{2,1,0:T(8,128)(2,1)} custom-call(f32[4,72,256]{2,1,0:T(8,128)} %get-tuple-element.17.self_ref, bf16[4,72,256]{2,1,0:T(8,128)(2,1)} %copy-done.10, bf16[4,72,256]{2,1,0:T(8,128)(2,1)} %copy-done.12, bf16[4,72,256]{2,1,0:T(8,128)(2,1)} %copy-done.14), custom_call_target="tpu_custom_call" | custom-call | tf_op jit(solution)/shard_map/x_sum/pallas_call | solution.py:209
  135.3 4.7 %all-to-all-start = ((bf16[8,36,256]{2,1,0:T(8,128)(2,1)}), bf16[8,36,256]{2,1,0:T(8,128)(2,1)S(1)}, u32[]{:S(2)}, u32[]{:S(2)}) async-start(bf16[8,36,256]{2,1,0:T(8,128)(2,1)} %x_sum.2), calls=%async_computation | async-start | bytes 327680 | tf_op jit(solution)/shard_map/all_to_all | solution.py:212
  140.7 6.5 %all-to-all-done.own_ref = bf16[8,36,256]{2,1,0:T(8,128)(2,1)S(1)} async-done(((bf16[8,36,256]{2,1,0:T(8,128)(2,1)}), bf16[8,36,256]{2,1,0:T(8,128)(2,1)S(1)}, u32[]{:S(2)}, u32[]{:S(2)}) %all-to-all-start) | async-done | bytes 147488 | tf_op jit(solution)/shard_map/all_to_all | solution.py:212
  147.9 2.6 %finish.1 = bf16[36,1024]{1,0:T(8,128)(2,1)} custom-call(s32[4]{0:T(128)} %pad_add_fusion.at_ref, bf16[8,36,256]{2,1,0:T(8,128)(2,1)} %copy-done.7, bf16[8,36,256]{2,1,0:T(8,128)(2,1)} %copy-done.6, f32[36,1]{1,0:T(8,128)} %copy.7.bias_ref), custom_call_target="tpu_custom_call" | custom-call | tf_op jit(solution)/shard_map/finish/pallas_call | solution.py:230
  (66 shorter events, 21.4 us)
Async XLA Ops:
  0.0 65.3 %collective-permute-start.1 = (bf16[1,4,512,1152]{3,2,1,0:T(8,128)(2,1)}, bf16[1,4,512,1152]{3,2,1,0:T(8,128)(2,1)}, u32[]{:S(2)}, u32[]{:S(2)}) collective-permute-start(bf16[1,4,512,1152]{3,2,1,0:T(8,128)(2,1)} %refs_2_.7), channel_id=1, source_target_pairs={{0,1},{1,0},{2,3},{3,2},{4,5},{5,4},{6,7},{7,6},{8,9},{9,8},{10,11... | collective-permute-start | bytes 14155784 | tf_op jit(solution)/shard_map/ppermute | solution.py:246
  7.8 15.7 %collective-permute-start.9 = (bf16[256,512]{1,0:T(8,128)(2,1)}, bf16[256,512]{1,0:T(8,128)(2,1)S(1)}, u32[]{:S(2)}, u32[]{:S(2)}) collective-permute-start(bf16[256,512]{1,0:T(8,128)(2,1)} %get-tuple-element.15), channel_id=1, source_target_pairs={{0,128},{1,129},{2,130},{3,131},{4,132},{5,133},{6,134},{7,135},{8... | collective-permute-start | bytes 786440 | tf_op jit(solution)/shard_map/ppermute | solution.py:249
  15.0 14.9 %collective-permute-start.10 = (bf16[256,512]{1,0:T(8,128)(2,1)}, bf16[256,512]{1,0:T(8,128)(2,1)S(1)}, u32[]{:S(2)}, u32[]{:S(2)}) collective-permute-start(bf16[256,512]{1,0:T(8,128)(2,1)} %get-tuple-element.16), channel_id=1, source_target_pairs={{0,129},{1,128},{2,131},{3,130},{4,133},{5,132},{6,135},{7,134},{8... | collective-permute-start | bytes 786440 | tf_op jit(solution)/shard_map/ppermute | solution.py:250
  29.9 35.4 %copy-start.1 = (bf16[2,256,512]{2,1,0:T(8,128)(2,1)}, bf16[2,256,512]{2,1,0:T(8,128)(2,1)S(1)}, u32[]{:S(2)}) copy-start(bf16[2,256,512]{2,1,0:T(8,128)(2,1)S(1)} %pad_maximum_fusion.1.refs_0_.refs_1_) | copy-start | bytes 1572868
  29.9 16.7 %collective-permute-start.11 = (bf16[2,256,512]{2,1,0:T(8,128)(2,1)S(1)}, bf16[2,256,512]{2,1,0:T(8,128)(2,1)S(1)}, u32[]{:S(2)}, u32[]{:S(2)}) collective-permute-start(bf16[2,256,512]{2,1,0:T(8,128)(2,1)S(1)} %pad_maximum_fusion.1.refs_0_.refs_1_), channel_id=1, source_target_pairs={{0,32},{32,64},{64,96},{1,33},{33,65},{65,97},{2,34},{34,66},{66,9... | collective-permute-start | bytes 1572872 | tf_op jit(solution)/shard_map/ppermute | solution.py:255
  31.2 1.8 %collective-permute-start = (bf16[256,512]{1,0:T(8,128)(2,1)}, bf16[256,512]{1,0:T(8,128)(2,1)S(1)}, u32[]{:S(2)}, u32[]{:S(2)}) collective-permute-start(bf16[256,512]{1,0:T(8,128)(2,1)} %get-tuple-element.16), channel_id=1, source_target_pairs={{0,1},{1,0},{2,3},{3,2},{4,5},{5,4},{6,7},{7,6},{8,9},{9,8},{10,11... | collective-permute-start | bytes 786440 | tf_op jit(solution)/shard_map/ppermute | solution.py:251
  31.3 17.9 %collective-permute-start.12 = (bf16[2,256,512]{2,1,0:T(8,128)(2,1)S(1)}, bf16[2,256,512]{2,1,0:T(8,128)(2,1)S(1)}, u32[]{:S(2)}, u32[]{:S(2)}) collective-permute-start(bf16[2,256,512]{2,1,0:T(8,128)(2,1)S(1)} %pad_maximum_fusion.1.refs_0_.refs_1_), channel_id=1, source_target_pairs={{0,96},{32,0},{1,97},{33,1},{2,98},{34,2},{3,99},{35,3},{4,100},{3... | collective-permute-start | bytes 1572872 | tf_op jit(solution)/shard_map/ppermute | solution.py:256
  34.1 36.1 %copy-start = (bf16[2,256,512]{2,1,0:T(8,128)(2,1)}, bf16[2,256,512]{2,1,0:T(8,128)(2,1)S(1)}, u32[]{:S(2)}) copy-start(bf16[2,256,512]{2,1,0:T(8,128)(2,1)S(1)} %pad_maximum_fusion.refs_0_.refs_1_) | copy-start | bytes 1572868
  34.1 23.8 %collective-permute-start.2 = (bf16[2,256,512]{2,1,0:T(8,128)(2,1)S(1)}, bf16[2,256,512]{2,1,0:T(8,128)(2,1)S(1)}, u32[]{:S(2)}, u32[]{:S(2)}) collective-permute-start(bf16[2,256,512]{2,1,0:T(8,128)(2,1)S(1)} %pad_maximum_fusion.refs_0_.refs_1_), channel_id=1, source_target_pairs={{0,32},{32,64},{64,96},{1,33},{33,65},{65,97},{2,34},{34,66},{66,9... | collective-permute-start | bytes 1572872 | tf_op jit(solution)/shard_map/ppermute | solution.py:255
  35.4 25.1 %collective-permute-start.3 = (bf16[2,256,512]{2,1,0:T(8,128)(2,1)S(1)}, bf16[2,256,512]{2,1,0:T(8,128)(2,1)S(1)}, u32[]{:S(2)}, u32[]{:S(2)}) collective-permute-start(bf16[2,256,512]{2,1,0:T(8,128)(2,1)S(1)} %pad_maximum_fusion.refs_0_.refs_1_), channel_id=1, source_target_pairs={{0,96},{32,0},{1,97},{33,1},{2,98},{34,2},{3,99},{35,3},{4,100},{3... | collective-permute-start | bytes 1572872 | tf_op jit(solution)/shard_map/ppermute | solution.py:256
  46.6 23.6 %copy-start.4 = (bf16[2,256,512]{2,1,0:T(8,128)(2,1)}, bf16[2,256,512]{2,1,0:T(8,128)(2,1)S(1)}, u32[]{:S(2)}) copy-start(bf16[2,256,512]{2,1,0:T(8,128)(2,1)S(1)} %collective-permute-done.11.refs_1_.refs_2_) | copy-start | bytes 1572868
  47.4 29.8 %collective-permute-start.13 = (bf16[256,512]{1,0:T(8,128)(2,1)}, bf16[256,512]{1,0:T(8,128)(2,1)}, u32[]{:S(2)}, u32[]{:S(2)}) collective-permute-start(bf16[256,512]{1,0:T(8,128)(2,1)} %slice_bitcast_fusion.1), channel_id=1, source_target_pairs={{32,64},{64,96},{33,65},{65,97},{34,66},{66,98},{35,67},{67,99},{3... | collective-permute-start | bytes 786440 | tf_op jit(solution)/shard_map/ppermute | solution.py:257
  50.0 27.2 %collective-permute-start.14 = (bf16[256,512]{1,0:T(8,128)(2,1)}, bf16[256,512]{1,0:T(8,128)(2,1)}, u32[]{:S(2)}, u32[]{:S(2)}) collective-permute-start(bf16[256,512]{1,0:T(8,128)(2,1)} %slice_bitcast_fusion), channel_id=1, source_target_pairs={{96,64},{0,96},{97,65},{1,97},{98,66},{2,98},{99,67},{3,99},{100,6... | collective-permute-start | bytes 786440 | tf_op jit(solution)/shard_map/ppermute | solution.py:258
  58.6 56.3 %collective-permute-start.4 = (bf16[256,512]{1,0:T(8,128)(2,1)}, bf16[256,512]{1,0:T(8,128)(2,1)S(1)}, u32[]{:S(2)}, u32[]{:S(2)}) collective-permute-start(bf16[256,512]{1,0:T(8,128)(2,1)} %slice_bitcast_fusion.3), channel_id=1, source_target_pairs={{32,64},{64,96},{33,65},{65,97},{34,66},{66,98},{35,67},{67,99},{3... | collective-permute-start | bytes 786440 | tf_op jit(solution)/shard_map/ppermute | solution.py:257
  61.2 53.7 %collective-permute-start.5 = (bf16[256,512]{1,0:T(8,128)(2,1)}, bf16[256,512]{1,0:T(8,128)(2,1)}, u32[]{:S(2)}, u32[]{:S(2)}) collective-permute-start(bf16[256,512]{1,0:T(8,128)(2,1)} %slice_bitcast_fusion.2), channel_id=1, source_target_pairs={{96,64},{0,96},{97,65},{1,97},{98,66},{2,98},{99,67},{3,99},{100,6... | collective-permute-start | bytes 786440 | tf_op jit(solution)/shard_map/ppermute | solution.py:258
  82.9 10.5 %collective-permute-start.15 = (bf16[4,72,256]{2,1,0:T(8,128)(2,1)}, bf16[4,72,256]{2,1,0:T(8,128)(2,1)S(1)}, u32[]{:S(2)}, u32[]{:S(2)}) collective-permute-start(bf16[4,72,256]{2,1,0:T(8,128)(2,1)} %get-tuple-element.22), channel_id=1, source_target_pairs={{0,2},{1,3},{2,4},{3,5},{4,6},{5,7},{6,0},{7,1},{8,10},{9,11},{10,... | collective-permute-start | bytes 442376 | tf_op jit(solution)/shard_map/ppermute | solution.py:207
  84.4 9.0 %collective-permute-start.16 = (bf16[4,72,256]{2,1,0:T(8,128)(2,1)}, bf16[4,72,256]{2,1,0:T(8,128)(2,1)S(1)}, u32[]{:S(2)}, u32[]{:S(2)}) collective-permute-start(bf16[4,72,256]{2,1,0:T(8,128)(2,1)} %get-tuple-element.23), channel_id=1, source_target_pairs={{0,4},{1,5},{2,6},{3,7},{4,0},{5,1},{6,2},{7,3},{8,12},{9,13},{10,... | collective-permute-start | bytes 442376 | tf_op jit(solution)/shard_map/ppermute | solution.py:207
  87.1 6.3 %collective-permute-start.17 = (bf16[4,72,256]{2,1,0:T(8,128)(2,1)}, bf16[4,72,256]{2,1,0:T(8,128)(2,1)S(1)}, u32[]{:S(2)}, u32[]{:S(2)}) collective-permute-start(bf16[4,72,256]{2,1,0:T(8,128)(2,1)} %get-tuple-element.24), channel_id=1, source_target_pairs={{0,6},{1,7},{2,0},{3,1},{4,2},{5,3},{6,4},{7,5},{8,14},{9,15},{10,... | collective-permute-start | bytes 442376 | tf_op jit(solution)/shard_map/ppermute | solution.py:207
  96.1 39.3 %all-to-all-start.1 = ((bf16[8,36,256]{2,1,0:T(8,128)(2,1)}), bf16[8,36,256]{2,1,0:T(8,128)(2,1)S(1)}, u32[]{:S(2)}, u32[]{:S(2)}) async-start(bf16[8,36,256]{2,1,0:T(8,128)(2,1)} %x_sum.3), calls=%async_computation.1 | async-start | bytes 327680 | tf_op jit(solution)/shard_map/all_to_all | solution.py:212
  114.9 25.1 %copy-start.15 = (f32[1,36]{1,0:T(1,128)S(1)}, f32[1,36]{1,0:T(1,128)}, u32[]{:S(2)}) copy-start(f32[1,36]{1,0:T(1,128)} %param.10) | copy-start | bytes 436
  121.3 10.8 %collective-permute-start.6 = (bf16[4,72,256]{2,1,0:T(8,128)(2,1)}, bf16[4,72,256]{2,1,0:T(8,128)(2,1)S(1)}, u32[]{:S(2)}, u32[]{:S(2)}) collective-permute-start(bf16[4,72,256]{2,1,0:T(8,128)(2,1)} %get-tuple-element.18), channel_id=1, source_target_pairs={{0,2},{1,3},{2,4},{3,5},{4,6},{5,7},{6,0},{7,1},{8,10},{9,11},{10,... | collective-permute-start | bytes 442376 | tf_op jit(solution)/shard_map/ppermute | solution.py:207
  121.9 10.3 %collective-permute-start.7 = (bf16[4,72,256]{2,1,0:T(8,128)(2,1)}, bf16[4,72,256]{2,1,0:T(8,128)(2,1)S(1)}, u32[]{:S(2)}, u32[]{:S(2)}) collective-permute-start(bf16[4,72,256]{2,1,0:T(8,128)(2,1)} %get-tuple-element.19), channel_id=1, source_target_pairs={{0,4},{1,5},{2,6},{3,7},{4,0},{5,1},{6,2},{7,3},{8,12},{9,13},{10,... | collective-permute-start | bytes 442376 | tf_op jit(solution)/shard_map/ppermute | solution.py:207
  124.3 8.5 %collective-permute-start.8 = (bf16[4,72,256]{2,1,0:T(8,128)(2,1)}, bf16[4,72,256]{2,1,0:T(8,128)(2,1)S(1)}, u32[]{:S(2)}, u32[]{:S(2)}) collective-permute-start(bf16[4,72,256]{2,1,0:T(8,128)(2,1)} %get-tuple-element.20), channel_id=1, source_target_pairs={{0,6},{1,7},{2,0},{3,1},{4,2},{5,3},{6,4},{7,5},{8,14},{9,15},{10,... | collective-permute-start | bytes 442376 | tf_op jit(solution)/shard_map/ppermute | solution.py:207
  135.3 11.9 %all-to-all-start = ((bf16[8,36,256]{2,1,0:T(8,128)(2,1)}), bf16[8,36,256]{2,1,0:T(8,128)(2,1)S(1)}, u32[]{:S(2)}, u32[]{:S(2)}) async-start(bf16[8,36,256]{2,1,0:T(8,128)(2,1)} %x_sum.2), calls=%async_computation | async-start | bytes 327680 | tf_op jit(solution)/shard_map/all_to_all | solution.py:212
  (12 other events, 60.4 us)

commit v3 on v0

v3 whole, which is shorter than its diff:
```python
import functools

import jax
import jax.numpy as jnp
from jax import lax
from jax.experimental import pallas as pl
from jax.experimental.pallas import tpu as pltpu
from jax.sharding import PartitionSpec as P


SEQ = 128
BF = jnp.bfloat16
F32 = jnp.float32

NX, NZ = 4, 4
PARTNER = [(i, i ^ 1) for i in range(32)]


def feat_at(z, x, c):
    return z * 8 + x * 2 + c


def x_pairs(by):
    return [
        (feat_at(z, x, c), feat_at(z, (x + by) % NX, c))
        for z in range(NZ) for x in range(NX) for c in range(2)
    ]


ZC_GROUPS = [[feat_at(z, x, c) for z in range(NZ) for c in range(2)] for x in range(NX)]


IN_VMEM = pl.BlockSpec(memory_space=pltpu.VMEM)
IN_SMEM = pl.BlockSpec(memory_space=pltpu.SMEM)
MIB = 1 << 20


def call(kernel, out_shape, operands, grant, scratch=(), flops=0):
    single = not isinstance(out_shape, (list, tuple))
    moved = sum(a.size * a.dtype.itemsize for a in operands)
    return pl.pallas_call(
        kernel,
        out_shape=out_shape,
        in_specs=[IN_SMEM] + [IN_VMEM] * (len(operands) - 1),
        out_specs=IN_VMEM if single else [IN_VMEM] * len(out_shape),
        scratch_shapes=list(scratch),
        compiler_params=pltpu.CompilerParams(vmem_limit_bytes=grant * MIB),
        cost_estimate=pl.CostEstimate(flops=flops, bytes_accessed=moved, transcendentals=0),
    )(*operands)


TILE = 384


def terms_of(at_ref, backs, weights, blocks, cols):
    total = None
    for i, (weight, block) in enumerate(zip(weights, blocks, strict=True)):
        acts = block[...]
        if backs[i // 2] == 3:
            acts = jnp.where(at_ref[1] == 3, acts, jnp.zeros_like(acts))
        term = jnp.dot(acts, weight[:, cols], preferred_element_type=F32)
        total = term if total is None else total + term
    return total


def split_blocks(refs):
    out = []
    for ref in refs:
        out += [ref.at[0], ref.at[1]] if len(ref.shape) == 3 else [ref]
    return out


def partial_kernel(backs, at_ref, *refs):
    weights, blocks, total_ref = refs[: 2 * len(backs)], refs[2 * len(backs) : -1], refs[-1]
    base_ref = None
    if len(blocks[0].shape) == 2 and blocks[0].shape == total_ref.shape:
        base_ref, *blocks = blocks
    blocks = split_blocks(blocks)
    for n in range(total_ref.shape[1] // TILE):
        cols = slice(n * TILE, (n + 1) * TILE)
        total = terms_of(at_ref, backs, weights, blocks, cols)
        total_ref[:, cols] = total if base_ref is None else total + base_ref[:, cols]


def partial(at, backs, blocks, weights, base=None):
    rows, cols = blocks[0].shape[-2], weights[0][0].shape[1]
    operands = [at] + [w for back in backs for w in weights[back]] + ([] if base is None else [base]) + blocks
    return call(
        functools.partial(partial_kernel, backs),
        jax.ShapeDtypeStruct((rows, cols), F32),
        operands, 12, flops=4 * len(backs) * rows * 512 * cols,
    )


def last_kernel(backs, at_ref, *refs):
    weights, (base_ref, *refs) = refs[: 2 * len(backs)], refs[2 * len(backs) :]
    turned = refs[-1]
    self_ref, *away = refs[-5:-1]
    blocks = split_blocks(refs[:-5])
    for n in range(base_ref.shape[1] // TILE):
        cols = slice(n * TILE, (n + 1) * TILE)
        total = terms_of(at_ref, backs, weights, blocks, cols) + base_ref[:, cols]
        turned[cols, :] = total.T
    for by in range(NX):
        owner = lax.rem(at_ref[2] + by, NX)
        for z in range(NZ):
            piece = turned[pl.ds(pl.multiple_of((z * NX + owner) * 72, 8), 72), :]
            if by == 0:
                self_ref[z] = piece
            else:
                away[by - 1][z] = piece.astype(BF)


def last(at, base, backs, blocks, weights):
    rows, cols = base.shape
    piece = (NZ, cols // (NX * NZ), rows)
    return call(
        functools.partial(last_kernel, backs),
        [jax.ShapeDtypeStruct(piece, F32)] + [jax.ShapeDtypeStruct(piece, BF)] * 3,
        [at] + [w for back in backs for w in weights[back]] + [base] + blocks, 12,
        scratch=[pltpu.VMEM((cols, rows), F32)], flops=4 * rows * 512 * cols,
    )


def x_sum_kernel(at_ref, *refs):
    *before, self_ref, a_ref, b_ref, c_ref, out_ref = refs
    for z in range(NZ):
        total = self_ref[z] + a_ref[z].astype(F32) + b_ref[z].astype(F32) + c_ref[z].astype(F32)
        total = total.astype(BF)
        for c, piece in enumerate((total[:36], total[36:])):
            if before:
                out_ref[2 * z + c, :36] = before[0][2 * z + c]
                out_ref[2 * z + c, 36:] = piece
            else:
                out_ref[2 * z + c] = piece


def x_sum(at, before, kept, came):
    shape = (2 * NZ, 72 if before else 36, 256)
    return call(x_sum_kernel, jax.ShapeDtypeStruct(shape, BF), [at, *before, kept, *came], 8)


def final_kernel(at_ref, chips_ref, bias_ref, out_ref):
    for c in range(2):
        chips = chips_ref[c].astype(F32)
        for z in range(1, NZ):
            chips = chips + chips_ref[2 * z + c].astype(F32)
        for block in range(2):
            total = (chips[block * 36 : (block + 1) * 36] + bias_ref[...]).astype(BF)
            for dp in range(2):

                @pl.when(at_ref[3] == dp)
                def _(total=total, start=(dp ^ block) * 512 + c * 256):
                    out_ref[:, start : start + 256] = total


def finish(at, chips, bias):
    return call(final_kernel, jax.ShapeDtypeStruct((36, 1024), BF), [at, chips, bias], 8)


def per_device(resid, enc_weight, enc_bias, dec_weight, dec_bias, lengths):
    target, feat, dp = lax.axis_index("layer"), lax.axis_index("feat"), lax.axis_index("dp")
    core = feat % 2
    at = jnp.stack([core, target, feat // 2 % NX, dp]).astype(jnp.int32)
    valid = (jnp.arange(SEQ)[None, :] < lengths[:, None]).reshape(-1).astype(F32)
    pre = jnp.dot(resid[0], enc_weight[0], preferred_element_type=F32) + enc_bias
    acts = (jax.nn.relu(pre) * valid[:, None]).astype(BF).reshape(2, 256, 512)
    keep = lax.dynamic_index_in_dim(acts, core, 0, keepdims=False)
    send = lax.dynamic_index_in_dim(acts, 1 - core, 0, keepdims=False)
    across = lambda flip: [(d * 32 + f, (1 - d) * 32 + (f ^ flip)) for d in range(2) for f in range(32)]
    other_mine = lax.ppermute(keep, ("dp", "feat"), across(0))
    other_theirs = lax.ppermute(send, ("dp", "feat"), across(1))
    own_theirs = lax.ppermute(send, "feat", PARTNER)
    w_theirs = lax.ppermute(dec_weight, "feat", PARTNER)
    weights = [
        [lax.dynamic_index_in_dim(w[0], jnp.maximum(target - back, 0), 0, keepdims=False) for w in (dec_weight, w_theirs)]
        for back in range(4)
    ]
    chips = []
    for mine, theirs in ((keep, own_theirs), (other_mine, other_theirs)):
        both = jnp.stack([mine, theirs])
        up = lax.ppermute(both, "layer", [(0, 1), (1, 2), (2, 3)])
        down = lax.ppermute(both, "layer", [(0, 3), (1, 0)])
        far_up = lax.ppermute(up[0], "layer", [(1, 2), (2, 3)])
        far_down = lax.ppermute(down[1], "layer", [(3, 2), (0, 3)])
        total = partial(at, (0,), [both], weights)
        total = partial(at, (1, 3), [up, down], weights, total)
        kept, *away = last(at, total, (2,), [far_up, far_down], weights)
        came = []
        for by, piece in enumerate(away):
            came.append(lax.ppermute(piece, "feat", x_pairs(by + 1)))
        chips = [x_sum(at, chips, kept, came)]
    chips = lax.all_to_all(chips[0], "feat", 0, 0, tiled=True, axis_index_groups=ZC_GROUPS)
    out = finish(at, chips, dec_bias.reshape(36, 1))
    return out.T[None]


def solution(mesh):
    in_specs = (
        P("layer", "dp", None),
        P("layer", None, "feat"),
        P("layer", "feat"),
        P("layer", None, "feat", "dp"),
        P("layer", ("dp", "feat")),
        P("dp"),
    )
    out_specs = P("layer", None, ("dp", "feat"))


    return jax.shard_map(per_device, mesh=mesh, in_specs=in_specs, out_specs=out_specs, check_vma=False)
```

time: 213 us -> 122 us (0.57)
  the two profiles are of different devices: /device:TPU:24 before, /device:TPU:1 now
where the time goes in v3:
time: 122 us
  starting transfers between devices  55.4 us (45%)
  waiting for transfers between devices  33.5 us (27%)
  Pallas kernels  15.9 us (13%)
  local copies, waits for them, and re-layouts  10.7 us (9%)
  matrix products  3.05 us (2%)
  other arithmetic  2.79 us (2%)
    all_to_all x1, starting transfers between devices, per_device(): lax.all_to_all(chips[0], 'feat', 0, 0, tiled=True, axis_index_groups=ZC_G...  17.9 us
    pallas_call x9, Pallas kernels, call(): pl.pallas_call(kernel, out_shape=out_shape, in_specs=[IN_SMEM] + [IN_VMEM...  15.9 us
    all_to_all x1, waiting for transfers between devices, per_device(): lax.all_to_all(chips[0], 'feat', 0, 0, tiled=True, axis_index_groups=ZC_G...  9.23 us
    ppermute x1, waiting for transfers between devices, per_device(): other_theirs = lax.ppermute(send, ('dp', 'feat'), across(1))  8.9 us
    ppermute x6, starting transfers between devices, per_device(): came.append(lax.ppermute(piece, 'feat', x_pairs(by + 1)))  8.06 us
    ppermute x2, starting transfers between devices, per_device(): up = lax.ppermute(both, 'layer', [(0, 1), (1, 2), (2, 3)])  7.86 us
    squeeze x2, local copies, waits for them, and re-layouts, per_device(): lax.dynamic_index_in_dim(w[0], jnp.maximum(target - back, 0), 0, keepdims...  7.8 us
    ppermute x2, starting transfers between devices, per_device(): far_down = lax.ppermute(down[1], 'layer', [(3, 2), (0, 3)])  6.66 us
  transfers between devices with their start and end apart: 19, of which 9 were waited for; matrix products, arithmetic and copies ran while one was open for 14% of the time, Pallas kernels for 11%

profile of v3, /device:TPU:1, one launch (start us, length us, event | category | flops | bytes accessed | tf_op | source)
XLA Modules:
  0.0 121.7 jit_solution(18422085571092047162)
XLA Ops:
  0.0 3.2 %collective-permute-start = (bf16[1,4,512,1152]{3,2,1,0:T(8,128)(2,1)}, bf16[1,4,512,1152]{3,2,1,0:T(8,128)(2,1)}, u32[]{:S(2)}, u32[]{:S(2)}) collective-permute-start(bf16[1,4,512,1152]{3,2,1,0:T(8,128)(2,1)} %param.9), channel_id=1, source_target_pairs={{0,1},{1,0},{2,3},{3,2},{4,5},{5,4},{6,7},{7,6},{8,9},{9,8},{10,11... | collective-permute-start | bytes 14155784 | tf_op jit(solution)/shard_map/ppermute | solution.py:174
  3.9 3.0 %fusion.18 = bf16[512,512]{1,0:T(8,128)(2,1)S(1)} fusion(bf16[1,2304,512]{2,1,0:T(8,128)(2,1)S(1)} %copy-done, bf16[1,512,2304]{2,1,0:T(8,128)(2,1)} %param.6, f32[512]{0:T(512)S(1)} %convert_bitcast_fusion, f32[512]{0:T(512)} %bitcast.69), kind=kOutput, calls=%fused_computation.6 | convolution fusion | flops 1209008128 | bytes 5246976 | tf_op jit(solution)/shard_map/dot_general | solution.py:166
  7.7 5.5 %collective-permute-start.9 = (bf16[256,512]{1,0:T(8,128)(2,1)S(1)}, bf16[256,512]{1,0:T(8,128)(2,1)S(1)}, u32[]{:S(2)}, u32[]{:S(2)}) collective-permute-start(bf16[256,512]{1,0:T(8,128)(2,1)S(1)} %bitcast.64), channel_id=1, source_target_pairs={{0,128},{1,129},{2,130},{3,131},{4,132},{5,133},{6,134},{7,135},{8... | collective-permute-start | bytes 786440 | tf_op jit(solution)/shard_map/ppermute | solution.py:171
  14.2 4.5 %collective-permute-done.9 = bf16[256,512]{1,0:T(8,128)(2,1)S(1)} collective-permute-done((bf16[256,512]{1,0:T(8,128)(2,1)S(1)}, bf16[256,512]{1,0:T(8,128)(2,1)S(1)}, u32[]{:S(2)}, u32[]{:S(2)}) %collective-permute-start.9) | collective-permute-done | bytes 262176 | tf_op jit(solution)/shard_map/ppermute | solution.py:171
  18.8 8.9 %collective-permute-done.10 = bf16[256,512]{1,0:T(8,128)(2,1)S(1)} collective-permute-done((bf16[256,512]{1,0:T(8,128)(2,1)}, bf16[256,512]{1,0:T(8,128)(2,1)S(1)}, u32[]{:S(2)}, u32[]{:S(2)}) %collective-permute-start.10) | collective-permute-done | bytes 262176 | tf_op jit(solution)/shard_map/ppermute | solution.py:172
  28.6 4.0 %collective-permute-start.11 = (bf16[2,256,512]{2,1,0:T(8,128)(2,1)}, bf16[2,256,512]{2,1,0:T(8,128)(2,1)}, u32[]{:S(2)}, u32[]{:S(2)}) collective-permute-start(bf16[2,256,512]{2,1,0:T(8,128)(2,1)} %pad_maximum_fusion.1.refs_2_), channel_id=1, source_target_pairs={{0,32},{32,64},{64,96},{1,33},{33,65},{65,97},{2,34},{34,66},{66,9... | collective-permute-start | bytes 1572872 | tf_op jit(solution)/shard_map/ppermute | solution.py:182
  32.6 1.9 %collective-permute-start.12 = (bf16[2,256,512]{2,1,0:T(8,128)(2,1)}, bf16[2,256,512]{2,1,0:T(8,128)(2,1)}, u32[]{:S(2)}, u32[]{:S(2)}) collective-permute-start(bf16[2,256,512]{2,1,0:T(8,128)(2,1)} %pad_maximum_fusion.1.refs_2_), channel_id=1, source_target_pairs={{0,96},{32,0},{1,97},{33,1},{2,98},{34,2},{3,99},{35,3},{4,100},{3... | collective-permute-start | bytes 1572872 | tf_op jit(solution)/shard_map/ppermute | solution.py:183
  34.5 4.7 %dynamic-slice_bitcast_fusion.1 = (bf16[512,1152]{1,0:T(8,128)(2,1)}, bf16[512,1152]{1,0:T(8,128)(2,1)}, bf16[512,1152]{1,0:T(8,128)(2,1)S(1)}, bf16[512,1152]{1,0:T(8,128)(2,1)}) fusion(bf16[1,4,512,1152]{3,2,1,0:T(8,128)(2,1)} %param.9, s32[]{:T(128)S(6)} %max.27, s32[]{:T(128)S(6)} %max.25, s32[]{:T(128)S(6)} %max.24, s32[]{:T(128)S(6)} %max.26), kind=kLoop, calls=%fused_computation.8 | loop fusion | bytes 9437200 | tf_op jit(solution)/shard_map/jit(dynamic_index_in_dim)/squeeze | solution.py:176
  40.3 3.9 %collective-permute-start.2 = (bf16[2,256,512]{2,1,0:T(8,128)(2,1)S(1)}, bf16[2,256,512]{2,1,0:T(8,128)(2,1)S(1)}, u32[]{:S(2)}, u32[]{:S(2)}) collective-permute-start(bf16[2,256,512]{2,1,0:T(8,128)(2,1)S(1)} %pad_maximum_fusion.refs_2_), channel_id=1, source_target_pairs={{0,32},{32,64},{64,96},{1,33},{33,65},{65,97},{2,34},{34,66},{66,9... | collective-permute-start | bytes 1572872 | tf_op jit(solution)/shard_map/ppermute | solution.py:182
  44.2 1.9 %collective-permute-start.3 = (bf16[2,256,512]{2,1,0:T(8,128)(2,1)S(1)}, bf16[2,256,512]{2,1,0:T(8,128)(2,1)S(1)}, u32[]{:S(2)}, u32[]{:S(2)}) collective-permute-start(bf16[2,256,512]{2,1,0:T(8,128)(2,1)S(1)} %pad_maximum_fusion.refs_2_), channel_id=1, source_target_pairs={{0,96},{32,0},{1,97},{33,1},{2,98},{34,2},{3,99},{35,3},{4,100},{3... | collective-permute-start | bytes 1572872 | tf_op jit(solution)/shard_map/ppermute | solution.py:183
  48.8 3.1 %collective-permute-start.14 = (bf16[256,512]{1,0:T(8,128)(2,1)S(1)}, bf16[256,512]{1,0:T(8,128)(2,1)S(1)}, u32[]{:S(2)}, u32[]{:S(2)}) collective-permute-start(bf16[256,512]{1,0:T(8,128)(2,1)S(1)} %slice_bitcast_fusion), channel_id=1, source_target_pairs={{96,64},{0,96},{97,65},{1,97},{98,66},{2,98},{99,67},{3,99},{100,6... | collective-permute-start | bytes 786440 | tf_op jit(solution)/shard_map/ppermute | solution.py:185
  51.9 2.4 %collective-permute-done.2.refs_5_ = bf16[2,256,512]{2,1,0:T(8,128)(2,1)S(1)} collective-permute-done((bf16[2,256,512]{2,1,0:T(8,128)(2,1)S(1)}, bf16[2,256,512]{2,1,0:T(8,128)(2,1)S(1)}, u32[]{:S(2)}, u32[]{:S(2)}) %collective-permute-start.2) | collective-permute-done | bytes 524320 | tf_op jit(solution)/shard_map/ppermute | solution.py:182
  55.0 3.2 %collective-permute-done.3.refs_6_ = bf16[2,256,512]{2,1,0:T(8,128)(2,1)S(1)} collective-permute-done((bf16[2,256,512]{2,1,0:T(8,128)(2,1)S(1)}, bf16[2,256,512]{2,1,0:T(8,128)(2,1)S(1)}, u32[]{:S(2)}, u32[]{:S(2)}) %collective-permute-start.3) | collective-permute-done | bytes 524320 | tf_op jit(solution)/shard_map/ppermute | solution.py:183
  58.3 3.6 %collective-permute-start.5 = (bf16[256,512]{1,0:T(8,128)(2,1)S(1)}, bf16[256,512]{1,0:T(8,128)(2,1)S(1)}, u32[]{:S(2)}, u32[]{:S(2)}) collective-permute-start(bf16[256,512]{1,0:T(8,128)(2,1)S(1)} %slice_bitcast_fusion.2), channel_id=1, source_target_pairs={{96,64},{0,96},{97,65},{1,97},{98,66},{2,98},{99,67},{3,99},{100,6... | collective-permute-start | bytes 786440 | tf_op jit(solution)/shard_map/ppermute | solution.py:185
  61.8 3.1 %dynamic-slice_bitcast_fusion = (bf16[512,1152]{1,0:T(8,128)(2,1)S(1)}, bf16[512,1152]{1,0:T(8,128)(2,1)S(1)}, bf16[512,1152]{1,0:T(8,128)(2,1)S(1)}, bf16[512,1152]{1,0:T(8,128)(2,1)S(1)}) fusion(bf16[1,4,512,1152]{3,2,1,0:T(8,128)(2,1)} %collective-permute-done, s32[]{:T(128)S(6)} %max.27, s32[]{:T(128)S(6)} %max.26, s32[]{:T(128)S(6)} %max.25, s32[]{:T(128)S(6)} %max.24), kind=kLoop, calls=%fused_computation.7 | loop fusion | bytes 9437200 | tf_op jit(solution)/shard_map/jit(dynamic_index_in_dim)/squeeze | solution.py:176
  66.6 2.4 %shard_map.65.refs_2_ = f32[256,1152]{1,0:T(8,128)S(1)} custom-call(s32[4]{0:T(128)S(1)} %pad_add_fusion.at_ref, bf16[512,1152]{1,0:T(8,128)(2,1)S(1)} %copy-done.1, bf16[512,1152]{1,0:T(8,128)(2,1)S(1)} %get-tuple-element.23.refs_1_, bf16[512,1152]{1,0:T(8,128)(2,1)S(1)} %copy-done.2, bf16[512,1152]{1,0:T(8,128)(2,1)S(1)} %get-tuple-element.22.refs_3_, ...), custom_call_target="tpu_custom_call" | custom-call | flops 1207959552 | bytes 6946832 | tf_op jit(solution)/shard_map/pallas_call | solution.py:41
  69.0 1.8 %shard_map.66 = (f32[4,72,256]{2,1,0:T(8,128)S(1)}, bf16[4,72,256]{2,1,0:T(8,128)(2,1)S(1)}, bf16[4,72,256]{2,1,0:T(8,128)(2,1)S(1)}, bf16[4,72,256]{2,1,0:T(8,128)(2,1)S(1)}) custom-call(s32[4]{0:T(128)S(1)} %pad_add_fusion.at_ref, bf16[512,1152]{1,0:T(8,128)(2,1)S(1)} %get-tuple-element.27.refs_0_, bf16[512,1152]{1,0:T(8,128)(2,1)S(1)} %get-tuple-element.24.refs_1_, ...), custom_call_target="tpu_custom_call" | custom-call | flops 603979776 | bytes 4063248 | tf_op jit(solution)/shard_map/pallas_call | solution.py:41
  72.3 2.0 %shard_map.68.refs_4_ = f32[256,1152]{1,0:T(8,128)S(1)} custom-call(s32[4]{0:T(128)S(1)} %pad_add_fusion.at_ref, bf16[512,1152]{1,0:T(8,128)(2,1)S(1)} %copy-done.3, bf16[512,1152]{1,0:T(8,128)(2,1)S(1)} %get-tuple-element.21.refs_1_, bf16[2,256,512]{2,1,0:T(8,128)(2,1)} %pad_maximum_fusion.1.refs_2_), custom_call_target="tpu_custom_call" | custom-call | flops 603979776 | bytes 2883600 | tf_op jit(solution)/shard_map/pallas_call | solution.py:41
  74.3 3.0 %shard_map.69.refs_2_ = f32[256,1152]{1,0:T(8,128)S(1)} custom-call(s32[4]{0:T(128)S(1)} %pad_add_fusion.at_ref, bf16[512,1152]{1,0:T(8,128)(2,1)S(1)} %copy-done.1, bf16[512,1152]{1,0:T(8,128)(2,1)S(1)} %get-tuple-element.23.refs_1_, bf16[512,1152]{1,0:T(8,128)(2,1)S(1)} %copy-done.2, bf16[512,1152]{1,0:T(8,128)(2,1)S(1)} %get-tuple-element.22.refs_3_, ...), custom_call_target="tpu_custom_call" | custom-call | flops 1207959552 | bytes 6946832 | tf_op jit(solution)/shard_map/pallas_call | solution.py:41
  77.4 1.8 %shard_map.70 = (f32[4,72,256]{2,1,0:T(8,128)S(1)}, bf16[4,72,256]{2,1,0:T(8,128)(2,1)S(1)}, bf16[4,72,256]{2,1,0:T(8,128)(2,1)S(1)}, bf16[4,72,256]{2,1,0:T(8,128)(2,1)S(1)}) custom-call(s32[4]{0:T(128)S(1)} %pad_add_fusion.at_ref, bf16[512,1152]{1,0:T(8,128)(2,1)S(1)} %get-tuple-element.27.refs_0_, bf16[512,1152]{1,0:T(8,128)(2,1)S(1)} %get-tuple-element.24.refs_1_, ...), custom_call_target="tpu_custom_call" | custom-call | flops 603979776 | bytes 4063248 | tf_op jit(solution)/shard_map/pallas_call | solution.py:41
  81.9 1.9 %collective-permute-start.8 = (bf16[4,72,256]{2,1,0:T(8,128)(2,1)S(1)}, bf16[4,72,256]{2,1,0:T(8,128)(2,1)S(1)}, u32[]{:S(2)}, u32[]{:S(2)}) collective-permute-start(bf16[4,72,256]{2,1,0:T(8,128)(2,1)S(1)} %get-tuple-element.16), channel_id=1, source_target_pairs={{0,6},{1,7},{2,0},{3,1},{4,2},{5,3},{6,4},{7,5},{8,14},{9,15},{10,... | collective-permute-start | bytes 442376 | tf_op jit(solution)/shard_map/ppermute | solution.py:191
  87.2 3.9 %collective-permute-done.16.refs_3_ = bf16[4,72,256]{2,1,0:T(8,128)(2,1)S(1)} collective-permute-done((bf16[4,72,256]{2,1,0:T(8,128)(2,1)S(1)}, bf16[4,72,256]{2,1,0:T(8,128)(2,1)S(1)}, u32[]{:S(2)}, u32[]{:S(2)}) %collective-permute-start.16) | collective-permute-done | bytes 147488 | tf_op jit(solution)/shard_map/ppermute | solution.py:191
  92.9 17.9 %all-to-all-start = ((bf16[8,72,256]{2,1,0:T(8,128)(2,1)}), bf16[8,72,256]{2,1,0:T(8,128)(2,1)S(1)}, u32[]{:S(2)}, u32[]{:S(2)}) async-start(bf16[8,72,256]{2,1,0:T(8,128)(2,1)} %shard_map.71), calls=%async_computation | async-start | bytes 589824 | tf_op jit(solution)/shard_map/all_to_all | solution.py:193
  110.9 9.2 %all-to-all-done.chips_ref = bf16[8,72,256]{2,1,0:T(8,128)(2,1)S(1)} async-done(((bf16[8,72,256]{2,1,0:T(8,128)(2,1)}), bf16[8,72,256]{2,1,0:T(8,128)(2,1)S(1)}, u32[]{:S(2)}, u32[]{:S(2)}) %all-to-all-start) | async-done | bytes 294944 | tf_op jit(solution)/shard_map/all_to_all | solution.py:193
  (48 shorter events, 20.6 us)
Async XLA Ops:
  0.0 3.9 %copy-start = (bf16[1,2304,512]{2,1,0:T(8,128)(2,1)S(1)}, bf16[1,2304,512]{2,1,0:T(8,128)(2,1)}, u32[]{:S(2)}) copy-start(bf16[1,2304,512]{2,1,0:T(8,128)(2,1)} %param.7) | copy-start | bytes 7077892
  0.0 61.8 %collective-permute-start = (bf16[1,4,512,1152]{3,2,1,0:T(8,128)(2,1)}, bf16[1,4,512,1152]{3,2,1,0:T(8,128)(2,1)}, u32[]{:S(2)}, u32[]{:S(2)}) collective-permute-start(bf16[1,4,512,1152]{3,2,1,0:T(8,128)(2,1)} %param.9), channel_id=1, source_target_pairs={{0,1},{1,0},{2,3},{3,2},{4,5},{5,4},{6,7},{7,6},{8,9},{9,8},{10,11... | collective-permute-start | bytes 14155784 | tf_op jit(solution)/shard_map/ppermute | solution.py:174
  7.7 24.8 %copy-start.4 = (bf16[1,256,512]{2,1,0:T(8,128)(2,1)}, bf16[1,256,512]{2,1,0:T(8,128)(2,1)S(1)}, u32[]{:S(2)}) copy-start(bf16[1,256,512]{2,1,0:T(8,128)(2,1)S(1)} %get-tuple-element.29) | copy-start | bytes 786436
  7.7 11.0 %collective-permute-start.9 = (bf16[256,512]{1,0:T(8,128)(2,1)S(1)}, bf16[256,512]{1,0:T(8,128)(2,1)S(1)}, u32[]{:S(2)}, u32[]{:S(2)}) collective-permute-start(bf16[256,512]{1,0:T(8,128)(2,1)S(1)} %bitcast.64), channel_id=1, source_target_pairs={{0,128},{1,129},{2,130},{3,131},{4,132},{5,133},{6,134},{7,135},{8... | collective-permute-start | bytes 786440 | tf_op jit(solution)/shard_map/ppermute | solution.py:171
  13.2 14.4 %collective-permute-start.10 = (bf16[256,512]{1,0:T(8,128)(2,1)}, bf16[256,512]{1,0:T(8,128)(2,1)S(1)}, u32[]{:S(2)}, u32[]{:S(2)}) collective-permute-start(bf16[256,512]{1,0:T(8,128)(2,1)} %get-tuple-element.30), channel_id=1, source_target_pairs={{0,129},{1,128},{2,131},{3,130},{4,133},{5,132},{6,135},{7,134},{8... | collective-permute-start | bytes 786440 | tf_op jit(solution)/shard_map/ppermute | solution.py:172
  14.2 24.9 %collective-permute-start.1 = (bf16[256,512]{1,0:T(8,128)(2,1)}, bf16[256,512]{1,0:T(8,128)(2,1)}, u32[]{:S(2)}, u32[]{:S(2)}) collective-permute-start(bf16[256,512]{1,0:T(8,128)(2,1)} %get-tuple-element.30), channel_id=1, source_target_pairs={{0,1},{1,0},{2,3},{3,2},{4,5},{5,4},{6,7},{7,6},{8,9},{9,8},{10,11... | collective-permute-start | bytes 786440 | tf_op jit(solution)/shard_map/ppermute | solution.py:173
  28.6 17.6 %collective-permute-start.11 = (bf16[2,256,512]{2,1,0:T(8,128)(2,1)}, bf16[2,256,512]{2,1,0:T(8,128)(2,1)}, u32[]{:S(2)}, u32[]{:S(2)}) collective-permute-start(bf16[2,256,512]{2,1,0:T(8,128)(2,1)} %pad_maximum_fusion.1.refs_2_), channel_id=1, source_target_pairs={{0,32},{32,64},{64,96},{1,33},{33,65},{65,97},{2,34},{34,66},{66,9... | collective-permute-start | bytes 1572872 | tf_op jit(solution)/shard_map/ppermute | solution.py:182
  32.6 15.2 %collective-permute-start.12 = (bf16[2,256,512]{2,1,0:T(8,128)(2,1)}, bf16[2,256,512]{2,1,0:T(8,128)(2,1)}, u32[]{:S(2)}, u32[]{:S(2)}) collective-permute-start(bf16[2,256,512]{2,1,0:T(8,128)(2,1)} %pad_maximum_fusion.1.refs_2_), channel_id=1, source_target_pairs={{0,96},{32,0},{1,97},{33,1},{2,98},{34,2},{3,99},{35,3},{4,100},{3... | collective-permute-start | bytes 1572872 | tf_op jit(solution)/shard_map/ppermute | solution.py:183
  40.3 14.0 %collective-permute-start.2 = (bf16[2,256,512]{2,1,0:T(8,128)(2,1)S(1)}, bf16[2,256,512]{2,1,0:T(8,128)(2,1)S(1)}, u32[]{:S(2)}, u32[]{:S(2)}) collective-permute-start(bf16[2,256,512]{2,1,0:T(8,128)(2,1)S(1)} %pad_maximum_fusion.refs_2_), channel_id=1, source_target_pairs={{0,32},{32,64},{64,96},{1,33},{33,65},{65,97},{2,34},{34,66},{66,9... | collective-permute-start | bytes 1572872 | tf_op jit(solution)/shard_map/ppermute | solution.py:182
  44.2 14.0 %collective-permute-start.3 = (bf16[2,256,512]{2,1,0:T(8,128)(2,1)S(1)}, bf16[2,256,512]{2,1,0:T(8,128)(2,1)S(1)}, u32[]{:S(2)}, u32[]{:S(2)}) collective-permute-start(bf16[2,256,512]{2,1,0:T(8,128)(2,1)S(1)} %pad_maximum_fusion.refs_2_), channel_id=1, source_target_pairs={{0,96},{32,0},{1,97},{33,1},{2,98},{34,2},{3,99},{35,3},{4,100},{3... | collective-permute-start | bytes 1572872 | tf_op jit(solution)/shard_map/ppermute | solution.py:183
  47.1 30.2 %collective-permute-start.13 = (bf16[256,512]{1,0:T(8,128)(2,1)S(1)}, bf16[256,512]{1,0:T(8,128)(2,1)S(1)}, u32[]{:S(2)}, u32[]{:S(2)}) collective-permute-start(bf16[256,512]{1,0:T(8,128)(2,1)S(1)} %slice_bitcast_fusion.1), channel_id=1, source_target_pairs={{32,64},{64,96},{33,65},{65,97},{34,66},{66,98},{35,67},{67,99},{3... | collective-permute-start | bytes 786440 | tf_op jit(solution)/shard_map/ppermute | solution.py:184
  48.8 28.6 %collective-permute-start.14 = (bf16[256,512]{1,0:T(8,128)(2,1)S(1)}, bf16[256,512]{1,0:T(8,128)(2,1)S(1)}, u32[]{:S(2)}, u32[]{:S(2)}) collective-permute-start(bf16[256,512]{1,0:T(8,128)(2,1)S(1)} %slice_bitcast_fusion), channel_id=1, source_target_pairs={{96,64},{0,96},{97,65},{1,97},{98,66},{2,98},{99,67},{3,99},{100,6... | collective-permute-start | bytes 786440 | tf_op jit(solution)/shard_map/ppermute | solution.py:185
  54.3 14.7 %collective-permute-start.4 = (bf16[256,512]{1,0:T(8,128)(2,1)S(1)}, bf16[256,512]{1,0:T(8,128)(2,1)S(1)}, u32[]{:S(2)}, u32[]{:S(2)}) collective-permute-start(bf16[256,512]{1,0:T(8,128)(2,1)S(1)} %slice_bitcast_fusion.3), channel_id=1, source_target_pairs={{32,64},{64,96},{33,65},{65,97},{34,66},{66,98},{35,67},{67,99},{3... | collective-permute-start | bytes 786440 | tf_op jit(solution)/shard_map/ppermute | solution.py:184
  58.2 6.7 %copy-start.3 = (bf16[512,1152]{1,0:T(8,128)(2,1)S(1)}, bf16[512,1152]{1,0:T(8,128)(2,1)}, u32[]{:S(2)}) copy-start(bf16[512,1152]{1,0:T(8,128)(2,1)} %get-tuple-element.25.refs_0_) | copy-start | bytes 3538948
  58.3 10.7 %collective-permute-start.5 = (bf16[256,512]{1,0:T(8,128)(2,1)S(1)}, bf16[256,512]{1,0:T(8,128)(2,1)S(1)}, u32[]{:S(2)}, u32[]{:S(2)}) collective-permute-start(bf16[256,512]{1,0:T(8,128)(2,1)S(1)} %slice_bitcast_fusion.2), channel_id=1, source_target_pairs={{96,64},{0,96},{97,65},{1,97},{98,66},{2,98},{99,67},{3,99},{100,6... | collective-permute-start | bytes 786440 | tf_op jit(solution)/shard_map/ppermute | solution.py:185
  65.0 1.6 %copy-start.2 = (bf16[512,1152]{1,0:T(8,128)(2,1)S(1)}, bf16[512,1152]{1,0:T(8,128)(2,1)}, u32[]{:S(2)}) copy-start(bf16[512,1152]{1,0:T(8,128)(2,1)} %get-tuple-element.28.refs_2_) | copy-start | bytes 3538948
  70.8 13.5 %collective-permute-start.6 = (bf16[4,72,256]{2,1,0:T(8,128)(2,1)S(1)}, bf16[4,72,256]{2,1,0:T(8,128)(2,1)S(1)}, u32[]{:S(2)}, u32[]{:S(2)}) collective-permute-start(bf16[4,72,256]{2,1,0:T(8,128)(2,1)S(1)} %get-tuple-element.14), channel_id=1, source_target_pairs={{0,2},{1,3},{2,4},{3,5},{4,6},{5,7},{6,0},{7,1},{8,10},{9,11},{10,... | collective-permute-start | bytes 442376 | tf_op jit(solution)/shard_map/ppermute | solution.py:191
  79.1 8.1 %collective-permute-start.15 = (bf16[4,72,256]{2,1,0:T(8,128)(2,1)S(1)}, bf16[4,72,256]{2,1,0:T(8,128)(2,1)S(1)}, u32[]{:S(2)}, u32[]{:S(2)}) collective-permute-start(bf16[4,72,256]{2,1,0:T(8,128)(2,1)S(1)} %get-tuple-element.18), channel_id=1, source_target_pairs={{0,2},{1,3},{2,4},{3,5},{4,6},{5,7},{6,0},{7,1},{8,10},{9,11},{10,... | collective-permute-start | bytes 442376 | tf_op jit(solution)/shard_map/ppermute | solution.py:191
  80.4 5.6 %collective-permute-start.7 = (bf16[4,72,256]{2,1,0:T(8,128)(2,1)S(1)}, bf16[4,72,256]{2,1,0:T(8,128)(2,1)S(1)}, u32[]{:S(2)}, u32[]{:S(2)}) collective-permute-start(bf16[4,72,256]{2,1,0:T(8,128)(2,1)S(1)} %get-tuple-element.15), channel_id=1, source_target_pairs={{0,4},{1,5},{2,6},{3,7},{4,0},{5,1},{6,2},{7,3},{8,12},{9,13},{10,... | collective-permute-start | bytes 442376 | tf_op jit(solution)/shard_map/ppermute | solution.py:191
  81.9 4.7 %collective-permute-start.8 = (bf16[4,72,256]{2,1,0:T(8,128)(2,1)S(1)}, bf16[4,72,256]{2,1,0:T(8,128)(2,1)S(1)}, u32[]{:S(2)}, u32[]{:S(2)}) collective-permute-start(bf16[4,72,256]{2,1,0:T(8,128)(2,1)S(1)} %get-tuple-element.16), channel_id=1, source_target_pairs={{0,6},{1,7},{2,0},{3,1},{4,2},{5,3},{6,4},{7,5},{8,14},{9,15},{10,... | collective-permute-start | bytes 442376 | tf_op jit(solution)/shard_map/ppermute | solution.py:191
  83.7 7.4 %collective-permute-start.16 = (bf16[4,72,256]{2,1,0:T(8,128)(2,1)S(1)}, bf16[4,72,256]{2,1,0:T(8,128)(2,1)S(1)}, u32[]{:S(2)}, u32[]{:S(2)}) collective-permute-start(bf16[4,72,256]{2,1,0:T(8,128)(2,1)S(1)} %get-tuple-element.19), channel_id=1, source_target_pairs={{0,4},{1,5},{2,6},{3,7},{4,0},{5,1},{6,2},{7,3},{8,12},{9,13},{10,... | collective-permute-start | bytes 442376 | tf_op jit(solution)/shard_map/ppermute | solution.py:191
  84.3 7.3 %collective-permute-start.17 = (bf16[4,72,256]{2,1,0:T(8,128)(2,1)S(1)}, bf16[4,72,256]{2,1,0:T(8,128)(2,1)S(1)}, u32[]{:S(2)}, u32[]{:S(2)}) collective-permute-start(bf16[4,72,256]{2,1,0:T(8,128)(2,1)S(1)} %get-tuple-element.20), channel_id=1, source_target_pairs={{0,6},{1,7},{2,0},{3,1},{4,2},{5,3},{6,4},{7,5},{8,14},{9,15},{10,... | collective-permute-start | bytes 442376 | tf_op jit(solution)/shard_map/ppermute | solution.py:191
  86.6 24.3 %copy-start.5 = (f32[1,36]{1,0:T(1,128)S(1)}, f32[1,36]{1,0:T(1,128)}, u32[]{:S(2)}) copy-start(f32[1,36]{1,0:T(1,128)} %param.10) | copy-start | bytes 436
  92.9 27.2 %all-to-all-start = ((bf16[8,72,256]{2,1,0:T(8,128)(2,1)}), bf16[8,72,256]{2,1,0:T(8,128)(2,1)S(1)}, u32[]{:S(2)}, u32[]{:S(2)}) async-start(bf16[8,72,256]{2,1,0:T(8,128)(2,1)} %shard_map.71), calls=%async_computation | async-start | bytes 589824 | tf_op jit(solution)/shard_map/all_to_all | solution.py:193
  (1 other events, 1.5 us)

commit v4 on v3

--- a/solution.py
+++ b/solution.py
@@ -50,15 +50,17 @@
 
 
 TILE = 384
+GRANT = 12
 
 
 def terms_of(at_ref, backs, weights, blocks, cols):
     total = None
-    for i, (weight, block) in enumerate(zip(weights, blocks, strict=True)):
+    for i, block in enumerate(blocks):
+        back = backs[i // 2]
         acts = block[...]
-        if backs[i // 2] == 3:
+        if back == 3:
             acts = jnp.where(at_ref[1] == 3, acts, jnp.zeros_like(acts))
-        term = jnp.dot(acts, weight[:, cols], preferred_element_type=F32)
+        term = jnp.dot(acts, weights[i][:, cols], preferred_element_type=F32)
         total = term if total is None else total + term
     return total
 
@@ -70,36 +72,38 @@
     return out
 
 
+def pick(weights, backs):
+    return [w for back in backs for w in weights[back]]
+
+
 def partial_kernel(backs, at_ref, *refs):
     weights, blocks, total_ref = refs[: 2 * len(backs)], refs[2 * len(backs) : -1], refs[-1]
-    base_ref = None
-    if len(blocks[0].shape) == 2 and blocks[0].shape == total_ref.shape:
-        base_ref, *blocks = blocks
     blocks = split_blocks(blocks)
     for n in range(total_ref.shape[1] // TILE):
         cols = slice(n * TILE, (n + 1) * TILE)
-        total = terms_of(at_ref, backs, weights, blocks, cols)
-        total_ref[:, cols] = total if base_ref is None else total + base_ref[:, cols]
-
-
-def partial(at, backs, blocks, weights, base=None):
+        total_ref[:, cols] = terms_of(at_ref, backs, weights, blocks, cols)
+
+
+def partial(at, weights, backs, blocks):
     rows, cols = blocks[0].shape[-2], weights[0][0].shape[1]
-    operands = [at] + [w for back in backs for w in weights[back]] + ([] if base is None else [base]) + blocks
     return call(
         functools.partial(partial_kernel, backs),
         jax.ShapeDtypeStruct((rows, cols), F32),
-        operands, 12, flops=4 * len(backs) * rows * 512 * cols,
-    )
-
-
-def last_kernel(backs, at_ref, *refs):
-    weights, (base_ref, *refs) = refs[: 2 * len(backs)], refs[2 * len(backs) :]
+        [at, *pick(weights, backs), *blocks], GRANT, flops=4 * len(backs) * rows * 512 * cols,
+    )
+
+
+def last_kernel(backs, has_base, at_ref, *refs):
+    weights, refs = refs[: 2 * len(backs)], refs[2 * len(backs) :]
     turned = refs[-1]
     self_ref, *away = refs[-5:-1]
-    blocks = split_blocks(refs[:-5])
-    for n in range(base_ref.shape[1] // TILE):
+    refs = refs[:-5]
+    blocks = split_blocks(refs[has_base:])
+    for n in range(turned.shape[0] // TILE):
         cols = slice(n * TILE, (n + 1) * TILE)
-        total = terms_of(at_ref, backs, weights, blocks, cols) + base_ref[:, cols]
+        total = terms_of(at_ref, backs, weights, blocks, cols)
+        if has_base:
+            total = total + refs[0][:, cols]
         turned[cols, :] = total.T
     for by in range(NX):
         owner = lax.rem(at_ref[2] + by, NX)
@@ -111,14 +115,14 @@
                 away[by - 1][z] = piece.astype(BF)
 
 
-def last(at, base, backs, blocks, weights):
-    rows, cols = base.shape
+def last(at, weights, base, backs, blocks):
+    rows, cols = blocks[0].shape[-2], weights[0][0].shape[1]
     piece = (NZ, cols // (NX * NZ), rows)
     return call(
-        functools.partial(last_kernel, backs),
+        functools.partial(last_kernel, backs, len(base)),
         [jax.ShapeDtypeStruct(piece, F32)] + [jax.ShapeDtypeStruct(piece, BF)] * 3,
-        [at] + [w for back in backs for w in weights[back]] + [base] + blocks, 12,
-        scratch=[pltpu.VMEM((cols, rows), F32)], flops=4 * rows * 512 * cols,
+        [at, *pick(weights, backs), *base, *blocks], GRANT,
+        scratch=[pltpu.VMEM((cols, rows), F32)], flops=4 * len(backs) * rows * 512 * cols,
     )
 
 
@@ -162,6 +166,7 @@
     target, feat, dp = lax.axis_index("layer"), lax.axis_index("feat"), lax.axis_index("dp")
     core = feat % 2
     at = jnp.stack([core, target, feat // 2 % NX, dp]).astype(jnp.int32)
+    w_theirs = lax.ppermute(dec_weight, "feat", PARTNER)
     valid = (jnp.arange(SEQ)[None, :] < lengths[:, None]).reshape(-1).astype(F32)
     pre = jnp.dot(resid[0], enc_weight[0], preferred_element_type=F32) + enc_bias
     acts = (jax.nn.relu(pre) * valid[:, None]).astype(BF).reshape(2, 256, 512)
@@ -171,21 +176,23 @@
     other_mine = lax.ppermute(keep, ("dp", "feat"), across(0))
     other_theirs = lax.ppermute(send, ("dp", "feat"), across(1))
     own_theirs = lax.ppermute(send, "feat", PARTNER)
-    w_theirs = lax.ppermute(dec_weight, "feat", PARTNER)
-    weights = [
-        [lax.dynamic_index_in_dim(w[0], jnp.maximum(target - back, 0), 0, keepdims=False) for w in (dec_weight, w_theirs)]
-        for back in range(4)
-    ]
+    sources = [jnp.maximum(target - back, 0) for back in range(4)]
+    mine_w = [lax.dynamic_index_in_dim(dec_weight[0], s, 0, keepdims=False) for s in sources]
+    theirs_w = [lax.dynamic_index_in_dim(w_theirs[0], s, 0, keepdims=False) for s in sources]
+    weights = list(zip(mine_w, theirs_w))
     chips = []
-    for mine, theirs in ((keep, own_theirs), (other_mine, other_theirs)):
+    for name, mine, theirs in (("own", keep, own_theirs), ("other", other_mine, other_theirs)):
         both = jnp.stack([mine, theirs])
         up = lax.ppermute(both, "layer", [(0, 1), (1, 2), (2, 3)])
         down = lax.ppermute(both, "layer", [(0, 3), (1, 0)])
         far_up = lax.ppermute(up[0], "layer", [(1, 2), (2, 3)])
         far_down = lax.ppermute(down[1], "layer", [(3, 2), (0, 3)])
-        total = partial(at, (0,), [both], weights)
-        total = partial(at, (1, 3), [up, down], weights, total)
-        kept, *away = last(at, total, (2,), [far_up, far_down], weights)
+        near, far = [both, up, down], [far_up, far_down]
+        if name == "own":
+            kept, *away = last(at, weights, [], (0, 1, 3, 2), near + far)
+        else:
+            total = partial(at, weights, (0, 1, 3), near)
+            kept, *away = last(at, weights, [total], (2,), far)
         came = []
         for by, piece in enumerate(away):
             came.append(lax.ppermute(piece, "feat", x_pairs(by + 1)))
@@ -207,4 +214,6 @@
     out_specs = P("layer", None, ("dp", "feat"))
 
 
-    return jax.shard_map(per_device, mesh=mesh, in_specs=in_specs, out_specs=out_specs, check_vma=False)
+    return jax.shard_map(
+        per_device, mesh=mesh, in_specs=in_specs, out_specs=out_specs, check_vma=False
+    )

time: 122 us -> 121 us (level)
  the two profiles are of different devices: /device:TPU:1 before, /device:TPU:24 now
where the time goes in v4:
time: 121 us
  starting transfers between devices  45.2 us (37%)
  waiting for transfers between devices  45.1 us (37%)
  Pallas kernels  13.6 us (11%)
  local copies, waits for them, and re-layouts  10.6 us (9%)
  matrix products  3.05 us (3%)
  other arithmetic  2.94 us (2%)
    pallas_call x6, Pallas kernels, call(): pl.pallas_call(kernel, out_shape=out_shape, in_specs=[IN_SMEM] + [IN_VMEM...  13.6 us
    all_to_all x1, starting transfers between devices, per_device(): lax.all_to_all(chips[0], 'feat', 0, 0, tiled=True, axis_index_groups=ZC_G...  12.9 us
    all_to_all x1, waiting for transfers between devices, per_device(): lax.all_to_all(chips[0], 'feat', 0, 0, tiled=True, axis_index_groups=ZC_G...  10.3 us
    ppermute x6, starting transfers between devices, per_device(): came.append(lax.ppermute(piece, 'feat', x_pairs(by + 1)))  9.75 us
    ppermute x2, waiting for transfers between devices, per_device(): up = lax.ppermute(both, 'layer', [(0, 1), (1, 2), (2, 3)])  9.69 us
    ppermute x1, waiting for transfers between devices, per_device(): other_mine = lax.ppermute(keep, ('dp', 'feat'), across(0))  7.64 us
    ppermute x2, starting transfers between devices, per_device(): far_down = lax.ppermute(down[1], 'layer', [(3, 2), (0, 3)])  7.45 us
    ppermute x1, starting transfers between devices, per_device(): other_mine = lax.ppermute(keep, ('dp', 'feat'), across(0))  7.19 us
  transfers between devices with their start and end apart: 19, of which 12 were waited for; matrix products, arithmetic and copies ran while one was open for 13% of the time, Pallas kernels for 9%

profile of v4, /device:TPU:24, one launch (start us, length us, event | category | flops | bytes accessed | tf_op | source)
XLA Modules:
  0.0 120.6 jit_solution(13786322627899631169)
XLA Ops:
  1.7 3.0 %fusion.18 = bf16[512,512]{1,0:T(8,128)(2,1)S(1)} fusion(bf16[1,2304,512]{2,1,0:T(8,128)(2,1)S(1)} %copy-done, bf16[1,512,2304]{2,1,0:T(8,128)(2,1)} %param.6, f32[512]{0:T(512)S(1)} %convert_bitcast_fusion, f32[512]{0:T(512)} %bitcast.69), kind=kOutput, calls=%fused_computation.6 | convolution fusion | flops 1209008128 | bytes 5246976 | tf_op jit(solution)/shard_map/dot_general | solution.py:171
  5.5 7.2 %collective-permute-start.9 = (bf16[256,512]{1,0:T(8,128)(2,1)S(1)}, bf16[256,512]{1,0:T(8,128)(2,1)S(1)}, u32[]{:S(2)}, u32[]{:S(2)}) collective-permute-start(bf16[256,512]{1,0:T(8,128)(2,1)S(1)} %bitcast.64), channel_id=1, source_target_pairs={{0,128},{1,129},{2,130},{3,131},{4,132},{5,133},{6,134},{7,135},{8... | collective-permute-start | bytes 786440 | tf_op jit(solution)/shard_map/ppermute | solution.py:176
  12.8 7.6 %collective-permute-done.9 = bf16[256,512]{1,0:T(8,128)(2,1)S(1)} collective-permute-done((bf16[256,512]{1,0:T(8,128)(2,1)S(1)}, bf16[256,512]{1,0:T(8,128)(2,1)S(1)}, u32[]{:S(2)}, u32[]{:S(2)}) %collective-permute-start.9) | collective-permute-done | bytes 262176 | tf_op jit(solution)/shard_map/ppermute | solution.py:176
  20.4 6.2 %collective-permute-done.10 = bf16[256,512]{1,0:T(8,128)(2,1)S(1)} collective-permute-done((bf16[256,512]{1,0:T(8,128)(2,1)}, bf16[256,512]{1,0:T(8,128)(2,1)S(1)}, u32[]{:S(2)}, u32[]{:S(2)}) %collective-permute-start.10) | collective-permute-done | bytes 262176 | tf_op jit(solution)/shard_map/ppermute | solution.py:177
  30.2 4.3 %dynamic-slice_bitcast_fusion.1 = (bf16[512,1152]{1,0:T(8,128)(2,1)}, bf16[512,1152]{1,0:T(8,128)(2,1)S(1)}, bf16[512,1152]{1,0:T(8,128)(2,1)}, bf16[512,1152]{1,0:T(8,128)(2,1)}) fusion(bf16[1,4,512,1152]{3,2,1,0:T(8,128)(2,1)} %param.9, s32[]{:T(128)S(6)} %max.23, s32[]{:T(128)S(6)} %max.21, s32[]{:T(128)S(6)} %max.20, s32[]{:T(128)S(6)} %max.22), kind=kLoop, calls=%fused_computation.8 | loop fusion | bytes 9437200 | tf_op jit(solution)/shard_map/jit(dynamic_index_in_dim)/squeeze | solution.py:180
  38.2 6.4 %collective-permute-done.11.refs_7_ = bf16[2,256,512]{2,1,0:T(8,128)(2,1)} collective-permute-done((bf16[2,256,512]{2,1,0:T(8,128)(2,1)}, bf16[2,256,512]{2,1,0:T(8,128)(2,1)}, u32[]{:S(2)}, u32[]{:S(2)}) %collective-permute-start.11) | collective-permute-done | bytes 524320 | tf_op jit(solution)/shard_map/ppermute | solution.py:186
  47.8 4.6 %collective-permute-start.14 = (bf16[256,512]{1,0:T(8,128)(2,1)S(1)}, bf16[256,512]{1,0:T(8,128)(2,1)S(1)}, u32[]{:S(2)}, u32[]{:S(2)}) collective-permute-start(bf16[256,512]{1,0:T(8,128)(2,1)S(1)} %slice_bitcast_fusion), channel_id=1, source_target_pairs={{96,64},{0,96},{97,65},{1,97},{98,66},{2,98},{99,67},{3,99},{100,6... | collective-permute-start | bytes 786440 | tf_op jit(solution)/shard_map/ppermute | solution.py:189
  52.4 3.3 %collective-permute-done.2.refs_9_ = bf16[2,256,512]{2,1,0:T(8,128)(2,1)S(1)} collective-permute-done((bf16[2,256,512]{2,1,0:T(8,128)(2,1)S(1)}, bf16[2,256,512]{2,1,0:T(8,128)(2,1)S(1)}, u32[]{:S(2)}, u32[]{:S(2)}) %collective-permute-start.2) | collective-permute-done | bytes 524320 | tf_op jit(solution)/shard_map/ppermute | solution.py:186
  57.0 1.9 %collective-permute-done.3.refs_10_ = bf16[2,256,512]{2,1,0:T(8,128)(2,1)S(1)} collective-permute-done((bf16[2,256,512]{2,1,0:T(8,128)(2,1)S(1)}, bf16[2,256,512]{2,1,0:T(8,128)(2,1)S(1)}, u32[]{:S(2)}, u32[]{:S(2)}) %collective-permute-start.3) | collective-permute-done | bytes 524320 | tf_op jit(solution)/shard_map/ppermute | solution.py:187
  59.0 2.9 %collective-permute-start.5 = (bf16[256,512]{1,0:T(8,128)(2,1)S(1)}, bf16[256,512]{1,0:T(8,128)(2,1)S(1)}, u32[]{:S(2)}, u32[]{:S(2)}) collective-permute-start(bf16[256,512]{1,0:T(8,128)(2,1)S(1)} %slice_bitcast_fusion.2), channel_id=1, source_target_pairs={{96,64},{0,96},{97,65},{1,97},{98,66},{2,98},{99,67},{3,99},{100,6... | collective-permute-start | bytes 786440 | tf_op jit(solution)/shard_map/ppermute | solution.py:189
  61.9 2.7 %dynamic-slice_bitcast_fusion = (bf16[512,1152]{1,0:T(8,128)(2,1)S(1)}, bf16[512,1152]{1,0:T(8,128)(2,1)S(1)}, bf16[512,1152]{1,0:T(8,128)(2,1)S(1)}, bf16[512,1152]{1,0:T(8,128)(2,1)S(1)}) fusion(bf16[1,4,512,1152]{3,2,1,0:T(8,128)(2,1)} %collective-permute-done, s32[]{:T(128)S(6)} %max.23, s32[]{:T(128)S(6)} %max.22, s32[]{:T(128)S(6)} %max.21, s32[]{:T(128)S(6)} %max.20), kind=kLoop, calls=%fused_computation.7 | loop fusion | bytes 9437200 | tf_op jit(solution)/shard_map/jit(dynamic_index_in_dim)/squeeze | solution.py:181
  66.0 2.8 %collective-permute-done.5.refs_12_ = bf16[256,512]{1,0:T(8,128)(2,1)S(1)} collective-permute-done((bf16[256,512]{1,0:T(8,128)(2,1)S(1)}, bf16[256,512]{1,0:T(8,128)(2,1)S(1)}, u32[]{:S(2)}, u32[]{:S(2)}) %collective-permute-start.5) | collective-permute-done | bytes 262176 | tf_op jit(solution)/shard_map/ppermute | solution.py:189
  68.7 4.3 %shard_map.64 = (f32[4,72,256]{2,1,0:T(8,128)S(1)}, bf16[4,72,256]{2,1,0:T(8,128)(2,1)S(1)}, bf16[4,72,256]{2,1,0:T(8,128)(2,1)S(1)}, bf16[4,72,256]{2,1,0:T(8,128)(2,1)S(1)}) custom-call(s32[4]{0:T(128)S(1)} %pad_add_fusion.at_ref, bf16[512,1152]{1,0:T(8,128)(2,1)S(1)} %copy-done.1, bf16[512,1152]{1,0:T(8,128)(2,1)S(1)} %get-tuple-element.24.refs_1_, ...), custom_call_target="tpu_custom_call" | custom-call | flops 2415919104 | bytes 11534352 | tf_op jit(solution)/shard_map/pallas_call | solution.py:41
  73.0 1.8 %collective-permute-start.6 = (bf16[4,72,256]{2,1,0:T(8,128)(2,1)S(1)}, bf16[4,72,256]{2,1,0:T(8,128)(2,1)S(1)}, u32[]{:S(2)}, u32[]{:S(2)}) collective-permute-start(bf16[4,72,256]{2,1,0:T(8,128)(2,1)S(1)} %get-tuple-element.14), channel_id=1, source_target_pairs={{0,2},{1,3},{2,4},{3,5},{4,6},{5,7},{6,0},{7,1},{8,10},{9,11},{10,... | collective-permute-start | bytes 442376 | tf_op jit(solution)/shard_map/ppermute | solution.py:198
  74.8 4.0 %shard_map.66.refs_2_ = f32[256,1152]{1,0:T(8,128)S(1)} custom-call(s32[4]{0:T(128)S(1)} %pad_add_fusion.at_ref, bf16[512,1152]{1,0:T(8,128)(2,1)S(1)} %copy-done.1, bf16[512,1152]{1,0:T(8,128)(2,1)S(1)} %get-tuple-element.24.refs_1_, bf16[512,1152]{1,0:T(8,128)(2,1)S(1)} %get-tuple-element.26.refs_2_, bf16[512,1152]{1,0:T(8,128)(2,1)S(1)} %get-tuple-element.23.refs_3_, ...), custom_call_target="tpu_custom_call" | custom-call | flops 1811939328 | bytes 8650768 | tf_op jit(solution)/shard_map/pallas_call | solution.py:41
  78.9 1.8 %shard_map.67 = (f32[4,72,256]{2,1,0:T(8,128)S(1)}, bf16[4,72,256]{2,1,0:T(8,128)(2,1)S(1)}, bf16[4,72,256]{2,1,0:T(8,128)(2,1)S(1)}, bf16[4,72,256]{2,1,0:T(8,128)(2,1)S(1)}) custom-call(s32[4]{0:T(128)S(1)} %pad_add_fusion.at_ref, bf16[512,1152]{1,0:T(8,128)(2,1)S(1)} %copy-done.3, bf16[512,1152]{1,0:T(8,128)(2,1)S(1)} %get-tuple-element.21.refs_7_.refs_1_, ...), custom_call_target="tpu_custom_call" | custom-call | flops 603979776 | bytes 4063248 | tf_op jit(solution)/shard_map/pallas_call | solution.py:41
  80.7 1.6 %collective-permute-start.15 = (bf16[4,72,256]{2,1,0:T(8,128)(2,1)S(1)}, bf16[4,72,256]{2,1,0:T(8,128)(2,1)S(1)}, u32[]{:S(2)}, u32[]{:S(2)}) collective-permute-start(bf16[4,72,256]{2,1,0:T(8,128)(2,1)S(1)} %get-tuple-element.18), channel_id=1, source_target_pairs={{0,2},{1,3},{2,4},{3,5},{4,6},{5,7},{6,0},{7,1},{8,10},{9,11},{10,... | collective-permute-start | bytes 442376 | tf_op jit(solution)/shard_map/ppermute | solution.py:198
  82.2 1.7 %collective-permute-start.7 = (bf16[4,72,256]{2,1,0:T(8,128)(2,1)S(1)}, bf16[4,72,256]{2,1,0:T(8,128)(2,1)S(1)}, u32[]{:S(2)}, u32[]{:S(2)}) collective-permute-start(bf16[4,72,256]{2,1,0:T(8,128)(2,1)S(1)} %get-tuple-element.15), channel_id=1, source_target_pairs={{0,4},{1,5},{2,6},{3,7},{4,0},{5,1},{6,2},{7,3},{8,12},{9,13},{10,... | collective-permute-start | bytes 442376 | tf_op jit(solution)/shard_map/ppermute | solution.py:198
  83.9 2.2 %collective-permute-start.8 = (bf16[4,72,256]{2,1,0:T(8,128)(2,1)S(1)}, bf16[4,72,256]{2,1,0:T(8,128)(2,1)S(1)}, u32[]{:S(2)}, u32[]{:S(2)}) collective-permute-start(bf16[4,72,256]{2,1,0:T(8,128)(2,1)S(1)} %get-tuple-element.16), channel_id=1, source_target_pairs={{0,6},{1,7},{2,0},{3,1},{4,2},{5,3},{6,4},{7,5},{8,14},{9,15},{10,... | collective-permute-start | bytes 442376 | tf_op jit(solution)/shard_map/ppermute | solution.py:198
  86.9 1.8 %collective-permute-start.17 = (bf16[4,72,256]{2,1,0:T(8,128)(2,1)S(1)}, bf16[4,72,256]{2,1,0:T(8,128)(2,1)S(1)}, u32[]{:S(2)}, u32[]{:S(2)}) collective-permute-start(bf16[4,72,256]{2,1,0:T(8,128)(2,1)S(1)} %get-tuple-element.20), channel_id=1, source_target_pairs={{0,6},{1,7},{2,0},{3,1},{4,2},{5,3},{6,4},{7,5},{8,14},{9,15},{10,... | collective-permute-start | bytes 442376 | tf_op jit(solution)/shard_map/ppermute | solution.py:198
  88.7 1.6 %collective-permute-done.7.refs_2_ = bf16[4,72,256]{2,1,0:T(8,128)(2,1)S(1)} collective-permute-done((bf16[4,72,256]{2,1,0:T(8,128)(2,1)S(1)}, bf16[4,72,256]{2,1,0:T(8,128)(2,1)S(1)}, u32[]{:S(2)}, u32[]{:S(2)}) %collective-permute-start.7) | collective-permute-done | bytes 147488 | tf_op jit(solution)/shard_map/ppermute | solution.py:198
  92.8 1.7 %collective-permute-done.17.refs_4_ = bf16[4,72,256]{2,1,0:T(8,128)(2,1)S(1)} collective-permute-done((bf16[4,72,256]{2,1,0:T(8,128)(2,1)S(1)}, bf16[4,72,256]{2,1,0:T(8,128)(2,1)S(1)}, u32[]{:S(2)}, u32[]{:S(2)}) %collective-permute-start.17) | collective-permute-done | bytes 147488 | tf_op jit(solution)/shard_map/ppermute | solution.py:198
  95.8 12.9 %all-to-all-start = ((bf16[8,72,256]{2,1,0:T(8,128)(2,1)}), bf16[8,72,256]{2,1,0:T(8,128)(2,1)S(1)}, u32[]{:S(2)}, u32[]{:S(2)}) async-start(bf16[8,72,256]{2,1,0:T(8,128)(2,1)} %shard_map.68), calls=%async_computation | async-start | bytes 589824 | tf_op jit(solution)/shard_map/all_to_all | solution.py:200
  108.8 10.3 %all-to-all-done.chips_ref = bf16[8,72,256]{2,1,0:T(8,128)(2,1)S(1)} async-done(((bf16[8,72,256]{2,1,0:T(8,128)(2,1)}), bf16[8,72,256]{2,1,0:T(8,128)(2,1)S(1)}, u32[]{:S(2)}, u32[]{:S(2)}) %all-to-all-start) | async-done | bytes 294944 | tf_op jit(solution)/shard_map/all_to_all | solution.py:200
  (45 shorter events, 21.9 us)
Async XLA Ops:
  0.0 61.9 %collective-permute-start = (bf16[1,4,512,1152]{3,2,1,0:T(8,128)(2,1)}, bf16[1,4,512,1152]{3,2,1,0:T(8,128)(2,1)}, u32[]{:S(2)}, u32[]{:S(2)}) collective-permute-start(bf16[1,4,512,1152]{3,2,1,0:T(8,128)(2,1)} %param.9), channel_id=1, source_target_pairs={{0,1},{1,0},{2,3},{3,2},{4,5},{5,4},{6,7},{7,6},{8,9},{9,8},{10,11... | collective-permute-start | bytes 14155784 | tf_op jit(solution)/shard_map/ppermute | solution.py:169
  5.5 23.4 %copy-start.4 = (bf16[1,256,512]{2,1,0:T(8,128)(2,1)}, bf16[1,256,512]{2,1,0:T(8,128)(2,1)S(1)}, u32[]{:S(2)}) copy-start(bf16[1,256,512]{2,1,0:T(8,128)(2,1)S(1)} %get-tuple-element.29) | copy-start | bytes 786436
  5.5 14.9 %collective-permute-start.9 = (bf16[256,512]{1,0:T(8,128)(2,1)S(1)}, bf16[256,512]{1,0:T(8,128)(2,1)S(1)}, u32[]{:S(2)}, u32[]{:S(2)}) collective-permute-start(bf16[256,512]{1,0:T(8,128)(2,1)S(1)} %bitcast.64), channel_id=1, source_target_pairs={{0,128},{1,129},{2,130},{3,131},{4,132},{5,133},{6,134},{7,135},{8... | collective-permute-start | bytes 786440 | tf_op jit(solution)/shard_map/ppermute | solution.py:176
  12.7 14.0 %collective-permute-start.10 = (bf16[256,512]{1,0:T(8,128)(2,1)}, bf16[256,512]{1,0:T(8,128)(2,1)S(1)}, u32[]{:S(2)}, u32[]{:S(2)}) collective-permute-start(bf16[256,512]{1,0:T(8,128)(2,1)} %get-tuple-element.30), channel_id=1, source_target_pairs={{0,129},{1,128},{2,131},{3,130},{4,133},{5,132},{6,135},{7,134},{8... | collective-permute-start | bytes 786440 | tf_op jit(solution)/shard_map/ppermute | solution.py:177
  12.7 21.8 %collective-permute-start.1 = (bf16[256,512]{1,0:T(8,128)(2,1)}, bf16[256,512]{1,0:T(8,128)(2,1)}, u32[]{:S(2)}, u32[]{:S(2)}) collective-permute-start(bf16[256,512]{1,0:T(8,128)(2,1)} %get-tuple-element.30), channel_id=1, source_target_pairs={{0,1},{1,0},{2,3},{3,2},{4,5},{5,4},{6,7},{7,6},{8,9},{9,8},{10,11... | collective-permute-start | bytes 786440 | tf_op jit(solution)/shard_map/ppermute | solution.py:178
  27.6 17.0 %collective-permute-start.11 = (bf16[2,256,512]{2,1,0:T(8,128)(2,1)}, bf16[2,256,512]{2,1,0:T(8,128)(2,1)}, u32[]{:S(2)}, u32[]{:S(2)}) collective-permute-start(bf16[2,256,512]{2,1,0:T(8,128)(2,1)} %pad_maximum_fusion.1.refs_6_), channel_id=1, source_target_pairs={{0,32},{32,64},{64,96},{1,33},{33,65},{65,97},{2,34},{34,66},{66,9... | collective-permute-start | bytes 1572872 | tf_op jit(solution)/shard_map/ppermute | solution.py:186
  28.9 18.0 %collective-permute-start.12 = (bf16[2,256,512]{2,1,0:T(8,128)(2,1)}, bf16[2,256,512]{2,1,0:T(8,128)(2,1)}, u32[]{:S(2)}, u32[]{:S(2)}) collective-permute-start(bf16[2,256,512]{2,1,0:T(8,128)(2,1)} %pad_maximum_fusion.1.refs_6_), channel_id=1, source_target_pairs={{0,96},{32,0},{1,97},{33,1},{2,98},{34,2},{3,99},{35,3},{4,100},{3... | collective-permute-start | bytes 1572872 | tf_op jit(solution)/shard_map/ppermute | solution.py:187
  35.5 20.2 %collective-permute-start.2 = (bf16[2,256,512]{2,1,0:T(8,128)(2,1)S(1)}, bf16[2,256,512]{2,1,0:T(8,128)(2,1)S(1)}, u32[]{:S(2)}, u32[]{:S(2)}) collective-permute-start(bf16[2,256,512]{2,1,0:T(8,128)(2,1)S(1)} %pad_maximum_fusion.refs_8_), channel_id=1, source_target_pairs={{0,32},{32,64},{64,96},{1,33},{33,65},{65,97},{2,34},{34,66},{66,9... | collective-permute-start | bytes 1572872 | tf_op jit(solution)/shard_map/ppermute | solution.py:186
  36.9 22.0 %collective-permute-start.3 = (bf16[2,256,512]{2,1,0:T(8,128)(2,1)S(1)}, bf16[2,256,512]{2,1,0:T(8,128)(2,1)S(1)}, u32[]{:S(2)}, u32[]{:S(2)}) collective-permute-start(bf16[2,256,512]{2,1,0:T(8,128)(2,1)S(1)} %pad_maximum_fusion.refs_8_), channel_id=1, source_target_pairs={{0,96},{32,0},{1,97},{33,1},{2,98},{34,2},{3,99},{35,3},{4,100},{3... | collective-permute-start | bytes 1572872 | tf_op jit(solution)/shard_map/ppermute | solution.py:187
  45.5 33.3 %collective-permute-start.13 = (bf16[256,512]{1,0:T(8,128)(2,1)S(1)}, bf16[256,512]{1,0:T(8,128)(2,1)S(1)}, u32[]{:S(2)}, u32[]{:S(2)}) collective-permute-start(bf16[256,512]{1,0:T(8,128)(2,1)S(1)} %slice_bitcast_fusion.1), channel_id=1, source_target_pairs={{32,64},{64,96},{33,65},{65,97},{34,66},{66,98},{35,67},{67,99},{3... | collective-permute-start | bytes 786440 | tf_op jit(solution)/shard_map/ppermute | solution.py:188
  47.8 31.0 %collective-permute-start.14 = (bf16[256,512]{1,0:T(8,128)(2,1)S(1)}, bf16[256,512]{1,0:T(8,128)(2,1)S(1)}, u32[]{:S(2)}, u32[]{:S(2)}) collective-permute-start(bf16[256,512]{1,0:T(8,128)(2,1)S(1)} %slice_bitcast_fusion), channel_id=1, source_target_pairs={{96,64},{0,96},{97,65},{1,97},{98,66},{2,98},{99,67},{3,99},{100,6... | collective-permute-start | bytes 786440 | tf_op jit(solution)/shard_map/ppermute | solution.py:189
  55.7 10.2 %collective-permute-start.4 = (bf16[256,512]{1,0:T(8,128)(2,1)S(1)}, bf16[256,512]{1,0:T(8,128)(2,1)S(1)}, u32[]{:S(2)}, u32[]{:S(2)}) collective-permute-start(bf16[256,512]{1,0:T(8,128)(2,1)S(1)} %slice_bitcast_fusion.3), channel_id=1, source_target_pairs={{32,64},{64,96},{33,65},{65,97},{34,66},{66,98},{35,67},{67,99},{3... | collective-permute-start | bytes 786440 | tf_op jit(solution)/shard_map/ppermute | solution.py:188
  59.0 9.8 %copy-start.1 = (bf16[512,1152]{1,0:T(8,128)(2,1)S(1)}, bf16[512,1152]{1,0:T(8,128)(2,1)}, u32[]{:S(2)}) copy-start(bf16[512,1152]{1,0:T(8,128)(2,1)} %get-tuple-element.27.refs_0_) | copy-start | bytes 3538948
  59.0 9.8 %copy-start.2 = (bf16[512,1152]{1,0:T(8,128)(2,1)S(1)}, bf16[512,1152]{1,0:T(8,128)(2,1)}, u32[]{:S(2)}) copy-start(bf16[512,1152]{1,0:T(8,128)(2,1)} %get-tuple-element.28.refs_4_) | copy-start | bytes 3538948
  59.0 9.8 %copy-start.3 = (bf16[512,1152]{1,0:T(8,128)(2,1)S(1)}, bf16[512,1152]{1,0:T(8,128)(2,1)}, u32[]{:S(2)}) copy-start(bf16[512,1152]{1,0:T(8,128)(2,1)} %get-tuple-element.25.refs_6_.refs_0_) | copy-start | bytes 3538948
  59.0 9.7 %collective-permute-start.5 = (bf16[256,512]{1,0:T(8,128)(2,1)S(1)}, bf16[256,512]{1,0:T(8,128)(2,1)S(1)}, u32[]{:S(2)}, u32[]{:S(2)}) collective-permute-start(bf16[256,512]{1,0:T(8,128)(2,1)S(1)} %slice_bitcast_fusion.2), channel_id=1, source_target_pairs={{96,64},{0,96},{97,65},{1,97},{98,66},{2,98},{99,67},{3,99},{100,6... | collective-permute-start | bytes 786440 | tf_op jit(solution)/shard_map/ppermute | solution.py:189
  73.0 13.8 %collective-permute-start.6 = (bf16[4,72,256]{2,1,0:T(8,128)(2,1)S(1)}, bf16[4,72,256]{2,1,0:T(8,128)(2,1)S(1)}, u32[]{:S(2)}, u32[]{:S(2)}) collective-permute-start(bf16[4,72,256]{2,1,0:T(8,128)(2,1)S(1)} %get-tuple-element.14), channel_id=1, source_target_pairs={{0,2},{1,3},{2,4},{3,5},{4,6},{5,7},{6,0},{7,1},{8,10},{9,11},{10,... | collective-permute-start | bytes 442376 | tf_op jit(solution)/shard_map/ppermute | solution.py:198
  80.7 11.2 %collective-permute-start.15 = (bf16[4,72,256]{2,1,0:T(8,128)(2,1)S(1)}, bf16[4,72,256]{2,1,0:T(8,128)(2,1)S(1)}, u32[]{:S(2)}, u32[]{:S(2)}) collective-permute-start(bf16[4,72,256]{2,1,0:T(8,128)(2,1)S(1)} %get-tuple-element.18), channel_id=1, source_target_pairs={{0,2},{1,3},{2,4},{3,5},{4,6},{5,7},{6,0},{7,1},{8,10},{9,11},{10,... | collective-permute-start | bytes 442376 | tf_op jit(solution)/shard_map/ppermute | solution.py:198
  82.2 8.0 %collective-permute-start.7 = (bf16[4,72,256]{2,1,0:T(8,128)(2,1)S(1)}, bf16[4,72,256]{2,1,0:T(8,128)(2,1)S(1)}, u32[]{:S(2)}, u32[]{:S(2)}) collective-permute-start(bf16[4,72,256]{2,1,0:T(8,128)(2,1)S(1)} %get-tuple-element.15), channel_id=1, source_target_pairs={{0,4},{1,5},{2,6},{3,7},{4,0},{5,1},{6,2},{7,3},{8,12},{9,13},{10,... | collective-permute-start | bytes 442376 | tf_op jit(solution)/shard_map/ppermute | solution.py:198
  83.9 7.3 %collective-permute-start.8 = (bf16[4,72,256]{2,1,0:T(8,128)(2,1)S(1)}, bf16[4,72,256]{2,1,0:T(8,128)(2,1)S(1)}, u32[]{:S(2)}, u32[]{:S(2)}) collective-permute-start(bf16[4,72,256]{2,1,0:T(8,128)(2,1)S(1)} %get-tuple-element.16), channel_id=1, source_target_pairs={{0,6},{1,7},{2,0},{3,1},{4,2},{5,3},{6,4},{7,5},{8,14},{9,15},{10,... | collective-permute-start | bytes 442376 | tf_op jit(solution)/shard_map/ppermute | solution.py:198
  86.1 6.6 %collective-permute-start.16 = (bf16[4,72,256]{2,1,0:T(8,128)(2,1)S(1)}, bf16[4,72,256]{2,1,0:T(8,128)(2,1)S(1)}, u32[]{:S(2)}, u32[]{:S(2)}) collective-permute-start(bf16[4,72,256]{2,1,0:T(8,128)(2,1)S(1)} %get-tuple-element.19), channel_id=1, source_target_pairs={{0,4},{1,5},{2,6},{3,7},{4,0},{5,1},{6,2},{7,3},{8,12},{9,13},{10,... | collective-permute-start | bytes 442376 | tf_op jit(solution)/shard_map/ppermute | solution.py:198
  86.9 7.6 %collective-permute-start.17 = (bf16[4,72,256]{2,1,0:T(8,128)(2,1)S(1)}, bf16[4,72,256]{2,1,0:T(8,128)(2,1)S(1)}, u32[]{:S(2)}, u32[]{:S(2)}) collective-permute-start(bf16[4,72,256]{2,1,0:T(8,128)(2,1)S(1)} %get-tuple-element.20), channel_id=1, source_target_pairs={{0,6},{1,7},{2,0},{3,1},{4,2},{5,3},{6,4},{7,5},{8,14},{9,15},{10,... | collective-permute-start | bytes 442376 | tf_op jit(solution)/shard_map/ppermute | solution.py:198
  91.3 17.5 %copy-start.5 = (f32[1,36]{1,0:T(1,128)S(1)}, f32[1,36]{1,0:T(1,128)}, u32[]{:S(2)}) copy-start(f32[1,36]{1,0:T(1,128)} %param.10) | copy-start | bytes 436
  95.8 23.4 %all-to-all-start = ((bf16[8,72,256]{2,1,0:T(8,128)(2,1)}), bf16[8,72,256]{2,1,0:T(8,128)(2,1)S(1)}, u32[]{:S(2)}, u32[]{:S(2)}) async-start(bf16[8,72,256]{2,1,0:T(8,128)(2,1)} %shard_map.68), calls=%async_computation | async-start | bytes 589824 | tf_op jit(solution)/shard_map/all_to_all | solution.py:200
  (1 other events, 1.7 us)

commit v5 on v4

--- a/solution.py
+++ b/solution.py
@@ -25,6 +25,10 @@
         (feat_at(z, x, c), feat_at(z, (x + by) % NX, c))
         for z in range(NZ) for x in range(NX) for c in range(2)
     ]
+
+
+def ring(by):
+    return [(i, (i + by) % 4) for i in range(4)]
 
 
 ZC_GROUPS = [[feat_at(z, x, c) for z in range(NZ) for c in range(2)] for x in range(NX)]
@@ -53,14 +57,10 @@
 GRANT = 12
 
 
-def terms_of(at_ref, backs, weights, blocks, cols):
+def terms_of(weights, blocks, cols):
     total = None
     for i, block in enumerate(blocks):
-        back = backs[i // 2]
-        acts = block[...]
-        if back == 3:
-            acts = jnp.where(at_ref[1] == 3, acts, jnp.zeros_like(acts))
-        term = jnp.dot(acts, weights[i][:, cols], preferred_element_type=F32)
+        term = jnp.dot(block[...], weights[i][:, cols], preferred_element_type=F32)
         total = term if total is None else total + term
     return total
 
@@ -81,7 +81,7 @@
     blocks = split_blocks(blocks)
     for n in range(total_ref.shape[1] // TILE):
         cols = slice(n * TILE, (n + 1) * TILE)
-        total_ref[:, cols] = terms_of(at_ref, backs, weights, blocks, cols)
+        total_ref[:, cols] = terms_of(weights, blocks, cols)
 
 
 def partial(at, weights, backs, blocks):
@@ -101,7 +101,7 @@
     blocks = split_blocks(refs[has_base:])
     for n in range(turned.shape[0] // TILE):
         cols = slice(n * TILE, (n + 1) * TILE)
-        total = terms_of(at_ref, backs, weights, blocks, cols)
+        total = terms_of(weights, blocks, cols)
         if has_base:
             total = total + refs[0][:, cols]
         turned[cols, :] = total.T
@@ -176,17 +176,20 @@
     other_mine = lax.ppermute(keep, ("dp", "feat"), across(0))
     other_theirs = lax.ppermute(send, ("dp", "feat"), across(1))
     own_theirs = lax.ppermute(send, "feat", PARTNER)
-    sources = [jnp.maximum(target - back, 0) for back in range(4)]
-    mine_w = [lax.dynamic_index_in_dim(dec_weight[0], s, 0, keepdims=False) for s in sources]
-    theirs_w = [lax.dynamic_index_in_dim(w_theirs[0], s, 0, keepdims=False) for s in sources]
+    def cut(decoders, back):
+        matrix = lax.dynamic_index_in_dim(decoders[0], jnp.maximum(target - back, 0), 0, keepdims=False)
+        return jnp.where(target >= back, matrix, jnp.zeros_like(matrix)) if back else matrix
+
+    mine_w = [cut(dec_weight, back) for back in range(4)]
+    theirs_w = [cut(w_theirs, back) for back in range(4)]
     weights = list(zip(mine_w, theirs_w))
     chips = []
     for name, mine, theirs in (("own", keep, own_theirs), ("other", other_mine, other_theirs)):
         both = jnp.stack([mine, theirs])
-        up = lax.ppermute(both, "layer", [(0, 1), (1, 2), (2, 3)])
-        down = lax.ppermute(both, "layer", [(0, 3), (1, 0)])
-        far_up = lax.ppermute(up[0], "layer", [(1, 2), (2, 3)])
-        far_down = lax.ppermute(down[1], "layer", [(3, 2), (0, 3)])
+        up = lax.ppermute(both, "layer", ring(1))
+        down = lax.ppermute(both, "layer", ring(-1))
+        far_up = lax.ppermute(up[0], "layer", ring(1))
+        far_down = lax.ppermute(down[1], "layer", ring(-1))
         near, far = [both, up, down], [far_up, far_down]
         if name == "own":
             kept, *away = last(at, weights, [], (0, 1, 3, 2), near + far)
@@ -214,6 +217,4 @@
     out_specs = P("layer", None, ("dp", "feat"))
 
 
-    return jax.shard_map(
-        per_device, mesh=mesh, in_specs=in_specs, out_specs=out_specs, check_vma=False
-    )
+    return jax.shard_map(per_device, mesh=mesh, in_specs=in_specs, out_specs=out_specs, check_vma=False)

time: 121 us -> 120 us (level)
  other arithmetic: 2.94 us -> 10.1 us
  starting transfers between devices: 45.2 us -> 38.2 us
  local copies, waits for them, and re-layouts: 10.6 us -> 3.61 us
  waiting for transfers between devices: 45.1 us -> 50.1 us
    select_n x0 -> x2, other arithmetic: none -> 7.12 us  [cut(): jnp.where(target >= back, matrix, jnp.zeros_like(matrix))]
    squeeze x6 -> x4, local copies, waits for them, and re-layouts: 8.95 us -> 1.97 us  [the longest x2 0.99 us: per_device(): far_down = lax.ppermute(down[1], 'layer', ring(-1))]
    ppermute x8, starting transfers between devices: 15.2 us -> 8.68 us  [the longest x2 3.01 us: per_device(): far_up = lax.ppermute(up[0], 'layer', ring(1))]
    ppermute x8, waiting for transfers between devices: 15.7 us -> 18.7 us  [the longest x2 12.6 us: per_device(): up = lax.ppermute(both, 'layer', ring(1))]
    ppermute x6, waiting for transfers between devices: 5.17 us -> 7.19 us  [per_device(): came.append(lax.ppermute(piece, 'feat', x_pairs(by + 1)))]
  transfers between devices with their start and end apart: 19 -> 19, of which waited for: 12 -> 10; matrix products, arithmetic and copies ran while one was open for 13% -> 13% of each run, Pallas kernels for 9% -> 9%
where the time goes in v5:
time: 120 us; the launch traced here: 119 us
  waiting for transfers between devices  50.1 us (42%)
  starting transfers between devices  38.2 us (32%)
  Pallas kernels  13.5 us (11%)
  other arithmetic  10.1 us (8%)
  local copies, waits for them, and re-layouts  3.61 us (3%)
  matrix products  3.05 us (3%)
    pallas_call x6, Pallas kernels, call(): pl.pallas_call(kernel, out_shape=out_shape, in_specs=[IN_SMEM] + [IN_VMEM...  13.5 us
    all_to_all x1, starting transfers between devices, per_device(): lax.all_to_all(chips[0], 'feat', 0, 0, tiled=True, axis_index_groups=ZC_G...  12.6 us
    ppermute x2, waiting for transfers between devices, per_device(): up = lax.ppermute(both, 'layer', ring(1))  12.6 us
    all_to_all x1, waiting for transfers between devices, per_device(): lax.all_to_all(chips[0], 'feat', 0, 0, tiled=True, axis_index_groups=ZC_G...  10.3 us
    ppermute x6, starting transfers between devices, per_device(): came.append(lax.ppermute(piece, 'feat', x_pairs(by + 1)))  9.57 us
    ppermute x1, waiting for transfers between devices, per_device(): other_mine = lax.ppermute(keep, ('dp', 'feat'), across(0))  7.64 us
    ppermute x1, starting transfers between devices, per_device(): other_mine = lax.ppermute(keep, ('dp', 'feat'), across(0))  7.19 us
    ppermute x6, waiting for transfers between devices, per_device(): came.append(lax.ppermute(piece, 'feat', x_pairs(by + 1)))  7.19 us
  transfers between devices with their start and end apart: 19, of which 10 were waited for; matrix products, arithmetic and copies ran while one was open for 13% of the time, Pallas kernels for 9%

profile of v5, /device:TPU:24, one launch (start us, length us, event | category | flops | bytes accessed | tf_op | source)
XLA Modules:
  0.0 118.7 jit_solution(1620048340322657290)
XLA Ops:
  1.7 3.0 %fusion.18 = bf16[512,512]{1,0:T(8,128)(2,1)S(1)} fusion(bf16[1,2304,512]{2,1,0:T(8,128)(2,1)S(1)} %copy-done, bf16[1,512,2304]{2,1,0:T(8,128)(2,1)} %param.6, f32[512]{0:T(512)S(1)} %convert_bitcast_fusion, f32[512]{0:T(512)} %bitcast.69), kind=kOutput, calls=%fused_computation.6 | convolution fusion | flops 1209008128 | bytes 5246976 | tf_op jit(solution)/shard_map/dot_general | solution.py:171
  5.5 7.2 %collective-permute-start.9 = (bf16[256,512]{1,0:T(8,128)(2,1)S(1)}, bf16[256,512]{1,0:T(8,128)(2,1)S(1)}, u32[]{:S(2)}, u32[]{:S(2)}) collective-permute-start(bf16[256,512]{1,0:T(8,128)(2,1)S(1)} %bitcast.64), channel_id=1, source_target_pairs={{0,128},{1,129},{2,130},{3,131},{4,132},{5,133},{6,134},{7,135},{8... | collective-permute-start | bytes 786440 | tf_op jit(solution)/shard_map/ppermute | solution.py:176
  12.8 7.6 %collective-permute-done.9 = bf16[256,512]{1,0:T(8,128)(2,1)S(1)} collective-permute-done((bf16[256,512]{1,0:T(8,128)(2,1)S(1)}, bf16[256,512]{1,0:T(8,128)(2,1)S(1)}, u32[]{:S(2)}, u32[]{:S(2)}) %collective-permute-start.9) | collective-permute-done | bytes 262176 | tf_op jit(solution)/shard_map/ppermute | solution.py:176
  20.4 6.2 %collective-permute-done.10 = bf16[256,512]{1,0:T(8,128)(2,1)S(1)} collective-permute-done((bf16[256,512]{1,0:T(8,128)(2,1)}, bf16[256,512]{1,0:T(8,128)(2,1)S(1)}, u32[]{:S(2)}, u32[]{:S(2)}) %collective-permute-start.10) | collective-permute-done | bytes 262176 | tf_op jit(solution)/shard_map/ppermute | solution.py:177
  27.8 1.8 %collective-permute-start.12 = (bf16[2,256,512]{2,1,0:T(8,128)(2,1)}, bf16[2,256,512]{2,1,0:T(8,128)(2,1)}, u32[]{:S(2)}, u32[]{:S(2)}) collective-permute-start(bf16[2,256,512]{2,1,0:T(8,128)(2,1)} %pad_maximum_fusion.1.refs_6_), channel_id=1, source_target_pairs={{0,96},{32,0},{64,32},{96,64},{1,97},{33,1},{65,33},{97,65},{2,98}... | collective-permute-start | bytes 1572872 | tf_op jit(solution)/shard_map/ppermute | solution.py:190
  29.6 4.3 %select_bitcast_fusion.1 = (bf16[512,1152]{1,0:T(8,128)(2,1)}, bf16[512,1152]{1,0:T(8,128)(2,1)S(1)}, bf16[512,1152]{1,0:T(8,128)(2,1)}, bf16[512,1152]{1,0:T(8,128)(2,1)}) fusion(bf16[1,4,512,1152]{3,2,1,0:T(8,128)(2,1)} %param.9, s32[]{:T(128)S(6)} %max.27, pred[]{:T(512)S(6)} %ge.14, s32[]{:T(128)S(6)} %max.25, pred[]{:T(512)S(6)} %ge.12, s32[]{:T(128)S(6)} %max.24, ...), kind=kLoop, calls=%fused_computation.8 | loop fusion | flops 1769472 | bytes 9437203 | tf_op jit(solution)/shard_map/jit(_where)/select_n | solution.py:181
  34.9 1.9 %collective-permute-start.2 = (bf16[2,256,512]{2,1,0:T(8,128)(2,1)S(1)}, bf16[2,256,512]{2,1,0:T(8,128)(2,1)S(1)}, u32[]{:S(2)}, u32[]{:S(2)}) collective-permute-start(bf16[2,256,512]{2,1,0:T(8,128)(2,1)S(1)} %pad_maximum_fusion.refs_8_), channel_id=1, source_target_pairs={{0,32},{32,64},{64,96},{96,0},{1,33},{33,65},{65,97},{97,1},{2,34}... | collective-permute-start | bytes 1572872 | tf_op jit(solution)/shard_map/ppermute | solution.py:189
  37.1 5.6 %collective-permute-done.11.refs_7_ = bf16[2,256,512]{2,1,0:T(8,128)(2,1)} collective-permute-done((bf16[2,256,512]{2,1,0:T(8,128)(2,1)}, bf16[2,256,512]{2,1,0:T(8,128)(2,1)}, u32[]{:S(2)}, u32[]{:S(2)}) %collective-permute-start.11) | collective-permute-done | bytes 524320 | tf_op jit(solution)/shard_map/ppermute | solution.py:189
  46.8 7.0 %collective-permute-done.2.refs_9_ = bf16[2,256,512]{2,1,0:T(8,128)(2,1)S(1)} collective-permute-done((bf16[2,256,512]{2,1,0:T(8,128)(2,1)S(1)}, bf16[2,256,512]{2,1,0:T(8,128)(2,1)S(1)}, u32[]{:S(2)}, u32[]{:S(2)}) %collective-permute-start.2) | collective-permute-done | bytes 524320 | tf_op jit(solution)/shard_map/ppermute | solution.py:189
  56.3 2.9 %select_bitcast_fusion = (bf16[512,1152]{1,0:T(8,128)(2,1)S(1)}, bf16[512,1152]{1,0:T(8,128)(2,1)S(1)}, bf16[512,1152]{1,0:T(8,128)(2,1)S(1)}, bf16[512,1152]{1,0:T(8,128)(2,1)S(1)}) fusion(bf16[1,4,512,1152]{3,2,1,0:T(8,128)(2,1)} %collective-permute-done, s32[]{:T(128)S(6)} %max.27, pred[]{:T(512)S(6)} %ge.14, s32[]{:T(128)S(6)} %max.26, pred[]{:T(512)S(6)} %ge.13, ...), kind=kLoop, calls=%fused_computation.7 | loop fusion | flops 1769472 | bytes 9437203 | tf_op jit(solution)/shard_map/jit(_where)/select_n | solution.py:181
  59.1 5.0 %collective-permute-done.4.refs_11_ = bf16[256,512]{1,0:T(8,128)(2,1)S(1)} collective-permute-done((bf16[256,512]{1,0:T(8,128)(2,1)S(1)}, bf16[256,512]{1,0:T(8,128)(2,1)S(1)}, u32[]{:S(2)}, u32[]{:S(2)}) %collective-permute-start.4) | collective-permute-done | bytes 262176 | tf_op jit(solution)/shard_map/ppermute | solution.py:191
  65.3 4.3 %shard_map.64 = (f32[4,72,256]{2,1,0:T(8,128)S(1)}, bf16[4,72,256]{2,1,0:T(8,128)(2,1)S(1)}, bf16[4,72,256]{2,1,0:T(8,128)(2,1)S(1)}, bf16[4,72,256]{2,1,0:T(8,128)(2,1)S(1)}) custom-call(s32[4]{0:T(128)S(1)} %pad_add_fusion.at_ref, bf16[512,1152]{1,0:T(8,128)(2,1)S(1)} %copy-done.1, bf16[512,1152]{1,0:T(8,128)(2,1)S(1)} %get-tuple-element.24.refs_1_, ...), custom_call_target="tpu_custom_call" | custom-call | flops 2415919104 | bytes 11534352 | tf_op jit(solution)/shard_map/pallas_call | solution.py:45
  69.6 1.6 %collective-permute-start.6 = (bf16[4,72,256]{2,1,0:T(8,128)(2,1)S(1)}, bf16[4,72,256]{2,1,0:T(8,128)(2,1)S(1)}, u32[]{:S(2)}, u32[]{:S(2)}) collective-permute-start(bf16[4,72,256]{2,1,0:T(8,128)(2,1)S(1)} %get-tuple-element.14), channel_id=1, source_target_pairs={{0,2},{1,3},{2,4},{3,5},{4,6},{5,7},{6,0},{7,1},{8,10},{9,11},{10,... | collective-permute-start | bytes 442376 | tf_op jit(solution)/shard_map/ppermute | solution.py:201
  71.2 4.0 %shard_map.66.refs_2_ = f32[256,1152]{1,0:T(8,128)S(1)} custom-call(s32[4]{0:T(128)S(1)} %pad_add_fusion.at_ref, bf16[512,1152]{1,0:T(8,128)(2,1)S(1)} %copy-done.1, bf16[512,1152]{1,0:T(8,128)(2,1)S(1)} %get-tuple-element.24.refs_1_, bf16[512,1152]{1,0:T(8,128)(2,1)S(1)} %get-tuple-element.26.refs_2_, bf16[512,1152]{1,0:T(8,128)(2,1)S(1)} %get-tuple-element.23.refs_3_, ...), custom_call_target="tpu_custom_call" | custom-call | flops 1811939328 | bytes 8650768 | tf_op jit(solution)/shard_map/pallas_call | solution.py:45
  75.2 1.8 %shard_map.67 = (f32[4,72,256]{2,1,0:T(8,128)S(1)}, bf16[4,72,256]{2,1,0:T(8,128)(2,1)S(1)}, bf16[4,72,256]{2,1,0:T(8,128)(2,1)S(1)}, bf16[4,72,256]{2,1,0:T(8,128)(2,1)S(1)}) custom-call(s32[4]{0:T(128)S(1)} %pad_add_fusion.at_ref, bf16[512,1152]{1,0:T(8,128)(2,1)S(1)} %copy-done.3, bf16[512,1152]{1,0:T(8,128)(2,1)S(1)} %get-tuple-element.21.refs_7_.refs_1_, ...), custom_call_target="tpu_custom_call" | custom-call | flops 603979776 | bytes 4063248 | tf_op jit(solution)/shard_map/pallas_call | solution.py:45
  77.0 1.6 %collective-permute-start.15 = (bf16[4,72,256]{2,1,0:T(8,128)(2,1)S(1)}, bf16[4,72,256]{2,1,0:T(8,128)(2,1)S(1)}, u32[]{:S(2)}, u32[]{:S(2)}) collective-permute-start(bf16[4,72,256]{2,1,0:T(8,128)(2,1)S(1)} %get-tuple-element.18), channel_id=1, source_target_pairs={{0,2},{1,3},{2,4},{3,5},{4,6},{5,7},{6,0},{7,1},{8,10},{9,11},{10,... | collective-permute-start | bytes 442376 | tf_op jit(solution)/shard_map/ppermute | solution.py:201
  78.6 1.7 %collective-permute-start.7 = (bf16[4,72,256]{2,1,0:T(8,128)(2,1)S(1)}, bf16[4,72,256]{2,1,0:T(8,128)(2,1)S(1)}, u32[]{:S(2)}, u32[]{:S(2)}) collective-permute-start(bf16[4,72,256]{2,1,0:T(8,128)(2,1)S(1)} %get-tuple-element.15), channel_id=1, source_target_pairs={{0,4},{1,5},{2,6},{3,7},{4,0},{5,1},{6,2},{7,3},{8,12},{9,13},{10,... | collective-permute-start | bytes 442376 | tf_op jit(solution)/shard_map/ppermute | solution.py:201
  80.3 2.1 %collective-permute-start.8 = (bf16[4,72,256]{2,1,0:T(8,128)(2,1)S(1)}, bf16[4,72,256]{2,1,0:T(8,128)(2,1)S(1)}, u32[]{:S(2)}, u32[]{:S(2)}) collective-permute-start(bf16[4,72,256]{2,1,0:T(8,128)(2,1)S(1)} %get-tuple-element.16), channel_id=1, source_target_pairs={{0,6},{1,7},{2,0},{3,1},{4,2},{5,3},{6,4},{7,5},{8,14},{9,15},{10,... | collective-permute-start | bytes 442376 | tf_op jit(solution)/shard_map/ppermute | solution.py:201
  83.3 1.8 %collective-permute-start.17 = (bf16[4,72,256]{2,1,0:T(8,128)(2,1)S(1)}, bf16[4,72,256]{2,1,0:T(8,128)(2,1)S(1)}, u32[]{:S(2)}, u32[]{:S(2)}) collective-permute-start(bf16[4,72,256]{2,1,0:T(8,128)(2,1)S(1)} %get-tuple-element.20), channel_id=1, source_target_pairs={{0,6},{1,7},{2,0},{3,1},{4,2},{5,3},{6,4},{7,5},{8,14},{9,15},{10,... | collective-permute-start | bytes 442376 | tf_op jit(solution)/shard_map/ppermute | solution.py:201
  85.0 2.3 %collective-permute-done.7.refs_2_ = bf16[4,72,256]{2,1,0:T(8,128)(2,1)S(1)} collective-permute-done((bf16[4,72,256]{2,1,0:T(8,128)(2,1)S(1)}, bf16[4,72,256]{2,1,0:T(8,128)(2,1)S(1)}, u32[]{:S(2)}, u32[]{:S(2)}) %collective-permute-start.7) | collective-permute-done | bytes 147488 | tf_op jit(solution)/shard_map/ppermute | solution.py:201
  87.3 1.8 %collective-permute-done.8.refs_3_ = bf16[4,72,256]{2,1,0:T(8,128)(2,1)S(1)} collective-permute-done((bf16[4,72,256]{2,1,0:T(8,128)(2,1)S(1)}, bf16[4,72,256]{2,1,0:T(8,128)(2,1)S(1)}, u32[]{:S(2)}, u32[]{:S(2)}) %collective-permute-start.8) | collective-permute-done | bytes 147488 | tf_op jit(solution)/shard_map/ppermute | solution.py:201
  89.7 3.1 %collective-permute-done.17.refs_4_ = bf16[4,72,256]{2,1,0:T(8,128)(2,1)S(1)} collective-permute-done((bf16[4,72,256]{2,1,0:T(8,128)(2,1)S(1)}, bf16[4,72,256]{2,1,0:T(8,128)(2,1)S(1)}, u32[]{:S(2)}, u32[]{:S(2)}) %collective-permute-start.17) | collective-permute-done | bytes 147488 | tf_op jit(solution)/shard_map/ppermute | solution.py:201
  94.2 12.6 %all-to-all-start = ((bf16[8,72,256]{2,1,0:T(8,128)(2,1)}), bf16[8,72,256]{2,1,0:T(8,128)(2,1)S(1)}, u32[]{:S(2)}, u32[]{:S(2)}) async-start(bf16[8,72,256]{2,1,0:T(8,128)(2,1)} %shard_map.68), calls=%async_computation | async-start | bytes 589824 | tf_op jit(solution)/shard_map/all_to_all | solution.py:203
  106.9 10.3 %all-to-all-done.chips_ref = bf16[8,72,256]{2,1,0:T(8,128)(2,1)S(1)} async-done(((bf16[8,72,256]{2,1,0:T(8,128)(2,1)}), bf16[8,72,256]{2,1,0:T(8,128)(2,1)S(1)}, u32[]{:S(2)}, u32[]{:S(2)}) %all-to-all-start) | async-done | bytes 294944 | tf_op jit(solution)/shard_map/all_to_all | solution.py:203
  (45 shorter events, 17.1 us)
Async XLA Ops:
  0.0 56.3 %collective-permute-start = (bf16[1,4,512,1152]{3,2,1,0:T(8,128)(2,1)}, bf16[1,4,512,1152]{3,2,1,0:T(8,128)(2,1)}, u32[]{:S(2)}, u32[]{:S(2)}) collective-permute-start(bf16[1,4,512,1152]{3,2,1,0:T(8,128)(2,1)} %param.9), channel_id=1, source_target_pairs={{0,1},{1,0},{2,3},{3,2},{4,5},{5,4},{6,7},{7,6},{8,9},{9,8},{10,11... | collective-permute-start | bytes 14155784 | tf_op jit(solution)/shard_map/ppermute | solution.py:169
  5.5 22.3 %copy-start.4 = (bf16[1,256,512]{2,1,0:T(8,128)(2,1)}, bf16[1,256,512]{2,1,0:T(8,128)(2,1)S(1)}, u32[]{:S(2)}) copy-start(bf16[1,256,512]{2,1,0:T(8,128)(2,1)S(1)} %get-tuple-element.29) | copy-start | bytes 786436
  5.5 14.9 %collective-permute-start.9 = (bf16[256,512]{1,0:T(8,128)(2,1)S(1)}, bf16[256,512]{1,0:T(8,128)(2,1)S(1)}, u32[]{:S(2)}, u32[]{:S(2)}) collective-permute-start(bf16[256,512]{1,0:T(8,128)(2,1)S(1)} %bitcast.64), channel_id=1, source_target_pairs={{0,128},{1,129},{2,130},{3,131},{4,132},{5,133},{6,134},{7,135},{8... | collective-permute-start | bytes 786440 | tf_op jit(solution)/shard_map/ppermute | solution.py:176
  12.7 14.0 %collective-permute-start.10 = (bf16[256,512]{1,0:T(8,128)(2,1)}, bf16[256,512]{1,0:T(8,128)(2,1)S(1)}, u32[]{:S(2)}, u32[]{:S(2)}) collective-permute-start(bf16[256,512]{1,0:T(8,128)(2,1)} %get-tuple-element.30), channel_id=1, source_target_pairs={{0,129},{1,128},{2,131},{3,130},{4,133},{5,132},{6,135},{7,134},{8... | collective-permute-start | bytes 786440 | tf_op jit(solution)/shard_map/ppermute | solution.py:177
  12.7 21.2 %collective-permute-start.1 = (bf16[256,512]{1,0:T(8,128)(2,1)}, bf16[256,512]{1,0:T(8,128)(2,1)}, u32[]{:S(2)}, u32[]{:S(2)}) collective-permute-start(bf16[256,512]{1,0:T(8,128)(2,1)} %get-tuple-element.30), channel_id=1, source_target_pairs={{0,1},{1,0},{2,3},{3,2},{4,5},{5,4},{6,7},{7,6},{8,9},{9,8},{10,11... | collective-permute-start | bytes 786440 | tf_op jit(solution)/shard_map/ppermute | solution.py:178
  27.6 15.1 %collective-permute-start.11 = (bf16[2,256,512]{2,1,0:T(8,128)(2,1)}, bf16[2,256,512]{2,1,0:T(8,128)(2,1)}, u32[]{:S(2)}, u32[]{:S(2)}) collective-permute-start(bf16[2,256,512]{2,1,0:T(8,128)(2,1)} %pad_maximum_fusion.1.refs_6_), channel_id=1, source_target_pairs={{0,32},{32,64},{64,96},{96,0},{1,33},{33,65},{65,97},{97,1},{2,34}... | collective-permute-start | bytes 1572872 | tf_op jit(solution)/shard_map/ppermute | solution.py:189
  27.8 17.4 %collective-permute-start.12 = (bf16[2,256,512]{2,1,0:T(8,128)(2,1)}, bf16[2,256,512]{2,1,0:T(8,128)(2,1)}, u32[]{:S(2)}, u32[]{:S(2)}) collective-permute-start(bf16[2,256,512]{2,1,0:T(8,128)(2,1)} %pad_maximum_fusion.1.refs_6_), channel_id=1, source_target_pairs={{0,96},{32,0},{64,32},{96,64},{1,97},{33,1},{65,33},{97,65},{2,98}... | collective-permute-start | bytes 1572872 | tf_op jit(solution)/shard_map/ppermute | solution.py:190
  34.9 18.9 %collective-permute-start.2 = (bf16[2,256,512]{2,1,0:T(8,128)(2,1)S(1)}, bf16[2,256,512]{2,1,0:T(8,128)(2,1)S(1)}, u32[]{:S(2)}, u32[]{:S(2)}) collective-permute-start(bf16[2,256,512]{2,1,0:T(8,128)(2,1)S(1)} %pad_maximum_fusion.refs_8_), channel_id=1, source_target_pairs={{0,32},{32,64},{64,96},{96,0},{1,33},{33,65},{65,97},{97,1},{2,34}... | collective-permute-start | bytes 1572872 | tf_op jit(solution)/shard_map/ppermute | solution.py:189
  36.9 18.4 %collective-permute-start.3 = (bf16[2,256,512]{2,1,0:T(8,128)(2,1)S(1)}, bf16[2,256,512]{2,1,0:T(8,128)(2,1)S(1)}, u32[]{:S(2)}, u32[]{:S(2)}) collective-permute-start(bf16[2,256,512]{2,1,0:T(8,128)(2,1)S(1)} %pad_maximum_fusion.refs_8_), channel_id=1, source_target_pairs={{0,96},{32,0},{64,32},{96,64},{1,97},{33,1},{65,33},{97,65},{2,98}... | collective-permute-start | bytes 1572872 | tf_op jit(solution)/shard_map/ppermute | solution.py:190
  43.7 31.6 %collective-permute-start.13 = (bf16[256,512]{1,0:T(8,128)(2,1)S(1)}, bf16[256,512]{1,0:T(8,128)(2,1)S(1)}, u32[]{:S(2)}, u32[]{:S(2)}) collective-permute-start(bf16[256,512]{1,0:T(8,128)(2,1)S(1)} %slice_bitcast_fusion.1), channel_id=1, source_target_pairs={{0,32},{32,64},{64,96},{96,0},{1,33},{33,65},{65,97},{97,1},{2,34}... | collective-permute-start | bytes 786440 | tf_op jit(solution)/shard_map/ppermute | solution.py:191
  46.1 29.1 %collective-permute-start.14 = (bf16[256,512]{1,0:T(8,128)(2,1)S(1)}, bf16[256,512]{1,0:T(8,128)(2,1)S(1)}, u32[]{:S(2)}, u32[]{:S(2)}) collective-permute-start(bf16[256,512]{1,0:T(8,128)(2,1)S(1)} %slice_bitcast_fusion), channel_id=1, source_target_pairs={{0,96},{32,0},{64,32},{96,64},{1,97},{33,1},{65,33},{97,65},{2,98}... | collective-permute-start | bytes 786440 | tf_op jit(solution)/shard_map/ppermute | solution.py:192
  53.8 10.2 %collective-permute-start.4 = (bf16[256,512]{1,0:T(8,128)(2,1)S(1)}, bf16[256,512]{1,0:T(8,128)(2,1)S(1)}, u32[]{:S(2)}, u32[]{:S(2)}) collective-permute-start(bf16[256,512]{1,0:T(8,128)(2,1)S(1)} %slice_bitcast_fusion.3), channel_id=1, source_target_pairs={{0,32},{32,64},{64,96},{96,0},{1,33},{33,65},{65,97},{97,1},{2,34}... | collective-permute-start | bytes 786440 | tf_op jit(solution)/shard_map/ppermute | solution.py:191
  55.4 9.9 %copy-start.1 = (bf16[512,1152]{1,0:T(8,128)(2,1)S(1)}, bf16[512,1152]{1,0:T(8,128)(2,1)}, u32[]{:S(2)}) copy-start(bf16[512,1152]{1,0:T(8,128)(2,1)} %get-tuple-element.27.refs_0_) | copy-start | bytes 3538948
  55.4 9.9 %copy-start.2 = (bf16[512,1152]{1,0:T(8,128)(2,1)S(1)}, bf16[512,1152]{1,0:T(8,128)(2,1)}, u32[]{:S(2)}) copy-start(bf16[512,1152]{1,0:T(8,128)(2,1)} %get-tuple-element.28.refs_4_) | copy-start | bytes 3538948
  55.4 9.9 %copy-start.3 = (bf16[512,1152]{1,0:T(8,128)(2,1)S(1)}, bf16[512,1152]{1,0:T(8,128)(2,1)}, u32[]{:S(2)}) copy-start(bf16[512,1152]{1,0:T(8,128)(2,1)} %get-tuple-element.25.refs_6_.refs_0_) | copy-start | bytes 3538948
  55.4 9.9 %collective-permute-start.5 = (bf16[256,512]{1,0:T(8,128)(2,1)S(1)}, bf16[256,512]{1,0:T(8,128)(2,1)S(1)}, u32[]{:S(2)}, u32[]{:S(2)}) collective-permute-start(bf16[256,512]{1,0:T(8,128)(2,1)S(1)} %slice_bitcast_fusion.2), channel_id=1, source_target_pairs={{0,96},{32,0},{64,32},{96,64},{1,97},{33,1},{65,33},{97,65},{2,98}... | collective-permute-start | bytes 786440 | tf_op jit(solution)/shard_map/ppermute | solution.py:192
  69.6 13.7 %collective-permute-start.6 = (bf16[4,72,256]{2,1,0:T(8,128)(2,1)S(1)}, bf16[4,72,256]{2,1,0:T(8,128)(2,1)S(1)}, u32[]{:S(2)}, u32[]{:S(2)}) collective-permute-start(bf16[4,72,256]{2,1,0:T(8,128)(2,1)S(1)} %get-tuple-element.14), channel_id=1, source_target_pairs={{0,2},{1,3},{2,4},{3,5},{4,6},{5,7},{6,0},{7,1},{8,10},{9,11},{10,... | collective-permute-start | bytes 442376 | tf_op jit(solution)/shard_map/ppermute | solution.py:201
  77.0 12.7 %collective-permute-start.15 = (bf16[4,72,256]{2,1,0:T(8,128)(2,1)S(1)}, bf16[4,72,256]{2,1,0:T(8,128)(2,1)S(1)}, u32[]{:S(2)}, u32[]{:S(2)}) collective-permute-start(bf16[4,72,256]{2,1,0:T(8,128)(2,1)S(1)} %get-tuple-element.18), channel_id=1, source_target_pairs={{0,2},{1,3},{2,4},{3,5},{4,6},{5,7},{6,0},{7,1},{8,10},{9,11},{10,... | collective-permute-start | bytes 442376 | tf_op jit(solution)/shard_map/ppermute | solution.py:201
  78.6 8.7 %collective-permute-start.7 = (bf16[4,72,256]{2,1,0:T(8,128)(2,1)S(1)}, bf16[4,72,256]{2,1,0:T(8,128)(2,1)S(1)}, u32[]{:S(2)}, u32[]{:S(2)}) collective-permute-start(bf16[4,72,256]{2,1,0:T(8,128)(2,1)S(1)} %get-tuple-element.15), channel_id=1, source_target_pairs={{0,4},{1,5},{2,6},{3,7},{4,0},{5,1},{6,2},{7,3},{8,12},{9,13},{10,... | collective-permute-start | bytes 442376 | tf_op jit(solution)/shard_map/ppermute | solution.py:201
  80.3 8.8 %collective-permute-start.8 = (bf16[4,72,256]{2,1,0:T(8,128)(2,1)S(1)}, bf16[4,72,256]{2,1,0:T(8,128)(2,1)S(1)}, u32[]{:S(2)}, u32[]{:S(2)}) collective-permute-start(bf16[4,72,256]{2,1,0:T(8,128)(2,1)S(1)} %get-tuple-element.16), channel_id=1, source_target_pairs={{0,6},{1,7},{2,0},{3,1},{4,2},{5,3},{6,4},{7,5},{8,14},{9,15},{10,... | collective-permute-start | bytes 442376 | tf_op jit(solution)/shard_map/ppermute | solution.py:201
  82.5 7.3 %collective-permute-start.16 = (bf16[4,72,256]{2,1,0:T(8,128)(2,1)S(1)}, bf16[4,72,256]{2,1,0:T(8,128)(2,1)S(1)}, u32[]{:S(2)}, u32[]{:S(2)}) collective-permute-start(bf16[4,72,256]{2,1,0:T(8,128)(2,1)S(1)} %get-tuple-element.19), channel_id=1, source_target_pairs={{0,4},{1,5},{2,6},{3,7},{4,0},{5,1},{6,2},{7,3},{8,12},{9,13},{10,... | collective-permute-start | bytes 442376 | tf_op jit(solution)/shard_map/ppermute | solution.py:201
  83.3 9.6 %collective-permute-start.17 = (bf16[4,72,256]{2,1,0:T(8,128)(2,1)S(1)}, bf16[4,72,256]{2,1,0:T(8,128)(2,1)S(1)}, u32[]{:S(2)}, u32[]{:S(2)}) collective-permute-start(bf16[4,72,256]{2,1,0:T(8,128)(2,1)S(1)} %get-tuple-element.20), channel_id=1, source_target_pairs={{0,6},{1,7},{2,0},{3,1},{4,2},{5,3},{6,4},{7,5},{8,14},{9,15},{10,... | collective-permute-start | bytes 442376 | tf_op jit(solution)/shard_map/ppermute | solution.py:201
  89.1 17.7 %copy-start.5 = (f32[1,36]{1,0:T(1,128)S(1)}, f32[1,36]{1,0:T(1,128)}, u32[]{:S(2)}) copy-start(f32[1,36]{1,0:T(1,128)} %param.10) | copy-start | bytes 436
  94.2 23.0 %all-to-all-start = ((bf16[8,72,256]{2,1,0:T(8,128)(2,1)}), bf16[8,72,256]{2,1,0:T(8,128)(2,1)S(1)}, u32[]{:S(2)}, u32[]{:S(2)}) async-start(bf16[8,72,256]{2,1,0:T(8,128)(2,1)} %shard_map.68), calls=%async_computation | async-start | bytes 589824 | tf_op jit(solution)/shard_map/all_to_all | solution.py:203
  (1 other events, 1.7 us)

commit v6 on v5

--- a/solution.py
+++ b/solution.py
@@ -57,10 +57,10 @@
 GRANT = 12
 
 
-def terms_of(weights, blocks, cols):
+def terms_of(backs, weights, blocks, cols):
     total = None
     for i, block in enumerate(blocks):
-        term = jnp.dot(block[...], weights[i][:, cols], preferred_element_type=F32)
+        term = jnp.dot(block[...], weights[i % 2][backs[i // 2], :, cols], preferred_element_type=F32)
         total = term if total is None else total + term
     return total
 
@@ -72,36 +72,62 @@
     return out
 
 
-def pick(weights, backs):
-    return [w for back in backs for w in weights[back]]
+def cut_kernel(at_ref, decoders_ref, out_ref, sems):
+    target = at_ref[1]
+    copies = [
+        pltpu.make_async_copy(decoders_ref.at[0, jnp.maximum(target - back, 0)], out_ref.at[back], sems.at[back])
+        for back in range(4)
+    ]
+    for copy in copies:
+        copy.start()
+    for back, copy in enumerate(copies):
+        copy.wait()
+        if back:
+
+            @pl.when(target < back)
+            def _(back=back):
+                out_ref[back] = jnp.zeros_like(out_ref[back])
+
+
+def cut(at, decoders):
+    return pl.pallas_call(
+        cut_kernel,
+        out_shape=jax.ShapeDtypeStruct(decoders.shape[1:], BF),
+        in_specs=[IN_SMEM, pl.BlockSpec(memory_space=pltpu.HBM)],
+        out_specs=IN_VMEM,
+        scratch_shapes=[pltpu.SemaphoreType.DMA((4,))],
+        compiler_params=pltpu.CompilerParams(vmem_limit_bytes=6 * MIB),
+        cost_estimate=pl.CostEstimate(flops=0, bytes_accessed=2 * decoders.size, transcendentals=0),
+        name="cut",
+    )(at, decoders)
 
 
 def partial_kernel(backs, at_ref, *refs):
-    weights, blocks, total_ref = refs[: 2 * len(backs)], refs[2 * len(backs) : -1], refs[-1]
+    weights, blocks, total_ref = refs[:2], refs[2:-1], refs[-1]
     blocks = split_blocks(blocks)
     for n in range(total_ref.shape[1] // TILE):
         cols = slice(n * TILE, (n + 1) * TILE)
-        total_ref[:, cols] = terms_of(weights, blocks, cols)
+        total_ref[:, cols] = terms_of(backs, weights, blocks, cols)
 
 
 def partial(at, weights, backs, blocks):
-    rows, cols = blocks[0].shape[-2], weights[0][0].shape[1]
+    rows, cols = blocks[0].shape[-2], weights[0].shape[2]
     return call(
         functools.partial(partial_kernel, backs),
         jax.ShapeDtypeStruct((rows, cols), F32),
-        [at, *pick(weights, backs), *blocks], GRANT, flops=4 * len(backs) * rows * 512 * cols,
+        [at, *weights, *blocks], GRANT, flops=4 * len(backs) * rows * 512 * cols,
     )
 
 
 def last_kernel(backs, has_base, at_ref, *refs):
-    weights, refs = refs[: 2 * len(backs)], refs[2 * len(backs) :]
+    weights, refs = refs[:2], refs[2:]
     turned = refs[-1]
     self_ref, *away = refs[-5:-1]
     refs = refs[:-5]
     blocks = split_blocks(refs[has_base:])
     for n in range(turned.shape[0] // TILE):
         cols = slice(n * TILE, (n + 1) * TILE)
-        total = terms_of(weights, blocks, cols)
+        total = terms_of(backs, weights, blocks, cols)
         if has_base:
             total = total + refs[0][:, cols]
         turned[cols, :] = total.T
@@ -116,12 +142,12 @@
 
 
 def last(at, weights, base, backs, blocks):
-    rows, cols = blocks[0].shape[-2], weights[0][0].shape[1]
+    rows, cols = blocks[0].shape[-2], weights[0].shape[2]
     piece = (NZ, cols // (NX * NZ), rows)
     return call(
         functools.partial(last_kernel, backs, len(base)),
         [jax.ShapeDtypeStruct(piece, F32)] + [jax.ShapeDtypeStruct(piece, BF)] * 3,
-        [at, *pick(weights, backs), *base, *blocks], GRANT,
+        [at, *weights, *base, *blocks], GRANT,
         scratch=[pltpu.VMEM((cols, rows), F32)], flops=4 * len(backs) * rows * 512 * cols,
     )
 
@@ -176,26 +202,19 @@
     other_mine = lax.ppermute(keep, ("dp", "feat"), across(0))
     other_theirs = lax.ppermute(send, ("dp", "feat"), across(1))
     own_theirs = lax.ppermute(send, "feat", PARTNER)
-    def cut(decoders, back):
-        matrix = lax.dynamic_index_in_dim(decoders[0], jnp.maximum(target - back, 0), 0, keepdims=False)
-        return jnp.where(target >= back, matrix, jnp.zeros_like(matrix)) if back else matrix
-
-    mine_w = [cut(dec_weight, back) for back in range(4)]
-    theirs_w = [cut(w_theirs, back) for back in range(4)]
-    weights = list(zip(mine_w, theirs_w))
+    mine_w = cut(at, dec_weight)
+    theirs_w = cut(at, w_theirs)
+    weights = (mine_w, theirs_w)
     chips = []
-    for name, mine, theirs in (("own", keep, own_theirs), ("other", other_mine, other_theirs)):
+    for mine, theirs in ((keep, own_theirs), (other_mine, other_theirs)):
         both = jnp.stack([mine, theirs])
         up = lax.ppermute(both, "layer", ring(1))
         down = lax.ppermute(both, "layer", ring(-1))
         far_up = lax.ppermute(up[0], "layer", ring(1))
         far_down = lax.ppermute(down[1], "layer", ring(-1))
         near, far = [both, up, down], [far_up, far_down]
-        if name == "own":
-            kept, *away = last(at, weights, [], (0, 1, 3, 2), near + far)
-        else:
-            total = partial(at, weights, (0, 1, 3), near)
-            kept, *away = last(at, weights, [total], (2,), far)
+        total = partial(at, weights, (0, 1, 3), near)
+        kept, *away = last(at, weights, [total], (2,), far)
         came = []
         for by, piece in enumerate(away):
             came.append(lax.ppermute(piece, "feat", x_pairs(by + 1)))

time: 120 us -> 116 us (0.967)
  the two profiles are of different devices: /device:TPU:24 before, /device:TPU:1 now
where the time goes in v6:
time: 116 us; the launch traced here: 115 us
  waiting for transfers between devices  45.2 us (39%)
  starting transfers between devices  41.9 us (36%)
  Pallas kernels  19.7 us (17%)
  local copies, waits for them, and re-layouts  4.46 us (4%)
  matrix products  3.05 us (3%)
    all_to_all x1, starting transfers between devices, per_device(): lax.all_to_all(chips[0], 'feat', 0, 0, tiled=True, axis_index_groups=ZC_G...  16.7 us
    ppermute x2, waiting for transfers between devices, per_device(): up = lax.ppermute(both, 'layer', ring(1))  16.3 us
    pallas_call x7, Pallas kernels, call(): pl.pallas_call(kernel, out_shape=out_shape, in_specs=[IN_SMEM] + [IN_VMEM...  14.3 us
    all_to_all x1, waiting for transfers between devices, per_device(): lax.all_to_all(chips[0], 'feat', 0, 0, tiled=True, axis_index_groups=ZC_G...  9.23 us
    ppermute x1, waiting for transfers between devices, per_device(): other_theirs = lax.ppermute(send, ('dp', 'feat'), across(1))  8.89 us
    ppermute x6, starting transfers between devices, per_device(): came.append(lax.ppermute(piece, 'feat', x_pairs(by + 1)))  7.89 us
    ppermute x6, waiting for transfers between devices, per_device(): came.append(lax.ppermute(piece, 'feat', x_pairs(by + 1)))  6.23 us
    ppermute x1, starting transfers between devices, per_device(): other_mine = lax.ppermute(keep, ('dp', 'feat'), across(0))  5.55 us
  transfers between devices with their start and end apart: 19, of which 9 were waited for; matrix products, arithmetic and copies ran while one was open for 5% of the time, Pallas kernels for 15%

profile of v6, /device:TPU:1, one launch (start us, length us, event | category | flops | bytes accessed | tf_op | source)
XLA Modules:
  0.0 115.3 jit_solution(4309702044970948401)
XLA Ops:
  0.0 3.2 %collective-permute-start = (bf16[1,4,512,1152]{3,2,1,0:T(8,128)(2,1)}, bf16[1,4,512,1152]{3,2,1,0:T(8,128)(2,1)}, u32[]{:S(2)}, u32[]{:S(2)}) collective-permute-start(bf16[1,4,512,1152]{3,2,1,0:T(8,128)(2,1)} %decoders_ref.1), channel_id=1, source_target_pairs={{0,1},{1,0},{2,3},{3,2},{4,5},{5,4},{6,7},{7,6},{8,9},{9,8},{10,11... | collective-permute-start | bytes 14155784 | tf_op jit(solution)/shard_map/ppermute | solution.py:195
  3.9 3.0 %fusion.18 = bf16[512,512]{1,0:T(8,128)(2,1)S(1)} fusion(bf16[1,2304,512]{2,1,0:T(8,128)(2,1)S(1)} %copy-done, bf16[1,512,2304]{2,1,0:T(8,128)(2,1)} %param.6, f32[512]{0:T(512)S(1)} %convert_bitcast_fusion, f32[512]{0:T(512)} %bitcast.54), kind=kOutput, calls=%fused_computation.6 | convolution fusion | flops 1209008128 | bytes 5246976 | tf_op jit(solution)/shard_map/dot_general | solution.py:197
  7.0 5.5 %collective-permute-start.9 = (bf16[256,512]{1,0:T(8,128)(2,1)S(1)}, bf16[256,512]{1,0:T(8,128)(2,1)S(1)}, u32[]{:S(2)}, u32[]{:S(2)}) collective-permute-start(bf16[256,512]{1,0:T(8,128)(2,1)S(1)} %bitcast.48), channel_id=1, source_target_pairs={{0,128},{1,129},{2,130},{3,131},{4,132},{5,133},{6,134},{7,135},{8... | collective-permute-start | bytes 786440 | tf_op jit(solution)/shard_map/ppermute | solution.py:202
  13.6 4.5 %collective-permute-done.9 = bf16[256,512]{1,0:T(8,128)(2,1)S(1)} collective-permute-done((bf16[256,512]{1,0:T(8,128)(2,1)S(1)}, bf16[256,512]{1,0:T(8,128)(2,1)S(1)}, u32[]{:S(2)}, u32[]{:S(2)}) %collective-permute-start.9) | collective-permute-done | bytes 262176 | tf_op jit(solution)/shard_map/ppermute | solution.py:202
  18.1 8.9 %collective-permute-done.10 = bf16[256,512]{1,0:T(8,128)(2,1)S(1)} collective-permute-done((bf16[256,512]{1,0:T(8,128)(2,1)S(1)}, bf16[256,512]{1,0:T(8,128)(2,1)S(1)}, u32[]{:S(2)}, u32[]{:S(2)}) %collective-permute-start.10) | collective-permute-done | bytes 262176 | tf_op jit(solution)/shard_map/ppermute | solution.py:203
  29.9 1.4 %collective-permute-start.3 = (bf16[2,256,512]{2,1,0:T(8,128)(2,1)S(1)}, bf16[2,256,512]{2,1,0:T(8,128)(2,1)S(1)}, u32[]{:S(2)}, u32[]{:S(2)}) collective-permute-start(bf16[2,256,512]{2,1,0:T(8,128)(2,1)S(1)} %pad_maximum_fusion.refs_2_), channel_id=1, source_target_pairs={{0,96},{32,0},{64,32},{96,64},{1,97},{33,1},{65,33},{97,65},{2,98}... | collective-permute-start | bytes 1572872 | tf_op jit(solution)/shard_map/ppermute | solution.py:212
  31.3 2.3 %copy-done.1 = bf16[1,4,512,1152]{3,2,1,0:T(8,128)(2,1)S(1)} copy-done((bf16[1,4,512,1152]{3,2,1,0:T(8,128)(2,1)S(1)}, bf16[1,4,512,1152]{3,2,1,0:T(8,128)(2,1)}, u32[]{:S(2)}) %copy-start.1) | copy-done | bytes 4718616
  33.7 1.8 %cut.2.refs_0_ = bf16[4,512,1152]{2,1,0:T(8,128)(2,1)S(1)} custom-call(s32[4]{0:T(128)S(1)} %pad_add_fusion.at_ref, bf16[1,4,512,1152]{3,2,1,0:T(8,128)(2,1)S(1)} %copy-done.1), custom_call_target="tpu_custom_call" | custom-call | bytes 4718592 | tf_op jit(solution)/shard_map/cut/pallas_call | solution.py:93
  35.7 6.1 %collective-permute-done.11.refs_3_ = bf16[2,256,512]{2,1,0:T(8,128)(2,1)} collective-permute-done((bf16[2,256,512]{2,1,0:T(8,128)(2,1)S(1)}, bf16[2,256,512]{2,1,0:T(8,128)(2,1)}, u32[]{:S(2)}, u32[]{:S(2)}) %collective-permute-start.11) | collective-permute-done | bytes 524320 | tf_op jit(solution)/shard_map/ppermute | solution.py:211
  42.8 10.2 %collective-permute-done.2.refs_3_ = bf16[2,256,512]{2,1,0:T(8,128)(2,1)} collective-permute-done((bf16[2,256,512]{2,1,0:T(8,128)(2,1)S(1)}, bf16[2,256,512]{2,1,0:T(8,128)(2,1)}, u32[]{:S(2)}, u32[]{:S(2)}) %collective-permute-start.2) | collective-permute-done | bytes 524320 | tf_op jit(solution)/shard_map/ppermute | solution.py:211
  54.1 2.7 %collective-permute-start.5 = (bf16[256,512]{1,0:T(8,128)(2,1)S(1)}, bf16[256,512]{1,0:T(8,128)(2,1)S(1)}, u32[]{:S(2)}, u32[]{:S(2)}) collective-permute-start(bf16[256,512]{1,0:T(8,128)(2,1)S(1)} %slice_bitcast_fusion.2), channel_id=1, source_target_pairs={{0,96},{32,0},{64,32},{96,64},{1,97},{33,1},{65,33},{97,65},{2,98}... | collective-permute-start | bytes 786440 | tf_op jit(solution)/shard_map/ppermute | solution.py:214
  57.1 3.6 %cut.3.refs_1_ = bf16[4,512,1152]{2,1,0:T(8,128)(2,1)S(1)} custom-call(s32[4]{0:T(128)S(1)} %pad_add_fusion.at_ref, bf16[1,4,512,1152]{3,2,1,0:T(8,128)(2,1)} %collective-permute-done.decoders_ref), custom_call_target="tpu_custom_call" | custom-call | bytes 4718592 | tf_op jit(solution)/shard_map/cut/pallas_call | solution.py:93
  60.7 3.7 %shard_map.64.refs_2_ = f32[256,1152]{1,0:T(8,128)S(1)} custom-call(s32[4]{0:T(128)S(1)} %pad_add_fusion.at_ref, bf16[4,512,1152]{2,1,0:T(8,128)(2,1)S(1)} %cut.2.refs_0_, bf16[4,512,1152]{2,1,0:T(8,128)(2,1)S(1)} %cut.3.refs_1_, bf16[2,256,512]{2,1,0:T(8,128)(2,1)S(1)} %pad_maximum_fusion.refs_2_, bf16[2,256,512]{2,1,0:T(8,128)(2,1)} %collective-permute-done.2.refs_3_, ...), custom_call_target="tpu_custom_call" | custom-call | flops 1811939328 | bytes 11010064 | tf_op jit(solution)/shard_map/pallas_call | solution.py:45
  64.4 1.8 %shard_map.65 = (f32[4,72,256]{2,1,0:T(8,128)S(1)}, bf16[4,72,256]{2,1,0:T(8,128)(2,1)S(1)}, bf16[4,72,256]{2,1,0:T(8,128)(2,1)S(1)}, bf16[4,72,256]{2,1,0:T(8,128)(2,1)S(1)}) custom-call(s32[4]{0:T(128)S(1)} %pad_add_fusion.at_ref, bf16[4,512,1152]{2,1,0:T(8,128)(2,1)S(1)} %cut.2.refs_0_, bf16[4,512,1152]{2,1,0:T(8,128)(2,1)S(1)} %cut.3.refs_1_, ...), custom_call_target="tpu_custom_call" | custom-call | flops 603979776 | bytes 11141136 | tf_op jit(solution)/shard_map/pallas_call | solution.py:45
  67.5 3.7 %shard_map.67.refs_2_ = f32[256,1152]{1,0:T(8,128)S(1)} custom-call(s32[4]{0:T(128)S(1)} %pad_add_fusion.at_ref, bf16[4,512,1152]{2,1,0:T(8,128)(2,1)S(1)} %cut.2.refs_0_, bf16[4,512,1152]{2,1,0:T(8,128)(2,1)S(1)} %cut.3.refs_1_, bf16[2,256,512]{2,1,0:T(8,128)(2,1)S(1)} %pad_maximum_fusion.1.refs_2_, bf16[2,256,512]{2,1,0:T(8,128)(2,1)} %collective-permute-done.11.refs_3_, ...), custom_call_target="tpu_custom_call" | custom-call | flops 1811939328 | bytes 11010064 | tf_op jit(solution)/shard_map/pallas_call | solution.py:45
  71.2 1.8 %shard_map.68 = (f32[4,72,256]{2,1,0:T(8,128)S(1)}, bf16[4,72,256]{2,1,0:T(8,128)(2,1)S(1)}, bf16[4,72,256]{2,1,0:T(8,128)(2,1)S(1)}, bf16[4,72,256]{2,1,0:T(8,128)(2,1)S(1)}) custom-call(s32[4]{0:T(128)S(1)} %pad_add_fusion.at_ref, bf16[4,512,1152]{2,1,0:T(8,128)(2,1)S(1)} %cut.2.refs_0_, bf16[4,512,1152]{2,1,0:T(8,128)(2,1)S(1)} %cut.3.refs_1_, ...), custom_call_target="tpu_custom_call" | custom-call | flops 603979776 | bytes 11141136 | tf_op jit(solution)/shard_map/pallas_call | solution.py:45
  74.3 1.4 %collective-permute-start.7 = (bf16[4,72,256]{2,1,0:T(8,128)(2,1)S(1)}, bf16[4,72,256]{2,1,0:T(8,128)(2,1)S(1)}, u32[]{:S(2)}, u32[]{:S(2)}) collective-permute-start(bf16[4,72,256]{2,1,0:T(8,128)(2,1)S(1)} %get-tuple-element.15), channel_id=1, source_target_pairs={{0,4},{1,5},{2,6},{3,7},{4,0},{5,1},{6,2},{7,3},{8,12},{9,13},{10,... | collective-permute-start | bytes 442376 | tf_op jit(solution)/shard_map/ppermute | solution.py:220
  75.7 1.9 %collective-permute-start.8 = (bf16[4,72,256]{2,1,0:T(8,128)(2,1)S(1)}, bf16[4,72,256]{2,1,0:T(8,128)(2,1)S(1)}, u32[]{:S(2)}, u32[]{:S(2)}) collective-permute-start(bf16[4,72,256]{2,1,0:T(8,128)(2,1)S(1)} %get-tuple-element.16), channel_id=1, source_target_pairs={{0,6},{1,7},{2,0},{3,1},{4,2},{5,3},{6,4},{7,5},{8,14},{9,15},{10,... | collective-permute-start | bytes 442376 | tf_op jit(solution)/shard_map/ppermute | solution.py:220
  78.1 1.5 %collective-permute-start.17 = (bf16[4,72,256]{2,1,0:T(8,128)(2,1)S(1)}, bf16[4,72,256]{2,1,0:T(8,128)(2,1)S(1)}, u32[]{:S(2)}, u32[]{:S(2)}) collective-permute-start(bf16[4,72,256]{2,1,0:T(8,128)(2,1)S(1)} %get-tuple-element.20), channel_id=1, source_target_pairs={{0,6},{1,7},{2,0},{3,1},{4,2},{5,3},{6,4},{7,5},{8,14},{9,15},{10,... | collective-permute-start | bytes 442376 | tf_op jit(solution)/shard_map/ppermute | solution.py:220
  81.3 3.6 %collective-permute-done.16.refs_3_ = bf16[4,72,256]{2,1,0:T(8,128)(2,1)S(1)} collective-permute-done((bf16[4,72,256]{2,1,0:T(8,128)(2,1)S(1)}, bf16[4,72,256]{2,1,0:T(8,128)(2,1)S(1)}, u32[]{:S(2)}, u32[]{:S(2)}) %collective-permute-start.16) | collective-permute-done | bytes 147488 | tf_op jit(solution)/shard_map/ppermute | solution.py:220
  84.9 1.5 %collective-permute-done.17.refs_4_ = bf16[4,72,256]{2,1,0:T(8,128)(2,1)S(1)} collective-permute-done((bf16[4,72,256]{2,1,0:T(8,128)(2,1)S(1)}, bf16[4,72,256]{2,1,0:T(8,128)(2,1)S(1)}, u32[]{:S(2)}, u32[]{:S(2)}) %collective-permute-start.17) | collective-permute-done | bytes 147488 | tf_op jit(solution)/shard_map/ppermute | solution.py:220
  87.7 16.7 %all-to-all-start = ((bf16[8,72,256]{2,1,0:T(8,128)(2,1)}), bf16[8,72,256]{2,1,0:T(8,128)(2,1)S(1)}, u32[]{:S(2)}, u32[]{:S(2)}) async-start(bf16[8,72,256]{2,1,0:T(8,128)(2,1)} %shard_map.69), calls=%async_computation | async-start | bytes 589824 | tf_op jit(solution)/shard_map/all_to_all | solution.py:222
  104.6 9.2 %all-to-all-done.chips_ref = bf16[8,72,256]{2,1,0:T(8,128)(2,1)S(1)} async-done(((bf16[8,72,256]{2,1,0:T(8,128)(2,1)}), bf16[8,72,256]{2,1,0:T(8,128)(2,1)S(1)}, u32[]{:S(2)}, u32[]{:S(2)}) %all-to-all-start) | async-done | bytes 294944 | tf_op jit(solution)/shard_map/all_to_all | solution.py:222
  113.8 1.5 %shard_map.70 = bf16[36,1024]{1,0:T(8,128)(2,1)} custom-call(s32[4]{0:T(128)S(1)} %pad_add_fusion.at_ref, bf16[8,72,256]{2,1,0:T(8,128)(2,1)S(1)} %all-to-all-done.chips_ref, f32[36,1]{1,0:T(8,128)S(1)} %copy.7.bias_ref), custom_call_target="tpu_custom_call" | custom-call | bytes 295072 | tf_op jit(solution)/shard_map/pallas_call | solution.py:45
  (40 shorter events, 13.6 us)
Async XLA Ops:
  0.0 3.9 %copy-start = (bf16[1,2304,512]{2,1,0:T(8,128)(2,1)S(1)}, bf16[1,2304,512]{2,1,0:T(8,128)(2,1)}, u32[]{:S(2)}) copy-start(bf16[1,2304,512]{2,1,0:T(8,128)(2,1)} %param.7) | copy-start | bytes 7077892
  0.0 57.1 %collective-permute-start = (bf16[1,4,512,1152]{3,2,1,0:T(8,128)(2,1)}, bf16[1,4,512,1152]{3,2,1,0:T(8,128)(2,1)}, u32[]{:S(2)}, u32[]{:S(2)}) collective-permute-start(bf16[1,4,512,1152]{3,2,1,0:T(8,128)(2,1)} %decoders_ref.1), channel_id=1, source_target_pairs={{0,1},{1,0},{2,3},{3,2},{4,5},{5,4},{6,7},{7,6},{8,9},{9,8},{10,11... | collective-permute-start | bytes 14155784 | tf_op jit(solution)/shard_map/ppermute | solution.py:195
  7.0 11.1 %collective-permute-start.9 = (bf16[256,512]{1,0:T(8,128)(2,1)S(1)}, bf16[256,512]{1,0:T(8,128)(2,1)S(1)}, u32[]{:S(2)}, u32[]{:S(2)}) collective-permute-start(bf16[256,512]{1,0:T(8,128)(2,1)S(1)} %bitcast.48), channel_id=1, source_target_pairs={{0,128},{1,129},{2,130},{3,131},{4,132},{5,133},{6,134},{7,135},{8... | collective-permute-start | bytes 786440 | tf_op jit(solution)/shard_map/ppermute | solution.py:202
  12.6 14.4 %collective-permute-start.10 = (bf16[256,512]{1,0:T(8,128)(2,1)S(1)}, bf16[256,512]{1,0:T(8,128)(2,1)S(1)}, u32[]{:S(2)}, u32[]{:S(2)}) collective-permute-start(bf16[256,512]{1,0:T(8,128)(2,1)S(1)} %get-tuple-element.22), channel_id=1, source_target_pairs={{0,129},{1,128},{2,131},{3,130},{4,133},{5,132},{6,135},{7,134},{8... | collective-permute-start | bytes 786440 | tf_op jit(solution)/shard_map/ppermute | solution.py:203
  13.6 14.8 %collective-permute-start.1 = (bf16[256,512]{1,0:T(8,128)(2,1)S(1)}, bf16[256,512]{1,0:T(8,128)(2,1)S(1)}, u32[]{:S(2)}, u32[]{:S(2)}) collective-permute-start(bf16[256,512]{1,0:T(8,128)(2,1)S(1)} %get-tuple-element.22), channel_id=1, source_target_pairs={{0,1},{1,0},{2,3},{3,2},{4,5},{5,4},{6,7},{7,6},{8,9},{9,8},{10,11... | collective-permute-start | bytes 786440 | tf_op jit(solution)/shard_map/ppermute | solution.py:204
  27.1 14.7 %collective-permute-start.11 = (bf16[2,256,512]{2,1,0:T(8,128)(2,1)S(1)}, bf16[2,256,512]{2,1,0:T(8,128)(2,1)}, u32[]{:S(2)}, u32[]{:S(2)}) collective-permute-start(bf16[2,256,512]{2,1,0:T(8,128)(2,1)S(1)} %pad_maximum_fusion.1.refs_2_), channel_id=1, source_target_pairs={{0,32},{32,64},{64,96},{96,0},{1,33},{33,65},{65,97},{97,1},{2,34}... | collective-permute-start | bytes 1572872 | tf_op jit(solution)/shard_map/ppermute | solution.py:211
  28.5 24.5 %collective-permute-start.2 = (bf16[2,256,512]{2,1,0:T(8,128)(2,1)S(1)}, bf16[2,256,512]{2,1,0:T(8,128)(2,1)}, u32[]{:S(2)}, u32[]{:S(2)}) collective-permute-start(bf16[2,256,512]{2,1,0:T(8,128)(2,1)S(1)} %pad_maximum_fusion.refs_2_), channel_id=1, source_target_pairs={{0,32},{32,64},{64,96},{96,0},{1,33},{33,65},{65,97},{97,1},{2,34}... | collective-permute-start | bytes 1572872 | tf_op jit(solution)/shard_map/ppermute | solution.py:211
  29.9 24.2 %collective-permute-start.3 = (bf16[2,256,512]{2,1,0:T(8,128)(2,1)S(1)}, bf16[2,256,512]{2,1,0:T(8,128)(2,1)S(1)}, u32[]{:S(2)}, u32[]{:S(2)}) collective-permute-start(bf16[2,256,512]{2,1,0:T(8,128)(2,1)S(1)} %pad_maximum_fusion.refs_2_), channel_id=1, source_target_pairs={{0,96},{32,0},{64,32},{96,64},{1,97},{33,1},{65,33},{97,65},{2,98}... | collective-permute-start | bytes 1572872 | tf_op jit(solution)/shard_map/ppermute | solution.py:212
  31.3 2.3 %copy-start.1 = (bf16[1,4,512,1152]{3,2,1,0:T(8,128)(2,1)S(1)}, bf16[1,4,512,1152]{3,2,1,0:T(8,128)(2,1)}, u32[]{:S(2)}) copy-start(bf16[1,4,512,1152]{3,2,1,0:T(8,128)(2,1)} %decoders_ref.1) | copy-start | bytes 14155780
  35.5 21.4 %collective-permute-start.12 = (bf16[2,256,512]{2,1,0:T(8,128)(2,1)S(1)}, bf16[2,256,512]{2,1,0:T(8,128)(2,1)S(1)}, u32[]{:S(2)}, u32[]{:S(2)}) collective-permute-start(bf16[2,256,512]{2,1,0:T(8,128)(2,1)S(1)} %pad_maximum_fusion.1.refs_2_), channel_id=1, source_target_pairs={{0,96},{32,0},{64,32},{96,64},{1,97},{33,1},{65,33},{97,65},{2,98}... | collective-permute-start | bytes 1572872 | tf_op jit(solution)/shard_map/ppermute | solution.py:212
  42.8 28.4 %collective-permute-start.13 = (bf16[256,512]{1,0:T(8,128)(2,1)S(1)}, bf16[256,512]{1,0:T(8,128)(2,1)S(1)}, u32[]{:S(2)}, u32[]{:S(2)}) collective-permute-start(bf16[256,512]{1,0:T(8,128)(2,1)S(1)} %slice_bitcast_fusion.1), channel_id=1, source_target_pairs={{0,32},{32,64},{64,96},{96,0},{1,33},{33,65},{65,97},{97,1},{2,34}... | collective-permute-start | bytes 786440 | tf_op jit(solution)/shard_map/ppermute | solution.py:213
  54.0 10.4 %collective-permute-start.4 = (bf16[256,512]{1,0:T(8,128)(2,1)S(1)}, bf16[256,512]{1,0:T(8,128)(2,1)S(1)}, u32[]{:S(2)}, u32[]{:S(2)}) collective-permute-start(bf16[256,512]{1,0:T(8,128)(2,1)S(1)} %slice_bitcast_fusion.3), channel_id=1, source_target_pairs={{0,32},{32,64},{64,96},{96,0},{1,33},{33,65},{65,97},{97,1},{2,34}... | collective-permute-start | bytes 786440 | tf_op jit(solution)/shard_map/ppermute | solution.py:213
  54.1 10.3 %collective-permute-start.5 = (bf16[256,512]{1,0:T(8,128)(2,1)S(1)}, bf16[256,512]{1,0:T(8,128)(2,1)S(1)}, u32[]{:S(2)}, u32[]{:S(2)}) collective-permute-start(bf16[256,512]{1,0:T(8,128)(2,1)S(1)} %slice_bitcast_fusion.2), channel_id=1, source_target_pairs={{0,96},{32,0},{64,32},{96,64},{1,97},{33,1},{65,33},{97,65},{2,98}... | collective-permute-start | bytes 786440 | tf_op jit(solution)/shard_map/ppermute | solution.py:214
  56.9 14.3 %collective-permute-start.14 = (bf16[256,512]{1,0:T(8,128)(2,1)S(1)}, bf16[256,512]{1,0:T(8,128)(2,1)S(1)}, u32[]{:S(2)}, u32[]{:S(2)}) collective-permute-start(bf16[256,512]{1,0:T(8,128)(2,1)S(1)} %slice_bitcast_fusion), channel_id=1, source_target_pairs={{0,96},{32,0},{64,32},{96,64},{1,97},{33,1},{65,33},{97,65},{2,98}... | collective-permute-start | bytes 786440 | tf_op jit(solution)/shard_map/ppermute | solution.py:214
  66.2 11.9 %collective-permute-start.6 = (bf16[4,72,256]{2,1,0:T(8,128)(2,1)S(1)}, bf16[4,72,256]{2,1,0:T(8,128)(2,1)S(1)}, u32[]{:S(2)}, u32[]{:S(2)}) collective-permute-start(bf16[4,72,256]{2,1,0:T(8,128)(2,1)S(1)} %get-tuple-element.14), channel_id=1, source_target_pairs={{0,2},{1,3},{2,4},{3,5},{4,6},{5,7},{6,0},{7,1},{8,10},{9,11},{10,... | collective-permute-start | bytes 442376 | tf_op jit(solution)/shard_map/ppermute | solution.py:220
  72.9 31.5 %copy-start.2 = (f32[1,36]{1,0:T(1,128)S(1)}, f32[1,36]{1,0:T(1,128)}, u32[]{:S(2)}) copy-start(f32[1,36]{1,0:T(1,128)} %param.10) | copy-start | bytes 436
  73.0 8.4 %collective-permute-start.15 = (bf16[4,72,256]{2,1,0:T(8,128)(2,1)S(1)}, bf16[4,72,256]{2,1,0:T(8,128)(2,1)S(1)}, u32[]{:S(2)}, u32[]{:S(2)}) collective-permute-start(bf16[4,72,256]{2,1,0:T(8,128)(2,1)S(1)} %get-tuple-element.18), channel_id=1, source_target_pairs={{0,2},{1,3},{2,4},{3,5},{4,6},{5,7},{6,0},{7,1},{8,10},{9,11},{10,... | collective-permute-start | bytes 442376 | tf_op jit(solution)/shard_map/ppermute | solution.py:220
  74.3 5.5 %collective-permute-start.7 = (bf16[4,72,256]{2,1,0:T(8,128)(2,1)S(1)}, bf16[4,72,256]{2,1,0:T(8,128)(2,1)S(1)}, u32[]{:S(2)}, u32[]{:S(2)}) collective-permute-start(bf16[4,72,256]{2,1,0:T(8,128)(2,1)S(1)} %get-tuple-element.15), channel_id=1, source_target_pairs={{0,4},{1,5},{2,6},{3,7},{4,0},{5,1},{6,2},{7,3},{8,12},{9,13},{10,... | collective-permute-start | bytes 442376 | tf_op jit(solution)/shard_map/ppermute | solution.py:220
  75.7 5.0 %collective-permute-start.8 = (bf16[4,72,256]{2,1,0:T(8,128)(2,1)S(1)}, bf16[4,72,256]{2,1,0:T(8,128)(2,1)S(1)}, u32[]{:S(2)}, u32[]{:S(2)}) collective-permute-start(bf16[4,72,256]{2,1,0:T(8,128)(2,1)S(1)} %get-tuple-element.16), channel_id=1, source_target_pairs={{0,6},{1,7},{2,0},{3,1},{4,2},{5,3},{6,4},{7,5},{8,14},{9,15},{10,... | collective-permute-start | bytes 442376 | tf_op jit(solution)/shard_map/ppermute | solution.py:220
  77.6 7.4 %collective-permute-start.16 = (bf16[4,72,256]{2,1,0:T(8,128)(2,1)S(1)}, bf16[4,72,256]{2,1,0:T(8,128)(2,1)S(1)}, u32[]{:S(2)}, u32[]{:S(2)}) collective-permute-start(bf16[4,72,256]{2,1,0:T(8,128)(2,1)S(1)} %get-tuple-element.19), channel_id=1, source_target_pairs={{0,4},{1,5},{2,6},{3,7},{4,0},{5,1},{6,2},{7,3},{8,12},{9,13},{10,... | collective-permute-start | bytes 442376 | tf_op jit(solution)/shard_map/ppermute | solution.py:220
  78.1 8.3 %collective-permute-start.17 = (bf16[4,72,256]{2,1,0:T(8,128)(2,1)S(1)}, bf16[4,72,256]{2,1,0:T(8,128)(2,1)S(1)}, u32[]{:S(2)}, u32[]{:S(2)}) collective-permute-start(bf16[4,72,256]{2,1,0:T(8,128)(2,1)S(1)} %get-tuple-element.20), channel_id=1, source_target_pairs={{0,6},{1,7},{2,0},{3,1},{4,2},{5,3},{6,4},{7,5},{8,14},{9,15},{10,... | collective-permute-start | bytes 442376 | tf_op jit(solution)/shard_map/ppermute | solution.py:220
  87.7 26.1 %all-to-all-start = ((bf16[8,72,256]{2,1,0:T(8,128)(2,1)}), bf16[8,72,256]{2,1,0:T(8,128)(2,1)S(1)}, u32[]{:S(2)}, u32[]{:S(2)}) async-start(bf16[8,72,256]{2,1,0:T(8,128)(2,1)} %shard_map.69), calls=%async_computation | async-start | bytes 589824 | tf_op jit(solution)/shard_map/all_to_all | solution.py:222

commit v7 on v6

--- a/solution.py
+++ b/solution.py
@@ -55,6 +55,7 @@
 
 TILE = 384
 GRANT = 12
+CUT_GRANT = 48
 
 
 def terms_of(backs, weights, blocks, cols):
@@ -72,34 +73,37 @@
     return out
 
 
-def cut_kernel(at_ref, decoders_ref, out_ref, sems):
+def cut_kernel(at_ref, mine_ref, theirs_ref, mine_out, theirs_out, sems):
     target = at_ref[1]
     copies = [
-        pltpu.make_async_copy(decoders_ref.at[0, jnp.maximum(target - back, 0)], out_ref.at[back], sems.at[back])
+        pltpu.make_async_copy(src.at[0, jnp.maximum(target - back, 0)], out.at[back], sems.at[i, back])
+        for i, (src, out) in enumerate(((mine_ref, mine_out), (theirs_ref, theirs_out)))
         for back in range(4)
     ]
     for copy in copies:
         copy.start()
-    for back, copy in enumerate(copies):
+    for copy in copies:
         copy.wait()
-        if back:
-
-            @pl.when(target < back)
-            def _(back=back):
-                out_ref[back] = jnp.zeros_like(out_ref[back])
-
-
-def cut(at, decoders):
+    for back in range(1, 4):
+
+        @pl.when(target < back)
+        def _(back=back):
+            for out in (mine_out, theirs_out):
+                out[back] = jnp.zeros_like(out[back])
+
+
+def cut(at, mine, theirs):
+    in_hbm = pl.BlockSpec(memory_space=pltpu.HBM)
     return pl.pallas_call(
         cut_kernel,
-        out_shape=jax.ShapeDtypeStruct(decoders.shape[1:], BF),
-        in_specs=[IN_SMEM, pl.BlockSpec(memory_space=pltpu.HBM)],
-        out_specs=IN_VMEM,
-        scratch_shapes=[pltpu.SemaphoreType.DMA((4,))],
-        compiler_params=pltpu.CompilerParams(vmem_limit_bytes=6 * MIB),
-        cost_estimate=pl.CostEstimate(flops=0, bytes_accessed=2 * decoders.size, transcendentals=0),
+        out_shape=[jax.ShapeDtypeStruct(mine.shape[1:], BF)] * 2,
+        in_specs=[IN_SMEM, in_hbm, in_hbm],
+        out_specs=[IN_VMEM] * 2,
+        scratch_shapes=[pltpu.SemaphoreType.DMA((2, 4))],
+        compiler_params=pltpu.CompilerParams(vmem_limit_bytes=CUT_GRANT * MIB),
+        cost_estimate=pl.CostEstimate(flops=0, bytes_accessed=4 * mine.size, transcendentals=0),
         name="cut",
-    )(at, decoders)
+    )(at, mine, theirs)
 
 
 def partial_kernel(backs, at_ref, *refs):
@@ -202,9 +206,7 @@
     other_mine = lax.ppermute(keep, ("dp", "feat"), across(0))
     other_theirs = lax.ppermute(send, ("dp", "feat"), across(1))
     own_theirs = lax.ppermute(send, "feat", PARTNER)
-    mine_w = cut(at, dec_weight)
-    theirs_w = cut(at, w_theirs)
-    weights = (mine_w, theirs_w)
+    weights = cut(at, dec_weight, w_theirs)
     chips = []
     for mine, theirs in ((keep, own_theirs), (other_mine, other_theirs)):
         both = jnp.stack([mine, theirs])

time: 116 us -> 124 us (1.069)
  waiting for transfers between devices: 45.2 us -> 48.5 us
  Pallas kernels: 19.7 us -> 22.7 us
  local copies, waits for them, and re-layouts: 4.46 us -> 6.57 us
    ppermute x2, waiting for transfers between devices: 16.3 us -> 19.6 us  [per_device(): up = lax.ppermute(both, 'layer', ring(1))]
    pallas_call x2 -> x1, Pallas kernels: 5.38 us -> 8.4 us  [cut(): pl.pallas_call(cut_kernel, out_shape=[jax.ShapeDtypeStruct(mine.shape[1:]...]
    squeeze x2, local copies, waits for them, and re-layouts: 0.04 us -> 1.45 us  [per_device(): far_down = lax.ppermute(down[1], 'layer', ring(-1))]
  transfers between devices with their start and end apart: 19 -> 19, of which waited for: 9 -> 9; matrix products, arithmetic and copies ran while one was open for 5% -> 7% of each run, Pallas kernels for 15% -> 16%
where the time goes in v7:
time: 124 us
  waiting for transfers between devices  48.5 us (39%)
  starting transfers between devices  41.8 us (34%)
  Pallas kernels  22.7 us (18%)
  local copies, waits for them, and re-layouts  6.57 us (5%)
  matrix products  3.05 us (2%)
    ppermute x2, waiting for transfers between devices, per_device(): up = lax.ppermute(both, 'layer', ring(1))  19.6 us
    all_to_all x1, starting transfers between devices, per_device(): lax.all_to_all(chips[0], 'feat', 0, 0, tiled=True, axis_index_groups=ZC_G...  16.7 us
    pallas_call x7, Pallas kernels, call(): pl.pallas_call(kernel, out_shape=out_shape, in_specs=[IN_SMEM] + [IN_VMEM...  14.3 us
    all_to_all x1, waiting for transfers between devices, per_device(): lax.all_to_all(chips[0], 'feat', 0, 0, tiled=True, axis_index_groups=ZC_G...  9.23 us
    ppermute x1, waiting for transfers between devices, per_device(): other_theirs = lax.ppermute(send, ('dp', 'feat'), across(1))  8.89 us
    pallas_call x1, Pallas kernels, cut(): pl.pallas_call(cut_kernel, out_shape=[jax.ShapeDtypeStruct(mine.shape[1:]...  8.4 us
    ppermute x6, starting transfers between devices, per_device(): came.append(lax.ppermute(piece, 'feat', x_pairs(by + 1)))  7.89 us
    ppermute x6, waiting for transfers between devices, per_device(): came.append(lax.ppermute(piece, 'feat', x_pairs(by + 1)))  6.25 us
  transfers between devices with their start and end apart: 19, of which 9 were waited for; matrix products, arithmetic and copies ran while one was open for 7% of the time, Pallas kernels for 16%

profile of v7, /device:TPU:1, one launch (start us, length us, event | category | flops | bytes accessed | tf_op | source)
XLA Modules:
  0.0 123.7 jit_solution(11711821095066030593)
XLA Ops:
  0.0 3.2 %collective-permute-start = (bf16[1,4,512,1152]{3,2,1,0:T(8,128)(2,1)}, bf16[1,4,512,1152]{3,2,1,0:T(8,128)(2,1)}, u32[]{:S(2)}, u32[]{:S(2)}) collective-permute-start(bf16[1,4,512,1152]{3,2,1,0:T(8,128)(2,1)} %mine_ref.1), channel_id=1, source_target_pairs={{0,1},{1,0},{2,3},{3,2},{4,5},{5,4},{6,7},{7,6},{8,9},{9,8},{10,11... | collective-permute-start | bytes 14155784 | tf_op jit(solution)/shard_map/ppermute | solution.py:199
  3.9 3.0 %fusion.18 = bf16[512,512]{1,0:T(8,128)(2,1)S(1)} fusion(bf16[1,2304,512]{2,1,0:T(8,128)(2,1)S(1)} %copy-done, bf16[1,512,2304]{2,1,0:T(8,128)(2,1)} %param.6, f32[512]{0:T(512)S(1)} %convert_bitcast_fusion, f32[512]{0:T(512)} %bitcast.54), kind=kOutput, calls=%fused_computation.6 | convolution fusion | flops 1209008128 | bytes 5246976 | tf_op jit(solution)/shard_map/dot_general | solution.py:201
  7.0 5.5 %collective-permute-start.9 = (bf16[256,512]{1,0:T(8,128)(2,1)S(1)}, bf16[256,512]{1,0:T(8,128)(2,1)S(1)}, u32[]{:S(2)}, u32[]{:S(2)}) collective-permute-start(bf16[256,512]{1,0:T(8,128)(2,1)S(1)} %bitcast.48), channel_id=1, source_target_pairs={{0,128},{1,129},{2,130},{3,131},{4,132},{5,133},{6,134},{7,135},{8... | collective-permute-start | bytes 786440 | tf_op jit(solution)/shard_map/ppermute | solution.py:206
  13.6 4.5 %collective-permute-done.9 = bf16[256,512]{1,0:T(8,128)(2,1)S(1)} collective-permute-done((bf16[256,512]{1,0:T(8,128)(2,1)S(1)}, bf16[256,512]{1,0:T(8,128)(2,1)S(1)}, u32[]{:S(2)}, u32[]{:S(2)}) %collective-permute-start.9) | collective-permute-done | bytes 262176 | tf_op jit(solution)/shard_map/ppermute | solution.py:206
  18.1 8.9 %collective-permute-done.10 = bf16[256,512]{1,0:T(8,128)(2,1)S(1)} collective-permute-done((bf16[256,512]{1,0:T(8,128)(2,1)S(1)}, bf16[256,512]{1,0:T(8,128)(2,1)S(1)}, u32[]{:S(2)}, u32[]{:S(2)}) %collective-permute-start.10) | collective-permute-done | bytes 262176 | tf_op jit(solution)/shard_map/ppermute | solution.py:207
  29.9 1.4 %collective-permute-start.3 = (bf16[2,256,512]{2,1,0:T(8,128)(2,1)S(1)}, bf16[2,256,512]{2,1,0:T(8,128)(2,1)S(1)}, u32[]{:S(2)}, u32[]{:S(2)}) collective-permute-start(bf16[2,256,512]{2,1,0:T(8,128)(2,1)S(1)} %pad_maximum_fusion.refs_2_), channel_id=1, source_target_pairs={{0,96},{32,0},{64,32},{96,64},{1,97},{33,1},{65,33},{97,65},{2,98}... | collective-permute-start | bytes 1572872 | tf_op jit(solution)/shard_map/ppermute | solution.py:214
  31.7 10.1 %collective-permute-done.11.refs_3_ = bf16[2,256,512]{2,1,0:T(8,128)(2,1)} collective-permute-done((bf16[2,256,512]{2,1,0:T(8,128)(2,1)S(1)}, bf16[2,256,512]{2,1,0:T(8,128)(2,1)}, u32[]{:S(2)}, u32[]{:S(2)}) %collective-permute-start.11) | collective-permute-done | bytes 524320 | tf_op jit(solution)/shard_map/ppermute | solution.py:213
  41.8 1.7 %slice_bitcast_fusion.1 = bf16[256,512]{1,0:T(8,128)(2,1)} fusion(bf16[2,256,512]{2,1,0:T(8,128)(2,1)} %collective-permute-done.11.refs_3_), kind=kLoop, calls=%fused_computation.10 | loop fusion | bytes 524288 | tf_op jit(solution)/shard_map/squeeze | solution.py:215
  43.5 9.6 %collective-permute-done.2.refs_3_ = bf16[2,256,512]{2,1,0:T(8,128)(2,1)} collective-permute-done((bf16[2,256,512]{2,1,0:T(8,128)(2,1)S(1)}, bf16[2,256,512]{2,1,0:T(8,128)(2,1)}, u32[]{:S(2)}, u32[]{:S(2)}) %collective-permute-start.2) | collective-permute-done | bytes 524320 | tf_op jit(solution)/shard_map/ppermute | solution.py:213
  54.8 2.7 %collective-permute-start.5 = (bf16[256,512]{1,0:T(8,128)(2,1)}, bf16[256,512]{1,0:T(8,128)(2,1)S(1)}, u32[]{:S(2)}, u32[]{:S(2)}) collective-permute-start(bf16[256,512]{1,0:T(8,128)(2,1)} %slice_bitcast_fusion.2), channel_id=1, source_target_pairs={{0,96},{32,0},{64,32},{96,64},{1,97},{33,1},{65,33},{97,65},{2,98}... | collective-permute-start | bytes 786440 | tf_op jit(solution)/shard_map/ppermute | solution.py:216
  58.4 8.4 %cut.1 = (bf16[4,512,1152]{2,1,0:T(8,128)(2,1)S(1)}, bf16[4,512,1152]{2,1,0:T(8,128)(2,1)}) custom-call(s32[4]{0:T(128)S(1)} %pad_add_fusion.at_ref, bf16[1,4,512,1152]{3,2,1,0:T(8,128)(2,1)} %mine_ref.1, bf16[1,4,512,1152]{3,2,1,0:T(8,128)(2,1)} %collective-permute-done.theirs_ref), custom_call_target="tpu_custom_call" | custom-call | bytes 9437184 | tf_op jit(solution)/shard_map/cut/pallas_call | solution.py:97
  66.8 2.3 %copy-done.1 = bf16[4,512,1152]{2,1,0:T(8,128)(2,1)S(1)} copy-done((bf16[4,512,1152]{2,1,0:T(8,128)(2,1)S(1)}, bf16[4,512,1152]{2,1,0:T(8,128)(2,1)}, u32[]{:S(2)}) %copy-start.1) | copy-done | bytes 4718616
  69.1 3.7 %shard_map.64.refs_2_ = f32[256,1152]{1,0:T(8,128)S(1)} custom-call(s32[4]{0:T(128)S(1)} %pad_add_fusion.at_ref, bf16[4,512,1152]{2,1,0:T(8,128)(2,1)S(1)} %get-tuple-element.15.refs_0_, bf16[4,512,1152]{2,1,0:T(8,128)(2,1)S(1)} %copy-done.1, bf16[2,256,512]{2,1,0:T(8,128)(2,1)S(1)} %pad_maximum_fusion.refs_2_, ...), custom_call_target="tpu_custom_call" | custom-call | flops 1811939328 | bytes 11010064 | tf_op jit(solution)/shard_map/pallas_call | solution.py:45
  72.8 1.8 %shard_map.65 = (f32[4,72,256]{2,1,0:T(8,128)S(1)}, bf16[4,72,256]{2,1,0:T(8,128)(2,1)S(1)}, bf16[4,72,256]{2,1,0:T(8,128)(2,1)S(1)}, bf16[4,72,256]{2,1,0:T(8,128)(2,1)S(1)}) custom-call(s32[4]{0:T(128)S(1)} %pad_add_fusion.at_ref, bf16[4,512,1152]{2,1,0:T(8,128)(2,1)S(1)} %get-tuple-element.15.refs_0_, bf16[4,512,1152]{2,1,0:T(8,128)(2,1)S(1)} %copy-done.1, ...), custom_call_target="tpu_custom_call" | custom-call | flops 603979776 | bytes 11141136 | tf_op jit(solution)/shard_map/pallas_call | solution.py:45
  75.9 3.7 %shard_map.67.refs_2_ = f32[256,1152]{1,0:T(8,128)S(1)} custom-call(s32[4]{0:T(128)S(1)} %pad_add_fusion.at_ref, bf16[4,512,1152]{2,1,0:T(8,128)(2,1)S(1)} %get-tuple-element.15.refs_0_, bf16[4,512,1152]{2,1,0:T(8,128)(2,1)S(1)} %copy-done.1, bf16[2,256,512]{2,1,0:T(8,128)(2,1)S(1)} %pad_maximum_fusion.1.refs_2_, ...), custom_call_target="tpu_custom_call" | custom-call | flops 1811939328 | bytes 11010064 | tf_op jit(solution)/shard_map/pallas_call | solution.py:45
  79.6 1.8 %shard_map.68 = (f32[4,72,256]{2,1,0:T(8,128)S(1)}, bf16[4,72,256]{2,1,0:T(8,128)(2,1)S(1)}, bf16[4,72,256]{2,1,0:T(8,128)(2,1)S(1)}, bf16[4,72,256]{2,1,0:T(8,128)(2,1)S(1)}) custom-call(s32[4]{0:T(128)S(1)} %pad_add_fusion.at_ref, bf16[4,512,1152]{2,1,0:T(8,128)(2,1)S(1)} %get-tuple-element.15.refs_0_, bf16[4,512,1152]{2,1,0:T(8,128)(2,1)S(1)} %copy-done.1, ...), custom_call_target="tpu_custom_call" | custom-call | flops 603979776 | bytes 11141136 | tf_op jit(solution)/shard_map/pallas_call | solution.py:45
  82.7 1.4 %collective-permute-start.7 = (bf16[4,72,256]{2,1,0:T(8,128)(2,1)S(1)}, bf16[4,72,256]{2,1,0:T(8,128)(2,1)S(1)}, u32[]{:S(2)}, u32[]{:S(2)}) collective-permute-start(bf16[4,72,256]{2,1,0:T(8,128)(2,1)S(1)} %get-tuple-element.19), channel_id=1, source_target_pairs={{0,4},{1,5},{2,6},{3,7},{4,0},{5,1},{6,2},{7,3},{8,12},{9,13},{10,... | collective-permute-start | bytes 442376 | tf_op jit(solution)/shard_map/ppermute | solution.py:222
  84.1 1.9 %collective-permute-start.8 = (bf16[4,72,256]{2,1,0:T(8,128)(2,1)S(1)}, bf16[4,72,256]{2,1,0:T(8,128)(2,1)S(1)}, u32[]{:S(2)}, u32[]{:S(2)}) collective-permute-start(bf16[4,72,256]{2,1,0:T(8,128)(2,1)S(1)} %get-tuple-element.20), channel_id=1, source_target_pairs={{0,6},{1,7},{2,0},{3,1},{4,2},{5,3},{6,4},{7,5},{8,14},{9,15},{10,... | collective-permute-start | bytes 442376 | tf_op jit(solution)/shard_map/ppermute | solution.py:222
  86.5 1.5 %collective-permute-start.17 = (bf16[4,72,256]{2,1,0:T(8,128)(2,1)S(1)}, bf16[4,72,256]{2,1,0:T(8,128)(2,1)S(1)}, u32[]{:S(2)}, u32[]{:S(2)}) collective-permute-start(bf16[4,72,256]{2,1,0:T(8,128)(2,1)S(1)} %get-tuple-element.24), channel_id=1, source_target_pairs={{0,6},{1,7},{2,0},{3,1},{4,2},{5,3},{6,4},{7,5},{8,14},{9,15},{10,... | collective-permute-start | bytes 442376 | tf_op jit(solution)/shard_map/ppermute | solution.py:222
  89.7 3.6 %collective-permute-done.16.refs_3_ = bf16[4,72,256]{2,1,0:T(8,128)(2,1)S(1)} collective-permute-done((bf16[4,72,256]{2,1,0:T(8,128)(2,1)S(1)}, bf16[4,72,256]{2,1,0:T(8,128)(2,1)S(1)}, u32[]{:S(2)}, u32[]{:S(2)}) %collective-permute-start.16) | collective-permute-done | bytes 147488 | tf_op jit(solution)/shard_map/ppermute | solution.py:222
  93.3 1.5 %collective-permute-done.17.refs_4_ = bf16[4,72,256]{2,1,0:T(8,128)(2,1)S(1)} collective-permute-done((bf16[4,72,256]{2,1,0:T(8,128)(2,1)S(1)}, bf16[4,72,256]{2,1,0:T(8,128)(2,1)S(1)}, u32[]{:S(2)}, u32[]{:S(2)}) %collective-permute-start.17) | collective-permute-done | bytes 147488 | tf_op jit(solution)/shard_map/ppermute | solution.py:222
  96.2 16.7 %all-to-all-start = ((bf16[8,72,256]{2,1,0:T(8,128)(2,1)}), bf16[8,72,256]{2,1,0:T(8,128)(2,1)S(1)}, u32[]{:S(2)}, u32[]{:S(2)}) async-start(bf16[8,72,256]{2,1,0:T(8,128)(2,1)} %shard_map.69), calls=%async_computation | async-start | bytes 589824 | tf_op jit(solution)/shard_map/all_to_all | solution.py:224
  113.0 9.2 %all-to-all-done.chips_ref = bf16[8,72,256]{2,1,0:T(8,128)(2,1)S(1)} async-done(((bf16[8,72,256]{2,1,0:T(8,128)(2,1)}), bf16[8,72,256]{2,1,0:T(8,128)(2,1)S(1)}, u32[]{:S(2)}, u32[]{:S(2)}) %all-to-all-start) | async-done | bytes 294944 | tf_op jit(solution)/shard_map/all_to_all | solution.py:224
  122.2 1.5 %shard_map.70 = bf16[36,1024]{1,0:T(8,128)(2,1)} custom-call(s32[4]{0:T(128)S(1)} %pad_add_fusion.at_ref, bf16[8,72,256]{2,1,0:T(8,128)(2,1)S(1)} %all-to-all-done.chips_ref, f32[36,1]{1,0:T(8,128)S(1)} %copy.7.bias_ref), custom_call_target="tpu_custom_call" | custom-call | bytes 295072 | tf_op jit(solution)/shard_map/pallas_call | solution.py:45
  (39 shorter events, 14.1 us)
Async XLA Ops:
  0.0 3.9 %copy-start = (bf16[1,2304,512]{2,1,0:T(8,128)(2,1)S(1)}, bf16[1,2304,512]{2,1,0:T(8,128)(2,1)}, u32[]{:S(2)}) copy-start(bf16[1,2304,512]{2,1,0:T(8,128)(2,1)} %param.7) | copy-start | bytes 7077892
  0.0 58.4 %collective-permute-start = (bf16[1,4,512,1152]{3,2,1,0:T(8,128)(2,1)}, bf16[1,4,512,1152]{3,2,1,0:T(8,128)(2,1)}, u32[]{:S(2)}, u32[]{:S(2)}) collective-permute-start(bf16[1,4,512,1152]{3,2,1,0:T(8,128)(2,1)} %mine_ref.1), channel_id=1, source_target_pairs={{0,1},{1,0},{2,3},{3,2},{4,5},{5,4},{6,7},{7,6},{8,9},{9,8},{10,11... | collective-permute-start | bytes 14155784 | tf_op jit(solution)/shard_map/ppermute | solution.py:199
  7.0 11.1 %collective-permute-start.9 = (bf16[256,512]{1,0:T(8,128)(2,1)S(1)}, bf16[256,512]{1,0:T(8,128)(2,1)S(1)}, u32[]{:S(2)}, u32[]{:S(2)}) collective-permute-start(bf16[256,512]{1,0:T(8,128)(2,1)S(1)} %bitcast.48), channel_id=1, source_target_pairs={{0,128},{1,129},{2,130},{3,131},{4,132},{5,133},{6,134},{7,135},{8... | collective-permute-start | bytes 786440 | tf_op jit(solution)/shard_map/ppermute | solution.py:206
  12.6 14.4 %collective-permute-start.10 = (bf16[256,512]{1,0:T(8,128)(2,1)S(1)}, bf16[256,512]{1,0:T(8,128)(2,1)S(1)}, u32[]{:S(2)}, u32[]{:S(2)}) collective-permute-start(bf16[256,512]{1,0:T(8,128)(2,1)S(1)} %get-tuple-element.26), channel_id=1, source_target_pairs={{0,129},{1,128},{2,131},{3,130},{4,133},{5,132},{6,135},{7,134},{8... | collective-permute-start | bytes 786440 | tf_op jit(solution)/shard_map/ppermute | solution.py:207
  13.6 14.8 %collective-permute-start.1 = (bf16[256,512]{1,0:T(8,128)(2,1)S(1)}, bf16[256,512]{1,0:T(8,128)(2,1)S(1)}, u32[]{:S(2)}, u32[]{:S(2)}) collective-permute-start(bf16[256,512]{1,0:T(8,128)(2,1)S(1)} %get-tuple-element.26), channel_id=1, source_target_pairs={{0,1},{1,0},{2,3},{3,2},{4,5},{5,4},{6,7},{7,6},{8,9},{9,8},{10,11... | collective-permute-start | bytes 786440 | tf_op jit(solution)/shard_map/ppermute | solution.py:208
  27.1 14.7 %collective-permute-start.11 = (bf16[2,256,512]{2,1,0:T(8,128)(2,1)S(1)}, bf16[2,256,512]{2,1,0:T(8,128)(2,1)}, u32[]{:S(2)}, u32[]{:S(2)}) collective-permute-start(bf16[2,256,512]{2,1,0:T(8,128)(2,1)S(1)} %pad_maximum_fusion.1.refs_2_), channel_id=1, source_target_pairs={{0,32},{32,64},{64,96},{96,0},{1,33},{33,65},{65,97},{97,1},{2,34}... | collective-permute-start | bytes 1572872 | tf_op jit(solution)/shard_map/ppermute | solution.py:213
  28.5 24.5 %collective-permute-start.2 = (bf16[2,256,512]{2,1,0:T(8,128)(2,1)S(1)}, bf16[2,256,512]{2,1,0:T(8,128)(2,1)}, u32[]{:S(2)}, u32[]{:S(2)}) collective-permute-start(bf16[2,256,512]{2,1,0:T(8,128)(2,1)S(1)} %pad_maximum_fusion.refs_2_), channel_id=1, source_target_pairs={{0,32},{32,64},{64,96},{96,0},{1,33},{33,65},{65,97},{97,1},{2,34}... | collective-permute-start | bytes 1572872 | tf_op jit(solution)/shard_map/ppermute | solution.py:213
  29.9 24.2 %collective-permute-start.3 = (bf16[2,256,512]{2,1,0:T(8,128)(2,1)S(1)}, bf16[2,256,512]{2,1,0:T(8,128)(2,1)S(1)}, u32[]{:S(2)}, u32[]{:S(2)}) collective-permute-start(bf16[2,256,512]{2,1,0:T(8,128)(2,1)S(1)} %pad_maximum_fusion.refs_2_), channel_id=1, source_target_pairs={{0,96},{32,0},{64,32},{96,64},{1,97},{33,1},{65,33},{97,65},{2,98}... | collective-permute-start | bytes 1572872 | tf_op jit(solution)/shard_map/ppermute | solution.py:214
  31.3 26.1 %collective-permute-start.12 = (bf16[2,256,512]{2,1,0:T(8,128)(2,1)S(1)}, bf16[2,256,512]{2,1,0:T(8,128)(2,1)S(1)}, u32[]{:S(2)}, u32[]{:S(2)}) collective-permute-start(bf16[2,256,512]{2,1,0:T(8,128)(2,1)S(1)} %pad_maximum_fusion.1.refs_2_), channel_id=1, source_target_pairs={{0,96},{32,0},{64,32},{96,64},{1,97},{33,1},{65,33},{97,65},{2,98}... | collective-permute-start | bytes 1572872 | tf_op jit(solution)/shard_map/ppermute | solution.py:214
  43.5 36.1 %collective-permute-start.13 = (bf16[256,512]{1,0:T(8,128)(2,1)}, bf16[256,512]{1,0:T(8,128)(2,1)S(1)}, u32[]{:S(2)}, u32[]{:S(2)}) collective-permute-start(bf16[256,512]{1,0:T(8,128)(2,1)} %slice_bitcast_fusion.1), channel_id=1, source_target_pairs={{0,32},{32,64},{64,96},{96,0},{1,33},{33,65},{65,97},{97,1},{2,34}... | collective-permute-start | bytes 786440 | tf_op jit(solution)/shard_map/ppermute | solution.py:215
  54.0 18.8 %collective-permute-start.4 = (bf16[256,512]{1,0:T(8,128)(2,1)S(1)}, bf16[256,512]{1,0:T(8,128)(2,1)S(1)}, u32[]{:S(2)}, u32[]{:S(2)}) collective-permute-start(bf16[256,512]{1,0:T(8,128)(2,1)S(1)} %slice_bitcast_fusion.3), channel_id=1, source_target_pairs={{0,32},{32,64},{64,96},{96,0},{1,33},{33,65},{65,97},{97,1},{2,34}... | collective-permute-start | bytes 786440 | tf_op jit(solution)/shard_map/ppermute | solution.py:215
  54.8 18.0 %collective-permute-start.5 = (bf16[256,512]{1,0:T(8,128)(2,1)}, bf16[256,512]{1,0:T(8,128)(2,1)S(1)}, u32[]{:S(2)}, u32[]{:S(2)}) collective-permute-start(bf16[256,512]{1,0:T(8,128)(2,1)} %slice_bitcast_fusion.2), channel_id=1, source_target_pairs={{0,96},{32,0},{64,32},{96,64},{1,97},{33,1},{65,33},{97,65},{2,98}... | collective-permute-start | bytes 786440 | tf_op jit(solution)/shard_map/ppermute | solution.py:216
  58.2 21.4 %collective-permute-start.14 = (bf16[256,512]{1,0:T(8,128)(2,1)}, bf16[256,512]{1,0:T(8,128)(2,1)S(1)}, u32[]{:S(2)}, u32[]{:S(2)}) collective-permute-start(bf16[256,512]{1,0:T(8,128)(2,1)} %slice_bitcast_fusion), channel_id=1, source_target_pairs={{0,96},{32,0},{64,32},{96,64},{1,97},{33,1},{65,33},{97,65},{2,98}... | collective-permute-start | bytes 786440 | tf_op jit(solution)/shard_map/ppermute | solution.py:216
  66.8 2.3 %copy-start.1 = (bf16[4,512,1152]{2,1,0:T(8,128)(2,1)S(1)}, bf16[4,512,1152]{2,1,0:T(8,128)(2,1)}, u32[]{:S(2)}) copy-start(bf16[4,512,1152]{2,1,0:T(8,128)(2,1)} %get-tuple-element.16.refs_1_) | copy-start | bytes 14155780
  74.6 11.9 %collective-permute-start.6 = (bf16[4,72,256]{2,1,0:T(8,128)(2,1)S(1)}, bf16[4,72,256]{2,1,0:T(8,128)(2,1)S(1)}, u32[]{:S(2)}, u32[]{:S(2)}) collective-permute-start(bf16[4,72,256]{2,1,0:T(8,128)(2,1)S(1)} %get-tuple-element.18), channel_id=1, source_target_pairs={{0,2},{1,3},{2,4},{3,5},{4,6},{5,7},{6,0},{7,1},{8,10},{9,11},{10,... | collective-permute-start | bytes 442376 | tf_op jit(solution)/shard_map/ppermute | solution.py:222
  81.4 31.5 %copy-start.2 = (f32[1,36]{1,0:T(1,128)S(1)}, f32[1,36]{1,0:T(1,128)}, u32[]{:S(2)}) copy-start(f32[1,36]{1,0:T(1,128)} %param.10) | copy-start | bytes 436
  81.4 8.4 %collective-permute-start.15 = (bf16[4,72,256]{2,1,0:T(8,128)(2,1)S(1)}, bf16[4,72,256]{2,1,0:T(8,128)(2,1)S(1)}, u32[]{:S(2)}, u32[]{:S(2)}) collective-permute-start(bf16[4,72,256]{2,1,0:T(8,128)(2,1)S(1)} %get-tuple-element.22), channel_id=1, source_target_pairs={{0,2},{1,3},{2,4},{3,5},{4,6},{5,7},{6,0},{7,1},{8,10},{9,11},{10,... | collective-permute-start | bytes 442376 | tf_op jit(solution)/shard_map/ppermute | solution.py:222
  82.7 5.5 %collective-permute-start.7 = (bf16[4,72,256]{2,1,0:T(8,128)(2,1)S(1)}, bf16[4,72,256]{2,1,0:T(8,128)(2,1)S(1)}, u32[]{:S(2)}, u32[]{:S(2)}) collective-permute-start(bf16[4,72,256]{2,1,0:T(8,128)(2,1)S(1)} %get-tuple-element.19), channel_id=1, source_target_pairs={{0,4},{1,5},{2,6},{3,7},{4,0},{5,1},{6,2},{7,3},{8,12},{9,13},{10,... | collective-permute-start | bytes 442376 | tf_op jit(solution)/shard_map/ppermute | solution.py:222
  84.1 5.0 %collective-permute-start.8 = (bf16[4,72,256]{2,1,0:T(8,128)(2,1)S(1)}, bf16[4,72,256]{2,1,0:T(8,128)(2,1)S(1)}, u32[]{:S(2)}, u32[]{:S(2)}) collective-permute-start(bf16[4,72,256]{2,1,0:T(8,128)(2,1)S(1)} %get-tuple-element.20), channel_id=1, source_target_pairs={{0,6},{1,7},{2,0},{3,1},{4,2},{5,3},{6,4},{7,5},{8,14},{9,15},{10,... | collective-permute-start | bytes 442376 | tf_op jit(solution)/shard_map/ppermute | solution.py:222
  86.0 7.4 %collective-permute-start.16 = (bf16[4,72,256]{2,1,0:T(8,128)(2,1)S(1)}, bf16[4,72,256]{2,1,0:T(8,128)(2,1)S(1)}, u32[]{:S(2)}, u32[]{:S(2)}) collective-permute-start(bf16[4,72,256]{2,1,0:T(8,128)(2,1)S(1)} %get-tuple-element.23), channel_id=1, source_target_pairs={{0,4},{1,5},{2,6},{3,7},{4,0},{5,1},{6,2},{7,3},{8,12},{9,13},{10,... | collective-permute-start | bytes 442376 | tf_op jit(solution)/shard_map/ppermute | solution.py:222
  86.5 8.3 %collective-permute-start.17 = (bf16[4,72,256]{2,1,0:T(8,128)(2,1)S(1)}, bf16[4,72,256]{2,1,0:T(8,128)(2,1)S(1)}, u32[]{:S(2)}, u32[]{:S(2)}) collective-permute-start(bf16[4,72,256]{2,1,0:T(8,128)(2,1)S(1)} %get-tuple-element.24), channel_id=1, source_target_pairs={{0,6},{1,7},{2,0},{3,1},{4,2},{5,3},{6,4},{7,5},{8,14},{9,15},{10,... | collective-permute-start | bytes 442376 | tf_op jit(solution)/shard_map/ppermute | solution.py:222
  96.2 26.1 %all-to-all-start = ((bf16[8,72,256]{2,1,0:T(8,128)(2,1)}), bf16[8,72,256]{2,1,0:T(8,128)(2,1)S(1)}, u32[]{:S(2)}, u32[]{:S(2)}) async-start(bf16[8,72,256]{2,1,0:T(8,128)(2,1)} %shard_map.69), calls=%async_computation | async-start | bytes 589824 | tf_op jit(solution)/shard_map/all_to_all | solution.py:224

commit v8 on v6

--- a/solution.py
+++ b/solution.py
@@ -55,6 +55,7 @@
 
 TILE = 384
 GRANT = 12
+CUT_GRANT = 6
 
 
 def terms_of(backs, weights, blocks, cols):
@@ -96,7 +97,7 @@
         in_specs=[IN_SMEM, pl.BlockSpec(memory_space=pltpu.HBM)],
         out_specs=IN_VMEM,
         scratch_shapes=[pltpu.SemaphoreType.DMA((4,))],
-        compiler_params=pltpu.CompilerParams(vmem_limit_bytes=6 * MIB),
+        compiler_params=pltpu.CompilerParams(vmem_limit_bytes=CUT_GRANT * MIB),
         cost_estimate=pl.CostEstimate(flops=0, bytes_accessed=2 * decoders.size, transcendentals=0),
         name="cut",
     )(at, decoders)
@@ -192,7 +193,6 @@
     target, feat, dp = lax.axis_index("layer"), lax.axis_index("feat"), lax.axis_index("dp")
     core = feat % 2
     at = jnp.stack([core, target, feat // 2 % NX, dp]).astype(jnp.int32)
-    w_theirs = lax.ppermute(dec_weight, "feat", PARTNER)
     valid = (jnp.arange(SEQ)[None, :] < lengths[:, None]).reshape(-1).astype(F32)
     pre = jnp.dot(resid[0], enc_weight[0], preferred_element_type=F32) + enc_bias
     acts = (jax.nn.relu(pre) * valid[:, None]).astype(BF).reshape(2, 256, 512)
@@ -202,9 +202,9 @@
     other_mine = lax.ppermute(keep, ("dp", "feat"), across(0))
     other_theirs = lax.ppermute(send, ("dp", "feat"), across(1))
     own_theirs = lax.ppermute(send, "feat", PARTNER)
-    mine_w = cut(at, dec_weight)
-    theirs_w = cut(at, w_theirs)
-    weights = (mine_w, theirs_w)
+    w_mine = cut(at, dec_weight)
+    w_theirs = lax.ppermute(w_mine, "feat", PARTNER)
+    weights = (w_mine, w_theirs)
     chips = []
     for mine, theirs in ((keep, own_theirs), (other_mine, other_theirs)):
         both = jnp.stack([mine, theirs])

time: 116 us -> 122 us (1.052)
  Pallas kernels: 19.7 us -> 30.2 us
  starting transfers between devices: 41.9 us -> 37.7 us
  waiting for transfers between devices: 45.2 us -> 47.6 us
  local copies, waits for them, and re-layouts: 4.46 us -> 2.72 us
    pallas_call x7, Pallas kernels: 14.3 us -> 26.3 us  [call(): pl.pallas_call(kernel, out_shape=out_shape, in_specs=[IN_SMEM] + [IN_VMEM...]
    ppermute x1, waiting for transfers between devices: 4.52 us -> 14.8 us  [per_device(): other_mine = lax.ppermute(keep, ('dp', 'feat'), across(0))]
    ppermute x2, waiting for transfers between devices: 16.3 us -> 8.53 us  [per_device(): up = lax.ppermute(both, 'layer', ring(1))]
    all_to_all x1, starting transfers between devices: 16.7 us -> 9.32 us  [per_device(): lax.all_to_all(chips[0], 'feat', 0, 0, tiled=True, axis_index_groups=ZC_G...]
    ppermute x1, starting transfers between devices: 1.03 us -> 6.94 us  [per_device(): other_theirs = lax.ppermute(send, ('dp', 'feat'), across(1))]
    ppermute x1, starting transfers between devices: 5.55 us -> 0.01 us  [per_device(): other_mine = lax.ppermute(keep, ('dp', 'feat'), across(0))]
    ppermute x1, waiting for transfers between devices: 0.01 us -> 4.81 us  [per_device(): own_theirs = lax.ppermute(send, 'feat', PARTNER)]
    ppermute x1, waiting for transfers between devices: 8.89 us -> 6.23 us  [per_device(): other_theirs = lax.ppermute(send, ('dp', 'feat'), across(1))]
  transfers between devices with their start and end apart: 19 -> 19, of which waited for: 9 -> 7; matrix products, arithmetic and copies ran while one was open for 5% -> 3% of each run, Pallas kernels for 15% -> 19%
where the time goes in v8:
time: 122 us
  waiting for transfers between devices  47.6 us (39%)
  starting transfers between devices  37.7 us (31%)
  Pallas kernels  30.2 us (25%)
  matrix products  3.05 us (2%)
  local copies, waits for them, and re-layouts  2.72 us (2%)
    pallas_call x7, Pallas kernels, call(): pl.pallas_call(kernel, out_shape=out_shape, in_specs=[IN_SMEM] + [IN_VMEM...  26.3 us
    ppermute x1, waiting for transfers between devices, per_device(): other_mine = lax.ppermute(keep, ('dp', 'feat'), across(0))  14.8 us
    all_to_all x1, starting transfers between devices, per_device(): lax.all_to_all(chips[0], 'feat', 0, 0, tiled=True, axis_index_groups=ZC_G...  9.32 us
    all_to_all x1, waiting for transfers between devices, per_device(): lax.all_to_all(chips[0], 'feat', 0, 0, tiled=True, axis_index_groups=ZC_G...  9.23 us
    ppermute x2, waiting for transfers between devices, per_device(): up = lax.ppermute(both, 'layer', ring(1))  8.53 us
    ppermute x6, starting transfers between devices, per_device(): came.append(lax.ppermute(piece, 'feat', x_pairs(by + 1)))  7.79 us
    ppermute x1, starting transfers between devices, per_device(): other_theirs = lax.ppermute(send, ('dp', 'feat'), across(1))  6.94 us
    ppermute x1, waiting for transfers between devices, per_device(): other_theirs = lax.ppermute(send, ('dp', 'feat'), across(1))  6.23 us
  transfers between devices with their start and end apart: 19, of which 7 were waited for; matrix products, arithmetic and copies ran while one was open for 3% of the time, Pallas kernels for 19%

profile of v8, /device:TPU:1, one launch (start us, length us, event | category | flops | bytes accessed | tf_op | source)
XLA Modules:
  0.0 121.8 jit_solution(6816508023921994502)
XLA Ops:
  0.1 2.5 %copy-done.1 = bf16[1,4,512,1152]{3,2,1,0:T(8,128)(2,1)S(1)} copy-done((bf16[1,4,512,1152]{3,2,1,0:T(8,128)(2,1)S(1)}, bf16[1,4,512,1152]{3,2,1,0:T(8,128)(2,1)}, u32[]{:S(2)}) %copy-start.1) | copy-done | bytes 4718616
  2.6 3.9 %cut.1.refs_0_ = bf16[4,512,1152]{2,1,0:T(8,128)(2,1)} custom-call(s32[4]{0:T(128)S(1)} %pad_add_fusion.at_ref, bf16[1,4,512,1152]{3,2,1,0:T(8,128)(2,1)S(1)} %copy-done.1), custom_call_target="tpu_custom_call" | custom-call | bytes 4718592 | tf_op jit(solution)/shard_map/cut/pallas_call | solution.py:94
  6.5 3.3 %collective-permute-start = (bf16[4,512,1152]{2,1,0:T(8,128)(2,1)}, bf16[4,512,1152]{2,1,0:T(8,128)(2,1)}, u32[]{:S(2)}, u32[]{:S(2)}) collective-permute-start(bf16[4,512,1152]{2,1,0:T(8,128)(2,1)} %cut.1.refs_0_), channel_id=1, source_target_pairs={{0,1},{1,0},{2,3},{3,2},{4,5},{5,4},{6,7},{7,6},{8,9},{9,8},{10,11... | collective-permute-start | bytes 14155784 | tf_op jit(solution)/shard_map/ppermute | solution.py:206
  9.9 3.0 %fusion.18 = bf16[512,512]{1,0:T(8,128)(2,1)S(1)} fusion(bf16[1,2304,512]{2,1,0:T(8,128)(2,1)S(1)} %copy-done, bf16[1,512,2304]{2,1,0:T(8,128)(2,1)} %param.6, f32[512]{0:T(512)S(1)} %convert_bitcast_fusion, f32[512]{0:T(512)S(1)} %bitcast.54), kind=kOutput, calls=%fused_computation.6 | convolution fusion | flops 1209008128 | bytes 5246976 | tf_op jit(solution)/shard_map/dot_general | solution.py:197
  13.1 4.8 %collective-permute-done.1 = bf16[256,512]{1,0:T(8,128)(2,1)S(1)} collective-permute-done((bf16[256,512]{1,0:T(8,128)(2,1)S(1)}, bf16[256,512]{1,0:T(8,128)(2,1)S(1)}, u32[]{:S(2)}, u32[]{:S(2)}) %collective-permute-start.1) | collective-permute-done | bytes 262176 | tf_op jit(solution)/shard_map/ppermute | solution.py:204
  18.1 6.9 %collective-permute-start.10 = (bf16[256,512]{1,0:T(8,128)(2,1)S(1)}, bf16[256,512]{1,0:T(8,128)(2,1)S(1)}, u32[]{:S(2)}, u32[]{:S(2)}) collective-permute-start(bf16[256,512]{1,0:T(8,128)(2,1)S(1)} %get-tuple-element.22), channel_id=1, source_target_pairs={{0,129},{1,128},{2,131},{3,130},{4,133},{5,132},{6,135},{7,134},{8... | collective-permute-start | bytes 786440 | tf_op jit(solution)/shard_map/ppermute | solution.py:203
  25.0 1.6 %collective-permute-start.3 = (bf16[2,256,512]{2,1,0:T(8,128)(2,1)S(1)}, bf16[2,256,512]{2,1,0:T(8,128)(2,1)S(1)}, u32[]{:S(2)}, u32[]{:S(2)}) collective-permute-start(bf16[2,256,512]{2,1,0:T(8,128)(2,1)S(1)} %pad_maximum_fusion.refs_2_), channel_id=1, source_target_pairs={{0,96},{32,0},{64,32},{96,64},{1,97},{33,1},{65,33},{97,65},{2,98}... | collective-permute-start | bytes 1572872 | tf_op jit(solution)/shard_map/ppermute | solution.py:212
  26.7 6.2 %collective-permute-done.10 = bf16[256,512]{1,0:T(8,128)(2,1)S(1)} collective-permute-done((bf16[256,512]{1,0:T(8,128)(2,1)S(1)}, bf16[256,512]{1,0:T(8,128)(2,1)S(1)}, u32[]{:S(2)}, u32[]{:S(2)}) %collective-permute-start.10) | collective-permute-done | bytes 262176 | tf_op jit(solution)/shard_map/ppermute | solution.py:203
  32.9 14.8 %collective-permute-done.9 = bf16[256,512]{1,0:T(8,128)(2,1)S(1)} collective-permute-done((bf16[256,512]{1,0:T(8,128)(2,1)S(1)}, bf16[256,512]{1,0:T(8,128)(2,1)S(1)}, u32[]{:S(2)}, u32[]{:S(2)}) %collective-permute-start.9) | collective-permute-done | bytes 262176 | tf_op jit(solution)/shard_map/ppermute | solution.py:202
  49.1 1.5 %collective-permute-start.12 = (bf16[2,256,512]{2,1,0:T(8,128)(2,1)S(1)}, bf16[2,256,512]{2,1,0:T(8,128)(2,1)S(1)}, u32[]{:S(2)}, u32[]{:S(2)}) collective-permute-start(bf16[2,256,512]{2,1,0:T(8,128)(2,1)S(1)} %pad_maximum_fusion.1.refs_2_), channel_id=1, source_target_pairs={{0,96},{32,0},{64,32},{96,64},{1,97},{33,1},{65,33},{97,65},{2,98}... | collective-permute-start | bytes 1572872 | tf_op jit(solution)/shard_map/ppermute | solution.py:212
  50.7 2.7 %collective-permute-start.5 = (bf16[256,512]{1,0:T(8,128)(2,1)S(1)}, bf16[256,512]{1,0:T(8,128)(2,1)S(1)}, u32[]{:S(2)}, u32[]{:S(2)}) collective-permute-start(bf16[256,512]{1,0:T(8,128)(2,1)S(1)} %slice_bitcast_fusion.2), channel_id=1, source_target_pairs={{0,96},{32,0},{64,32},{96,64},{1,97},{33,1},{65,33},{97,65},{2,98}... | collective-permute-start | bytes 786440 | tf_op jit(solution)/shard_map/ppermute | solution.py:214
  53.4 8.5 %collective-permute-done.11.refs_3_ = bf16[2,256,512]{2,1,0:T(8,128)(2,1)S(1)} collective-permute-done((bf16[2,256,512]{2,1,0:T(8,128)(2,1)S(1)}, bf16[2,256,512]{2,1,0:T(8,128)(2,1)S(1)}, u32[]{:S(2)}, u32[]{:S(2)}) %collective-permute-start.11) | collective-permute-done | bytes 524320 | tf_op jit(solution)/shard_map/ppermute | solution.py:211
  62.1 2.9 %collective-permute-start.14 = (bf16[256,512]{1,0:T(8,128)(2,1)S(1)}, bf16[256,512]{1,0:T(8,128)(2,1)S(1)}, u32[]{:S(2)}, u32[]{:S(2)}) collective-permute-start(bf16[256,512]{1,0:T(8,128)(2,1)S(1)} %slice_bitcast_fusion), channel_id=1, source_target_pairs={{0,96},{32,0},{64,32},{96,64},{1,97},{33,1},{65,33},{97,65},{2,98}... | collective-permute-start | bytes 786440 | tf_op jit(solution)/shard_map/ppermute | solution.py:214
  65.0 6.4 %shard_map.64.refs_2_ = f32[256,1152]{1,0:T(8,128)S(1)} custom-call(s32[4]{0:T(128)S(1)} %pad_add_fusion.at_ref, bf16[4,512,1152]{2,1,0:T(8,128)(2,1)} %cut.1.refs_0_, bf16[4,512,1152]{2,1,0:T(8,128)(2,1)} %collective-permute-done.refs_1_, bf16[2,256,512]{2,1,0:T(8,128)(2,1)S(1)} %pad_maximum_fusion.refs_2_, ...), custom_call_target="tpu_custom_call" | custom-call | flops 1811939328 | bytes 11010064 | tf_op jit(solution)/shard_map/pallas_call | solution.py:45
  71.4 5.0 %shard_map.65 = (f32[4,72,256]{2,1,0:T(8,128)S(1)}, bf16[4,72,256]{2,1,0:T(8,128)(2,1)S(1)}, bf16[4,72,256]{2,1,0:T(8,128)(2,1)S(1)}, bf16[4,72,256]{2,1,0:T(8,128)(2,1)S(1)}) custom-call(s32[4]{0:T(128)S(1)} %pad_add_fusion.at_ref, bf16[4,512,1152]{2,1,0:T(8,128)(2,1)} %cut.1.refs_0_, bf16[4,512,1152]{2,1,0:T(8,128)(2,1)} %collective-permute-done.refs_1_, ...), custom_call_target="tpu_custom_call" | custom-call | flops 603979776 | bytes 11141136 | tf_op jit(solution)/shard_map/pallas_call | solution.py:45
  77.7 2.5 %collective-permute-start.7 = (bf16[4,72,256]{2,1,0:T(8,128)(2,1)S(1)}, bf16[4,72,256]{2,1,0:T(8,128)(2,1)S(1)}, u32[]{:S(2)}, u32[]{:S(2)}) collective-permute-start(bf16[4,72,256]{2,1,0:T(8,128)(2,1)S(1)} %get-tuple-element.15), channel_id=1, source_target_pairs={{0,4},{1,5},{2,6},{3,7},{4,0},{5,1},{6,2},{7,3},{8,12},{9,13},{10,... | collective-permute-start | bytes 442376 | tf_op jit(solution)/shard_map/ppermute | solution.py:220
  81.3 6.4 %shard_map.67.refs_2_ = f32[256,1152]{1,0:T(8,128)S(1)} custom-call(s32[4]{0:T(128)S(1)} %pad_add_fusion.at_ref, bf16[4,512,1152]{2,1,0:T(8,128)(2,1)} %cut.1.refs_0_, bf16[4,512,1152]{2,1,0:T(8,128)(2,1)} %collective-permute-done.refs_1_, bf16[2,256,512]{2,1,0:T(8,128)(2,1)S(1)} %pad_maximum_fusion.1.refs_2_, ...), custom_call_target="tpu_custom_call" | custom-call | flops 1811939328 | bytes 11010064 | tf_op jit(solution)/shard_map/pallas_call | solution.py:45
  87.8 5.0 %shard_map.68 = (f32[4,72,256]{2,1,0:T(8,128)S(1)}, bf16[4,72,256]{2,1,0:T(8,128)(2,1)S(1)}, bf16[4,72,256]{2,1,0:T(8,128)(2,1)S(1)}, bf16[4,72,256]{2,1,0:T(8,128)(2,1)S(1)}) custom-call(s32[4]{0:T(128)S(1)} %pad_add_fusion.at_ref, bf16[4,512,1152]{2,1,0:T(8,128)(2,1)} %cut.1.refs_0_, bf16[4,512,1152]{2,1,0:T(8,128)(2,1)} %collective-permute-done.refs_1_, ...), custom_call_target="tpu_custom_call" | custom-call | flops 603979776 | bytes 11141136 | tf_op jit(solution)/shard_map/pallas_call | solution.py:45
  94.1 1.6 %collective-permute-start.17 = (bf16[4,72,256]{2,1,0:T(8,128)(2,1)S(1)}, bf16[4,72,256]{2,1,0:T(8,128)(2,1)S(1)}, u32[]{:S(2)}, u32[]{:S(2)}) collective-permute-start(bf16[4,72,256]{2,1,0:T(8,128)(2,1)S(1)} %get-tuple-element.20), channel_id=1, source_target_pairs={{0,6},{1,7},{2,0},{3,1},{4,2},{5,3},{6,4},{7,5},{8,14},{9,15},{10,... | collective-permute-start | bytes 442376 | tf_op jit(solution)/shard_map/ppermute | solution.py:220
  96.3 3.3 %collective-permute-done.15.refs_2_ = bf16[4,72,256]{2,1,0:T(8,128)(2,1)S(1)} collective-permute-done((bf16[4,72,256]{2,1,0:T(8,128)(2,1)S(1)}, bf16[4,72,256]{2,1,0:T(8,128)(2,1)S(1)}, u32[]{:S(2)}, u32[]{:S(2)}) %collective-permute-start.15) | collective-permute-done | bytes 147488 | tf_op jit(solution)/shard_map/ppermute | solution.py:220
  100.3 1.3 %shard_map.69 = bf16[8,72,256]{2,1,0:T(8,128)(2,1)} custom-call(s32[4]{0:T(128)S(1)} %pad_add_fusion.at_ref, bf16[8,36,256]{2,1,0:T(8,128)(2,1)S(1)} %shard_map.66.refs_0_, f32[4,72,256]{2,1,0:T(8,128)S(1)} %get-tuple-element.17.refs_1_, bf16[4,72,256]{2,1,0:T(8,128)(2,1)S(1)} %collective-permute-done.15.refs_2_, ...), custom_call_target="tpu_custom_call" | custom-call | bytes 884752 | tf_op jit(solution)/shard_map/pallas_call | solution.py:45
  101.6 9.3 %all-to-all-start = ((bf16[8,72,256]{2,1,0:T(8,128)(2,1)}), bf16[8,72,256]{2,1,0:T(8,128)(2,1)S(1)}, u32[]{:S(2)}, u32[]{:S(2)}) async-start(bf16[8,72,256]{2,1,0:T(8,128)(2,1)} %shard_map.69), calls=%async_computation | async-start | bytes 589824 | tf_op jit(solution)/shard_map/all_to_all | solution.py:222
  111.1 9.2 %all-to-all-done.chips_ref = bf16[8,72,256]{2,1,0:T(8,128)(2,1)S(1)} async-done(((bf16[8,72,256]{2,1,0:T(8,128)(2,1)}), bf16[8,72,256]{2,1,0:T(8,128)(2,1)S(1)}, u32[]{:S(2)}, u32[]{:S(2)}) %all-to-all-start) | async-done | bytes 294944 | tf_op jit(solution)/shard_map/all_to_all | solution.py:222
  120.3 1.5 %shard_map.70 = bf16[36,1024]{1,0:T(8,128)(2,1)} custom-call(s32[4]{0:T(128)S(1)} %pad_add_fusion.at_ref, bf16[8,72,256]{2,1,0:T(8,128)(2,1)S(1)} %all-to-all-done.chips_ref, f32[36,1]{1,0:T(8,128)S(1)} %copy.7.bias_ref), custom_call_target="tpu_custom_call" | custom-call | bytes 295072 | tf_op jit(solution)/shard_map/pallas_call | solution.py:45
  (43 shorter events, 7.1 us)
Async XLA Ops:
  0.0 9.9 %copy-start = (bf16[1,2304,512]{2,1,0:T(8,128)(2,1)S(1)}, bf16[1,2304,512]{2,1,0:T(8,128)(2,1)}, u32[]{:S(2)}) copy-start(bf16[1,2304,512]{2,1,0:T(8,128)(2,1)} %param.7) | copy-start | bytes 7077892
  0.1 2.5 %copy-start.1 = (bf16[1,4,512,1152]{3,2,1,0:T(8,128)(2,1)S(1)}, bf16[1,4,512,1152]{3,2,1,0:T(8,128)(2,1)}, u32[]{:S(2)}) copy-start(bf16[1,4,512,1152]{3,2,1,0:T(8,128)(2,1)} %decoders_ref.1) | copy-start | bytes 14155780
  2.6 7.2 %copy-start.2 = (s32[4]{0:T(128)S(1)}, s32[4]{0:T(128)}, u32[]{:S(2)}) copy-start(s32[4]{0:T(128)} %param.11) | copy-start | bytes 52
  2.6 7.3 %copy-start.4 = (f32[1,512]{1,0:T(1,128)S(1)}, f32[1,512]{1,0:T(1,128)}, u32[]{:S(2)}) copy-start(f32[1,512]{1,0:T(1,128)} %param.8) | copy-start | bytes 6148
  6.5 58.5 %collective-permute-start = (bf16[4,512,1152]{2,1,0:T(8,128)(2,1)}, bf16[4,512,1152]{2,1,0:T(8,128)(2,1)}, u32[]{:S(2)}, u32[]{:S(2)}) collective-permute-start(bf16[4,512,1152]{2,1,0:T(8,128)(2,1)} %cut.1.refs_0_), channel_id=1, source_target_pairs={{0,1},{1,0},{2,3},{3,2},{4,5},{5,4},{6,7},{7,6},{8,9},{9,8},{10,11... | collective-permute-start | bytes 14155784 | tf_op jit(solution)/shard_map/ppermute | solution.py:206
  13.0 4.9 %collective-permute-start.1 = (bf16[256,512]{1,0:T(8,128)(2,1)S(1)}, bf16[256,512]{1,0:T(8,128)(2,1)S(1)}, u32[]{:S(2)}, u32[]{:S(2)}) collective-permute-start(bf16[256,512]{1,0:T(8,128)(2,1)S(1)} %get-tuple-element.22), channel_id=1, source_target_pairs={{0,1},{1,0},{2,3},{3,2},{4,5},{5,4},{6,7},{7,6},{8,9},{9,8},{10,11... | collective-permute-start | bytes 786440 | tf_op jit(solution)/shard_map/ppermute | solution.py:204
  18.0 32.5 %collective-permute-start.2 = (bf16[2,256,512]{2,1,0:T(8,128)(2,1)S(1)}, bf16[2,256,512]{2,1,0:T(8,128)(2,1)S(1)}, u32[]{:S(2)}, u32[]{:S(2)}) collective-permute-start(bf16[2,256,512]{2,1,0:T(8,128)(2,1)S(1)} %pad_maximum_fusion.refs_2_), channel_id=1, source_target_pairs={{0,32},{32,64},{64,96},{96,0},{1,33},{33,65},{65,97},{97,1},{2,34}... | collective-permute-start | bytes 1572872 | tf_op jit(solution)/shard_map/ppermute | solution.py:211
  18.1 14.8 %collective-permute-start.10 = (bf16[256,512]{1,0:T(8,128)(2,1)S(1)}, bf16[256,512]{1,0:T(8,128)(2,1)S(1)}, u32[]{:S(2)}, u32[]{:S(2)}) collective-permute-start(bf16[256,512]{1,0:T(8,128)(2,1)S(1)} %get-tuple-element.22), channel_id=1, source_target_pairs={{0,129},{1,128},{2,131},{3,130},{4,133},{5,132},{6,135},{7,134},{8... | collective-permute-start | bytes 786440 | tf_op jit(solution)/shard_map/ppermute | solution.py:203
  25.0 22.7 %collective-permute-start.9 = (bf16[256,512]{1,0:T(8,128)(2,1)S(1)}, bf16[256,512]{1,0:T(8,128)(2,1)S(1)}, u32[]{:S(2)}, u32[]{:S(2)}) collective-permute-start(bf16[256,512]{1,0:T(8,128)(2,1)S(1)} %bitcast.48), channel_id=1, source_target_pairs={{0,128},{1,129},{2,130},{3,131},{4,132},{5,133},{6,134},{7,135},{8... | collective-permute-start | bytes 786440 | tf_op jit(solution)/shard_map/ppermute | solution.py:202
  25.0 25.6 %collective-permute-start.3 = (bf16[2,256,512]{2,1,0:T(8,128)(2,1)S(1)}, bf16[2,256,512]{2,1,0:T(8,128)(2,1)S(1)}, u32[]{:S(2)}, u32[]{:S(2)}) collective-permute-start(bf16[2,256,512]{2,1,0:T(8,128)(2,1)S(1)} %pad_maximum_fusion.refs_2_), channel_id=1, source_target_pairs={{0,96},{32,0},{64,32},{96,64},{1,97},{33,1},{65,33},{97,65},{2,98}... | collective-permute-start | bytes 1572872 | tf_op jit(solution)/shard_map/ppermute | solution.py:212
  47.8 14.2 %collective-permute-start.11 = (bf16[2,256,512]{2,1,0:T(8,128)(2,1)S(1)}, bf16[2,256,512]{2,1,0:T(8,128)(2,1)S(1)}, u32[]{:S(2)}, u32[]{:S(2)}) collective-permute-start(bf16[2,256,512]{2,1,0:T(8,128)(2,1)S(1)} %pad_maximum_fusion.1.refs_2_), channel_id=1, source_target_pairs={{0,32},{32,64},{64,96},{96,0},{1,33},{33,65},{65,97},{97,1},{2,34}... | collective-permute-start | bytes 1572872 | tf_op jit(solution)/shard_map/ppermute | solution.py:211
  49.1 13.0 %collective-permute-start.12 = (bf16[2,256,512]{2,1,0:T(8,128)(2,1)S(1)}, bf16[2,256,512]{2,1,0:T(8,128)(2,1)S(1)}, u32[]{:S(2)}, u32[]{:S(2)}) collective-permute-start(bf16[2,256,512]{2,1,0:T(8,128)(2,1)S(1)} %pad_maximum_fusion.1.refs_2_), channel_id=1, source_target_pairs={{0,96},{32,0},{64,32},{96,64},{1,97},{33,1},{65,33},{97,65},{2,98}... | collective-permute-start | bytes 1572872 | tf_op jit(solution)/shard_map/ppermute | solution.py:212
  50.5 20.8 %collective-permute-start.4 = (bf16[256,512]{1,0:T(8,128)(2,1)S(1)}, bf16[256,512]{1,0:T(8,128)(2,1)S(1)}, u32[]{:S(2)}, u32[]{:S(2)}) collective-permute-start(bf16[256,512]{1,0:T(8,128)(2,1)S(1)} %slice_bitcast_fusion.3), channel_id=1, source_target_pairs={{0,32},{32,64},{64,96},{96,0},{1,33},{33,65},{65,97},{97,1},{2,34}... | collective-permute-start | bytes 786440 | tf_op jit(solution)/shard_map/ppermute | solution.py:213
  50.7 20.7 %collective-permute-start.5 = (bf16[256,512]{1,0:T(8,128)(2,1)S(1)}, bf16[256,512]{1,0:T(8,128)(2,1)S(1)}, u32[]{:S(2)}, u32[]{:S(2)}) collective-permute-start(bf16[256,512]{1,0:T(8,128)(2,1)S(1)} %slice_bitcast_fusion.2), channel_id=1, source_target_pairs={{0,96},{32,0},{64,32},{96,64},{1,97},{33,1},{65,33},{97,65},{2,98}... | collective-permute-start | bytes 786440 | tf_op jit(solution)/shard_map/ppermute | solution.py:214
  61.9 25.8 %collective-permute-start.13 = (bf16[256,512]{1,0:T(8,128)(2,1)S(1)}, bf16[256,512]{1,0:T(8,128)(2,1)S(1)}, u32[]{:S(2)}, u32[]{:S(2)}) collective-permute-start(bf16[256,512]{1,0:T(8,128)(2,1)S(1)} %slice_bitcast_fusion.1), channel_id=1, source_target_pairs={{0,32},{32,64},{64,96},{96,0},{1,33},{33,65},{65,97},{97,1},{2,34}... | collective-permute-start | bytes 786440 | tf_op jit(solution)/shard_map/ppermute | solution.py:213
  62.1 25.7 %collective-permute-start.14 = (bf16[256,512]{1,0:T(8,128)(2,1)S(1)}, bf16[256,512]{1,0:T(8,128)(2,1)S(1)}, u32[]{:S(2)}, u32[]{:S(2)}) collective-permute-start(bf16[256,512]{1,0:T(8,128)(2,1)S(1)} %slice_bitcast_fusion), channel_id=1, source_target_pairs={{0,96},{32,0},{64,32},{96,64},{1,97},{33,1},{65,33},{97,65},{2,98}... | collective-permute-start | bytes 786440 | tf_op jit(solution)/shard_map/ppermute | solution.py:214
  76.4 17.6 %collective-permute-start.6 = (bf16[4,72,256]{2,1,0:T(8,128)(2,1)S(1)}, bf16[4,72,256]{2,1,0:T(8,128)(2,1)S(1)}, u32[]{:S(2)}, u32[]{:S(2)}) collective-permute-start(bf16[4,72,256]{2,1,0:T(8,128)(2,1)S(1)} %get-tuple-element.14), channel_id=1, source_target_pairs={{0,2},{1,3},{2,4},{3,5},{4,6},{5,7},{6,0},{7,1},{8,10},{9,11},{10,... | collective-permute-start | bytes 442376 | tf_op jit(solution)/shard_map/ppermute | solution.py:220
  77.7 18.0 %collective-permute-start.7 = (bf16[4,72,256]{2,1,0:T(8,128)(2,1)S(1)}, bf16[4,72,256]{2,1,0:T(8,128)(2,1)S(1)}, u32[]{:S(2)}, u32[]{:S(2)}) collective-permute-start(bf16[4,72,256]{2,1,0:T(8,128)(2,1)S(1)} %get-tuple-element.15), channel_id=1, source_target_pairs={{0,4},{1,5},{2,6},{3,7},{4,0},{5,1},{6,2},{7,3},{8,12},{9,13},{10,... | collective-permute-start | bytes 442376 | tf_op jit(solution)/shard_map/ppermute | solution.py:220
  80.2 15.5 %collective-permute-start.8 = (bf16[4,72,256]{2,1,0:T(8,128)(2,1)S(1)}, bf16[4,72,256]{2,1,0:T(8,128)(2,1)S(1)}, u32[]{:S(2)}, u32[]{:S(2)}) collective-permute-start(bf16[4,72,256]{2,1,0:T(8,128)(2,1)S(1)} %get-tuple-element.16), channel_id=1, source_target_pairs={{0,6},{1,7},{2,0},{3,1},{4,2},{5,3},{6,4},{7,5},{8,14},{9,15},{10,... | collective-permute-start | bytes 442376 | tf_op jit(solution)/shard_map/ppermute | solution.py:220
  92.8 18.1 %copy-start.3 = (f32[1,36]{1,0:T(1,128)S(1)}, f32[1,36]{1,0:T(1,128)}, u32[]{:S(2)}) copy-start(f32[1,36]{1,0:T(1,128)} %param.10) | copy-start | bytes 436
  92.8 6.9 %collective-permute-start.15 = (bf16[4,72,256]{2,1,0:T(8,128)(2,1)S(1)}, bf16[4,72,256]{2,1,0:T(8,128)(2,1)S(1)}, u32[]{:S(2)}, u32[]{:S(2)}) collective-permute-start(bf16[4,72,256]{2,1,0:T(8,128)(2,1)S(1)} %get-tuple-element.18), channel_id=1, source_target_pairs={{0,2},{1,3},{2,4},{3,5},{4,6},{5,7},{6,0},{7,1},{8,10},{9,11},{10,... | collective-permute-start | bytes 442376 | tf_op jit(solution)/shard_map/ppermute | solution.py:220
  93.2 6.5 %collective-permute-start.16 = (bf16[4,72,256]{2,1,0:T(8,128)(2,1)S(1)}, bf16[4,72,256]{2,1,0:T(8,128)(2,1)S(1)}, u32[]{:S(2)}, u32[]{:S(2)}) collective-permute-start(bf16[4,72,256]{2,1,0:T(8,128)(2,1)S(1)} %get-tuple-element.19), channel_id=1, source_target_pairs={{0,4},{1,5},{2,6},{3,7},{4,0},{5,1},{6,2},{7,3},{8,12},{9,13},{10,... | collective-permute-start | bytes 442376 | tf_op jit(solution)/shard_map/ppermute | solution.py:220
  94.1 6.2 %collective-permute-start.17 = (bf16[4,72,256]{2,1,0:T(8,128)(2,1)S(1)}, bf16[4,72,256]{2,1,0:T(8,128)(2,1)S(1)}, u32[]{:S(2)}, u32[]{:S(2)}) collective-permute-start(bf16[4,72,256]{2,1,0:T(8,128)(2,1)S(1)} %get-tuple-element.20), channel_id=1, source_target_pairs={{0,6},{1,7},{2,0},{3,1},{4,2},{5,3},{6,4},{7,5},{8,14},{9,15},{10,... | collective-permute-start | bytes 442376 | tf_op jit(solution)/shard_map/ppermute | solution.py:220
  101.6 18.7 %all-to-all-start = ((bf16[8,72,256]{2,1,0:T(8,128)(2,1)}), bf16[8,72,256]{2,1,0:T(8,128)(2,1)S(1)}, u32[]{:S(2)}, u32[]{:S(2)}) async-start(bf16[8,72,256]{2,1,0:T(8,128)(2,1)} %shard_map.69), calls=%async_computation | async-start | bytes 589824 | tf_op jit(solution)/shard_map/all_to_all | solution.py:222

commit v9 on v8

--- a/solution.py
+++ b/solution.py
@@ -55,7 +55,7 @@
 
 TILE = 384
 GRANT = 12
-CUT_GRANT = 6
+CUT_GRANT = 48
 
 
 def terms_of(backs, weights, blocks, cols):
@@ -153,6 +153,11 @@
     )
 
 
+def decode(at, weights, near, far):
+    total = partial(at, weights, (0, 1, 3), near)
+    return last(at, weights, [total], (2,), far)
+
+
 def x_sum_kernel(at_ref, *refs):
     *before, self_ref, a_ref, b_ref, c_ref, out_ref = refs
     for z in range(NZ):
@@ -205,16 +210,25 @@
     w_mine = cut(at, dec_weight)
     w_theirs = lax.ppermute(w_mine, "feat", PARTNER)
     weights = (w_mine, w_theirs)
+    def shift(array, by):
+        return lax.ppermute(array, "layer", ring(by))
+
+    both = jnp.stack([keep, own_theirs])
+    up, down = shift(both, 1), shift(both, -1)
+    up_mine = up[0]
+    down_theirs = down[1]
+    far = [shift(up_mine, 1), shift(down_theirs, -1)]
+    near = [both, up, down]
+    own = decode(at, weights, near, far)
+
+    up_mine, down_mine = shift(other_mine, 1), shift(other_mine, -1)
+    up_theirs, down_theirs = shift(other_theirs, 1), shift(other_theirs, -1)
+    far = [shift(up_mine, 1), shift(down_theirs, -1)]
+    near = [other_mine, other_theirs, up_mine, up_theirs, down_mine, down_theirs]
+    other = decode(at, weights, near, far)
+
     chips = []
-    for mine, theirs in ((keep, own_theirs), (other_mine, other_theirs)):
-        both = jnp.stack([mine, theirs])
-        up = lax.ppermute(both, "layer", ring(1))
-        down = lax.ppermute(both, "layer", ring(-1))
-        far_up = lax.ppermute(up[0], "layer", ring(1))
-        far_down = lax.ppermute(down[1], "layer", ring(-1))
-        near, far = [both, up, down], [far_up, far_down]
-        total = partial(at, weights, (0, 1, 3), near)
-        kept, *away = last(at, weights, [total], (2,), far)
+    for (kept, *away) in (own, other):
         came = []
         for by, piece in enumerate(away):
             came.append(lax.ppermute(piece, "feat", x_pairs(by + 1)))

time: 122 us -> 117 us (0.959)
  waiting for transfers between devices: 47.6 us -> 34.9 us
  starting transfers between devices: 37.7 us -> 46.2 us
  local copies, waits for them, and re-layouts: 2.72 us -> 0.2 us
  Pallas kernels: 30.2 us -> 31.8 us
    ppermute x1, waiting for transfers between devices: 14.8 us -> 5.35 us  [per_device(): other_mine = lax.ppermute(keep, ('dp', 'feat'), across(0))]
    all_to_all x1, starting transfers between devices: 9.32 us -> 17.1 us  [per_device(): lax.all_to_all(chips[0], 'feat', 0, 0, tiled=True, axis_index_groups=ZC_G...]
    ppermute x1, starting transfers between devices: 6.94 us -> 1.27 us  [per_device(): other_theirs = lax.ppermute(send, ('dp', 'feat'), across(1))]
    ppermute x1, starting transfers between devices: 0.01 us -> 5.2 us  [per_device(): other_mine = lax.ppermute(keep, ('dp', 'feat'), across(0))]
    ppermute x8 -> x10, waiting for transfers between devices: 8.54 us -> 3.59 us  [shift(): return lax.ppermute(array, 'layer', ring(by))]
    unnamed x10 -> x8, local copies, waits for them, and re-layouts: 2.51 us -> 0.02 us
    ppermute x1, waiting for transfers between devices: 6.23 us -> 7.99 us  [per_device(): other_theirs = lax.ppermute(send, ('dp', 'feat'), across(1))]
    pallas_call x1, Pallas kernels: 3.94 us -> 5.55 us  [cut(): pl.pallas_call(cut_kernel, out_shape=jax.ShapeDtypeStruct(decoders.shape[...]
  transfers between devices with their start and end apart: 19 -> 21, of which waited for: 7 -> 7; matrix products, arithmetic and copies ran while one was open for 3% -> 3% of each run, Pallas kernels for 19% -> 20%
where the time goes in v9:
time: 117 us; the launch traced here: 116 us
  starting transfers between devices  46.2 us (39%)
  waiting for transfers between devices  34.9 us (30%)
  Pallas kernels  31.8 us (27%)
  matrix products  3.05 us (3%)
    pallas_call x7, Pallas kernels, call(): pl.pallas_call(kernel, out_shape=out_shape, in_specs=[IN_SMEM] + [IN_VMEM...  26.2 us
    all_to_all x1, starting transfers between devices, per_device(): lax.all_to_all(chips[0], 'feat', 0, 0, tiled=True, axis_index_groups=ZC_G...  17.1 us
    ppermute x10, starting transfers between devices, shift(): return lax.ppermute(array, 'layer', ring(by))  11.4 us
    all_to_all x1, waiting for transfers between devices, per_device(): lax.all_to_all(chips[0], 'feat', 0, 0, tiled=True, axis_index_groups=ZC_G...  9.23 us
    ppermute x1, waiting for transfers between devices, per_device(): other_theirs = lax.ppermute(send, ('dp', 'feat'), across(1))  7.99 us
    ppermute x6, starting transfers between devices, per_device(): came.append(lax.ppermute(piece, 'feat', x_pairs(by + 1)))  7.79 us
    pallas_call x1, Pallas kernels, cut(): pl.pallas_call(cut_kernel, out_shape=jax.ShapeDtypeStruct(decoders.shape[...  5.55 us
    ppermute x1, waiting for transfers between devices, per_device(): other_mine = lax.ppermute(keep, ('dp', 'feat'), across(0))  5.35 us
  transfers between devices with their start and end apart: 21, of which 7 were waited for; matrix products, arithmetic and copies ran while one was open for 3% of the time, Pallas kernels for 20%

profile of v9, /device:TPU:1, one launch (start us, length us, event | category | flops | bytes accessed | tf_op | source)
XLA Modules:
  0.0 116.5 jit_solution(11026505141085528809)
XLA Ops:
  0.1 5.5 %cut.1.refs_0_ = bf16[4,512,1152]{2,1,0:T(8,128)(2,1)} custom-call(s32[4]{0:T(128)S(1)} %pad_add_fusion.at_ref, bf16[1,4,512,1152]{3,2,1,0:T(8,128)(2,1)} %decoders_ref.1), custom_call_target="tpu_custom_call" | custom-call | bytes 4718592 | tf_op jit(solution)/shard_map/cut/pallas_call | solution.py:94
  5.6 3.3 %collective-permute-start = (bf16[4,512,1152]{2,1,0:T(8,128)(2,1)}, bf16[4,512,1152]{2,1,0:T(8,128)(2,1)}, u32[]{:S(2)}, u32[]{:S(2)}) collective-permute-start(bf16[4,512,1152]{2,1,0:T(8,128)(2,1)} %cut.1.refs_0_), channel_id=1, source_target_pairs={{0,1},{1,0},{2,3},{3,2},{4,5},{5,4},{6,7},{7,6},{8,9},{9,8},{10,11... | collective-permute-start | bytes 14155784 | tf_op jit(solution)/shard_map/ppermute | solution.py:211
  9.0 3.0 %fusion.18 = bf16[512,512]{1,0:T(8,128)(2,1)S(1)} fusion(bf16[1,2304,512]{2,1,0:T(8,128)(2,1)S(1)} %copy-done, bf16[1,512,2304]{2,1,0:T(8,128)(2,1)} %param.6, f32[512]{0:T(512)S(1)} %convert_bitcast_fusion, f32[512]{0:T(512)S(1)} %bitcast.46), kind=kOutput, calls=%fused_computation.6 | convolution fusion | flops 1209008128 | bytes 5246976 | tf_op jit(solution)/shard_map/dot_general | solution.py:202
  12.2 4.8 %collective-permute-done.1 = bf16[256,512]{1,0:T(8,128)(2,1)S(1)} collective-permute-done((bf16[256,512]{1,0:T(8,128)(2,1)S(1)}, bf16[256,512]{1,0:T(8,128)(2,1)S(1)}, u32[]{:S(2)}, u32[]{:S(2)}) %collective-permute-start.1) | collective-permute-done | bytes 262176 | tf_op jit(solution)/shard_map/ppermute | solution.py:209
  17.2 2.7 %collective-permute-start.3 = (bf16[2,256,512]{2,1,0:T(8,128)(2,1)S(1)}, bf16[2,256,512]{2,1,0:T(8,128)(2,1)S(1)}, u32[]{:S(2)}, u32[]{:S(2)}) collective-permute-start(bf16[2,256,512]{2,1,0:T(8,128)(2,1)S(1)} %pad_maximum_fusion.refs_2_), channel_id=1, source_target_pairs={{0,96},{32,0},{64,32},{96,64},{1,97},{33,1},{65,33},{97,65},{2,98}... | collective-permute-start | bytes 1572872 | tf_op jit(solution)/shard_map/ppermute | solution.py:214
  19.9 5.2 %collective-permute-start.9 = (bf16[256,512]{1,0:T(8,128)(2,1)S(1)}, bf16[256,512]{1,0:T(8,128)(2,1)S(1)}, u32[]{:S(2)}, u32[]{:S(2)}) collective-permute-start(bf16[256,512]{1,0:T(8,128)(2,1)S(1)} %bitcast.42), channel_id=1, source_target_pairs={{0,128},{1,129},{2,130},{3,131},{4,132},{5,133},{6,134},{7,135},{8... | collective-permute-start | bytes 786440 | tf_op jit(solution)/shard_map/ppermute | solution.py:207
  26.3 5.4 %collective-permute-done.9.refs_2_ = bf16[256,512]{1,0:T(8,128)(2,1)S(1)} collective-permute-done((bf16[256,512]{1,0:T(8,128)(2,1)S(1)}, bf16[256,512]{1,0:T(8,128)(2,1)S(1)}, u32[]{:S(2)}, u32[]{:S(2)}) %collective-permute-start.9) | collective-permute-done | bytes 262176 | tf_op jit(solution)/shard_map/ppermute | solution.py:207
  31.7 8.0 %collective-permute-done.10.refs_3_ = bf16[256,512]{1,0:T(8,128)(2,1)S(1)} collective-permute-done((bf16[256,512]{1,0:T(8,128)(2,1)S(1)}, bf16[256,512]{1,0:T(8,128)(2,1)S(1)}, u32[]{:S(2)}, u32[]{:S(2)}) %collective-permute-start.10) | collective-permute-done | bytes 262176 | tf_op jit(solution)/shard_map/ppermute | solution.py:208
  41.3 2.3 %collective-permute-start.5 = (bf16[256,512]{1,0:T(8,128)(2,1)S(1)}, bf16[256,512]{1,0:T(8,128)(2,1)S(1)}, u32[]{:S(2)}, u32[]{:S(2)}) collective-permute-start(bf16[256,512]{1,0:T(8,128)(2,1)S(1)} %slice_bitcast_fusion), channel_id=1, source_target_pairs={{0,96},{32,0},{64,32},{96,64},{1,97},{33,1},{65,33},{97,65},{2,98}... | collective-permute-start | bytes 786440 | tf_op jit(solution)/shard_map/ppermute | solution.py:214
  43.6 3.6 %collective-permute-done.14.refs_7_ = bf16[256,512]{1,0:T(8,128)(2,1)S(1)} collective-permute-done((bf16[256,512]{1,0:T(8,128)(2,1)S(1)}, bf16[256,512]{1,0:T(8,128)(2,1)S(1)}, u32[]{:S(2)}, u32[]{:S(2)}) %collective-permute-start.14) | collective-permute-done | bytes 262176 | tf_op jit(solution)/shard_map/ppermute | solution.py:214
  47.2 2.1 %collective-permute-start.13 = (bf16[256,512]{1,0:T(8,128)(2,1)S(1)}, bf16[256,512]{1,0:T(8,128)(2,1)S(1)}, u32[]{:S(2)}, u32[]{:S(2)}) collective-permute-start(bf16[256,512]{1,0:T(8,128)(2,1)S(1)} %collective-permute-done.9.refs_2_), channel_id=1, source_target_pairs={{0,96},{32,0},{64,32},{96,64},{1,97},{33,1},{65,33},{97,65},{2,98}... | collective-permute-start | bytes 786440 | tf_op jit(solution)/shard_map/ppermute | solution.py:214
  49.3 2.7 %collective-permute-start.16 = (bf16[256,512]{1,0:T(8,128)(2,1)S(1)}, bf16[256,512]{1,0:T(8,128)(2,1)S(1)}, u32[]{:S(2)}, u32[]{:S(2)}) collective-permute-start(bf16[256,512]{1,0:T(8,128)(2,1)S(1)} %collective-permute-done.14.refs_7_), channel_id=1, source_target_pairs={{0,96},{32,0},{64,32},{96,64},{1,97},{33,1},{65,33},{97,65},{2,98}... | collective-permute-start | bytes 786440 | tf_op jit(solution)/shard_map/ppermute | solution.py:214
  52.0 6.4 %shard_map.64.refs_2_ = f32[256,1152]{1,0:T(8,128)S(1)} custom-call(s32[4]{0:T(128)S(1)} %pad_add_fusion.at_ref, bf16[4,512,1152]{2,1,0:T(8,128)(2,1)} %cut.1.refs_0_, bf16[4,512,1152]{2,1,0:T(8,128)(2,1)} %collective-permute-done.refs_1_, bf16[2,256,512]{2,1,0:T(8,128)(2,1)S(1)} %pad_maximum_fusion.refs_2_, ...), custom_call_target="tpu_custom_call" | custom-call | flops 1811939328 | bytes 11010064 | tf_op jit(solution)/shard_map/pallas_call | solution.py:45
  58.4 5.0 %shard_map.65 = (f32[4,72,256]{2,1,0:T(8,128)S(1)}, bf16[4,72,256]{2,1,0:T(8,128)(2,1)S(1)}, bf16[4,72,256]{2,1,0:T(8,128)(2,1)S(1)}, bf16[4,72,256]{2,1,0:T(8,128)(2,1)S(1)}) custom-call(s32[4]{0:T(128)S(1)} %pad_add_fusion.at_ref, bf16[4,512,1152]{2,1,0:T(8,128)(2,1)} %cut.1.refs_0_, bf16[4,512,1152]{2,1,0:T(8,128)(2,1)} %collective-permute-done.refs_1_, ...), custom_call_target="tpu_custom_call" | custom-call | flops 603979776 | bytes 11141136 | tf_op jit(solution)/shard_map/pallas_call | solution.py:45
  63.4 1.3 %collective-permute-start.6 = (bf16[4,72,256]{2,1,0:T(8,128)(2,1)S(1)}, bf16[4,72,256]{2,1,0:T(8,128)(2,1)S(1)}, u32[]{:S(2)}, u32[]{:S(2)}) collective-permute-start(bf16[4,72,256]{2,1,0:T(8,128)(2,1)S(1)} %get-tuple-element.14), channel_id=1, source_target_pairs={{0,2},{1,3},{2,4},{3,5},{4,6},{5,7},{6,0},{7,1},{8,10},{9,11},{10,... | collective-permute-start | bytes 442376 | tf_op jit(solution)/shard_map/ppermute | solution.py:234
  64.7 2.4 %collective-permute-start.7 = (bf16[4,72,256]{2,1,0:T(8,128)(2,1)S(1)}, bf16[4,72,256]{2,1,0:T(8,128)(2,1)S(1)}, u32[]{:S(2)}, u32[]{:S(2)}) collective-permute-start(bf16[4,72,256]{2,1,0:T(8,128)(2,1)S(1)} %get-tuple-element.15), channel_id=1, source_target_pairs={{0,4},{1,5},{2,6},{3,7},{4,0},{5,1},{6,2},{7,3},{8,12},{9,13},{10,... | collective-permute-start | bytes 442376 | tf_op jit(solution)/shard_map/ppermute | solution.py:234
  68.3 6.4 %shard_map.67.refs_2_ = f32[256,1152]{1,0:T(8,128)S(1)} custom-call(s32[4]{0:T(128)S(1)} %pad_add_fusion.at_ref, bf16[4,512,1152]{2,1,0:T(8,128)(2,1)} %cut.1.refs_0_, bf16[4,512,1152]{2,1,0:T(8,128)(2,1)} %collective-permute-done.refs_1_, bf16[256,512]{1,0:T(8,128)(2,1)S(1)} %collective-permute-done.9.refs_2_, ...), custom_call_target="tpu_custom_call" | custom-call | flops 1811939328 | bytes 11010064 | tf_op jit(solution)/shard_map/pallas_call | solution.py:45
  74.7 5.0 %shard_map.68 = (f32[4,72,256]{2,1,0:T(8,128)S(1)}, bf16[4,72,256]{2,1,0:T(8,128)(2,1)S(1)}, bf16[4,72,256]{2,1,0:T(8,128)(2,1)S(1)}, bf16[4,72,256]{2,1,0:T(8,128)(2,1)S(1)}) custom-call(s32[4]{0:T(128)S(1)} %pad_add_fusion.at_ref, bf16[4,512,1152]{2,1,0:T(8,128)(2,1)} %cut.1.refs_0_, bf16[4,512,1152]{2,1,0:T(8,128)(2,1)} %collective-permute-done.refs_1_, ...), custom_call_target="tpu_custom_call" | custom-call | flops 603979776 | bytes 11141136 | tf_op jit(solution)/shard_map/pallas_call | solution.py:45
  81.0 1.6 %collective-permute-start.19 = (bf16[4,72,256]{2,1,0:T(8,128)(2,1)S(1)}, bf16[4,72,256]{2,1,0:T(8,128)(2,1)S(1)}, u32[]{:S(2)}, u32[]{:S(2)}) collective-permute-start(bf16[4,72,256]{2,1,0:T(8,128)(2,1)S(1)} %get-tuple-element.20), channel_id=1, source_target_pairs={{0,6},{1,7},{2,0},{3,1},{4,2},{5,3},{6,4},{7,5},{8,14},{9,15},{10,... | collective-permute-start | bytes 442376 | tf_op jit(solution)/shard_map/ppermute | solution.py:234
  83.3 3.3 %collective-permute-done.17.refs_2_ = bf16[4,72,256]{2,1,0:T(8,128)(2,1)S(1)} collective-permute-done((bf16[4,72,256]{2,1,0:T(8,128)(2,1)S(1)}, bf16[4,72,256]{2,1,0:T(8,128)(2,1)S(1)}, u32[]{:S(2)}, u32[]{:S(2)}) %collective-permute-start.17) | collective-permute-done | bytes 147488 | tf_op jit(solution)/shard_map/ppermute | solution.py:234
  87.2 1.3 %shard_map.69 = bf16[8,72,256]{2,1,0:T(8,128)(2,1)} custom-call(s32[4]{0:T(128)S(1)} %pad_add_fusion.at_ref, bf16[8,36,256]{2,1,0:T(8,128)(2,1)S(1)} %shard_map.66.refs_0_, f32[4,72,256]{2,1,0:T(8,128)S(1)} %get-tuple-element.17.refs_1_, bf16[4,72,256]{2,1,0:T(8,128)(2,1)S(1)} %collective-permute-done.17.refs_2_, ...), custom_call_target="tpu_custom_call" | custom-call | bytes 884752 | tf_op jit(solution)/shard_map/pallas_call | solution.py:45
  88.6 17.1 %all-to-all-start = ((bf16[8,72,256]{2,1,0:T(8,128)(2,1)}), bf16[8,72,256]{2,1,0:T(8,128)(2,1)S(1)}, u32[]{:S(2)}, u32[]{:S(2)}) async-start(bf16[8,72,256]{2,1,0:T(8,128)(2,1)} %shard_map.69), calls=%async_computation | async-start | bytes 589824 | tf_op jit(solution)/shard_map/all_to_all | solution.py:236
  105.8 9.2 %all-to-all-done.chips_ref = bf16[8,72,256]{2,1,0:T(8,128)(2,1)S(1)} async-done(((bf16[8,72,256]{2,1,0:T(8,128)(2,1)}), bf16[8,72,256]{2,1,0:T(8,128)(2,1)S(1)}, u32[]{:S(2)}, u32[]{:S(2)}) %all-to-all-start) | async-done | bytes 294944 | tf_op jit(solution)/shard_map/all_to_all | solution.py:236
  115.0 1.5 %shard_map.70 = bf16[36,1024]{1,0:T(8,128)(2,1)} custom-call(s32[4]{0:T(128)S(1)} %pad_add_fusion.at_ref, bf16[8,72,256]{2,1,0:T(8,128)(2,1)S(1)} %all-to-all-done.chips_ref, f32[36,1]{1,0:T(8,128)S(1)} %copy.7.bias_ref), custom_call_target="tpu_custom_call" | custom-call | bytes 295072 | tf_op jit(solution)/shard_map/pallas_call | solution.py:45
  (42 shorter events, 7.1 us)
Async XLA Ops:
  0.0 9.0 %copy-start = (bf16[1,2304,512]{2,1,0:T(8,128)(2,1)S(1)}, bf16[1,2304,512]{2,1,0:T(8,128)(2,1)}, u32[]{:S(2)}) copy-start(bf16[1,2304,512]{2,1,0:T(8,128)(2,1)} %param.7) | copy-start | bytes 7077892
  0.1 8.9 %copy-start.3 = (f32[1,512]{1,0:T(1,128)S(1)}, f32[1,512]{1,0:T(1,128)}, u32[]{:S(2)}) copy-start(f32[1,512]{1,0:T(1,128)} %param.8) | copy-start | bytes 6148
  5.6 43.6 %collective-permute-start = (bf16[4,512,1152]{2,1,0:T(8,128)(2,1)}, bf16[4,512,1152]{2,1,0:T(8,128)(2,1)}, u32[]{:S(2)}, u32[]{:S(2)}) collective-permute-start(bf16[4,512,1152]{2,1,0:T(8,128)(2,1)} %cut.1.refs_0_), channel_id=1, source_target_pairs={{0,1},{1,0},{2,3},{3,2},{4,5},{5,4},{6,7},{7,6},{8,9},{9,8},{10,11... | collective-permute-start | bytes 14155784 | tf_op jit(solution)/shard_map/ppermute | solution.py:211
  12.1 4.9 %collective-permute-start.1 = (bf16[256,512]{1,0:T(8,128)(2,1)S(1)}, bf16[256,512]{1,0:T(8,128)(2,1)S(1)}, u32[]{:S(2)}, u32[]{:S(2)}) collective-permute-start(bf16[256,512]{1,0:T(8,128)(2,1)S(1)} %get-tuple-element.22), channel_id=1, source_target_pairs={{0,1},{1,0},{2,3},{3,2},{4,5},{5,4},{6,7},{7,6},{8,9},{9,8},{10,11... | collective-permute-start | bytes 786440 | tf_op jit(solution)/shard_map/ppermute | solution.py:209
  17.1 23.6 %collective-permute-start.2 = (bf16[2,256,512]{2,1,0:T(8,128)(2,1)S(1)}, bf16[2,256,512]{2,1,0:T(8,128)(2,1)S(1)}, u32[]{:S(2)}, u32[]{:S(2)}) collective-permute-start(bf16[2,256,512]{2,1,0:T(8,128)(2,1)S(1)} %pad_maximum_fusion.refs_2_), channel_id=1, source_target_pairs={{0,32},{32,64},{64,96},{96,0},{1,33},{33,65},{65,97},{97,1},{2,34}... | collective-permute-start | bytes 1572872 | tf_op jit(solution)/shard_map/ppermute | solution.py:214
  17.2 24.1 %collective-permute-start.3 = (bf16[2,256,512]{2,1,0:T(8,128)(2,1)S(1)}, bf16[2,256,512]{2,1,0:T(8,128)(2,1)S(1)}, u32[]{:S(2)}, u32[]{:S(2)}) collective-permute-start(bf16[2,256,512]{2,1,0:T(8,128)(2,1)S(1)} %pad_maximum_fusion.refs_2_), channel_id=1, source_target_pairs={{0,96},{32,0},{64,32},{96,64},{1,97},{33,1},{65,33},{97,65},{2,98}... | collective-permute-start | bytes 1572872 | tf_op jit(solution)/shard_map/ppermute | solution.py:214
  19.9 11.8 %collective-permute-start.9 = (bf16[256,512]{1,0:T(8,128)(2,1)S(1)}, bf16[256,512]{1,0:T(8,128)(2,1)S(1)}, u32[]{:S(2)}, u32[]{:S(2)}) collective-permute-start(bf16[256,512]{1,0:T(8,128)(2,1)S(1)} %bitcast.42), channel_id=1, source_target_pairs={{0,128},{1,129},{2,130},{3,131},{4,132},{5,133},{6,134},{7,135},{8... | collective-permute-start | bytes 786440 | tf_op jit(solution)/shard_map/ppermute | solution.py:207
  25.1 14.6 %collective-permute-start.10 = (bf16[256,512]{1,0:T(8,128)(2,1)S(1)}, bf16[256,512]{1,0:T(8,128)(2,1)S(1)}, u32[]{:S(2)}, u32[]{:S(2)}) collective-permute-start(bf16[256,512]{1,0:T(8,128)(2,1)S(1)} %get-tuple-element.22), channel_id=1, source_target_pairs={{0,129},{1,128},{2,131},{3,130},{4,133},{5,132},{6,135},{7,134},{8... | collective-permute-start | bytes 786440 | tf_op jit(solution)/shard_map/ppermute | solution.py:208
  31.7 11.9 %collective-permute-start.11 = (bf16[256,512]{1,0:T(8,128)(2,1)S(1)}, bf16[256,512]{1,0:T(8,128)(2,1)S(1)}, u32[]{:S(2)}, u32[]{:S(2)}) collective-permute-start(bf16[256,512]{1,0:T(8,128)(2,1)S(1)} %collective-permute-done.9.refs_2_), channel_id=1, source_target_pairs={{0,32},{32,64},{64,96},{96,0},{1,33},{33,65},{65,97},{97,1},{2,34}... | collective-permute-start | bytes 786440 | tf_op jit(solution)/shard_map/ppermute | solution.py:214
  39.7 7.5 %collective-permute-start.14 = (bf16[256,512]{1,0:T(8,128)(2,1)S(1)}, bf16[256,512]{1,0:T(8,128)(2,1)S(1)}, u32[]{:S(2)}, u32[]{:S(2)}) collective-permute-start(bf16[256,512]{1,0:T(8,128)(2,1)S(1)} %collective-permute-done.10.refs_3_), channel_id=1, source_target_pairs={{0,96},{32,0},{64,32},{96,64},{1,97},{33,1},{65,33},{97,65},{2,98}... | collective-permute-start | bytes 786440 | tf_op jit(solution)/shard_map/ppermute | solution.py:214
  40.7 8.5 %collective-permute-start.4 = (bf16[256,512]{1,0:T(8,128)(2,1)S(1)}, bf16[256,512]{1,0:T(8,128)(2,1)S(1)}, u32[]{:S(2)}, u32[]{:S(2)}) collective-permute-start(bf16[256,512]{1,0:T(8,128)(2,1)S(1)} %slice_bitcast_fusion.1), channel_id=1, source_target_pairs={{0,32},{32,64},{64,96},{96,0},{1,33},{33,65},{65,97},{97,1},{2,34}... | collective-permute-start | bytes 786440 | tf_op jit(solution)/shard_map/ppermute | solution.py:214
  41.3 17.1 %collective-permute-start.5 = (bf16[256,512]{1,0:T(8,128)(2,1)S(1)}, bf16[256,512]{1,0:T(8,128)(2,1)S(1)}, u32[]{:S(2)}, u32[]{:S(2)}) collective-permute-start(bf16[256,512]{1,0:T(8,128)(2,1)S(1)} %slice_bitcast_fusion), channel_id=1, source_target_pairs={{0,96},{32,0},{64,32},{96,64},{1,97},{33,1},{65,33},{97,65},{2,98}... | collective-permute-start | bytes 786440 | tf_op jit(solution)/shard_map/ppermute | solution.py:214
  43.6 21.1 %collective-permute-start.12 = (bf16[256,512]{1,0:T(8,128)(2,1)S(1)}, bf16[256,512]{1,0:T(8,128)(2,1)S(1)}, u32[]{:S(2)}, u32[]{:S(2)}) collective-permute-start(bf16[256,512]{1,0:T(8,128)(2,1)S(1)} %collective-permute-done.10.refs_3_), channel_id=1, source_target_pairs={{0,32},{32,64},{64,96},{96,0},{1,33},{33,65},{65,97},{97,1},{2,34}... | collective-permute-start | bytes 786440 | tf_op jit(solution)/shard_map/ppermute | solution.py:214
  47.2 20.0 %collective-permute-start.13 = (bf16[256,512]{1,0:T(8,128)(2,1)S(1)}, bf16[256,512]{1,0:T(8,128)(2,1)S(1)}, u32[]{:S(2)}, u32[]{:S(2)}) collective-permute-start(bf16[256,512]{1,0:T(8,128)(2,1)S(1)} %collective-permute-done.9.refs_2_), channel_id=1, source_target_pairs={{0,96},{32,0},{64,32},{96,64},{1,97},{33,1},{65,33},{97,65},{2,98}... | collective-permute-start | bytes 786440 | tf_op jit(solution)/shard_map/ppermute | solution.py:214
  49.3 25.4 %collective-permute-start.15 = (bf16[256,512]{1,0:T(8,128)(2,1)S(1)}, bf16[256,512]{1,0:T(8,128)(2,1)S(1)}, u32[]{:S(2)}, u32[]{:S(2)}) collective-permute-start(bf16[256,512]{1,0:T(8,128)(2,1)S(1)} %collective-permute-done.11.refs_4_), channel_id=1, source_target_pairs={{0,32},{32,64},{64,96},{96,0},{1,33},{33,65},{65,97},{97,1},{2,34}... | collective-permute-start | bytes 786440 | tf_op jit(solution)/shard_map/ppermute | solution.py:214
  49.3 25.4 %collective-permute-start.16 = (bf16[256,512]{1,0:T(8,128)(2,1)S(1)}, bf16[256,512]{1,0:T(8,128)(2,1)S(1)}, u32[]{:S(2)}, u32[]{:S(2)}) collective-permute-start(bf16[256,512]{1,0:T(8,128)(2,1)S(1)} %collective-permute-done.14.refs_7_), channel_id=1, source_target_pairs={{0,96},{32,0},{64,32},{96,64},{1,97},{33,1},{65,33},{97,65},{2,98}... | collective-permute-start | bytes 786440 | tf_op jit(solution)/shard_map/ppermute | solution.py:214
  63.4 17.6 %collective-permute-start.6 = (bf16[4,72,256]{2,1,0:T(8,128)(2,1)S(1)}, bf16[4,72,256]{2,1,0:T(8,128)(2,1)S(1)}, u32[]{:S(2)}, u32[]{:S(2)}) collective-permute-start(bf16[4,72,256]{2,1,0:T(8,128)(2,1)S(1)} %get-tuple-element.14), channel_id=1, source_target_pairs={{0,2},{1,3},{2,4},{3,5},{4,6},{5,7},{6,0},{7,1},{8,10},{9,11},{10,... | collective-permute-start | bytes 442376 | tf_op jit(solution)/shard_map/ppermute | solution.py:234
  64.7 18.0 %collective-permute-start.7 = (bf16[4,72,256]{2,1,0:T(8,128)(2,1)S(1)}, bf16[4,72,256]{2,1,0:T(8,128)(2,1)S(1)}, u32[]{:S(2)}, u32[]{:S(2)}) collective-permute-start(bf16[4,72,256]{2,1,0:T(8,128)(2,1)S(1)} %get-tuple-element.15), channel_id=1, source_target_pairs={{0,4},{1,5},{2,6},{3,7},{4,0},{5,1},{6,2},{7,3},{8,12},{9,13},{10,... | collective-permute-start | bytes 442376 | tf_op jit(solution)/shard_map/ppermute | solution.py:234
  67.1 15.5 %collective-permute-start.8 = (bf16[4,72,256]{2,1,0:T(8,128)(2,1)S(1)}, bf16[4,72,256]{2,1,0:T(8,128)(2,1)S(1)}, u32[]{:S(2)}, u32[]{:S(2)}) collective-permute-start(bf16[4,72,256]{2,1,0:T(8,128)(2,1)S(1)} %get-tuple-element.16), channel_id=1, source_target_pairs={{0,6},{1,7},{2,0},{3,1},{4,2},{5,3},{6,4},{7,5},{8,14},{9,15},{10,... | collective-permute-start | bytes 442376 | tf_op jit(solution)/shard_map/ppermute | solution.py:234
  79.7 25.9 %copy-start.2 = (f32[1,36]{1,0:T(1,128)S(1)}, f32[1,36]{1,0:T(1,128)}, u32[]{:S(2)}) copy-start(f32[1,36]{1,0:T(1,128)} %param.10) | copy-start | bytes 436
  79.7 6.9 %collective-permute-start.17 = (bf16[4,72,256]{2,1,0:T(8,128)(2,1)S(1)}, bf16[4,72,256]{2,1,0:T(8,128)(2,1)S(1)}, u32[]{:S(2)}, u32[]{:S(2)}) collective-permute-start(bf16[4,72,256]{2,1,0:T(8,128)(2,1)S(1)} %get-tuple-element.18), channel_id=1, source_target_pairs={{0,2},{1,3},{2,4},{3,5},{4,6},{5,7},{6,0},{7,1},{8,10},{9,11},{10,... | collective-permute-start | bytes 442376 | tf_op jit(solution)/shard_map/ppermute | solution.py:234
  80.1 6.5 %collective-permute-start.18 = (bf16[4,72,256]{2,1,0:T(8,128)(2,1)S(1)}, bf16[4,72,256]{2,1,0:T(8,128)(2,1)S(1)}, u32[]{:S(2)}, u32[]{:S(2)}) collective-permute-start(bf16[4,72,256]{2,1,0:T(8,128)(2,1)S(1)} %get-tuple-element.19), channel_id=1, source_target_pairs={{0,4},{1,5},{2,6},{3,7},{4,0},{5,1},{6,2},{7,3},{8,12},{9,13},{10,... | collective-permute-start | bytes 442376 | tf_op jit(solution)/shard_map/ppermute | solution.py:234
  81.0 6.2 %collective-permute-start.19 = (bf16[4,72,256]{2,1,0:T(8,128)(2,1)S(1)}, bf16[4,72,256]{2,1,0:T(8,128)(2,1)S(1)}, u32[]{:S(2)}, u32[]{:S(2)}) collective-permute-start(bf16[4,72,256]{2,1,0:T(8,128)(2,1)S(1)} %get-tuple-element.20), channel_id=1, source_target_pairs={{0,6},{1,7},{2,0},{3,1},{4,2},{5,3},{6,4},{7,5},{8,14},{9,15},{10,... | collective-permute-start | bytes 442376 | tf_op jit(solution)/shard_map/ppermute | solution.py:234
  88.6 26.4 %all-to-all-start = ((bf16[8,72,256]{2,1,0:T(8,128)(2,1)}), bf16[8,72,256]{2,1,0:T(8,128)(2,1)S(1)}, u32[]{:S(2)}, u32[]{:S(2)}) async-start(bf16[8,72,256]{2,1,0:T(8,128)(2,1)} %shard_map.69), calls=%async_computation | async-start | bytes 589824 | tf_op jit(solution)/shard_map/all_to_all | solution.py:236
  (1 other events, 8.8 us)

commit v10 on v9

--- a/solution.py
+++ b/solution.py
@@ -53,7 +53,7 @@
     )(*operands)
 
 
-TILE = 384
+TILES = (slice(0, 512), slice(512, 1024), slice(1024, 1152))
 GRANT = 12
 CUT_GRANT = 48
 
@@ -64,13 +64,6 @@
         term = jnp.dot(block[...], weights[i % 2][backs[i // 2], :, cols], preferred_element_type=F32)
         total = term if total is None else total + term
     return total
-
-
-def split_blocks(refs):
-    out = []
-    for ref in refs:
-        out += [ref.at[0], ref.at[1]] if len(ref.shape) == 3 else [ref]
-    return out
 
 
 def cut_kernel(at_ref, decoders_ref, out_ref, sems):
@@ -105,9 +98,7 @@
 
 def partial_kernel(backs, at_ref, *refs):
     weights, blocks, total_ref = refs[:2], refs[2:-1], refs[-1]
-    blocks = split_blocks(blocks)
-    for n in range(total_ref.shape[1] // TILE):
-        cols = slice(n * TILE, (n + 1) * TILE)
+    for cols in TILES:
         total_ref[:, cols] = terms_of(backs, weights, blocks, cols)
 
 
@@ -125,9 +116,8 @@
     turned = refs[-1]
     self_ref, *away = refs[-5:-1]
     refs = refs[:-5]
-    blocks = split_blocks(refs[has_base:])
-    for n in range(turned.shape[0] // TILE):
-        cols = slice(n * TILE, (n + 1) * TILE)
+    blocks = refs[has_base:]
+    for cols in TILES:
         total = terms_of(backs, weights, blocks, cols)
         if has_base:
             total = total + refs[0][:, cols]
@@ -213,22 +203,20 @@
     def shift(array, by):
         return lax.ppermute(array, "layer", ring(by))
 
-    both = jnp.stack([keep, own_theirs])
-    up, down = shift(both, 1), shift(both, -1)
-    up_mine = up[0]
-    down_theirs = down[1]
-    far = [shift(up_mine, 1), shift(down_theirs, -1)]
-    near = [both, up, down]
-    own = decode(at, weights, near, far)
-
-    up_mine, down_mine = shift(other_mine, 1), shift(other_mine, -1)
-    up_theirs, down_theirs = shift(other_theirs, 1), shift(other_theirs, -1)
-    far = [shift(up_mine, 1), shift(down_theirs, -1)]
-    near = [other_mine, other_theirs, up_mine, up_theirs, down_mine, down_theirs]
-    other = decode(at, weights, near, far)
+    blocks = {}
+    for name, mine, theirs in (("own", keep, own_theirs), ("other", other_mine, other_theirs)):
+        up_mine, down_mine = shift(mine, 1), shift(mine, -1)
+        up_theirs, down_theirs = shift(theirs, 1), shift(theirs, -1)
+        onward = up_mine, down_theirs
+        if name == "own":
+            ahead = jnp.maximum(up_mine, 0)
+            onward = ahead, jnp.maximum(down_theirs, 0)
+        far = [shift(onward[0], 1), shift(onward[1], -1)]
+        near = [mine, theirs, up_mine, up_theirs, down_mine, down_theirs]
+        blocks[name] = decode(at, weights, near, far)
 
     chips = []
-    for (kept, *away) in (own, other):
+    for (kept, *away) in blocks.values():
         came = []
         for by, piece in enumerate(away):
             came.append(lax.ppermute(piece, "feat", x_pairs(by + 1)))

time: 117 us -> 109 us (0.932)
  the two profiles are of different devices: /device:TPU:1 before, /device:TPU:24 now
where the time goes in v10:
time: 109 us; the launch traced here: 108 us
  starting transfers between devices  46.9 us (43%)
  Pallas kernels  30.4 us (28%)
  waiting for transfers between devices  26.8 us (25%)
  matrix products  3.05 us (3%)
    pallas_call x7, Pallas kernels, call(): pl.pallas_call(kernel, out_shape=out_shape, in_specs=[IN_SMEM] + [IN_VMEM...  25.2 us
    ppermute x12, starting transfers between devices, shift(): return lax.ppermute(array, 'layer', ring(by))  16.2 us
    all_to_all x1, starting transfers between devices, per_device(): lax.all_to_all(chips[0], 'feat', 0, 0, tiled=True, axis_index_groups=ZC_G...  11.5 us
    all_to_all x1, waiting for transfers between devices, per_device(): lax.all_to_all(chips[0], 'feat', 0, 0, tiled=True, axis_index_groups=ZC_G...  10.3 us
    ppermute x6, starting transfers between devices, per_device(): came.append(lax.ppermute(piece, 'feat', x_pairs(by + 1)))  9.19 us
    ppermute x1, starting transfers between devices, per_device(): other_mine = lax.ppermute(keep, ('dp', 'feat'), across(0))  6.92 us
    ppermute x12, waiting for transfers between devices, shift(): return lax.ppermute(array, 'layer', ring(by))  5.32 us
    pallas_call x1, Pallas kernels, cut(): pl.pallas_call(cut_kernel, out_shape=jax.ShapeDtypeStruct(decoders.shape[...  5.19 us
  transfers between devices with their start and end apart: 23, of which 8 were waited for; matrix products, arithmetic and copies ran while one was open for 3% of the time, Pallas kernels for 21%

profile of v10, /device:TPU:24, one launch (start us, length us, event | category | flops | bytes accessed | tf_op | source)
XLA Modules:
  0.0 107.6 jit_solution(17690328961280005139)
XLA Ops:
  0.1 5.2 %cut.1.refs_0_ = bf16[4,512,1152]{2,1,0:T(8,128)(2,1)} custom-call(s32[4]{0:T(128)S(1)} %pad_add_fusion.at_ref, bf16[1,4,512,1152]{3,2,1,0:T(8,128)(2,1)} %decoders_ref.1), custom_call_target="tpu_custom_call" | custom-call | bytes 4718592 | tf_op jit(solution)/shard_map/cut/pallas_call | solution.py:87
  5.5 3.0 %fusion.18 = bf16[512,512]{1,0:T(8,128)(2,1)S(1)} fusion(bf16[1,2304,512]{2,1,0:T(8,128)(2,1)S(1)} %copy-done, bf16[1,512,2304]{2,1,0:T(8,128)(2,1)} %param.6, f32[512]{0:T(512)S(1)} %convert_bitcast_fusion, f32[512]{0:T(512)S(1)} %bitcast.40), kind=kOutput, calls=%fused_computation.6 | convolution fusion | flops 1209008128 | bytes 5246976 | tf_op jit(solution)/shard_map/dot_general | solution.py:192
  9.1 2.3 %collective-permute-start.2 = (bf16[256,512]{1,0:T(8,128)(2,1)S(1)}, bf16[256,512]{1,0:T(8,128)(2,1)S(1)}, u32[]{:S(2)}, u32[]{:S(2)}) collective-permute-start(bf16[256,512]{1,0:T(8,128)(2,1)S(1)} %get-tuple-element.22.refs_2_), channel_id=1, source_target_pairs={{0,32},{32,64},{64,96},{96,0},{1,33},{33,65},{65,97},{97,1},{2,34}... | collective-permute-start | bytes 786440 | tf_op jit(solution)/shard_map/ppermute | solution.py:204
  11.4 6.9 %collective-permute-start.11 = (bf16[256,512]{1,0:T(8,128)(2,1)S(1)}, bf16[256,512]{1,0:T(8,128)(2,1)S(1)}, u32[]{:S(2)}, u32[]{:S(2)}) collective-permute-start(bf16[256,512]{1,0:T(8,128)(2,1)S(1)} %get-tuple-element.22.refs_2_), channel_id=1, source_target_pairs={{0,128},{1,129},{2,130},{3,131},{4,132},{5,133},{6,134},{7,135},{8... | collective-permute-start | bytes 786440 | tf_op jit(solution)/shard_map/ppermute | solution.py:197
  18.4 2.4 %collective-permute-start.12 = (bf16[256,512]{1,0:T(8,128)(2,1)S(1)}, bf16[256,512]{1,0:T(8,128)(2,1)S(1)}, u32[]{:S(2)}, u32[]{:S(2)}) collective-permute-start(bf16[256,512]{1,0:T(8,128)(2,1)S(1)} %get-tuple-element.21), channel_id=1, source_target_pairs={{0,129},{1,128},{2,131},{3,130},{4,133},{5,132},{6,135},{7,134},{8... | collective-permute-start | bytes 786440 | tf_op jit(solution)/shard_map/ppermute | solution.py:198
  21.6 2.4 %collective-permute-start.3 = (bf16[256,512]{1,0:T(8,128)(2,1)S(1)}, bf16[256,512]{1,0:T(8,128)(2,1)S(1)}, u32[]{:S(2)}, u32[]{:S(2)}) collective-permute-start(bf16[256,512]{1,0:T(8,128)(2,1)S(1)} %collective-permute-done.1.refs_3_), channel_id=1, source_target_pairs={{0,32},{32,64},{64,96},{96,0},{1,33},{33,65},{65,97},{97,1},{2,34}... | collective-permute-start | bytes 786440 | tf_op jit(solution)/shard_map/ppermute | solution.py:204
  24.1 2.1 %collective-permute-done.11.refs_2_ = bf16[256,512]{1,0:T(8,128)(2,1)S(1)} collective-permute-done((bf16[256,512]{1,0:T(8,128)(2,1)S(1)}, bf16[256,512]{1,0:T(8,128)(2,1)S(1)}, u32[]{:S(2)}, u32[]{:S(2)}) %collective-permute-start.11) | collective-permute-done | bytes 262176 | tf_op jit(solution)/shard_map/ppermute | solution.py:197
  26.1 1.8 %collective-permute-start.6 = (bf16[256,512]{1,0:T(8,128)(2,1)S(1)}, bf16[256,512]{1,0:T(8,128)(2,1)S(1)}, u32[]{:S(2)}, u32[]{:S(2)}) collective-permute-start(bf16[256,512]{1,0:T(8,128)(2,1)S(1)} %broadcast_maximum_fusion.1), channel_id=1, source_target_pairs={{0,32},{32,64},{64,96},{96,0},{1,33},{33,65},{65,97},{97,1},{2,34}... | collective-permute-start | bytes 786440 | tf_op jit(solution)/shard_map/ppermute | solution.py:204
  27.9 4.2 %collective-permute-done.12.refs_3_ = bf16[256,512]{1,0:T(8,128)(2,1)S(1)} collective-permute-done((bf16[256,512]{1,0:T(8,128)(2,1)S(1)}, bf16[256,512]{1,0:T(8,128)(2,1)S(1)}, u32[]{:S(2)}, u32[]{:S(2)}) %collective-permute-start.12) | collective-permute-done | bytes 262176 | tf_op jit(solution)/shard_map/ppermute | solution.py:198
  32.2 1.8 %collective-permute-start.13 = (bf16[256,512]{1,0:T(8,128)(2,1)S(1)}, bf16[256,512]{1,0:T(8,128)(2,1)S(1)}, u32[]{:S(2)}, u32[]{:S(2)}) collective-permute-start(bf16[256,512]{1,0:T(8,128)(2,1)S(1)} %collective-permute-done.11.refs_2_), channel_id=1, source_target_pairs={{0,32},{32,64},{64,96},{96,0},{1,33},{33,65},{65,97},{97,1},{2,34}... | collective-permute-start | bytes 786440 | tf_op jit(solution)/shard_map/ppermute | solution.py:204
  36.4 3.7 %collective-permute-start.14 = (bf16[256,512]{1,0:T(8,128)(2,1)S(1)}, bf16[256,512]{1,0:T(8,128)(2,1)S(1)}, u32[]{:S(2)}, u32[]{:S(2)}) collective-permute-start(bf16[256,512]{1,0:T(8,128)(2,1)S(1)} %collective-permute-done.12.refs_3_), channel_id=1, source_target_pairs={{0,32},{32,64},{64,96},{96,0},{1,33},{33,65},{65,97},{97,1},{2,34}... | collective-permute-start | bytes 786440 | tf_op jit(solution)/shard_map/ppermute | solution.py:204
  40.0 1.9 %collective-permute-done.13.refs_4_ = bf16[256,512]{1,0:T(8,128)(2,1)S(1)} collective-permute-done((bf16[256,512]{1,0:T(8,128)(2,1)S(1)}, bf16[256,512]{1,0:T(8,128)(2,1)S(1)}, u32[]{:S(2)}, u32[]{:S(2)}) %collective-permute-start.13) | collective-permute-done | bytes 262176 | tf_op jit(solution)/shard_map/ppermute | solution.py:204
  42.2 2.1 %collective-permute-done.16.refs_7_ = bf16[256,512]{1,0:T(8,128)(2,1)S(1)} collective-permute-done((bf16[256,512]{1,0:T(8,128)(2,1)S(1)}, bf16[256,512]{1,0:T(8,128)(2,1)S(1)}, u32[]{:S(2)}, u32[]{:S(2)}) %collective-permute-start.16) | collective-permute-done | bytes 262176 | tf_op jit(solution)/shard_map/ppermute | solution.py:204
  46.4 6.0 %shard_map.64.refs_2_ = f32[256,1152]{1,0:T(8,128)S(1)} custom-call(s32[4]{0:T(128)S(1)} %pad_add_fusion.at_ref, bf16[4,512,1152]{2,1,0:T(8,128)(2,1)} %cut.1.refs_0_, bf16[4,512,1152]{2,1,0:T(8,128)(2,1)} %collective-permute-done.refs_1_, bf16[256,512]{1,0:T(8,128)(2,1)S(1)} %get-tuple-element.22.refs_2_, ...), custom_call_target="tpu_custom_call" | custom-call | flops 1811939328 | bytes 11010064 | tf_op jit(solution)/shard_map/pallas_call | solution.py:45
  52.4 4.9 %shard_map.65 = (f32[4,72,256]{2,1,0:T(8,128)S(1)}, bf16[4,72,256]{2,1,0:T(8,128)(2,1)S(1)}, bf16[4,72,256]{2,1,0:T(8,128)(2,1)S(1)}, bf16[4,72,256]{2,1,0:T(8,128)(2,1)S(1)}) custom-call(s32[4]{0:T(128)S(1)} %pad_add_fusion.at_ref, bf16[4,512,1152]{2,1,0:T(8,128)(2,1)} %cut.1.refs_0_, bf16[4,512,1152]{2,1,0:T(8,128)(2,1)} %collective-permute-done.refs_1_, ...), custom_call_target="tpu_custom_call" | custom-call | flops 603979776 | bytes 11141136 | tf_op jit(solution)/shard_map/pallas_call | solution.py:45
  57.3 1.6 %collective-permute-start.8 = (bf16[4,72,256]{2,1,0:T(8,128)(2,1)S(1)}, bf16[4,72,256]{2,1,0:T(8,128)(2,1)S(1)}, u32[]{:S(2)}, u32[]{:S(2)}) collective-permute-start(bf16[4,72,256]{2,1,0:T(8,128)(2,1)S(1)} %get-tuple-element.14), channel_id=1, source_target_pairs={{0,2},{1,3},{2,4},{3,5},{4,6},{5,7},{6,0},{7,1},{8,10},{9,11},{10,... | collective-permute-start | bytes 442376 | tf_op jit(solution)/shard_map/ppermute | solution.py:222
  58.9 2.7 %collective-permute-start.9 = (bf16[4,72,256]{2,1,0:T(8,128)(2,1)S(1)}, bf16[4,72,256]{2,1,0:T(8,128)(2,1)S(1)}, u32[]{:S(2)}, u32[]{:S(2)}) collective-permute-start(bf16[4,72,256]{2,1,0:T(8,128)(2,1)S(1)} %get-tuple-element.15), channel_id=1, source_target_pairs={{0,4},{1,5},{2,6},{3,7},{4,0},{5,1},{6,2},{7,3},{8,12},{9,13},{10,... | collective-permute-start | bytes 442376 | tf_op jit(solution)/shard_map/ppermute | solution.py:222
  63.0 6.0 %shard_map.67.refs_2_ = f32[256,1152]{1,0:T(8,128)S(1)} custom-call(s32[4]{0:T(128)S(1)} %pad_add_fusion.at_ref, bf16[4,512,1152]{2,1,0:T(8,128)(2,1)} %cut.1.refs_0_, bf16[4,512,1152]{2,1,0:T(8,128)(2,1)} %collective-permute-done.refs_1_, bf16[256,512]{1,0:T(8,128)(2,1)S(1)} %collective-permute-done.11.refs_2_, ...), custom_call_target="tpu_custom_call" | custom-call | flops 1811939328 | bytes 11010064 | tf_op jit(solution)/shard_map/pallas_call | solution.py:45
  69.1 4.9 %shard_map.68 = (f32[4,72,256]{2,1,0:T(8,128)S(1)}, bf16[4,72,256]{2,1,0:T(8,128)(2,1)S(1)}, bf16[4,72,256]{2,1,0:T(8,128)(2,1)S(1)}, bf16[4,72,256]{2,1,0:T(8,128)(2,1)S(1)}) custom-call(s32[4]{0:T(128)S(1)} %pad_add_fusion.at_ref, bf16[4,512,1152]{2,1,0:T(8,128)(2,1)} %cut.1.refs_0_, bf16[4,512,1152]{2,1,0:T(8,128)(2,1)} %collective-permute-done.refs_1_, ...), custom_call_target="tpu_custom_call" | custom-call | flops 603979776 | bytes 11141136 | tf_op jit(solution)/shard_map/pallas_call | solution.py:45
  75.5 1.9 %collective-permute-start.21 = (bf16[4,72,256]{2,1,0:T(8,128)(2,1)S(1)}, bf16[4,72,256]{2,1,0:T(8,128)(2,1)S(1)}, u32[]{:S(2)}, u32[]{:S(2)}) collective-permute-start(bf16[4,72,256]{2,1,0:T(8,128)(2,1)S(1)} %get-tuple-element.20), channel_id=1, source_target_pairs={{0,6},{1,7},{2,0},{3,1},{4,2},{5,3},{6,4},{7,5},{8,14},{9,15},{10,... | collective-permute-start | bytes 442376 | tf_op jit(solution)/shard_map/ppermute | solution.py:222
  78.1 3.9 %collective-permute-done.19.refs_2_ = bf16[4,72,256]{2,1,0:T(8,128)(2,1)S(1)} collective-permute-done((bf16[4,72,256]{2,1,0:T(8,128)(2,1)S(1)}, bf16[4,72,256]{2,1,0:T(8,128)(2,1)S(1)}, u32[]{:S(2)}, u32[]{:S(2)}) %collective-permute-start.19) | collective-permute-done | bytes 147488 | tf_op jit(solution)/shard_map/ppermute | solution.py:222
  84.2 11.5 %all-to-all-start = ((bf16[8,72,256]{2,1,0:T(8,128)(2,1)}), bf16[8,72,256]{2,1,0:T(8,128)(2,1)S(1)}, u32[]{:S(2)}, u32[]{:S(2)}) async-start(bf16[8,72,256]{2,1,0:T(8,128)(2,1)} %shard_map.69), calls=%async_computation | async-start | bytes 589824 | tf_op jit(solution)/shard_map/all_to_all | solution.py:224
  95.8 10.3 %all-to-all-done.chips_ref = bf16[8,72,256]{2,1,0:T(8,128)(2,1)S(1)} async-done(((bf16[8,72,256]{2,1,0:T(8,128)(2,1)}), bf16[8,72,256]{2,1,0:T(8,128)(2,1)S(1)}, u32[]{:S(2)}, u32[]{:S(2)}) %all-to-all-start) | async-done | bytes 294944 | tf_op jit(solution)/shard_map/all_to_all | solution.py:224
  106.1 1.5 %shard_map.70 = bf16[36,1024]{1,0:T(8,128)(2,1)} custom-call(s32[4]{0:T(128)S(1)} %pad_add_fusion.at_ref, bf16[8,72,256]{2,1,0:T(8,128)(2,1)S(1)} %all-to-all-done.chips_ref, f32[36,1]{1,0:T(8,128)S(1)} %copy.7.bias_ref), custom_call_target="tpu_custom_call" | custom-call | bytes 295072 | tf_op jit(solution)/shard_map/pallas_call | solution.py:45
  (45 shorter events, 12.3 us)
Async XLA Ops:
  5.3 40.4 %collective-permute-start = (bf16[4,512,1152]{2,1,0:T(8,128)(2,1)}, bf16[4,512,1152]{2,1,0:T(8,128)(2,1)}, u32[]{:S(2)}, u32[]{:S(2)}) collective-permute-start(bf16[4,512,1152]{2,1,0:T(8,128)(2,1)} %cut.1.refs_0_), channel_id=1, source_target_pairs={{0,1},{1,0},{2,3},{3,2},{4,5},{5,4},{6,7},{7,6},{8,9},{9,8},{10,11... | collective-permute-start | bytes 14155784 | tf_op jit(solution)/shard_map/ppermute | solution.py:201
  8.6 9.8 %collective-permute-start.1 = (bf16[256,512]{1,0:T(8,128)(2,1)S(1)}, bf16[256,512]{1,0:T(8,128)(2,1)S(1)}, u32[]{:S(2)}, u32[]{:S(2)}) collective-permute-start(bf16[256,512]{1,0:T(8,128)(2,1)S(1)} %get-tuple-element.21), channel_id=1, source_target_pairs={{0,1},{1,0},{2,3},{3,2},{4,5},{5,4},{6,7},{7,6},{8,9},{9,8},{10,11... | collective-permute-start | bytes 786440 | tf_op jit(solution)/shard_map/ppermute | solution.py:199
  9.1 11.6 %collective-permute-start.2 = (bf16[256,512]{1,0:T(8,128)(2,1)S(1)}, bf16[256,512]{1,0:T(8,128)(2,1)S(1)}, u32[]{:S(2)}, u32[]{:S(2)}) collective-permute-start(bf16[256,512]{1,0:T(8,128)(2,1)S(1)} %get-tuple-element.22.refs_2_), channel_id=1, source_target_pairs={{0,32},{32,64},{64,96},{96,0},{1,33},{33,65},{65,97},{97,1},{2,34}... | collective-permute-start | bytes 786440 | tf_op jit(solution)/shard_map/ppermute | solution.py:204
  11.4 10.2 %collective-permute-start.4 = (bf16[256,512]{1,0:T(8,128)(2,1)S(1)}, bf16[256,512]{1,0:T(8,128)(2,1)S(1)}, u32[]{:S(2)}, u32[]{:S(2)}) collective-permute-start(bf16[256,512]{1,0:T(8,128)(2,1)S(1)} %get-tuple-element.22.refs_2_), channel_id=1, source_target_pairs={{0,96},{32,0},{64,32},{96,64},{1,97},{33,1},{65,33},{97,65},{2,98}... | collective-permute-start | bytes 786440 | tf_op jit(solution)/shard_map/ppermute | solution.py:204
  11.4 14.7 %collective-permute-start.11 = (bf16[256,512]{1,0:T(8,128)(2,1)S(1)}, bf16[256,512]{1,0:T(8,128)(2,1)S(1)}, u32[]{:S(2)}, u32[]{:S(2)}) collective-permute-start(bf16[256,512]{1,0:T(8,128)(2,1)S(1)} %get-tuple-element.22.refs_2_), channel_id=1, source_target_pairs={{0,128},{1,129},{2,130},{3,131},{4,132},{5,133},{6,134},{7,135},{8... | collective-permute-start | bytes 786440 | tf_op jit(solution)/shard_map/ppermute | solution.py:197
  18.4 13.8 %collective-permute-start.12 = (bf16[256,512]{1,0:T(8,128)(2,1)S(1)}, bf16[256,512]{1,0:T(8,128)(2,1)S(1)}, u32[]{:S(2)}, u32[]{:S(2)}) collective-permute-start(bf16[256,512]{1,0:T(8,128)(2,1)S(1)} %get-tuple-element.21), channel_id=1, source_target_pairs={{0,129},{1,128},{2,131},{3,130},{4,133},{5,132},{6,135},{7,134},{8... | collective-permute-start | bytes 786440 | tf_op jit(solution)/shard_map/ppermute | solution.py:198
  20.8 13.2 %collective-permute-start.5 = (bf16[256,512]{1,0:T(8,128)(2,1)S(1)}, bf16[256,512]{1,0:T(8,128)(2,1)S(1)}, u32[]{:S(2)}, u32[]{:S(2)}) collective-permute-start(bf16[256,512]{1,0:T(8,128)(2,1)S(1)} %collective-permute-done.1.refs_3_), channel_id=1, source_target_pairs={{0,96},{32,0},{64,32},{96,64},{1,97},{33,1},{65,33},{97,65},{2,98}... | collective-permute-start | bytes 786440 | tf_op jit(solution)/shard_map/ppermute | solution.py:204
  21.6 12.6 %collective-permute-start.3 = (bf16[256,512]{1,0:T(8,128)(2,1)S(1)}, bf16[256,512]{1,0:T(8,128)(2,1)S(1)}, u32[]{:S(2)}, u32[]{:S(2)}) collective-permute-start(bf16[256,512]{1,0:T(8,128)(2,1)S(1)} %collective-permute-done.1.refs_3_), channel_id=1, source_target_pairs={{0,32},{32,64},{64,96},{96,0},{1,33},{33,65},{65,97},{97,1},{2,34}... | collective-permute-start | bytes 786440 | tf_op jit(solution)/shard_map/ppermute | solution.py:204
  26.1 10.2 %collective-permute-start.6 = (bf16[256,512]{1,0:T(8,128)(2,1)S(1)}, bf16[256,512]{1,0:T(8,128)(2,1)S(1)}, u32[]{:S(2)}, u32[]{:S(2)}) collective-permute-start(bf16[256,512]{1,0:T(8,128)(2,1)S(1)} %broadcast_maximum_fusion.1), channel_id=1, source_target_pairs={{0,32},{32,64},{64,96},{96,0},{1,33},{33,65},{65,97},{97,1},{2,34}... | collective-permute-start | bytes 786440 | tf_op jit(solution)/shard_map/ppermute | solution.py:204
  32.2 9.8 %collective-permute-start.13 = (bf16[256,512]{1,0:T(8,128)(2,1)S(1)}, bf16[256,512]{1,0:T(8,128)(2,1)S(1)}, u32[]{:S(2)}, u32[]{:S(2)}) collective-permute-start(bf16[256,512]{1,0:T(8,128)(2,1)S(1)} %collective-permute-done.11.refs_2_), channel_id=1, source_target_pairs={{0,32},{32,64},{64,96},{96,0},{1,33},{33,65},{65,97},{97,1},{2,34}... | collective-permute-start | bytes 786440 | tf_op jit(solution)/shard_map/ppermute | solution.py:204
  34.0 10.4 %collective-permute-start.16 = (bf16[256,512]{1,0:T(8,128)(2,1)S(1)}, bf16[256,512]{1,0:T(8,128)(2,1)S(1)}, u32[]{:S(2)}, u32[]{:S(2)}) collective-permute-start(bf16[256,512]{1,0:T(8,128)(2,1)S(1)} %collective-permute-done.12.refs_3_), channel_id=1, source_target_pairs={{0,96},{32,0},{64,32},{96,64},{1,97},{33,1},{65,33},{97,65},{2,98}... | collective-permute-start | bytes 786440 | tf_op jit(solution)/shard_map/ppermute | solution.py:204
  34.2 18.2 %collective-permute-start.7 = (bf16[256,512]{1,0:T(8,128)(2,1)S(1)}, bf16[256,512]{1,0:T(8,128)(2,1)S(1)}, u32[]{:S(2)}, u32[]{:S(2)}) collective-permute-start(bf16[256,512]{1,0:T(8,128)(2,1)S(1)} %broadcast_maximum_fusion), channel_id=1, source_target_pairs={{0,96},{32,0},{64,32},{96,64},{1,97},{33,1},{65,33},{97,65},{2,98}... | collective-permute-start | bytes 786440 | tf_op jit(solution)/shard_map/ppermute | solution.py:204
  36.4 22.5 %collective-permute-start.14 = (bf16[256,512]{1,0:T(8,128)(2,1)S(1)}, bf16[256,512]{1,0:T(8,128)(2,1)S(1)}, u32[]{:S(2)}, u32[]{:S(2)}) collective-permute-start(bf16[256,512]{1,0:T(8,128)(2,1)S(1)} %collective-permute-done.12.refs_3_), channel_id=1, source_target_pairs={{0,32},{32,64},{64,96},{96,0},{1,33},{33,65},{65,97},{97,1},{2,34}... | collective-permute-start | bytes 786440 | tf_op jit(solution)/shard_map/ppermute | solution.py:204
  42.0 19.6 %collective-permute-start.15 = (bf16[256,512]{1,0:T(8,128)(2,1)S(1)}, bf16[256,512]{1,0:T(8,128)(2,1)S(1)}, u32[]{:S(2)}, u32[]{:S(2)}) collective-permute-start(bf16[256,512]{1,0:T(8,128)(2,1)S(1)} %collective-permute-done.11.refs_2_), channel_id=1, source_target_pairs={{0,96},{32,0},{64,32},{96,64},{1,97},{33,1},{65,33},{97,65},{2,98}... | collective-permute-start | bytes 786440 | tf_op jit(solution)/shard_map/ppermute | solution.py:204
  44.3 24.7 %collective-permute-start.17 = (bf16[256,512]{1,0:T(8,128)(2,1)S(1)}, bf16[256,512]{1,0:T(8,128)(2,1)S(1)}, u32[]{:S(2)}, u32[]{:S(2)}) collective-permute-start(bf16[256,512]{1,0:T(8,128)(2,1)S(1)} %collective-permute-done.13.refs_4_), channel_id=1, source_target_pairs={{0,32},{32,64},{64,96},{96,0},{1,33},{33,65},{65,97},{97,1},{2,34}... | collective-permute-start | bytes 786440 | tf_op jit(solution)/shard_map/ppermute | solution.py:204
  45.7 23.4 %collective-permute-start.18 = (bf16[256,512]{1,0:T(8,128)(2,1)S(1)}, bf16[256,512]{1,0:T(8,128)(2,1)S(1)}, u32[]{:S(2)}, u32[]{:S(2)}) collective-permute-start(bf16[256,512]{1,0:T(8,128)(2,1)S(1)} %collective-permute-done.16.refs_7_), channel_id=1, source_target_pairs={{0,96},{32,0},{64,32},{96,64},{1,97},{33,1},{65,33},{97,65},{2,98}... | collective-permute-start | bytes 786440 | tf_op jit(solution)/shard_map/ppermute | solution.py:204
  57.3 18.2 %collective-permute-start.8 = (bf16[4,72,256]{2,1,0:T(8,128)(2,1)S(1)}, bf16[4,72,256]{2,1,0:T(8,128)(2,1)S(1)}, u32[]{:S(2)}, u32[]{:S(2)}) collective-permute-start(bf16[4,72,256]{2,1,0:T(8,128)(2,1)S(1)} %get-tuple-element.14), channel_id=1, source_target_pairs={{0,2},{1,3},{2,4},{3,5},{4,6},{5,7},{6,0},{7,1},{8,10},{9,11},{10,... | collective-permute-start | bytes 442376 | tf_op jit(solution)/shard_map/ppermute | solution.py:222
  58.9 18.6 %collective-permute-start.9 = (bf16[4,72,256]{2,1,0:T(8,128)(2,1)S(1)}, bf16[4,72,256]{2,1,0:T(8,128)(2,1)S(1)}, u32[]{:S(2)}, u32[]{:S(2)}) collective-permute-start(bf16[4,72,256]{2,1,0:T(8,128)(2,1)S(1)} %get-tuple-element.15), channel_id=1, source_target_pairs={{0,4},{1,5},{2,6},{3,7},{4,0},{5,1},{6,2},{7,3},{8,12},{9,13},{10,... | collective-permute-start | bytes 442376 | tf_op jit(solution)/shard_map/ppermute | solution.py:222
  61.6 15.8 %collective-permute-start.10 = (bf16[4,72,256]{2,1,0:T(8,128)(2,1)S(1)}, bf16[4,72,256]{2,1,0:T(8,128)(2,1)S(1)}, u32[]{:S(2)}, u32[]{:S(2)}) collective-permute-start(bf16[4,72,256]{2,1,0:T(8,128)(2,1)S(1)} %get-tuple-element.16), channel_id=1, source_target_pairs={{0,6},{1,7},{2,0},{3,1},{4,2},{5,3},{6,4},{7,5},{8,14},{9,15},{10,... | collective-permute-start | bytes 442376 | tf_op jit(solution)/shard_map/ppermute | solution.py:222
  74.0 21.7 %copy-start.2 = (f32[1,36]{1,0:T(1,128)S(1)}, f32[1,36]{1,0:T(1,128)}, u32[]{:S(2)}) copy-start(f32[1,36]{1,0:T(1,128)} %param.10) | copy-start | bytes 436
  74.0 8.0 %collective-permute-start.19 = (bf16[4,72,256]{2,1,0:T(8,128)(2,1)S(1)}, bf16[4,72,256]{2,1,0:T(8,128)(2,1)S(1)}, u32[]{:S(2)}, u32[]{:S(2)}) collective-permute-start(bf16[4,72,256]{2,1,0:T(8,128)(2,1)S(1)} %get-tuple-element.18), channel_id=1, source_target_pairs={{0,2},{1,3},{2,4},{3,5},{4,6},{5,7},{6,0},{7,1},{8,10},{9,11},{10,... | collective-permute-start | bytes 442376 | tf_op jit(solution)/shard_map/ppermute | solution.py:222
  74.7 7.3 %collective-permute-start.20 = (bf16[4,72,256]{2,1,0:T(8,128)(2,1)S(1)}, bf16[4,72,256]{2,1,0:T(8,128)(2,1)S(1)}, u32[]{:S(2)}, u32[]{:S(2)}) collective-permute-start(bf16[4,72,256]{2,1,0:T(8,128)(2,1)S(1)} %get-tuple-element.19), channel_id=1, source_target_pairs={{0,4},{1,5},{2,6},{3,7},{4,0},{5,1},{6,2},{7,3},{8,12},{9,13},{10,... | collective-permute-start | bytes 442376 | tf_op jit(solution)/shard_map/ppermute | solution.py:222
  75.5 7.4 %collective-permute-start.21 = (bf16[4,72,256]{2,1,0:T(8,128)(2,1)S(1)}, bf16[4,72,256]{2,1,0:T(8,128)(2,1)S(1)}, u32[]{:S(2)}, u32[]{:S(2)}) collective-permute-start(bf16[4,72,256]{2,1,0:T(8,128)(2,1)S(1)} %get-tuple-element.20), channel_id=1, source_target_pairs={{0,6},{1,7},{2,0},{3,1},{4,2},{5,3},{6,4},{7,5},{8,14},{9,15},{10,... | collective-permute-start | bytes 442376 | tf_op jit(solution)/shard_map/ppermute | solution.py:222
  84.2 21.9 %all-to-all-start = ((bf16[8,72,256]{2,1,0:T(8,128)(2,1)}), bf16[8,72,256]{2,1,0:T(8,128)(2,1)S(1)}, u32[]{:S(2)}, u32[]{:S(2)}) async-start(bf16[8,72,256]{2,1,0:T(8,128)(2,1)} %shard_map.69), calls=%async_computation | async-start | bytes 589824 | tf_op jit(solution)/shard_map/all_to_all | solution.py:224
  (3 other events, 16.2 us)

commit v11 on v10

--- a/solution.py
+++ b/solution.py
@@ -188,11 +188,17 @@
     target, feat, dp = lax.axis_index("layer"), lax.axis_index("feat"), lax.axis_index("dp")
     core = feat % 2
     at = jnp.stack([core, target, feat // 2 % NX, dp]).astype(jnp.int32)
-    valid = (jnp.arange(SEQ)[None, :] < lengths[:, None]).reshape(-1).astype(F32)
-    pre = jnp.dot(resid[0], enc_weight[0], preferred_element_type=F32) + enc_bias
-    acts = (jax.nn.relu(pre) * valid[:, None]).astype(BF).reshape(2, 256, 512)
-    keep = lax.dynamic_index_in_dim(acts, core, 0, keepdims=False)
-    send = lax.dynamic_index_in_dim(acts, 1 - core, 0, keepdims=False)
+
+    def encode(half):
+        rows = lax.dynamic_index_in_dim(resid[0].reshape(2, 256, 2304), half, 0, keepdims=False)
+        first, second = (lax.dynamic_index_in_dim(lengths, 2 * half + s, keepdims=False) for s in range(2))
+        pre = jnp.dot(rows, enc_weight[0], preferred_element_type=F32) + enc_bias
+        row = lax.broadcasted_iota(jnp.int32, pre.shape, 0)
+        limit = jnp.where(row < SEQ, first, SEQ + second)
+        return jnp.where(row < limit, jax.nn.relu(pre), 0.0).astype(BF)
+
+    keep = encode(core)
+    send = encode(1 - core)
     across = lambda flip: [(d * 32 + f, (1 - d) * 32 + (f ^ flip)) for d in range(2) for f in range(32)]
     other_mine = lax.ppermute(keep, ("dp", "feat"), across(0))
     other_theirs = lax.ppermute(send, ("dp", "feat"), across(1))
@@ -200,6 +206,7 @@
     w_mine = cut(at, dec_weight)
     w_theirs = lax.ppermute(w_mine, "feat", PARTNER)
     weights = (w_mine, w_theirs)
+
     def shift(array, by):
         return lax.ppermute(array, "layer", ring(by))
 

time: 109 us -> 114 us (1.046)
  starting transfers between devices: 46.9 us -> 42.5 us
  waiting for transfers between devices: 26.8 us -> 31.2 us
  matrix products: 3.05 us -> 4.89 us
  between operations: 0.16 us -> 1.48 us
    ppermute x1, starting transfers between devices: 2.42 us -> 0.01 us  [per_device(): other_theirs = lax.ppermute(send, ('dp', 'feat'), across(1))]
    ppermute x1, waiting for transfers between devices: 2.08 us -> 4.42 us  [per_device(): other_mine = lax.ppermute(keep, ('dp', 'feat'), across(0))]
    ppermute x12, waiting for transfers between devices: 5.32 us -> 7.37 us  [shift(): return lax.ppermute(array, 'layer', ring(by))]
    ppermute x12, starting transfers between devices: 16.2 us -> 14.3 us  [shift(): return lax.ppermute(array, 'layer', ring(by))]
    dot_general x1 -> x2, matrix products: 3.05 us -> 4.89 us  [encode(): pre = jnp.dot(rows, enc_weight[0], preferred_element_type=F32) + enc_bias]
    lt x0 -> x2, other arithmetic: none -> 1.2 us  [encode(): return jnp.where(row < limit, jax.nn.relu(pre), 0.0).astype(BF)]
  transfers between devices with their start and end apart: 23 -> 23, of which waited for: 8 -> 8; matrix products, arithmetic and copies ran while one was open for 3% -> 6% of each run, Pallas kernels for 21% -> 20%
where the time goes in v11:
time: 114 us; the launch traced here: 112 us
  starting transfers between devices  42.5 us (37%)
  waiting for transfers between devices  31.2 us (27%)
  Pallas kernels  30.3 us (27%)
  matrix products  4.89 us (4%)
  between operations  1.48 us (1%)
  other arithmetic  1.32 us (1%)
    pallas_call x7, Pallas kernels, call(): pl.pallas_call(kernel, out_shape=out_shape, in_specs=[IN_SMEM] + [IN_VMEM...  25.1 us
    ppermute x12, starting transfers between devices, shift(): return lax.ppermute(array, 'layer', ring(by))  14.3 us
    all_to_all x1, starting transfers between devices, per_device(): lax.all_to_all(chips[0], 'feat', 0, 0, tiled=True, axis_index_groups=ZC_G...  11.5 us
    all_to_all x1, waiting for transfers between devices, per_device(): lax.all_to_all(chips[0], 'feat', 0, 0, tiled=True, axis_index_groups=ZC_G...  10.3 us
    ppermute x6, starting transfers between devices, per_device(): came.append(lax.ppermute(piece, 'feat', x_pairs(by + 1)))  9.19 us
    ppermute x12, waiting for transfers between devices, shift(): return lax.ppermute(array, 'layer', ring(by))  7.37 us
    ppermute x1, starting transfers between devices, per_device(): other_mine = lax.ppermute(keep, ('dp', 'feat'), across(0))  6.92 us
    pallas_call x1, Pallas kernels, cut(): pl.pallas_call(cut_kernel, out_shape=jax.ShapeDtypeStruct(decoders.shape[...  5.19 us
  transfers between devices with their start and end apart: 23, of which 8 were waited for; matrix products, arithmetic and copies ran while one was open for 6% of the time, Pallas kernels for 20%

profile of v11, /device:TPU:24, one launch (start us, length us, event | category | flops | bytes accessed | tf_op | source)
XLA Modules:
  0.0 112.5 jit_solution(2427598841722997978)
XLA Ops:
  0.1 5.2 %cut.1.refs_0_ = bf16[4,512,1152]{2,1,0:T(8,128)(2,1)} custom-call(s32[4]{0:T(128)S(1)} %pad_add_fusion.at_ref, bf16[1,4,512,1152]{3,2,1,0:T(8,128)(2,1)} %decoders_ref.1), custom_call_target="tpu_custom_call" | custom-call | bytes 4718592 | tf_op jit(solution)/shard_map/cut/pallas_call | solution.py:87
  7.5 2.4 %fusion.25 = bf16[256,512]{1,0:T(8,128)(2,1)S(1)} fusion(bf16[1,2304,512]{2,1,0:T(8,128)(2,1)} %param.7, bf16[2,256,2304]{2,1,0:T(8,128)(2,1)S(1)} %bitcast.42, s32[]{:T(128)S(6)} %select_n.62, f32[512]{0:T(512)S(1)} %bitcast.44, pred[256]{0:T(512)(128)(4,1)S(1)} %select_compare_fusion), kind=kOutput, calls=%fused_computation.11 | convolution fusion | flops 604504064 | bytes 3803652 | tf_op jit(solution)/shard_map/dot_general | solution.py:195
  11.6 2.4 %fusion.22.refs_2_ = bf16[256,512]{1,0:T(8,128)(2,1)S(1)} fusion(bf16[1,2304,512]{2,1,0:T(8,128)(2,1)} %param.7, bf16[2,256,2304]{2,1,0:T(8,128)(2,1)S(1)} %bitcast.41, s32[]{:T(128)S(6)} %select_n.57, f32[512]{0:T(512)S(1)} %bitcast.45, pred[256]{0:T(512)(128)(4,1)S(1)} %select_compare_fusion.1), kind=kOutput, calls=%fused_computation.10 | convolution fusion | flops 604504064 | bytes 3803652 | tf_op jit(solution)/shard_map/dot_general | solution.py:195
  14.1 2.4 %collective-permute-start.2 = (bf16[256,512]{1,0:T(8,128)(2,1)S(1)}, bf16[256,512]{1,0:T(8,128)(2,1)S(1)}, u32[]{:S(2)}, u32[]{:S(2)}) collective-permute-start(bf16[256,512]{1,0:T(8,128)(2,1)S(1)} %fusion.22.refs_2_), channel_id=1, source_target_pairs={{0,32},{32,64},{64,96},{96,0},{1,33},{33,65},{65,97},{97,1},{2,34}... | collective-permute-start | bytes 786440 | tf_op jit(solution)/shard_map/ppermute | solution.py:211
  16.4 6.9 %collective-permute-start.11 = (bf16[256,512]{1,0:T(8,128)(2,1)S(1)}, bf16[256,512]{1,0:T(8,128)(2,1)S(1)}, u32[]{:S(2)}, u32[]{:S(2)}) collective-permute-start(bf16[256,512]{1,0:T(8,128)(2,1)S(1)} %fusion.22.refs_2_), channel_id=1, source_target_pairs={{0,128},{1,129},{2,130},{3,131},{4,132},{5,133},{6,134},{7,135},{8... | collective-permute-start | bytes 786440 | tf_op jit(solution)/shard_map/ppermute | solution.py:203
  26.7 4.4 %collective-permute-done.11.refs_2_ = bf16[256,512]{1,0:T(8,128)(2,1)S(1)} collective-permute-done((bf16[256,512]{1,0:T(8,128)(2,1)S(1)}, bf16[256,512]{1,0:T(8,128)(2,1)S(1)}, u32[]{:S(2)}, u32[]{:S(2)}) %collective-permute-start.11) | collective-permute-done | bytes 262176 | tf_op jit(solution)/shard_map/ppermute | solution.py:203
  31.1 1.8 %collective-permute-start.6 = (bf16[256,512]{1,0:T(8,128)(2,1)S(1)}, bf16[256,512]{1,0:T(8,128)(2,1)S(1)}, u32[]{:S(2)}, u32[]{:S(2)}) collective-permute-start(bf16[256,512]{1,0:T(8,128)(2,1)S(1)} %broadcast_maximum_fusion.1), channel_id=1, source_target_pairs={{0,32},{32,64},{64,96},{96,0},{1,33},{33,65},{65,97},{97,1},{2,34}... | collective-permute-start | bytes 786440 | tf_op jit(solution)/shard_map/ppermute | solution.py:211
  32.9 4.2 %collective-permute-done.12.refs_3_ = bf16[256,512]{1,0:T(8,128)(2,1)S(1)} collective-permute-done((bf16[256,512]{1,0:T(8,128)(2,1)S(1)}, bf16[256,512]{1,0:T(8,128)(2,1)S(1)}, u32[]{:S(2)}, u32[]{:S(2)}) %collective-permute-start.12) | collective-permute-done | bytes 262176 | tf_op jit(solution)/shard_map/ppermute | solution.py:204
  37.1 1.8 %collective-permute-start.13 = (bf16[256,512]{1,0:T(8,128)(2,1)S(1)}, bf16[256,512]{1,0:T(8,128)(2,1)S(1)}, u32[]{:S(2)}, u32[]{:S(2)}) collective-permute-start(bf16[256,512]{1,0:T(8,128)(2,1)S(1)} %collective-permute-done.11.refs_2_), channel_id=1, source_target_pairs={{0,32},{32,64},{64,96},{96,0},{1,33},{33,65},{65,97},{97,1},{2,34}... | collective-permute-start | bytes 786440 | tf_op jit(solution)/shard_map/ppermute | solution.py:211
  40.1 2.4 %collective-permute-start.14 = (bf16[256,512]{1,0:T(8,128)(2,1)S(1)}, bf16[256,512]{1,0:T(8,128)(2,1)S(1)}, u32[]{:S(2)}, u32[]{:S(2)}) collective-permute-start(bf16[256,512]{1,0:T(8,128)(2,1)S(1)} %collective-permute-done.12.refs_3_), channel_id=1, source_target_pairs={{0,32},{32,64},{64,96},{96,0},{1,33},{33,65},{65,97},{97,1},{2,34}... | collective-permute-start | bytes 786440 | tf_op jit(solution)/shard_map/ppermute | solution.py:211
  42.5 3.8 %collective-permute-done.13.refs_4_ = bf16[256,512]{1,0:T(8,128)(2,1)S(1)} collective-permute-done((bf16[256,512]{1,0:T(8,128)(2,1)S(1)}, bf16[256,512]{1,0:T(8,128)(2,1)S(1)}, u32[]{:S(2)}, u32[]{:S(2)}) %collective-permute-start.13) | collective-permute-done | bytes 262176 | tf_op jit(solution)/shard_map/ppermute | solution.py:211
  47.2 2.2 %collective-permute-done.16.refs_7_ = bf16[256,512]{1,0:T(8,128)(2,1)S(1)} collective-permute-done((bf16[256,512]{1,0:T(8,128)(2,1)S(1)}, bf16[256,512]{1,0:T(8,128)(2,1)S(1)}, u32[]{:S(2)}, u32[]{:S(2)}) %collective-permute-start.16) | collective-permute-done | bytes 262176 | tf_op jit(solution)/shard_map/ppermute | solution.py:211
  49.6 1.8 %collective-permute-start.18 = (bf16[256,512]{1,0:T(8,128)(2,1)S(1)}, bf16[256,512]{1,0:T(8,128)(2,1)S(1)}, u32[]{:S(2)}, u32[]{:S(2)}) collective-permute-start(bf16[256,512]{1,0:T(8,128)(2,1)S(1)} %collective-permute-done.16.refs_7_), channel_id=1, source_target_pairs={{0,96},{32,0},{64,32},{96,64},{1,97},{33,1},{65,33},{97,65},{2,98}... | collective-permute-start | bytes 786440 | tf_op jit(solution)/shard_map/ppermute | solution.py:211
  51.4 6.0 %shard_map.64.refs_2_ = f32[256,1152]{1,0:T(8,128)S(1)} custom-call(s32[4]{0:T(128)S(1)} %pad_add_fusion.at_ref, bf16[4,512,1152]{2,1,0:T(8,128)(2,1)} %cut.1.refs_0_, bf16[4,512,1152]{2,1,0:T(8,128)(2,1)} %collective-permute-done.refs_1_, bf16[256,512]{1,0:T(8,128)(2,1)S(1)} %fusion.22.refs_2_, bf16[256,512]{1,0:T(8,128)(2,1)S(1)} %collective-permute-done.1.refs_3_, ...), custom_call_target="tpu_custom_call" | custom-call | flops 1811939328 | bytes 11010064 | tf_op jit(solution)/shard_map/pallas_call | solution.py:45
  57.4 4.9 %shard_map.65 = (f32[4,72,256]{2,1,0:T(8,128)S(1)}, bf16[4,72,256]{2,1,0:T(8,128)(2,1)S(1)}, bf16[4,72,256]{2,1,0:T(8,128)(2,1)S(1)}, bf16[4,72,256]{2,1,0:T(8,128)(2,1)S(1)}) custom-call(s32[4]{0:T(128)S(1)} %pad_add_fusion.at_ref, bf16[4,512,1152]{2,1,0:T(8,128)(2,1)} %cut.1.refs_0_, bf16[4,512,1152]{2,1,0:T(8,128)(2,1)} %collective-permute-done.refs_1_, ...), custom_call_target="tpu_custom_call" | custom-call | flops 603979776 | bytes 11141136 | tf_op jit(solution)/shard_map/pallas_call | solution.py:45
  62.3 1.6 %collective-permute-start.8 = (bf16[4,72,256]{2,1,0:T(8,128)(2,1)S(1)}, bf16[4,72,256]{2,1,0:T(8,128)(2,1)S(1)}, u32[]{:S(2)}, u32[]{:S(2)}) collective-permute-start(bf16[4,72,256]{2,1,0:T(8,128)(2,1)S(1)} %get-tuple-element.14), channel_id=1, source_target_pairs={{0,2},{1,3},{2,4},{3,5},{4,6},{5,7},{6,0},{7,1},{8,10},{9,11},{10,... | collective-permute-start | bytes 442376 | tf_op jit(solution)/shard_map/ppermute | solution.py:229
  63.8 2.7 %collective-permute-start.9 = (bf16[4,72,256]{2,1,0:T(8,128)(2,1)S(1)}, bf16[4,72,256]{2,1,0:T(8,128)(2,1)S(1)}, u32[]{:S(2)}, u32[]{:S(2)}) collective-permute-start(bf16[4,72,256]{2,1,0:T(8,128)(2,1)S(1)} %get-tuple-element.15), channel_id=1, source_target_pairs={{0,4},{1,5},{2,6},{3,7},{4,0},{5,1},{6,2},{7,3},{8,12},{9,13},{10,... | collective-permute-start | bytes 442376 | tf_op jit(solution)/shard_map/ppermute | solution.py:229
  68.0 6.0 %shard_map.67.refs_2_ = f32[256,1152]{1,0:T(8,128)S(1)} custom-call(s32[4]{0:T(128)S(1)} %pad_add_fusion.at_ref, bf16[4,512,1152]{2,1,0:T(8,128)(2,1)} %cut.1.refs_0_, bf16[4,512,1152]{2,1,0:T(8,128)(2,1)} %collective-permute-done.refs_1_, bf16[256,512]{1,0:T(8,128)(2,1)S(1)} %collective-permute-done.11.refs_2_, ...), custom_call_target="tpu_custom_call" | custom-call | flops 1811939328 | bytes 11010064 | tf_op jit(solution)/shard_map/pallas_call | solution.py:45
  74.0 4.9 %shard_map.68 = (f32[4,72,256]{2,1,0:T(8,128)S(1)}, bf16[4,72,256]{2,1,0:T(8,128)(2,1)S(1)}, bf16[4,72,256]{2,1,0:T(8,128)(2,1)S(1)}, bf16[4,72,256]{2,1,0:T(8,128)(2,1)S(1)}) custom-call(s32[4]{0:T(128)S(1)} %pad_add_fusion.at_ref, bf16[4,512,1152]{2,1,0:T(8,128)(2,1)} %cut.1.refs_0_, bf16[4,512,1152]{2,1,0:T(8,128)(2,1)} %collective-permute-done.refs_1_, ...), custom_call_target="tpu_custom_call" | custom-call | flops 603979776 | bytes 11141136 | tf_op jit(solution)/shard_map/pallas_call | solution.py:45
  80.5 1.9 %collective-permute-start.21 = (bf16[4,72,256]{2,1,0:T(8,128)(2,1)S(1)}, bf16[4,72,256]{2,1,0:T(8,128)(2,1)S(1)}, u32[]{:S(2)}, u32[]{:S(2)}) collective-permute-start(bf16[4,72,256]{2,1,0:T(8,128)(2,1)S(1)} %get-tuple-element.20), channel_id=1, source_target_pairs={{0,6},{1,7},{2,0},{3,1},{4,2},{5,3},{6,4},{7,5},{8,14},{9,15},{10,... | collective-permute-start | bytes 442376 | tf_op jit(solution)/shard_map/ppermute | solution.py:229
  83.0 3.9 %collective-permute-done.19.refs_2_ = bf16[4,72,256]{2,1,0:T(8,128)(2,1)S(1)} collective-permute-done((bf16[4,72,256]{2,1,0:T(8,128)(2,1)S(1)}, bf16[4,72,256]{2,1,0:T(8,128)(2,1)S(1)}, u32[]{:S(2)}, u32[]{:S(2)}) %collective-permute-start.19) | collective-permute-done | bytes 147488 | tf_op jit(solution)/shard_map/ppermute | solution.py:229
  89.1 11.5 %all-to-all-start = ((bf16[8,72,256]{2,1,0:T(8,128)(2,1)}), bf16[8,72,256]{2,1,0:T(8,128)(2,1)S(1)}, u32[]{:S(2)}, u32[]{:S(2)}) async-start(bf16[8,72,256]{2,1,0:T(8,128)(2,1)} %shard_map.69), calls=%async_computation | async-start | bytes 589824 | tf_op jit(solution)/shard_map/all_to_all | solution.py:231
  100.7 10.3 %all-to-all-done.chips_ref = bf16[8,72,256]{2,1,0:T(8,128)(2,1)S(1)} async-done(((bf16[8,72,256]{2,1,0:T(8,128)(2,1)}), bf16[8,72,256]{2,1,0:T(8,128)(2,1)S(1)}, u32[]{:S(2)}, u32[]{:S(2)}) %all-to-all-start) | async-done | bytes 294944 | tf_op jit(solution)/shard_map/all_to_all | solution.py:231
  111.0 1.5 %shard_map.70 = bf16[36,1024]{1,0:T(8,128)(2,1)} custom-call(s32[4]{0:T(128)S(1)} %pad_add_fusion.at_ref, bf16[8,72,256]{2,1,0:T(8,128)(2,1)S(1)} %all-to-all-done.chips_ref, f32[36,1]{1,0:T(8,128)S(1)} %copy.7.bias_ref), custom_call_target="tpu_custom_call" | custom-call | bytes 295072 | tf_op jit(solution)/shard_map/pallas_call | solution.py:45
  (47 shorter events, 14.1 us)
Async XLA Ops:
  5.3 44.3 %collective-permute-start = (bf16[4,512,1152]{2,1,0:T(8,128)(2,1)}, bf16[4,512,1152]{2,1,0:T(8,128)(2,1)}, u32[]{:S(2)}, u32[]{:S(2)}) collective-permute-start(bf16[4,512,1152]{2,1,0:T(8,128)(2,1)} %cut.1.refs_0_), channel_id=1, source_target_pairs={{0,1},{1,0},{2,3},{3,2},{4,5},{5,4},{6,7},{7,6},{8,9},{9,8},{10,11... | collective-permute-start | bytes 14155784 | tf_op jit(solution)/shard_map/ppermute | solution.py:207
  9.9 13.4 %collective-permute-start.1 = (bf16[256,512]{1,0:T(8,128)(2,1)S(1)}, bf16[256,512]{1,0:T(8,128)(2,1)S(1)}, u32[]{:S(2)}, u32[]{:S(2)}) collective-permute-start(bf16[256,512]{1,0:T(8,128)(2,1)S(1)} %fusion.25), channel_id=1, source_target_pairs={{0,1},{1,0},{2,3},{3,2},{4,5},{5,4},{6,7},{7,6},{8,9},{9,8},{10,11... | collective-permute-start | bytes 786440 | tf_op jit(solution)/shard_map/ppermute | solution.py:205
  14.1 9.3 %collective-permute-start.2 = (bf16[256,512]{1,0:T(8,128)(2,1)S(1)}, bf16[256,512]{1,0:T(8,128)(2,1)S(1)}, u32[]{:S(2)}, u32[]{:S(2)}) collective-permute-start(bf16[256,512]{1,0:T(8,128)(2,1)S(1)} %fusion.22.refs_2_), channel_id=1, source_target_pairs={{0,32},{32,64},{64,96},{96,0},{1,33},{33,65},{65,97},{97,1},{2,34}... | collective-permute-start | bytes 786440 | tf_op jit(solution)/shard_map/ppermute | solution.py:211
  16.4 9.2 %collective-permute-start.4 = (bf16[256,512]{1,0:T(8,128)(2,1)S(1)}, bf16[256,512]{1,0:T(8,128)(2,1)S(1)}, u32[]{:S(2)}, u32[]{:S(2)}) collective-permute-start(bf16[256,512]{1,0:T(8,128)(2,1)S(1)} %fusion.22.refs_2_), channel_id=1, source_target_pairs={{0,96},{32,0},{64,32},{96,64},{1,97},{33,1},{65,33},{97,65},{2,98}... | collective-permute-start | bytes 786440 | tf_op jit(solution)/shard_map/ppermute | solution.py:211
  16.4 14.7 %collective-permute-start.11 = (bf16[256,512]{1,0:T(8,128)(2,1)S(1)}, bf16[256,512]{1,0:T(8,128)(2,1)S(1)}, u32[]{:S(2)}, u32[]{:S(2)}) collective-permute-start(bf16[256,512]{1,0:T(8,128)(2,1)S(1)} %fusion.22.refs_2_), channel_id=1, source_target_pairs={{0,128},{1,129},{2,130},{3,131},{4,132},{5,133},{6,134},{7,135},{8... | collective-permute-start | bytes 786440 | tf_op jit(solution)/shard_map/ppermute | solution.py:203
  23.4 13.8 %collective-permute-start.12 = (bf16[256,512]{1,0:T(8,128)(2,1)S(1)}, bf16[256,512]{1,0:T(8,128)(2,1)S(1)}, u32[]{:S(2)}, u32[]{:S(2)}) collective-permute-start(bf16[256,512]{1,0:T(8,128)(2,1)S(1)} %fusion.25), channel_id=1, source_target_pairs={{0,129},{1,128},{2,131},{3,130},{4,133},{5,132},{6,135},{7,134},{8... | collective-permute-start | bytes 786440 | tf_op jit(solution)/shard_map/ppermute | solution.py:204
  23.4 15.6 %collective-permute-start.5 = (bf16[256,512]{1,0:T(8,128)(2,1)S(1)}, bf16[256,512]{1,0:T(8,128)(2,1)S(1)}, u32[]{:S(2)}, u32[]{:S(2)}) collective-permute-start(bf16[256,512]{1,0:T(8,128)(2,1)S(1)} %collective-permute-done.1.refs_3_), channel_id=1, source_target_pairs={{0,96},{32,0},{64,32},{96,64},{1,97},{33,1},{65,33},{97,65},{2,98}... | collective-permute-start | bytes 786440 | tf_op jit(solution)/shard_map/ppermute | solution.py:211
  25.6 13.6 %collective-permute-start.3 = (bf16[256,512]{1,0:T(8,128)(2,1)S(1)}, bf16[256,512]{1,0:T(8,128)(2,1)S(1)}, u32[]{:S(2)}, u32[]{:S(2)}) collective-permute-start(bf16[256,512]{1,0:T(8,128)(2,1)S(1)} %collective-permute-done.1.refs_3_), channel_id=1, source_target_pairs={{0,32},{32,64},{64,96},{96,0},{1,33},{33,65},{65,97},{97,1},{2,34}... | collective-permute-start | bytes 786440 | tf_op jit(solution)/shard_map/ppermute | solution.py:211
  31.1 9.0 %collective-permute-start.6 = (bf16[256,512]{1,0:T(8,128)(2,1)S(1)}, bf16[256,512]{1,0:T(8,128)(2,1)S(1)}, u32[]{:S(2)}, u32[]{:S(2)}) collective-permute-start(bf16[256,512]{1,0:T(8,128)(2,1)S(1)} %broadcast_maximum_fusion.1), channel_id=1, source_target_pairs={{0,32},{32,64},{64,96},{96,0},{1,33},{33,65},{65,97},{97,1},{2,34}... | collective-permute-start | bytes 786440 | tf_op jit(solution)/shard_map/ppermute | solution.py:211
  37.1 9.2 %collective-permute-start.13 = (bf16[256,512]{1,0:T(8,128)(2,1)S(1)}, bf16[256,512]{1,0:T(8,128)(2,1)S(1)}, u32[]{:S(2)}, u32[]{:S(2)}) collective-permute-start(bf16[256,512]{1,0:T(8,128)(2,1)S(1)} %collective-permute-done.11.refs_2_), channel_id=1, source_target_pairs={{0,32},{32,64},{64,96},{96,0},{1,33},{33,65},{65,97},{97,1},{2,34}... | collective-permute-start | bytes 786440 | tf_op jit(solution)/shard_map/ppermute | solution.py:211
  39.0 10.4 %collective-permute-start.16 = (bf16[256,512]{1,0:T(8,128)(2,1)S(1)}, bf16[256,512]{1,0:T(8,128)(2,1)S(1)}, u32[]{:S(2)}, u32[]{:S(2)}) collective-permute-start(bf16[256,512]{1,0:T(8,128)(2,1)S(1)} %collective-permute-done.12.refs_3_), channel_id=1, source_target_pairs={{0,96},{32,0},{64,32},{96,64},{1,97},{33,1},{65,33},{97,65},{2,98}... | collective-permute-start | bytes 786440 | tf_op jit(solution)/shard_map/ppermute | solution.py:211
  39.2 18.2 %collective-permute-start.7 = (bf16[256,512]{1,0:T(8,128)(2,1)S(1)}, bf16[256,512]{1,0:T(8,128)(2,1)S(1)}, u32[]{:S(2)}, u32[]{:S(2)}) collective-permute-start(bf16[256,512]{1,0:T(8,128)(2,1)S(1)} %broadcast_maximum_fusion), channel_id=1, source_target_pairs={{0,96},{32,0},{64,32},{96,64},{1,97},{33,1},{65,33},{97,65},{2,98}... | collective-permute-start | bytes 786440 | tf_op jit(solution)/shard_map/ppermute | solution.py:211
  40.1 23.7 %collective-permute-start.14 = (bf16[256,512]{1,0:T(8,128)(2,1)S(1)}, bf16[256,512]{1,0:T(8,128)(2,1)S(1)}, u32[]{:S(2)}, u32[]{:S(2)}) collective-permute-start(bf16[256,512]{1,0:T(8,128)(2,1)S(1)} %collective-permute-done.12.refs_3_), channel_id=1, source_target_pairs={{0,32},{32,64},{64,96},{96,0},{1,33},{33,65},{65,97},{97,1},{2,34}... | collective-permute-start | bytes 786440 | tf_op jit(solution)/shard_map/ppermute | solution.py:211
  46.3 20.2 %collective-permute-start.15 = (bf16[256,512]{1,0:T(8,128)(2,1)S(1)}, bf16[256,512]{1,0:T(8,128)(2,1)S(1)}, u32[]{:S(2)}, u32[]{:S(2)}) collective-permute-start(bf16[256,512]{1,0:T(8,128)(2,1)S(1)} %collective-permute-done.11.refs_2_), channel_id=1, source_target_pairs={{0,96},{32,0},{64,32},{96,64},{1,97},{33,1},{65,33},{97,65},{2,98}... | collective-permute-start | bytes 786440 | tf_op jit(solution)/shard_map/ppermute | solution.py:211
  49.3 24.6 %collective-permute-start.17 = (bf16[256,512]{1,0:T(8,128)(2,1)S(1)}, bf16[256,512]{1,0:T(8,128)(2,1)S(1)}, u32[]{:S(2)}, u32[]{:S(2)}) collective-permute-start(bf16[256,512]{1,0:T(8,128)(2,1)S(1)} %collective-permute-done.13.refs_4_), channel_id=1, source_target_pairs={{0,32},{32,64},{64,96},{96,0},{1,33},{33,65},{65,97},{97,1},{2,34}... | collective-permute-start | bytes 786440 | tf_op jit(solution)/shard_map/ppermute | solution.py:211
  49.6 24.4 %collective-permute-start.18 = (bf16[256,512]{1,0:T(8,128)(2,1)S(1)}, bf16[256,512]{1,0:T(8,128)(2,1)S(1)}, u32[]{:S(2)}, u32[]{:S(2)}) collective-permute-start(bf16[256,512]{1,0:T(8,128)(2,1)S(1)} %collective-permute-done.16.refs_7_), channel_id=1, source_target_pairs={{0,96},{32,0},{64,32},{96,64},{1,97},{33,1},{65,33},{97,65},{2,98}... | collective-permute-start | bytes 786440 | tf_op jit(solution)/shard_map/ppermute | solution.py:211
  62.3 18.2 %collective-permute-start.8 = (bf16[4,72,256]{2,1,0:T(8,128)(2,1)S(1)}, bf16[4,72,256]{2,1,0:T(8,128)(2,1)S(1)}, u32[]{:S(2)}, u32[]{:S(2)}) collective-permute-start(bf16[4,72,256]{2,1,0:T(8,128)(2,1)S(1)} %get-tuple-element.14), channel_id=1, source_target_pairs={{0,2},{1,3},{2,4},{3,5},{4,6},{5,7},{6,0},{7,1},{8,10},{9,11},{10,... | collective-permute-start | bytes 442376 | tf_op jit(solution)/shard_map/ppermute | solution.py:229
  63.8 18.5 %collective-permute-start.9 = (bf16[4,72,256]{2,1,0:T(8,128)(2,1)S(1)}, bf16[4,72,256]{2,1,0:T(8,128)(2,1)S(1)}, u32[]{:S(2)}, u32[]{:S(2)}) collective-permute-start(bf16[4,72,256]{2,1,0:T(8,128)(2,1)S(1)} %get-tuple-element.15), channel_id=1, source_target_pairs={{0,4},{1,5},{2,6},{3,7},{4,0},{5,1},{6,2},{7,3},{8,12},{9,13},{10,... | collective-permute-start | bytes 442376 | tf_op jit(solution)/shard_map/ppermute | solution.py:229
  66.6 15.8 %collective-permute-start.10 = (bf16[4,72,256]{2,1,0:T(8,128)(2,1)S(1)}, bf16[4,72,256]{2,1,0:T(8,128)(2,1)S(1)}, u32[]{:S(2)}, u32[]{:S(2)}) collective-permute-start(bf16[4,72,256]{2,1,0:T(8,128)(2,1)S(1)} %get-tuple-element.16), channel_id=1, source_target_pairs={{0,6},{1,7},{2,0},{3,1},{4,2},{5,3},{6,4},{7,5},{8,14},{9,15},{10,... | collective-permute-start | bytes 442376 | tf_op jit(solution)/shard_map/ppermute | solution.py:229
  78.9 21.7 %copy-start.2 = (f32[1,36]{1,0:T(1,128)S(1)}, f32[1,36]{1,0:T(1,128)}, u32[]{:S(2)}) copy-start(f32[1,36]{1,0:T(1,128)} %param.10) | copy-start | bytes 436
  78.9 8.0 %collective-permute-start.19 = (bf16[4,72,256]{2,1,0:T(8,128)(2,1)S(1)}, bf16[4,72,256]{2,1,0:T(8,128)(2,1)S(1)}, u32[]{:S(2)}, u32[]{:S(2)}) collective-permute-start(bf16[4,72,256]{2,1,0:T(8,128)(2,1)S(1)} %get-tuple-element.18), channel_id=1, source_target_pairs={{0,2},{1,3},{2,4},{3,5},{4,6},{5,7},{6,0},{7,1},{8,10},{9,11},{10,... | collective-permute-start | bytes 442376 | tf_op jit(solution)/shard_map/ppermute | solution.py:229
  79.6 7.3 %collective-permute-start.20 = (bf16[4,72,256]{2,1,0:T(8,128)(2,1)S(1)}, bf16[4,72,256]{2,1,0:T(8,128)(2,1)S(1)}, u32[]{:S(2)}, u32[]{:S(2)}) collective-permute-start(bf16[4,72,256]{2,1,0:T(8,128)(2,1)S(1)} %get-tuple-element.19), channel_id=1, source_target_pairs={{0,4},{1,5},{2,6},{3,7},{4,0},{5,1},{6,2},{7,3},{8,12},{9,13},{10,... | collective-permute-start | bytes 442376 | tf_op jit(solution)/shard_map/ppermute | solution.py:229
  80.5 7.4 %collective-permute-start.21 = (bf16[4,72,256]{2,1,0:T(8,128)(2,1)S(1)}, bf16[4,72,256]{2,1,0:T(8,128)(2,1)S(1)}, u32[]{:S(2)}, u32[]{:S(2)}) collective-permute-start(bf16[4,72,256]{2,1,0:T(8,128)(2,1)S(1)} %get-tuple-element.20), channel_id=1, source_target_pairs={{0,6},{1,7},{2,0},{3,1},{4,2},{5,3},{6,4},{7,5},{8,14},{9,15},{10,... | collective-permute-start | bytes 442376 | tf_op jit(solution)/shard_map/ppermute | solution.py:229
  89.1 21.9 %all-to-all-start = ((bf16[8,72,256]{2,1,0:T(8,128)(2,1)}), bf16[8,72,256]{2,1,0:T(8,128)(2,1)S(1)}, u32[]{:S(2)}, u32[]{:S(2)}) async-start(bf16[8,72,256]{2,1,0:T(8,128)(2,1)} %shard_map.69), calls=%async_computation | async-start | bytes 589824 | tf_op jit(solution)/shard_map/all_to_all | solution.py:231
  (3 other events, 20.2 us)

commit v12 on v10

--- a/solution.py
+++ b/solution.py
@@ -31,7 +31,11 @@
     return [(i, (i + by) % 4) for i in range(4)]
 
 
-ZC_GROUPS = [[feat_at(z, x, c) for z in range(NZ) for c in range(2)] for x in range(NX)]
+def z_pairs(k):
+    return [
+        (feat_at(z, x, c), feat_at(z ^ k, x, c))
+        for z in range(NZ) for x in range(NX) for c in range(2)
+    ]
 
 
 IN_VMEM = pl.BlockSpec(memory_space=pltpu.VMEM)
@@ -148,46 +152,69 @@
     return last(at, weights, [total], (2,), far)
 
 
+def x_total(refs, z):
+    self_ref, a_ref, b_ref, c_ref = refs
+    return self_ref[z] + a_ref[z].astype(F32) + b_ref[z].astype(F32) + c_ref[z].astype(F32)
+
+
 def x_sum_kernel(at_ref, *refs):
-    *before, self_ref, a_ref, b_ref, c_ref, out_ref = refs
     for z in range(NZ):
-        total = self_ref[z] + a_ref[z].astype(F32) + b_ref[z].astype(F32) + c_ref[z].astype(F32)
-        total = total.astype(BF)
-        for c, piece in enumerate((total[:36], total[36:])):
-            if before:
-                out_ref[2 * z + c, :36] = before[0][2 * z + c]
-                out_ref[2 * z + c, 36:] = piece
-            else:
-                out_ref[2 * z + c] = piece
-
-
-def x_sum(at, before, kept, came):
-    shape = (2 * NZ, 72 if before else 36, 256)
-    return call(x_sum_kernel, jax.ShapeDtypeStruct(shape, BF), [at, *before, kept, *came], 8)
-
-
-def final_kernel(at_ref, chips_ref, bias_ref, out_ref):
-    for c in range(2):
-        chips = chips_ref[c].astype(F32)
-        for z in range(1, NZ):
-            chips = chips + chips_ref[2 * z + c].astype(F32)
-        for block in range(2):
-            total = (chips[block * 36 : (block + 1) * 36] + bias_ref[...]).astype(BF)
-            for dp in range(2):
-
-                @pl.when(at_ref[3] == dp)
-                def _(total=total, start=(dp ^ block) * 512 + c * 256):
-                    out_ref[:, start : start + 256] = total
-
-
-def finish(at, chips, bias):
-    return call(final_kernel, jax.ShapeDtypeStruct((36, 1024), BF), [at, chips, bias], 8)
+        refs[-1][z] = x_total(refs[:-1], z)
+
+
+def x_sum(at, kept, came):
+    return call(x_sum_kernel, jax.ShapeDtypeStruct(kept.shape, F32), [at, kept, *came], 8)
+
+
+def x_cut_kernel(at_ref, before_ref, *refs):
+    for k, out_ref in enumerate(refs[4:]):
+        z = at_ref[4] ^ k
+        out_ref[0] = before_ref[z].astype(out_ref.dtype)
+        out_ref[1] = x_total(refs[:4], z).astype(out_ref.dtype)
+
+
+def x_cut(at, before, kept, came):
+    shape = (2, *kept.shape[1:])
+    out = [jax.ShapeDtypeStruct(shape, F32)] + [jax.ShapeDtypeStruct(shape, BF)] * 3
+    return call(x_cut_kernel, out, [at, before, kept, *came], 8)
+
+
+def z_sum_kernel(at_ref, kept_ref, a_ref, b_ref, c_ref, mine_ref, away_ref):
+    total = kept_ref[...] + a_ref[...].astype(F32) + b_ref[...].astype(F32) + c_ref[...].astype(F32)
+    low, high = total[:, :36], total[:, 36:]
+    for core, (mine, away) in enumerate(((low, high), (high, low))):
+
+        @pl.when(at_ref[0] == core)
+        def _(mine=mine, away=away):
+            mine_ref[...] = mine
+            away_ref[...] = away
+
+
+def z_sum(at, kept, came):
+    out = [jax.ShapeDtypeStruct((2, 36, 256), F32)] * 2
+    return call(z_sum_kernel, out, [at, kept, *came], 8)
+
+
+def final_kernel(at_ref, mine_ref, came_ref, bias_ref, out_ref):
+    for core in range(2):
+        for dp in range(2):
+
+            @pl.when((at_ref[0] == core) & (at_ref[3] == dp))
+            def _(core=core, dp=dp):
+                for ref, half in ((mine_ref, core), (came_ref, 1 - core)):
+                    for block in range(2):
+                        start = (dp ^ block) * 512 + half * 256
+                        out_ref[:, start : start + 256] = (ref[block] + bias_ref[...]).astype(BF)
+
+
+def finish(at, mine, came, bias):
+    return call(final_kernel, jax.ShapeDtypeStruct((36, 1024), BF), [at, mine, came, bias], 8)
 
 
 def per_device(resid, enc_weight, enc_bias, dec_weight, dec_bias, lengths):
     target, feat, dp = lax.axis_index("layer"), lax.axis_index("feat"), lax.axis_index("dp")
     core = feat % 2
-    at = jnp.stack([core, target, feat // 2 % NX, dp]).astype(jnp.int32)
+    at = jnp.stack([core, target, feat // 2 % NX, dp, feat // 8]).astype(jnp.int32)
     valid = (jnp.arange(SEQ)[None, :] < lengths[:, None]).reshape(-1).astype(F32)
     pre = jnp.dot(resid[0], enc_weight[0], preferred_element_type=F32) + enc_bias
     acts = (jax.nn.relu(pre) * valid[:, None]).astype(BF).reshape(2, 256, 512)
@@ -215,14 +242,20 @@
         near = [mine, theirs, up_mine, up_theirs, down_mine, down_theirs]
         blocks[name] = decode(at, weights, near, far)
 
-    chips = []
-    for (kept, *away) in blocks.values():
+    for name, (kept, *away) in blocks.items():
         came = []
         for by, piece in enumerate(away):
             came.append(lax.ppermute(piece, "feat", x_pairs(by + 1)))
-        chips = [x_sum(at, chips, kept, came)]
-    chips = lax.all_to_all(chips[0], "feat", 0, 0, tiled=True, axis_index_groups=ZC_GROUPS)
-    out = finish(at, chips, dec_bias.reshape(36, 1))
+        if name == "own":
+            before = x_sum(at, kept, came)
+        else:
+            kept, *away = x_cut(at, before, kept, came)
+    came = []
+    for k in (3, 2, 1):
+        came.append(lax.ppermute(away[k - 1], "feat", z_pairs(k)))
+    mine, away = z_sum(at, kept, came)
+    came = lax.ppermute(away, "feat", PARTNER)
+    out = finish(at, mine, came, dec_bias.reshape(36, 1))
     return out.T[None]
 
 

time: 109 us -> 104 us (0.954)
  the two profiles are of different devices: /device:TPU:24 before, /device:TPU:1 now
where the time goes in v12:
time: 104 us
  starting transfers between devices  44.8 us (43%)
  Pallas kernels  30.4 us (29%)
  waiting for transfers between devices  25.6 us (25%)
  matrix products  3.05 us (3%)
    pallas_call x8, Pallas kernels, call(): pl.pallas_call(kernel, out_shape=out_shape, in_specs=[IN_SMEM] + [IN_VMEM...  24.8 us
    ppermute x12, starting transfers between devices, shift(): return lax.ppermute(array, 'layer', ring(by))  10.5 us
    ppermute x3, starting transfers between devices, per_device(): came.append(lax.ppermute(away[k - 1], 'feat', z_pairs(k)))  10.5 us
    ppermute x1, waiting for transfers between devices, per_device(): other_theirs = lax.ppermute(send, ('dp', 'feat'), across(1))  8.03 us
    ppermute x6, starting transfers between devices, per_device(): came.append(lax.ppermute(piece, 'feat', x_pairs(by + 1)))  7.77 us
    ppermute x12, waiting for transfers between devices, shift(): return lax.ppermute(array, 'layer', ring(by))  7.2 us
    pallas_call x1, Pallas kernels, cut(): pl.pallas_call(cut_kernel, out_shape=jax.ShapeDtypeStruct(decoders.shape[...  5.53 us
    ppermute x1, starting transfers between devices, per_device(): other_mine = lax.ppermute(keep, ('dp', 'feat'), across(0))  5.2 us
  transfers between devices with their start and end apart: 26, of which 8 were waited for; matrix products, arithmetic and copies ran while one was open for 3% of the time, Pallas kernels for 21%

profile of v12, /device:TPU:1, one launch (start us, length us, event | category | flops | bytes accessed | tf_op | source)
XLA Modules:
  0.0 104.3 jit_solution(14658763435288513885)
XLA Ops:
  0.1 5.5 %cut.1.refs_0_ = bf16[4,512,1152]{2,1,0:T(8,128)(2,1)} custom-call(s32[5]{0:T(128)S(1)} %stack.23.at_ref, bf16[1,4,512,1152]{3,2,1,0:T(8,128)(2,1)} %decoders_ref.1), custom_call_target="tpu_custom_call" | custom-call | bytes 4718592 | tf_op jit(solution)/shard_map/cut/pallas_call | solution.py:91
  5.6 3.3 %collective-permute-start = (bf16[4,512,1152]{2,1,0:T(8,128)(2,1)}, bf16[4,512,1152]{2,1,0:T(8,128)(2,1)}, u32[]{:S(2)}, u32[]{:S(2)}) collective-permute-start(bf16[4,512,1152]{2,1,0:T(8,128)(2,1)} %cut.1.refs_0_), channel_id=1, source_target_pairs={{0,1},{1,0},{2,3},{3,2},{4,5},{5,4},{6,7},{7,6},{8,9},{9,8},{10,11... | collective-permute-start | bytes 14155784 | tf_op jit(solution)/shard_map/ppermute | solution.py:228
  9.0 3.0 %fusion.18 = bf16[512,512]{1,0:T(8,128)(2,1)S(1)} fusion(bf16[1,2304,512]{2,1,0:T(8,128)(2,1)S(1)} %copy-done, bf16[1,512,2304]{2,1,0:T(8,128)(2,1)} %param.6, f32[512]{0:T(512)S(1)} %convert_bitcast_fusion, f32[512]{0:T(512)S(1)} %bitcast.41), kind=kOutput, calls=%fused_computation.6 | convolution fusion | flops 1209008128 | bytes 5246976 | tf_op jit(solution)/shard_map/dot_general | solution.py:219
  12.3 2.7 %collective-permute-start.4 = (bf16[256,512]{1,0:T(8,128)(2,1)S(1)}, bf16[256,512]{1,0:T(8,128)(2,1)S(1)}, u32[]{:S(2)}, u32[]{:S(2)}) collective-permute-start(bf16[256,512]{1,0:T(8,128)(2,1)S(1)} %get-tuple-element.34.refs_2_), channel_id=1, source_target_pairs={{0,96},{32,0},{64,32},{96,64},{1,97},{33,1},{65,33},{97,65},{2,98}... | collective-permute-start | bytes 786440 | tf_op jit(solution)/shard_map/ppermute | solution.py:231
  15.0 5.2 %collective-permute-start.11 = (bf16[256,512]{1,0:T(8,128)(2,1)S(1)}, bf16[256,512]{1,0:T(8,128)(2,1)S(1)}, u32[]{:S(2)}, u32[]{:S(2)}) collective-permute-start(bf16[256,512]{1,0:T(8,128)(2,1)S(1)} %get-tuple-element.34.refs_2_), channel_id=1, source_target_pairs={{0,128},{1,129},{2,130},{3,131},{4,132},{5,133},{6,134},{7,135},{8... | collective-permute-start | bytes 786440 | tf_op jit(solution)/shard_map/ppermute | solution.py:224
  20.2 2.3 %collective-permute-start.12 = (bf16[256,512]{1,0:T(8,128)(2,1)S(1)}, bf16[256,512]{1,0:T(8,128)(2,1)S(1)}, u32[]{:S(2)}, u32[]{:S(2)}) collective-permute-start(bf16[256,512]{1,0:T(8,128)(2,1)S(1)} %get-tuple-element.33), channel_id=1, source_target_pairs={{0,129},{1,128},{2,131},{3,130},{4,133},{5,132},{6,135},{7,134},{8... | collective-permute-start | bytes 786440 | tf_op jit(solution)/shard_map/ppermute | solution.py:225
  22.5 2.4 %collective-permute-start.5 = (bf16[256,512]{1,0:T(8,128)(2,1)S(1)}, bf16[256,512]{1,0:T(8,128)(2,1)S(1)}, u32[]{:S(2)}, u32[]{:S(2)}) collective-permute-start(bf16[256,512]{1,0:T(8,128)(2,1)S(1)} %collective-permute-done.1.refs_3_), channel_id=1, source_target_pairs={{0,96},{32,0},{64,32},{96,64},{1,97},{33,1},{65,33},{97,65},{2,98}... | collective-permute-start | bytes 786440 | tf_op jit(solution)/shard_map/ppermute | solution.py:231
  24.9 1.8 %collective-permute-done.11.refs_2_ = bf16[256,512]{1,0:T(8,128)(2,1)S(1)} collective-permute-done((bf16[256,512]{1,0:T(8,128)(2,1)S(1)}, bf16[256,512]{1,0:T(8,128)(2,1)S(1)}, u32[]{:S(2)}, u32[]{:S(2)}) %collective-permute-start.11) | collective-permute-done | bytes 262176 | tf_op jit(solution)/shard_map/ppermute | solution.py:224
  26.7 8.0 %collective-permute-done.12.refs_3_ = bf16[256,512]{1,0:T(8,128)(2,1)S(1)} collective-permute-done((bf16[256,512]{1,0:T(8,128)(2,1)S(1)}, bf16[256,512]{1,0:T(8,128)(2,1)S(1)}, u32[]{:S(2)}, u32[]{:S(2)}) %collective-permute-start.12) | collective-permute-done | bytes 262176 | tf_op jit(solution)/shard_map/ppermute | solution.py:225
  34.8 2.7 %collective-permute-start.16 = (bf16[256,512]{1,0:T(8,128)(2,1)S(1)}, bf16[256,512]{1,0:T(8,128)(2,1)S(1)}, u32[]{:S(2)}, u32[]{:S(2)}) collective-permute-start(bf16[256,512]{1,0:T(8,128)(2,1)S(1)} %collective-permute-done.12.refs_3_), channel_id=1, source_target_pairs={{0,96},{32,0},{64,32},{96,64},{1,97},{33,1},{65,33},{97,65},{2,98}... | collective-permute-start | bytes 786440 | tf_op jit(solution)/shard_map/ppermute | solution.py:231
  37.6 1.6 %collective-permute-done.6.refs_3_ = bf16[256,512]{1,0:T(8,128)(2,1)S(1)} collective-permute-done((bf16[256,512]{1,0:T(8,128)(2,1)S(1)}, bf16[256,512]{1,0:T(8,128)(2,1)S(1)}, u32[]{:S(2)}, u32[]{:S(2)}) %collective-permute-start.6) | collective-permute-done | bytes 262176 | tf_op jit(solution)/shard_map/ppermute | solution.py:231
  39.2 5.6 %collective-permute-done.13.refs_4_ = bf16[256,512]{1,0:T(8,128)(2,1)S(1)} collective-permute-done((bf16[256,512]{1,0:T(8,128)(2,1)S(1)}, bf16[256,512]{1,0:T(8,128)(2,1)S(1)}, u32[]{:S(2)}, u32[]{:S(2)}) %collective-permute-start.13) | collective-permute-done | bytes 262176 | tf_op jit(solution)/shard_map/ppermute | solution.py:231
  44.8 1.5 %collective-permute-start.17 = (bf16[256,512]{1,0:T(8,128)(2,1)S(1)}, bf16[256,512]{1,0:T(8,128)(2,1)S(1)}, u32[]{:S(2)}, u32[]{:S(2)}) collective-permute-start(bf16[256,512]{1,0:T(8,128)(2,1)S(1)} %collective-permute-done.13.refs_4_), channel_id=1, source_target_pairs={{0,32},{32,64},{64,96},{96,0},{1,33},{33,65},{65,97},{97,1},{2,34}... | collective-permute-start | bytes 786440 | tf_op jit(solution)/shard_map/ppermute | solution.py:231
  47.5 6.0 %shard_map.64.refs_2_ = f32[256,1152]{1,0:T(8,128)S(1)} custom-call(s32[5]{0:T(128)S(1)} %stack.23.at_ref, bf16[4,512,1152]{2,1,0:T(8,128)(2,1)} %cut.1.refs_0_, bf16[4,512,1152]{2,1,0:T(8,128)(2,1)} %collective-permute-done.refs_1_, bf16[256,512]{1,0:T(8,128)(2,1)S(1)} %get-tuple-element.34.refs_2_, bf16[256,512]{1,0:T(8,128)(2,1)S(1)} %collective-permute-done.1.refs_3_, ...), custom_call_target="tpu_custom_call" | custom-call | flops 1811939328 | bytes 11010068 | tf_op jit(solution)/shard_map/pallas_call | solution.py:49
  53.4 4.9 %shard_map.65 = (f32[4,72,256]{2,1,0:T(8,128)S(1)}, bf16[4,72,256]{2,1,0:T(8,128)(2,1)S(1)}, bf16[4,72,256]{2,1,0:T(8,128)(2,1)S(1)}, bf16[4,72,256]{2,1,0:T(8,128)(2,1)S(1)}) custom-call(s32[5]{0:T(128)S(1)} %stack.23.at_ref, bf16[4,512,1152]{2,1,0:T(8,128)(2,1)} %cut.1.refs_0_, bf16[4,512,1152]{2,1,0:T(8,128)(2,1)} %collective-permute-done.refs_1_, ...), custom_call_target="tpu_custom_call" | custom-call | flops 603979776 | bytes 11141140 | tf_op jit(solution)/shard_map/pallas_call | solution.py:49
  59.6 2.5 %collective-permute-start.9 = (bf16[4,72,256]{2,1,0:T(8,128)(2,1)S(1)}, bf16[4,72,256]{2,1,0:T(8,128)(2,1)S(1)}, u32[]{:S(2)}, u32[]{:S(2)}) collective-permute-start(bf16[4,72,256]{2,1,0:T(8,128)(2,1)S(1)} %get-tuple-element.21), channel_id=1, source_target_pairs={{0,4},{1,5},{2,6},{3,7},{4,0},{5,1},{6,2},{7,3},{8,12},{9,13},{10,... | collective-permute-start | bytes 442376 | tf_op jit(solution)/shard_map/ppermute | solution.py:248
  63.2 6.0 %shard_map.67.refs_2_ = f32[256,1152]{1,0:T(8,128)S(1)} custom-call(s32[5]{0:T(128)S(1)} %stack.23.at_ref, bf16[4,512,1152]{2,1,0:T(8,128)(2,1)} %cut.1.refs_0_, bf16[4,512,1152]{2,1,0:T(8,128)(2,1)} %collective-permute-done.refs_1_, bf16[256,512]{1,0:T(8,128)(2,1)S(1)} %collective-permute-done.11.refs_2_, ...), custom_call_target="tpu_custom_call" | custom-call | flops 1811939328 | bytes 11010068 | tf_op jit(solution)/shard_map/pallas_call | solution.py:49
  69.2 4.9 %shard_map.68 = (f32[4,72,256]{2,1,0:T(8,128)S(1)}, bf16[4,72,256]{2,1,0:T(8,128)(2,1)S(1)}, bf16[4,72,256]{2,1,0:T(8,128)(2,1)S(1)}, bf16[4,72,256]{2,1,0:T(8,128)(2,1)S(1)}) custom-call(s32[5]{0:T(128)S(1)} %stack.23.at_ref, bf16[4,512,1152]{2,1,0:T(8,128)(2,1)} %cut.1.refs_0_, bf16[4,512,1152]{2,1,0:T(8,128)(2,1)} %collective-permute-done.refs_1_, ...), custom_call_target="tpu_custom_call" | custom-call | flops 603979776 | bytes 11141140 | tf_op jit(solution)/shard_map/pallas_call | solution.py:49
  75.4 1.6 %collective-permute-start.21 = (bf16[4,72,256]{2,1,0:T(8,128)(2,1)S(1)}, bf16[4,72,256]{2,1,0:T(8,128)(2,1)S(1)}, u32[]{:S(2)}, u32[]{:S(2)}) collective-permute-start(bf16[4,72,256]{2,1,0:T(8,128)(2,1)S(1)} %get-tuple-element.26), channel_id=1, source_target_pairs={{0,6},{1,7},{2,0},{3,1},{4,2},{5,3},{6,4},{7,5},{8,14},{9,15},{10,... | collective-permute-start | bytes 442376 | tf_op jit(solution)/shard_map/ppermute | solution.py:248
  77.6 3.4 %collective-permute-done.19.refs_1_ = bf16[4,72,256]{2,1,0:T(8,128)(2,1)S(1)} collective-permute-done((bf16[4,72,256]{2,1,0:T(8,128)(2,1)S(1)}, bf16[4,72,256]{2,1,0:T(8,128)(2,1)S(1)}, u32[]{:S(2)}, u32[]{:S(2)}) %collective-permute-start.19) | collective-permute-done | bytes 147488 | tf_op jit(solution)/shard_map/ppermute | solution.py:248
  82.3 6.4 %collective-permute-start.22 = (bf16[2,72,256]{2,1,0:T(8,128)(2,1)S(1)}, bf16[2,72,256]{2,1,0:T(8,128)(2,1)S(1)}, u32[]{:S(2)}, u32[]{:S(2)}) collective-permute-start(bf16[2,72,256]{2,1,0:T(8,128)(2,1)S(1)} %get-tuple-element.28), channel_id=1, source_target_pairs={{0,24},{1,25},{2,26},{3,27},{4,28},{5,29},{6,30},{7,31},{8,16},{9,... | collective-permute-start | bytes 221192 | tf_op jit(solution)/shard_map/ppermute | solution.py:255
  88.7 4.1 %collective-permute-start.23 = (bf16[2,72,256]{2,1,0:T(8,128)(2,1)S(1)}, bf16[2,72,256]{2,1,0:T(8,128)(2,1)S(1)}, u32[]{:S(2)}, u32[]{:S(2)}) collective-permute-start(bf16[2,72,256]{2,1,0:T(8,128)(2,1)S(1)} %get-tuple-element.29), channel_id=1, source_target_pairs={{0,16},{1,17},{2,18},{3,19},{4,20},{5,21},{6,22},{7,23},{8,24},{9,... | collective-permute-start | bytes 221192 | tf_op jit(solution)/shard_map/ppermute | solution.py:255
  92.8 3.7 %collective-permute-done.23.b_ref = bf16[2,72,256]{2,1,0:T(8,128)(2,1)S(1)} collective-permute-done((bf16[2,72,256]{2,1,0:T(8,128)(2,1)S(1)}, bf16[2,72,256]{2,1,0:T(8,128)(2,1)S(1)}, u32[]{:S(2)}, u32[]{:S(2)}) %collective-permute-start.23) | collective-permute-done | bytes 73760 | tf_op jit(solution)/shard_map/ppermute | solution.py:255
  97.0 5.0 %collective-permute-start.25 = (f32[2,36,256]{2,1,0:T(8,128)S(1)}, f32[2,36,256]{2,1,0:T(8,128)S(1)}, u32[]{:S(2)}, u32[]{:S(2)}) collective-permute-start(f32[2,36,256]{2,1,0:T(8,128)S(1)} %get-tuple-element.32), channel_id=1, source_target_pairs={{0,1},{1,0},{2,3},{3,2},{4,5},{5,4},{6,7},{7,6},{8,9},{9,8},{10,11... | collective-permute-start | bytes 221192 | tf_op jit(solution)/shard_map/ppermute | solution.py:257
  (52 shorter events, 10.1 us)
Async XLA Ops:
  5.6 40.6 %collective-permute-start = (bf16[4,512,1152]{2,1,0:T(8,128)(2,1)}, bf16[4,512,1152]{2,1,0:T(8,128)(2,1)}, u32[]{:S(2)}, u32[]{:S(2)}) collective-permute-start(bf16[4,512,1152]{2,1,0:T(8,128)(2,1)} %cut.1.refs_0_), channel_id=1, source_target_pairs={{0,1},{1,0},{2,3},{3,2},{4,5},{5,4},{6,7},{7,6},{8,9},{9,8},{10,11... | collective-permute-start | bytes 14155784 | tf_op jit(solution)/shard_map/ppermute | solution.py:228
  12.1 8.1 %collective-permute-start.1 = (bf16[256,512]{1,0:T(8,128)(2,1)S(1)}, bf16[256,512]{1,0:T(8,128)(2,1)S(1)}, u32[]{:S(2)}, u32[]{:S(2)}) collective-permute-start(bf16[256,512]{1,0:T(8,128)(2,1)S(1)} %get-tuple-element.33), channel_id=1, source_target_pairs={{0,1},{1,0},{2,3},{3,2},{4,5},{5,4},{6,7},{7,6},{8,9},{9,8},{10,11... | collective-permute-start | bytes 786440 | tf_op jit(solution)/shard_map/ppermute | solution.py:226
  12.2 10.3 %collective-permute-start.2 = (bf16[256,512]{1,0:T(8,128)(2,1)S(1)}, bf16[256,512]{1,0:T(8,128)(2,1)S(1)}, u32[]{:S(2)}, u32[]{:S(2)}) collective-permute-start(bf16[256,512]{1,0:T(8,128)(2,1)S(1)} %get-tuple-element.34.refs_2_), channel_id=1, source_target_pairs={{0,32},{32,64},{64,96},{96,0},{1,33},{33,65},{65,97},{97,1},{2,34}... | collective-permute-start | bytes 786440 | tf_op jit(solution)/shard_map/ppermute | solution.py:231
  12.3 12.6 %collective-permute-start.4 = (bf16[256,512]{1,0:T(8,128)(2,1)S(1)}, bf16[256,512]{1,0:T(8,128)(2,1)S(1)}, u32[]{:S(2)}, u32[]{:S(2)}) collective-permute-start(bf16[256,512]{1,0:T(8,128)(2,1)S(1)} %get-tuple-element.34.refs_2_), channel_id=1, source_target_pairs={{0,96},{32,0},{64,32},{96,64},{1,97},{33,1},{65,33},{97,65},{2,98}... | collective-permute-start | bytes 786440 | tf_op jit(solution)/shard_map/ppermute | solution.py:231
  15.0 11.8 %collective-permute-start.11 = (bf16[256,512]{1,0:T(8,128)(2,1)S(1)}, bf16[256,512]{1,0:T(8,128)(2,1)S(1)}, u32[]{:S(2)}, u32[]{:S(2)}) collective-permute-start(bf16[256,512]{1,0:T(8,128)(2,1)S(1)} %get-tuple-element.34.refs_2_), channel_id=1, source_target_pairs={{0,128},{1,129},{2,130},{3,131},{4,132},{5,133},{6,134},{7,135},{8... | collective-permute-start | bytes 786440 | tf_op jit(solution)/shard_map/ppermute | solution.py:224
  20.2 14.6 %collective-permute-start.12 = (bf16[256,512]{1,0:T(8,128)(2,1)S(1)}, bf16[256,512]{1,0:T(8,128)(2,1)S(1)}, u32[]{:S(2)}, u32[]{:S(2)}) collective-permute-start(bf16[256,512]{1,0:T(8,128)(2,1)S(1)} %get-tuple-element.33), channel_id=1, source_target_pairs={{0,129},{1,128},{2,131},{3,130},{4,133},{5,132},{6,135},{7,134},{8... | collective-permute-start | bytes 786440 | tf_op jit(solution)/shard_map/ppermute | solution.py:225
  22.5 12.3 %collective-permute-start.5 = (bf16[256,512]{1,0:T(8,128)(2,1)S(1)}, bf16[256,512]{1,0:T(8,128)(2,1)S(1)}, u32[]{:S(2)}, u32[]{:S(2)}) collective-permute-start(bf16[256,512]{1,0:T(8,128)(2,1)S(1)} %collective-permute-done.1.refs_3_), channel_id=1, source_target_pairs={{0,96},{32,0},{64,32},{96,64},{1,97},{33,1},{65,33},{97,65},{2,98}... | collective-permute-start | bytes 786440 | tf_op jit(solution)/shard_map/ppermute | solution.py:231
  24.9 12.6 %collective-permute-start.3 = (bf16[256,512]{1,0:T(8,128)(2,1)S(1)}, bf16[256,512]{1,0:T(8,128)(2,1)S(1)}, u32[]{:S(2)}, u32[]{:S(2)}) collective-permute-start(bf16[256,512]{1,0:T(8,128)(2,1)S(1)} %collective-permute-done.1.refs_3_), channel_id=1, source_target_pairs={{0,32},{32,64},{64,96},{96,0},{1,33},{33,65},{65,97},{97,1},{2,34}... | collective-permute-start | bytes 786440 | tf_op jit(solution)/shard_map/ppermute | solution.py:231
  26.7 12.4 %collective-permute-start.6 = (bf16[256,512]{1,0:T(8,128)(2,1)S(1)}, bf16[256,512]{1,0:T(8,128)(2,1)S(1)}, u32[]{:S(2)}, u32[]{:S(2)}) collective-permute-start(bf16[256,512]{1,0:T(8,128)(2,1)S(1)} %broadcast_maximum_fusion.1), channel_id=1, source_target_pairs={{0,32},{32,64},{64,96},{96,0},{1,33},{33,65},{65,97},{97,1},{2,34}... | collective-permute-start | bytes 786440 | tf_op jit(solution)/shard_map/ppermute | solution.py:231
  34.8 10.0 %collective-permute-start.13 = (bf16[256,512]{1,0:T(8,128)(2,1)S(1)}, bf16[256,512]{1,0:T(8,128)(2,1)S(1)}, u32[]{:S(2)}, u32[]{:S(2)}) collective-permute-start(bf16[256,512]{1,0:T(8,128)(2,1)S(1)} %collective-permute-done.11.refs_2_), channel_id=1, source_target_pairs={{0,32},{32,64},{64,96},{96,0},{1,33},{33,65},{65,97},{97,1},{2,34}... | collective-permute-start | bytes 786440 | tf_op jit(solution)/shard_map/ppermute | solution.py:231
  34.8 10.0 %collective-permute-start.16 = (bf16[256,512]{1,0:T(8,128)(2,1)S(1)}, bf16[256,512]{1,0:T(8,128)(2,1)S(1)}, u32[]{:S(2)}, u32[]{:S(2)}) collective-permute-start(bf16[256,512]{1,0:T(8,128)(2,1)S(1)} %collective-permute-done.12.refs_3_), channel_id=1, source_target_pairs={{0,96},{32,0},{64,32},{96,64},{1,97},{33,1},{65,33},{97,65},{2,98}... | collective-permute-start | bytes 786440 | tf_op jit(solution)/shard_map/ppermute | solution.py:231
  37.5 15.9 %collective-permute-start.7 = (bf16[256,512]{1,0:T(8,128)(2,1)S(1)}, bf16[256,512]{1,0:T(8,128)(2,1)S(1)}, u32[]{:S(2)}, u32[]{:S(2)}) collective-permute-start(bf16[256,512]{1,0:T(8,128)(2,1)S(1)} %broadcast_maximum_fusion), channel_id=1, source_target_pairs={{0,96},{32,0},{64,32},{96,64},{1,97},{33,1},{65,33},{97,65},{2,98}... | collective-permute-start | bytes 786440 | tf_op jit(solution)/shard_map/ppermute | solution.py:231
  39.1 20.5 %collective-permute-start.14 = (bf16[256,512]{1,0:T(8,128)(2,1)S(1)}, bf16[256,512]{1,0:T(8,128)(2,1)S(1)}, u32[]{:S(2)}, u32[]{:S(2)}) collective-permute-start(bf16[256,512]{1,0:T(8,128)(2,1)S(1)} %collective-permute-done.12.refs_3_), channel_id=1, source_target_pairs={{0,32},{32,64},{64,96},{96,0},{1,33},{33,65},{65,97},{97,1},{2,34}... | collective-permute-start | bytes 786440 | tf_op jit(solution)/shard_map/ppermute | solution.py:231
  44.8 17.3 %collective-permute-start.15 = (bf16[256,512]{1,0:T(8,128)(2,1)S(1)}, bf16[256,512]{1,0:T(8,128)(2,1)S(1)}, u32[]{:S(2)}, u32[]{:S(2)}) collective-permute-start(bf16[256,512]{1,0:T(8,128)(2,1)S(1)} %collective-permute-done.11.refs_2_), channel_id=1, source_target_pairs={{0,96},{32,0},{64,32},{96,64},{1,97},{33,1},{65,33},{97,65},{2,98}... | collective-permute-start | bytes 786440 | tf_op jit(solution)/shard_map/ppermute | solution.py:231
  44.8 24.4 %collective-permute-start.17 = (bf16[256,512]{1,0:T(8,128)(2,1)S(1)}, bf16[256,512]{1,0:T(8,128)(2,1)S(1)}, u32[]{:S(2)}, u32[]{:S(2)}) collective-permute-start(bf16[256,512]{1,0:T(8,128)(2,1)S(1)} %collective-permute-done.13.refs_4_), channel_id=1, source_target_pairs={{0,32},{32,64},{64,96},{96,0},{1,33},{33,65},{65,97},{97,1},{2,34}... | collective-permute-start | bytes 786440 | tf_op jit(solution)/shard_map/ppermute | solution.py:231
  46.2 23.0 %collective-permute-start.18 = (bf16[256,512]{1,0:T(8,128)(2,1)S(1)}, bf16[256,512]{1,0:T(8,128)(2,1)S(1)}, u32[]{:S(2)}, u32[]{:S(2)}) collective-permute-start(bf16[256,512]{1,0:T(8,128)(2,1)S(1)} %collective-permute-done.16.refs_7_), channel_id=1, source_target_pairs={{0,96},{32,0},{64,32},{96,64},{1,97},{33,1},{65,33},{97,65},{2,98}... | collective-permute-start | bytes 786440 | tf_op jit(solution)/shard_map/ppermute | solution.py:231
  58.3 17.1 %collective-permute-start.8 = (bf16[4,72,256]{2,1,0:T(8,128)(2,1)S(1)}, bf16[4,72,256]{2,1,0:T(8,128)(2,1)S(1)}, u32[]{:S(2)}, u32[]{:S(2)}) collective-permute-start(bf16[4,72,256]{2,1,0:T(8,128)(2,1)S(1)} %get-tuple-element.20), channel_id=1, source_target_pairs={{0,2},{1,3},{2,4},{3,5},{4,6},{5,7},{6,0},{7,1},{8,10},{9,11},{10,... | collective-permute-start | bytes 442376 | tf_op jit(solution)/shard_map/ppermute | solution.py:248
  59.6 17.4 %collective-permute-start.9 = (bf16[4,72,256]{2,1,0:T(8,128)(2,1)S(1)}, bf16[4,72,256]{2,1,0:T(8,128)(2,1)S(1)}, u32[]{:S(2)}, u32[]{:S(2)}) collective-permute-start(bf16[4,72,256]{2,1,0:T(8,128)(2,1)S(1)} %get-tuple-element.21), channel_id=1, source_target_pairs={{0,4},{1,5},{2,6},{3,7},{4,0},{5,1},{6,2},{7,3},{8,12},{9,13},{10,... | collective-permute-start | bytes 442376 | tf_op jit(solution)/shard_map/ppermute | solution.py:248
  62.1 15.0 %collective-permute-start.10 = (bf16[4,72,256]{2,1,0:T(8,128)(2,1)S(1)}, bf16[4,72,256]{2,1,0:T(8,128)(2,1)S(1)}, u32[]{:S(2)}, u32[]{:S(2)}) collective-permute-start(bf16[4,72,256]{2,1,0:T(8,128)(2,1)S(1)} %get-tuple-element.22), channel_id=1, source_target_pairs={{0,6},{1,7},{2,0},{3,1},{4,2},{5,3},{6,4},{7,5},{8,14},{9,15},{10,... | collective-permute-start | bytes 442376 | tf_op jit(solution)/shard_map/ppermute | solution.py:248
  74.1 6.9 %collective-permute-start.19 = (bf16[4,72,256]{2,1,0:T(8,128)(2,1)S(1)}, bf16[4,72,256]{2,1,0:T(8,128)(2,1)S(1)}, u32[]{:S(2)}, u32[]{:S(2)}) collective-permute-start(bf16[4,72,256]{2,1,0:T(8,128)(2,1)S(1)} %get-tuple-element.24), channel_id=1, source_target_pairs={{0,2},{1,3},{2,4},{3,5},{4,6},{5,7},{6,0},{7,1},{8,10},{9,11},{10,... | collective-permute-start | bytes 442376 | tf_op jit(solution)/shard_map/ppermute | solution.py:248
  74.5 6.5 %collective-permute-start.20 = (bf16[4,72,256]{2,1,0:T(8,128)(2,1)S(1)}, bf16[4,72,256]{2,1,0:T(8,128)(2,1)S(1)}, u32[]{:S(2)}, u32[]{:S(2)}) collective-permute-start(bf16[4,72,256]{2,1,0:T(8,128)(2,1)S(1)} %get-tuple-element.25), channel_id=1, source_target_pairs={{0,4},{1,5},{2,6},{3,7},{4,0},{5,1},{6,2},{7,3},{8,12},{9,13},{10,... | collective-permute-start | bytes 442376 | tf_op jit(solution)/shard_map/ppermute | solution.py:248
  75.4 6.2 %collective-permute-start.21 = (bf16[4,72,256]{2,1,0:T(8,128)(2,1)S(1)}, bf16[4,72,256]{2,1,0:T(8,128)(2,1)S(1)}, u32[]{:S(2)}, u32[]{:S(2)}) collective-permute-start(bf16[4,72,256]{2,1,0:T(8,128)(2,1)S(1)} %get-tuple-element.26), channel_id=1, source_target_pairs={{0,6},{1,7},{2,0},{3,1},{4,2},{5,3},{6,4},{7,5},{8,14},{9,15},{10,... | collective-permute-start | bytes 442376 | tf_op jit(solution)/shard_map/ppermute | solution.py:248
  82.3 10.5 %collective-permute-start.22 = (bf16[2,72,256]{2,1,0:T(8,128)(2,1)S(1)}, bf16[2,72,256]{2,1,0:T(8,128)(2,1)S(1)}, u32[]{:S(2)}, u32[]{:S(2)}) collective-permute-start(bf16[2,72,256]{2,1,0:T(8,128)(2,1)S(1)} %get-tuple-element.28), channel_id=1, source_target_pairs={{0,24},{1,25},{2,26},{3,27},{4,28},{5,29},{6,30},{7,31},{8,16},{9,... | collective-permute-start | bytes 221192 | tf_op jit(solution)/shard_map/ppermute | solution.py:255
  88.7 7.8 %collective-permute-start.23 = (bf16[2,72,256]{2,1,0:T(8,128)(2,1)S(1)}, bf16[2,72,256]{2,1,0:T(8,128)(2,1)S(1)}, u32[]{:S(2)}, u32[]{:S(2)}) collective-permute-start(bf16[2,72,256]{2,1,0:T(8,128)(2,1)S(1)} %get-tuple-element.29), channel_id=1, source_target_pairs={{0,16},{1,17},{2,18},{3,19},{4,20},{5,21},{6,22},{7,23},{8,24},{9,... | collective-permute-start | bytes 221192 | tf_op jit(solution)/shard_map/ppermute | solution.py:255
  (6 other events, 64.3 us)

commit v13 on v12

--- a/solution.py
+++ b/solution.py
@@ -157,42 +157,34 @@
     return self_ref[z] + a_ref[z].astype(F32) + b_ref[z].astype(F32) + c_ref[z].astype(F32)
 
 
-def x_sum_kernel(at_ref, *refs):
-    for z in range(NZ):
-        refs[-1][z] = x_total(refs[:-1], z)
-
-
-def x_sum(at, kept, came):
-    return call(x_sum_kernel, jax.ShapeDtypeStruct(kept.shape, F32), [at, kept, *came], 8)
-
-
-def x_cut_kernel(at_ref, before_ref, *refs):
+def x_cut_kernel(at_ref, *refs):
     for k, out_ref in enumerate(refs[4:]):
-        z = at_ref[4] ^ k
-        out_ref[0] = before_ref[z].astype(out_ref.dtype)
-        out_ref[1] = x_total(refs[:4], z).astype(out_ref.dtype)
-
-
-def x_cut(at, before, kept, came):
-    shape = (2, *kept.shape[1:])
+        out_ref[...] = x_total(refs[:4], at_ref[4] ^ k).astype(out_ref.dtype)
+
+
+def x_cut(at, kept, came):
+    shape = kept.shape[1:]
     out = [jax.ShapeDtypeStruct(shape, F32)] + [jax.ShapeDtypeStruct(shape, BF)] * 3
-    return call(x_cut_kernel, out, [at, before, kept, *came], 8)
-
-
-def z_sum_kernel(at_ref, kept_ref, a_ref, b_ref, c_ref, mine_ref, away_ref):
-    total = kept_ref[...] + a_ref[...].astype(F32) + b_ref[...].astype(F32) + c_ref[...].astype(F32)
-    low, high = total[:, :36], total[:, 36:]
-    for core, (mine, away) in enumerate(((low, high), (high, low))):
-
-        @pl.when(at_ref[0] == core)
-        def _(mine=mine, away=away):
-            mine_ref[...] = mine
-            away_ref[...] = away
-
-
-def z_sum(at, kept, came):
+    return call(x_cut_kernel, out, [at, kept, *came], 8)
+
+
+def z_sum_kernel(at_ref, *refs):
+    mine_ref, away_ref = refs[-2:]
+    for block in range(2):
+        kept_ref, a_ref, b_ref, c_ref = refs[4 * block : 4 * block + 4]
+        total = kept_ref[...] + a_ref[...].astype(F32) + b_ref[...].astype(F32) + c_ref[...].astype(F32)
+        low, high = total[:36], total[36:]
+        for core, (mine, away) in enumerate(((low, high), (high, low))):
+
+            @pl.when(at_ref[0] == core)
+            def _(mine=mine, away=away, block=block):
+                mine_ref[block] = mine
+                away_ref[block] = away
+
+
+def z_sum(at, pieces):
     out = [jax.ShapeDtypeStruct((2, 36, 256), F32)] * 2
-    return call(z_sum_kernel, out, [at, kept, *came], 8)
+    return call(z_sum_kernel, out, [at, *pieces], 8)
 
 
 def final_kernel(at_ref, mine_ref, came_ref, bias_ref, out_ref):
@@ -242,18 +234,16 @@
         near = [mine, theirs, up_mine, up_theirs, down_mine, down_theirs]
         blocks[name] = decode(at, weights, near, far)
 
-    for name, (kept, *away) in blocks.items():
+    pieces = []
+    for (kept, *away) in blocks.values():
         came = []
         for by, piece in enumerate(away):
             came.append(lax.ppermute(piece, "feat", x_pairs(by + 1)))
-        if name == "own":
-            before = x_sum(at, kept, came)
-        else:
-            kept, *away = x_cut(at, before, kept, came)
-    came = []
-    for k in (3, 2, 1):
-        came.append(lax.ppermute(away[k - 1], "feat", z_pairs(k)))
-    mine, away = z_sum(at, kept, came)
+        kept, *away = x_cut(at, kept, came)
+        pieces.append(kept)
+        for k in (3, 2, 1):
+            pieces.append(lax.ppermute(away[k - 1], "feat", z_pairs(k)))
+    mine, away = z_sum(at, pieces)
     came = lax.ppermute(away, "feat", PARTNER)
     out = finish(at, mine, came, dec_bias.reshape(36, 1))
     return out.T[None]

time: 104 us -> 105 us (level)
  starting transfers between devices: 44.8 us -> 51 us
  waiting for transfers between devices: 25.6 us -> 19.9 us
    ppermute x3 -> x6, starting transfers between devices: 10.5 us -> 16.3 us  [per_device(): pieces.append(lax.ppermute(away[k - 1], 'feat', z_pairs(k)))]
    ppermute x6, waiting for transfers between devices: 3.99 us -> 0.02 us  [per_device(): came.append(lax.ppermute(piece, 'feat', x_pairs(by + 1)))]
    ppermute x3 -> x6, waiting for transfers between devices: 3.67 us -> 1.93 us  [per_device(): pieces.append(lax.ppermute(away[k - 1], 'feat', z_pairs(k)))]
  transfers between devices with their start and end apart: 26 -> 29, of which waited for: 8 -> 8; matrix products, arithmetic and copies ran while one was open for 3% -> 3% of each run, Pallas kernels for 21% -> 22%
where the time goes in v13:
time: 105 us
  starting transfers between devices  51 us (49%)
  Pallas kernels  30.5 us (29%)
  waiting for transfers between devices  19.9 us (19%)
  matrix products  3.05 us (3%)
    pallas_call x8, Pallas kernels, call(): pl.pallas_call(kernel, out_shape=out_shape, in_specs=[IN_SMEM] + [IN_VMEM...  24.9 us
    ppermute x6, starting transfers between devices, per_device(): pieces.append(lax.ppermute(away[k - 1], 'feat', z_pairs(k)))  16.3 us
    ppermute x12, starting transfers between devices, shift(): return lax.ppermute(array, 'layer', ring(by))  10.5 us
    ppermute x1, waiting for transfers between devices, per_device(): other_theirs = lax.ppermute(send, ('dp', 'feat'), across(1))  8.03 us
    ppermute x6, starting transfers between devices, per_device(): came.append(lax.ppermute(piece, 'feat', x_pairs(by + 1)))  7.79 us
    ppermute x12, waiting for transfers between devices, shift(): return lax.ppermute(array, 'layer', ring(by))  7.2 us
    pallas_call x1, Pallas kernels, cut(): pl.pallas_call(cut_kernel, out_shape=jax.ShapeDtypeStruct(decoders.shape[...  5.54 us
    ppermute x1, starting transfers between devices, per_device(): came = lax.ppermute(away, 'feat', PARTNER)  5.44 us
  transfers between devices with their start and end apart: 29, of which 8 were waited for; matrix products, arithmetic and copies ran while one was open for 3% of the time, Pallas kernels for 22%

profile of v13, /device:TPU:1, one launch (start us, length us, event | category | flops | bytes accessed | tf_op | source)
XLA Modules:
  0.0 104.8 jit_solution(9149634142871663031)
XLA Ops:
  0.1 5.5 %cut.1.refs_0_ = bf16[4,512,1152]{2,1,0:T(8,128)(2,1)} custom-call(s32[5]{0:T(128)S(1)} %stack.23.at_ref, bf16[1,4,512,1152]{3,2,1,0:T(8,128)(2,1)} %decoders_ref.1), custom_call_target="tpu_custom_call" | custom-call | bytes 4718592 | tf_op jit(solution)/shard_map/cut/pallas_call | solution.py:91
  5.6 3.3 %collective-permute-start = (bf16[4,512,1152]{2,1,0:T(8,128)(2,1)}, bf16[4,512,1152]{2,1,0:T(8,128)(2,1)}, u32[]{:S(2)}, u32[]{:S(2)}) collective-permute-start(bf16[4,512,1152]{2,1,0:T(8,128)(2,1)} %cut.1.refs_0_), channel_id=1, source_target_pairs={{0,1},{1,0},{2,3},{3,2},{4,5},{5,4},{6,7},{7,6},{8,9},{9,8},{10,11... | collective-permute-start | bytes 14155784 | tf_op jit(solution)/shard_map/ppermute | solution.py:220
  9.0 3.0 %fusion.18 = bf16[512,512]{1,0:T(8,128)(2,1)S(1)} fusion(bf16[1,2304,512]{2,1,0:T(8,128)(2,1)S(1)} %copy-done, bf16[1,512,2304]{2,1,0:T(8,128)(2,1)} %param.6, f32[512]{0:T(512)S(1)} %convert_bitcast_fusion, f32[512]{0:T(512)S(1)} %bitcast.41), kind=kOutput, calls=%fused_computation.6 | convolution fusion | flops 1209008128 | bytes 5246976 | tf_op jit(solution)/shard_map/dot_general | solution.py:211
  12.3 2.7 %collective-permute-start.4 = (bf16[256,512]{1,0:T(8,128)(2,1)S(1)}, bf16[256,512]{1,0:T(8,128)(2,1)S(1)}, u32[]{:S(2)}, u32[]{:S(2)}) collective-permute-start(bf16[256,512]{1,0:T(8,128)(2,1)S(1)} %get-tuple-element.42.refs_2_), channel_id=1, source_target_pairs={{0,96},{32,0},{64,32},{96,64},{1,97},{33,1},{65,33},{97,65},{2,98}... | collective-permute-start | bytes 786440 | tf_op jit(solution)/shard_map/ppermute | solution.py:223
  15.0 5.2 %collective-permute-start.14 = (bf16[256,512]{1,0:T(8,128)(2,1)S(1)}, bf16[256,512]{1,0:T(8,128)(2,1)S(1)}, u32[]{:S(2)}, u32[]{:S(2)}) collective-permute-start(bf16[256,512]{1,0:T(8,128)(2,1)S(1)} %get-tuple-element.42.refs_2_), channel_id=1, source_target_pairs={{0,128},{1,129},{2,130},{3,131},{4,132},{5,133},{6,134},{7,135},{8... | collective-permute-start | bytes 786440 | tf_op jit(solution)/shard_map/ppermute | solution.py:216
  20.2 2.3 %collective-permute-start.15 = (bf16[256,512]{1,0:T(8,128)(2,1)S(1)}, bf16[256,512]{1,0:T(8,128)(2,1)S(1)}, u32[]{:S(2)}, u32[]{:S(2)}) collective-permute-start(bf16[256,512]{1,0:T(8,128)(2,1)S(1)} %get-tuple-element.41), channel_id=1, source_target_pairs={{0,129},{1,128},{2,131},{3,130},{4,133},{5,132},{6,135},{7,134},{8... | collective-permute-start | bytes 786440 | tf_op jit(solution)/shard_map/ppermute | solution.py:217
  22.5 2.4 %collective-permute-start.5 = (bf16[256,512]{1,0:T(8,128)(2,1)S(1)}, bf16[256,512]{1,0:T(8,128)(2,1)S(1)}, u32[]{:S(2)}, u32[]{:S(2)}) collective-permute-start(bf16[256,512]{1,0:T(8,128)(2,1)S(1)} %collective-permute-done.1.refs_3_), channel_id=1, source_target_pairs={{0,96},{32,0},{64,32},{96,64},{1,97},{33,1},{65,33},{97,65},{2,98}... | collective-permute-start | bytes 786440 | tf_op jit(solution)/shard_map/ppermute | solution.py:223
  24.9 1.8 %collective-permute-done.14.refs_2_ = bf16[256,512]{1,0:T(8,128)(2,1)S(1)} collective-permute-done((bf16[256,512]{1,0:T(8,128)(2,1)S(1)}, bf16[256,512]{1,0:T(8,128)(2,1)S(1)}, u32[]{:S(2)}, u32[]{:S(2)}) %collective-permute-start.14) | collective-permute-done | bytes 262176 | tf_op jit(solution)/shard_map/ppermute | solution.py:216
  26.8 8.0 %collective-permute-done.15.refs_3_ = bf16[256,512]{1,0:T(8,128)(2,1)S(1)} collective-permute-done((bf16[256,512]{1,0:T(8,128)(2,1)S(1)}, bf16[256,512]{1,0:T(8,128)(2,1)S(1)}, u32[]{:S(2)}, u32[]{:S(2)}) %collective-permute-start.15) | collective-permute-done | bytes 262176 | tf_op jit(solution)/shard_map/ppermute | solution.py:217
  34.8 2.7 %collective-permute-start.19 = (bf16[256,512]{1,0:T(8,128)(2,1)S(1)}, bf16[256,512]{1,0:T(8,128)(2,1)S(1)}, u32[]{:S(2)}, u32[]{:S(2)}) collective-permute-start(bf16[256,512]{1,0:T(8,128)(2,1)S(1)} %collective-permute-done.15.refs_3_), channel_id=1, source_target_pairs={{0,96},{32,0},{64,32},{96,64},{1,97},{33,1},{65,33},{97,65},{2,98}... | collective-permute-start | bytes 786440 | tf_op jit(solution)/shard_map/ppermute | solution.py:223
  37.6 1.6 %collective-permute-done.6.refs_3_ = bf16[256,512]{1,0:T(8,128)(2,1)S(1)} collective-permute-done((bf16[256,512]{1,0:T(8,128)(2,1)S(1)}, bf16[256,512]{1,0:T(8,128)(2,1)S(1)}, u32[]{:S(2)}, u32[]{:S(2)}) %collective-permute-start.6) | collective-permute-done | bytes 262176 | tf_op jit(solution)/shard_map/ppermute | solution.py:223
  39.2 5.6 %collective-permute-done.16.refs_4_ = bf16[256,512]{1,0:T(8,128)(2,1)S(1)} collective-permute-done((bf16[256,512]{1,0:T(8,128)(2,1)S(1)}, bf16[256,512]{1,0:T(8,128)(2,1)S(1)}, u32[]{:S(2)}, u32[]{:S(2)}) %collective-permute-start.16) | collective-permute-done | bytes 262176 | tf_op jit(solution)/shard_map/ppermute | solution.py:223
  47.5 6.0 %shard_map.64.refs_2_ = f32[256,1152]{1,0:T(8,128)S(1)} custom-call(s32[5]{0:T(128)S(1)} %stack.23.at_ref, bf16[4,512,1152]{2,1,0:T(8,128)(2,1)} %cut.1.refs_0_, bf16[4,512,1152]{2,1,0:T(8,128)(2,1)} %collective-permute-done.refs_1_, bf16[256,512]{1,0:T(8,128)(2,1)S(1)} %get-tuple-element.42.refs_2_, bf16[256,512]{1,0:T(8,128)(2,1)S(1)} %collective-permute-done.1.refs_3_, ...), custom_call_target="tpu_custom_call" | custom-call | flops 1811939328 | bytes 11010068 | tf_op jit(solution)/shard_map/pallas_call | solution.py:49
  53.5 4.9 %shard_map.65 = (f32[4,72,256]{2,1,0:T(8,128)S(1)}, bf16[4,72,256]{2,1,0:T(8,128)(2,1)S(1)}, bf16[4,72,256]{2,1,0:T(8,128)(2,1)S(1)}, bf16[4,72,256]{2,1,0:T(8,128)(2,1)S(1)}) custom-call(s32[5]{0:T(128)S(1)} %stack.23.at_ref, bf16[4,512,1152]{2,1,0:T(8,128)(2,1)} %cut.1.refs_0_, bf16[4,512,1152]{2,1,0:T(8,128)(2,1)} %collective-permute-done.refs_1_, ...), custom_call_target="tpu_custom_call" | custom-call | flops 603979776 | bytes 11141140 | tf_op jit(solution)/shard_map/pallas_call | solution.py:49
  59.7 2.4 %collective-permute-start.9 = (bf16[4,72,256]{2,1,0:T(8,128)(2,1)S(1)}, bf16[4,72,256]{2,1,0:T(8,128)(2,1)S(1)}, u32[]{:S(2)}, u32[]{:S(2)}) collective-permute-start(bf16[4,72,256]{2,1,0:T(8,128)(2,1)S(1)} %get-tuple-element.25), channel_id=1, source_target_pairs={{0,4},{1,5},{2,6},{3,7},{4,0},{5,1},{6,2},{7,3},{8,12},{9,13},{10,... | collective-permute-start | bytes 442376 | tf_op jit(solution)/shard_map/ppermute | solution.py:241
  63.3 6.0 %shard_map.67.refs_2_ = f32[256,1152]{1,0:T(8,128)S(1)} custom-call(s32[5]{0:T(128)S(1)} %stack.23.at_ref, bf16[4,512,1152]{2,1,0:T(8,128)(2,1)} %cut.1.refs_0_, bf16[4,512,1152]{2,1,0:T(8,128)(2,1)} %collective-permute-done.refs_1_, bf16[256,512]{1,0:T(8,128)(2,1)S(1)} %collective-permute-done.14.refs_2_, ...), custom_call_target="tpu_custom_call" | custom-call | flops 1811939328 | bytes 11010068 | tf_op jit(solution)/shard_map/pallas_call | solution.py:49
  69.3 4.9 %shard_map.68 = (f32[4,72,256]{2,1,0:T(8,128)S(1)}, bf16[4,72,256]{2,1,0:T(8,128)(2,1)S(1)}, bf16[4,72,256]{2,1,0:T(8,128)(2,1)S(1)}, bf16[4,72,256]{2,1,0:T(8,128)(2,1)S(1)}) custom-call(s32[5]{0:T(128)S(1)} %stack.23.at_ref, bf16[4,512,1152]{2,1,0:T(8,128)(2,1)} %cut.1.refs_0_, bf16[4,512,1152]{2,1,0:T(8,128)(2,1)} %collective-permute-done.refs_1_, ...), custom_call_target="tpu_custom_call" | custom-call | flops 603979776 | bytes 11141140 | tf_op jit(solution)/shard_map/pallas_call | solution.py:49
  75.5 1.6 %collective-permute-start.24 = (bf16[4,72,256]{2,1,0:T(8,128)(2,1)S(1)}, bf16[4,72,256]{2,1,0:T(8,128)(2,1)S(1)}, u32[]{:S(2)}, u32[]{:S(2)}) collective-permute-start(bf16[4,72,256]{2,1,0:T(8,128)(2,1)S(1)} %get-tuple-element.34), channel_id=1, source_target_pairs={{0,6},{1,7},{2,0},{3,1},{4,2},{5,3},{6,4},{7,5},{8,14},{9,15},{10,... | collective-permute-start | bytes 442376 | tf_op jit(solution)/shard_map/ppermute | solution.py:241
  77.8 6.0 %collective-permute-start.11 = (bf16[72,256]{1,0:T(8,128)(2,1)S(1)}, bf16[72,256]{1,0:T(8,128)(2,1)S(1)}, u32[]{:S(2)}, u32[]{:S(2)}) collective-permute-start(bf16[72,256]{1,0:T(8,128)(2,1)S(1)} %get-tuple-element.28), channel_id=1, source_target_pairs={{0,24},{1,25},{2,26},{3,27},{4,28},{5,29},{6,30},{7,31},{8,16},{9,... | collective-permute-start | bytes 110600 | tf_op jit(solution)/shard_map/ppermute | solution.py:245
  83.8 4.2 %collective-permute-start.12 = (bf16[72,256]{1,0:T(8,128)(2,1)S(1)}, bf16[72,256]{1,0:T(8,128)(2,1)S(1)}, u32[]{:S(2)}, u32[]{:S(2)}) collective-permute-start(bf16[72,256]{1,0:T(8,128)(2,1)S(1)} %get-tuple-element.29), channel_id=1, source_target_pairs={{0,16},{1,17},{2,18},{3,19},{4,20},{5,21},{6,22},{7,23},{8,24},{9,... | collective-permute-start | bytes 110600 | tf_op jit(solution)/shard_map/ppermute | solution.py:245
  88.0 2.4 %collective-permute-start.13 = (bf16[72,256]{1,0:T(8,128)(2,1)S(1)}, bf16[72,256]{1,0:T(8,128)(2,1)S(1)}, u32[]{:S(2)}, u32[]{:S(2)}) collective-permute-start(bf16[72,256]{1,0:T(8,128)(2,1)S(1)} %get-tuple-element.30), channel_id=1, source_target_pairs={{0,8},{1,9},{2,10},{3,11},{4,12},{5,13},{6,14},{7,15},{8,0},{9,1},... | collective-permute-start | bytes 110600 | tf_op jit(solution)/shard_map/ppermute | solution.py:245
  91.0 1.5 %collective-permute-start.25 = (bf16[72,256]{1,0:T(8,128)(2,1)S(1)}, bf16[72,256]{1,0:T(8,128)(2,1)S(1)}, u32[]{:S(2)}, u32[]{:S(2)}) collective-permute-start(bf16[72,256]{1,0:T(8,128)(2,1)S(1)} %get-tuple-element.36), channel_id=1, source_target_pairs={{0,24},{1,25},{2,26},{3,27},{4,28},{5,29},{6,30},{7,31},{8,16},{9,... | collective-permute-start | bytes 110600 | tf_op jit(solution)/shard_map/ppermute | solution.py:245
  92.8 1.8 %collective-permute-start.27 = (bf16[72,256]{1,0:T(8,128)(2,1)S(1)}, bf16[72,256]{1,0:T(8,128)(2,1)S(1)}, u32[]{:S(2)}, u32[]{:S(2)}) collective-permute-start(bf16[72,256]{1,0:T(8,128)(2,1)S(1)} %get-tuple-element.38), channel_id=1, source_target_pairs={{0,8},{1,9},{2,10},{3,11},{4,12},{5,13},{6,14},{7,15},{8,0},{9,1},... | collective-permute-start | bytes 110600 | tf_op jit(solution)/shard_map/ppermute | solution.py:245
  97.2 5.4 %collective-permute-start.28 = (f32[2,36,256]{2,1,0:T(8,128)S(1)}, f32[2,36,256]{2,1,0:T(8,128)S(1)}, u32[]{:S(2)}, u32[]{:S(2)}) collective-permute-start(f32[2,36,256]{2,1,0:T(8,128)S(1)} %get-tuple-element.40), channel_id=1, source_target_pairs={{0,1},{1,0},{2,3},{3,2},{4,5},{5,4},{6,7},{7,6},{8,9},{9,8},{10,11... | collective-permute-start | bytes 221192 | tf_op jit(solution)/shard_map/ppermute | solution.py:247
  (58 shorter events, 13.3 us)
Async XLA Ops:
  5.6 40.6 %collective-permute-start = (bf16[4,512,1152]{2,1,0:T(8,128)(2,1)}, bf16[4,512,1152]{2,1,0:T(8,128)(2,1)}, u32[]{:S(2)}, u32[]{:S(2)}) collective-permute-start(bf16[4,512,1152]{2,1,0:T(8,128)(2,1)} %cut.1.refs_0_), channel_id=1, source_target_pairs={{0,1},{1,0},{2,3},{3,2},{4,5},{5,4},{6,7},{7,6},{8,9},{9,8},{10,11... | collective-permute-start | bytes 14155784 | tf_op jit(solution)/shard_map/ppermute | solution.py:220
  12.1 8.1 %collective-permute-start.1 = (bf16[256,512]{1,0:T(8,128)(2,1)S(1)}, bf16[256,512]{1,0:T(8,128)(2,1)S(1)}, u32[]{:S(2)}, u32[]{:S(2)}) collective-permute-start(bf16[256,512]{1,0:T(8,128)(2,1)S(1)} %get-tuple-element.41), channel_id=1, source_target_pairs={{0,1},{1,0},{2,3},{3,2},{4,5},{5,4},{6,7},{7,6},{8,9},{9,8},{10,11... | collective-permute-start | bytes 786440 | tf_op jit(solution)/shard_map/ppermute | solution.py:218
  12.2 10.3 %collective-permute-start.2 = (bf16[256,512]{1,0:T(8,128)(2,1)S(1)}, bf16[256,512]{1,0:T(8,128)(2,1)S(1)}, u32[]{:S(2)}, u32[]{:S(2)}) collective-permute-start(bf16[256,512]{1,0:T(8,128)(2,1)S(1)} %get-tuple-element.42.refs_2_), channel_id=1, source_target_pairs={{0,32},{32,64},{64,96},{96,0},{1,33},{33,65},{65,97},{97,1},{2,34}... | collective-permute-start | bytes 786440 | tf_op jit(solution)/shard_map/ppermute | solution.py:223
  12.3 12.6 %collective-permute-start.4 = (bf16[256,512]{1,0:T(8,128)(2,1)S(1)}, bf16[256,512]{1,0:T(8,128)(2,1)S(1)}, u32[]{:S(2)}, u32[]{:S(2)}) collective-permute-start(bf16[256,512]{1,0:T(8,128)(2,1)S(1)} %get-tuple-element.42.refs_2_), channel_id=1, source_target_pairs={{0,96},{32,0},{64,32},{96,64},{1,97},{33,1},{65,33},{97,65},{2,98}... | collective-permute-start | bytes 786440 | tf_op jit(solution)/shard_map/ppermute | solution.py:223
  15.0 11.8 %collective-permute-start.14 = (bf16[256,512]{1,0:T(8,128)(2,1)S(1)}, bf16[256,512]{1,0:T(8,128)(2,1)S(1)}, u32[]{:S(2)}, u32[]{:S(2)}) collective-permute-start(bf16[256,512]{1,0:T(8,128)(2,1)S(1)} %get-tuple-element.42.refs_2_), channel_id=1, source_target_pairs={{0,128},{1,129},{2,130},{3,131},{4,132},{5,133},{6,134},{7,135},{8... | collective-permute-start | bytes 786440 | tf_op jit(solution)/shard_map/ppermute | solution.py:216
  20.2 14.6 %collective-permute-start.15 = (bf16[256,512]{1,0:T(8,128)(2,1)S(1)}, bf16[256,512]{1,0:T(8,128)(2,1)S(1)}, u32[]{:S(2)}, u32[]{:S(2)}) collective-permute-start(bf16[256,512]{1,0:T(8,128)(2,1)S(1)} %get-tuple-element.41), channel_id=1, source_target_pairs={{0,129},{1,128},{2,131},{3,130},{4,133},{5,132},{6,135},{7,134},{8... | collective-permute-start | bytes 786440 | tf_op jit(solution)/shard_map/ppermute | solution.py:217
  22.5 12.3 %collective-permute-start.5 = (bf16[256,512]{1,0:T(8,128)(2,1)S(1)}, bf16[256,512]{1,0:T(8,128)(2,1)S(1)}, u32[]{:S(2)}, u32[]{:S(2)}) collective-permute-start(bf16[256,512]{1,0:T(8,128)(2,1)S(1)} %collective-permute-done.1.refs_3_), channel_id=1, source_target_pairs={{0,96},{32,0},{64,32},{96,64},{1,97},{33,1},{65,33},{97,65},{2,98}... | collective-permute-start | bytes 786440 | tf_op jit(solution)/shard_map/ppermute | solution.py:223
  24.9 12.6 %collective-permute-start.3 = (bf16[256,512]{1,0:T(8,128)(2,1)S(1)}, bf16[256,512]{1,0:T(8,128)(2,1)S(1)}, u32[]{:S(2)}, u32[]{:S(2)}) collective-permute-start(bf16[256,512]{1,0:T(8,128)(2,1)S(1)} %collective-permute-done.1.refs_3_), channel_id=1, source_target_pairs={{0,32},{32,64},{64,96},{96,0},{1,33},{33,65},{65,97},{97,1},{2,34}... | collective-permute-start | bytes 786440 | tf_op jit(solution)/shard_map/ppermute | solution.py:223
  26.8 12.4 %collective-permute-start.6 = (bf16[256,512]{1,0:T(8,128)(2,1)S(1)}, bf16[256,512]{1,0:T(8,128)(2,1)S(1)}, u32[]{:S(2)}, u32[]{:S(2)}) collective-permute-start(bf16[256,512]{1,0:T(8,128)(2,1)S(1)} %broadcast_maximum_fusion.1), channel_id=1, source_target_pairs={{0,32},{32,64},{64,96},{96,0},{1,33},{33,65},{65,97},{97,1},{2,34}... | collective-permute-start | bytes 786440 | tf_op jit(solution)/shard_map/ppermute | solution.py:223
  34.8 10.0 %collective-permute-start.16 = (bf16[256,512]{1,0:T(8,128)(2,1)S(1)}, bf16[256,512]{1,0:T(8,128)(2,1)S(1)}, u32[]{:S(2)}, u32[]{:S(2)}) collective-permute-start(bf16[256,512]{1,0:T(8,128)(2,1)S(1)} %collective-permute-done.14.refs_2_), channel_id=1, source_target_pairs={{0,32},{32,64},{64,96},{96,0},{1,33},{33,65},{65,97},{97,1},{2,34}... | collective-permute-start | bytes 786440 | tf_op jit(solution)/shard_map/ppermute | solution.py:223
  34.8 10.0 %collective-permute-start.19 = (bf16[256,512]{1,0:T(8,128)(2,1)S(1)}, bf16[256,512]{1,0:T(8,128)(2,1)S(1)}, u32[]{:S(2)}, u32[]{:S(2)}) collective-permute-start(bf16[256,512]{1,0:T(8,128)(2,1)S(1)} %collective-permute-done.15.refs_3_), channel_id=1, source_target_pairs={{0,96},{32,0},{64,32},{96,64},{1,97},{33,1},{65,33},{97,65},{2,98}... | collective-permute-start | bytes 786440 | tf_op jit(solution)/shard_map/ppermute | solution.py:223
  37.5 16.0 %collective-permute-start.7 = (bf16[256,512]{1,0:T(8,128)(2,1)S(1)}, bf16[256,512]{1,0:T(8,128)(2,1)S(1)}, u32[]{:S(2)}, u32[]{:S(2)}) collective-permute-start(bf16[256,512]{1,0:T(8,128)(2,1)S(1)} %broadcast_maximum_fusion), channel_id=1, source_target_pairs={{0,96},{32,0},{64,32},{96,64},{1,97},{33,1},{65,33},{97,65},{2,98}... | collective-permute-start | bytes 786440 | tf_op jit(solution)/shard_map/ppermute | solution.py:223
  39.2 20.5 %collective-permute-start.17 = (bf16[256,512]{1,0:T(8,128)(2,1)S(1)}, bf16[256,512]{1,0:T(8,128)(2,1)S(1)}, u32[]{:S(2)}, u32[]{:S(2)}) collective-permute-start(bf16[256,512]{1,0:T(8,128)(2,1)S(1)} %collective-permute-done.15.refs_3_), channel_id=1, source_target_pairs={{0,32},{32,64},{64,96},{96,0},{1,33},{33,65},{65,97},{97,1},{2,34}... | collective-permute-start | bytes 786440 | tf_op jit(solution)/shard_map/ppermute | solution.py:223
  44.8 17.4 %collective-permute-start.18 = (bf16[256,512]{1,0:T(8,128)(2,1)S(1)}, bf16[256,512]{1,0:T(8,128)(2,1)S(1)}, u32[]{:S(2)}, u32[]{:S(2)}) collective-permute-start(bf16[256,512]{1,0:T(8,128)(2,1)S(1)} %collective-permute-done.14.refs_2_), channel_id=1, source_target_pairs={{0,96},{32,0},{64,32},{96,64},{1,97},{33,1},{65,33},{97,65},{2,98}... | collective-permute-start | bytes 786440 | tf_op jit(solution)/shard_map/ppermute | solution.py:223
  44.8 24.5 %collective-permute-start.20 = (bf16[256,512]{1,0:T(8,128)(2,1)S(1)}, bf16[256,512]{1,0:T(8,128)(2,1)S(1)}, u32[]{:S(2)}, u32[]{:S(2)}) collective-permute-start(bf16[256,512]{1,0:T(8,128)(2,1)S(1)} %collective-permute-done.16.refs_4_), channel_id=1, source_target_pairs={{0,32},{32,64},{64,96},{96,0},{1,33},{33,65},{65,97},{97,1},{2,34}... | collective-permute-start | bytes 786440 | tf_op jit(solution)/shard_map/ppermute | solution.py:223
  46.3 23.1 %collective-permute-start.21 = (bf16[256,512]{1,0:T(8,128)(2,1)S(1)}, bf16[256,512]{1,0:T(8,128)(2,1)S(1)}, u32[]{:S(2)}, u32[]{:S(2)}) collective-permute-start(bf16[256,512]{1,0:T(8,128)(2,1)S(1)} %collective-permute-done.19.refs_7_), channel_id=1, source_target_pairs={{0,96},{32,0},{64,32},{96,64},{1,97},{33,1},{65,33},{97,65},{2,98}... | collective-permute-start | bytes 786440 | tf_op jit(solution)/shard_map/ppermute | solution.py:223
  58.4 17.1 %collective-permute-start.8 = (bf16[4,72,256]{2,1,0:T(8,128)(2,1)S(1)}, bf16[4,72,256]{2,1,0:T(8,128)(2,1)S(1)}, u32[]{:S(2)}, u32[]{:S(2)}) collective-permute-start(bf16[4,72,256]{2,1,0:T(8,128)(2,1)S(1)} %get-tuple-element.24), channel_id=1, source_target_pairs={{0,2},{1,3},{2,4},{3,5},{4,6},{5,7},{6,0},{7,1},{8,10},{9,11},{10,... | collective-permute-start | bytes 442376 | tf_op jit(solution)/shard_map/ppermute | solution.py:241
  59.7 17.4 %collective-permute-start.9 = (bf16[4,72,256]{2,1,0:T(8,128)(2,1)S(1)}, bf16[4,72,256]{2,1,0:T(8,128)(2,1)S(1)}, u32[]{:S(2)}, u32[]{:S(2)}) collective-permute-start(bf16[4,72,256]{2,1,0:T(8,128)(2,1)S(1)} %get-tuple-element.25), channel_id=1, source_target_pairs={{0,4},{1,5},{2,6},{3,7},{4,0},{5,1},{6,2},{7,3},{8,12},{9,13},{10,... | collective-permute-start | bytes 442376 | tf_op jit(solution)/shard_map/ppermute | solution.py:241
  62.1 15.0 %collective-permute-start.10 = (bf16[4,72,256]{2,1,0:T(8,128)(2,1)S(1)}, bf16[4,72,256]{2,1,0:T(8,128)(2,1)S(1)}, u32[]{:S(2)}, u32[]{:S(2)}) collective-permute-start(bf16[4,72,256]{2,1,0:T(8,128)(2,1)S(1)} %get-tuple-element.26), channel_id=1, source_target_pairs={{0,6},{1,7},{2,0},{3,1},{4,2},{5,3},{6,4},{7,5},{8,14},{9,15},{10,... | collective-permute-start | bytes 442376 | tf_op jit(solution)/shard_map/ppermute | solution.py:241
  74.2 13.8 %collective-permute-start.22 = (bf16[4,72,256]{2,1,0:T(8,128)(2,1)S(1)}, bf16[4,72,256]{2,1,0:T(8,128)(2,1)S(1)}, u32[]{:S(2)}, u32[]{:S(2)}) collective-permute-start(bf16[4,72,256]{2,1,0:T(8,128)(2,1)S(1)} %get-tuple-element.32), channel_id=1, source_target_pairs={{0,2},{1,3},{2,4},{3,5},{4,6},{5,7},{6,0},{7,1},{8,10},{9,11},{10,... | collective-permute-start | bytes 442376 | tf_op jit(solution)/shard_map/ppermute | solution.py:241
  74.6 15.8 %collective-permute-start.23 = (bf16[4,72,256]{2,1,0:T(8,128)(2,1)S(1)}, bf16[4,72,256]{2,1,0:T(8,128)(2,1)S(1)}, u32[]{:S(2)}, u32[]{:S(2)}) collective-permute-start(bf16[4,72,256]{2,1,0:T(8,128)(2,1)S(1)} %get-tuple-element.33), channel_id=1, source_target_pairs={{0,4},{1,5},{2,6},{3,7},{4,0},{5,1},{6,2},{7,3},{8,12},{9,13},{10,... | collective-permute-start | bytes 442376 | tf_op jit(solution)/shard_map/ppermute | solution.py:241
  75.5 14.9 %collective-permute-start.24 = (bf16[4,72,256]{2,1,0:T(8,128)(2,1)S(1)}, bf16[4,72,256]{2,1,0:T(8,128)(2,1)S(1)}, u32[]{:S(2)}, u32[]{:S(2)}) collective-permute-start(bf16[4,72,256]{2,1,0:T(8,128)(2,1)S(1)} %get-tuple-element.34), channel_id=1, source_target_pairs={{0,6},{1,7},{2,0},{3,1},{4,2},{5,3},{6,4},{7,5},{8,14},{9,15},{10,... | collective-permute-start | bytes 442376 | tf_op jit(solution)/shard_map/ppermute | solution.py:241
  77.8 15.1 %collective-permute-start.11 = (bf16[72,256]{1,0:T(8,128)(2,1)S(1)}, bf16[72,256]{1,0:T(8,128)(2,1)S(1)}, u32[]{:S(2)}, u32[]{:S(2)}) collective-permute-start(bf16[72,256]{1,0:T(8,128)(2,1)S(1)} %get-tuple-element.28), channel_id=1, source_target_pairs={{0,24},{1,25},{2,26},{3,27},{4,28},{5,29},{6,30},{7,31},{8,16},{9,... | collective-permute-start | bytes 110600 | tf_op jit(solution)/shard_map/ppermute | solution.py:245
  83.8 10.9 %collective-permute-start.12 = (bf16[72,256]{1,0:T(8,128)(2,1)S(1)}, bf16[72,256]{1,0:T(8,128)(2,1)S(1)}, u32[]{:S(2)}, u32[]{:S(2)}) collective-permute-start(bf16[72,256]{1,0:T(8,128)(2,1)S(1)} %get-tuple-element.29), channel_id=1, source_target_pairs={{0,16},{1,17},{2,18},{3,19},{4,20},{5,21},{6,22},{7,23},{8,24},{9,... | collective-permute-start | bytes 110600 | tf_op jit(solution)/shard_map/ppermute | solution.py:245
  (9 other events, 85.7 us)

commit v14 on v12

--- a/solution.py
+++ b/solution.py
@@ -238,7 +238,10 @@
         if name == "own":
             ahead = jnp.maximum(up_mine, 0)
             onward = ahead, jnp.maximum(down_theirs, 0)
-        far = [shift(onward[0], 1), shift(onward[1], -1)]
+        if name == "own":
+            far = [shift(onward[0], 1), shift(onward[1], -1)]
+        else:
+            far = [shift(down_mine, -1), shift(up_theirs, 1)]
         near = [mine, theirs, up_mine, up_theirs, down_mine, down_theirs]
         blocks[name] = decode(at, weights, near, far)
 
@@ -251,7 +254,7 @@
         else:
             kept, *away = x_cut(at, before, kept, came)
     came = []
-    for k in (3, 2, 1):
+    for k in (2, 3, 1):
         came.append(lax.ppermute(away[k - 1], "feat", z_pairs(k)))
     mine, away = z_sum(at, kept, came)
     came = lax.ppermute(away, "feat", PARTNER)

time: 104 us -> 106 us (1.019)
  the two profiles are of different devices: /device:TPU:1 before, /device:TPU:24 now
where the time goes in v14:
time: 106 us; the launch traced here: 105 us
  starting transfers between devices  48.5 us (46%)
  Pallas kernels  30 us (28%)
  waiting for transfers between devices  22.8 us (22%)
  matrix products  3.05 us (3%)
    pallas_call x8, Pallas kernels, call(): pl.pallas_call(kernel, out_shape=out_shape, in_specs=[IN_SMEM] + [IN_VMEM...  24.8 us
    ppermute x12, starting transfers between devices, shift(): return lax.ppermute(array, 'layer', ring(by))  17.5 us
    ppermute x3, starting transfers between devices, per_device(): came.append(lax.ppermute(away[k - 1], 'feat', z_pairs(k)))  11.8 us
    ppermute x6, starting transfers between devices, per_device(): came.append(lax.ppermute(piece, 'feat', x_pairs(by + 1)))  9.18 us
    ppermute x1, starting transfers between devices, per_device(): other_mine = lax.ppermute(keep, ('dp', 'feat'), across(0))  6.91 us
    ppermute x12, waiting for transfers between devices, shift(): return lax.ppermute(array, 'layer', ring(by))  5.31 us
    pallas_call x1, Pallas kernels, cut(): pl.pallas_call(cut_kernel, out_shape=jax.ShapeDtypeStruct(decoders.shape[...  5.16 us
    ppermute x3, waiting for transfers between devices, per_device(): came.append(lax.ppermute(away[k - 1], 'feat', z_pairs(k)))  5.14 us
  transfers between devices with their start and end apart: 26, of which 11 were waited for; matrix products, arithmetic and copies ran while one was open for 3% of the time, Pallas kernels for 21%

profile of v14, /device:TPU:24, one launch (start us, length us, event | category | flops | bytes accessed | tf_op | source)
XLA Modules:
  0.0 104.8 jit_solution(6640001632682495862)
XLA Ops:
  0.1 5.2 %cut.1.refs_0_ = bf16[4,512,1152]{2,1,0:T(8,128)(2,1)} custom-call(s32[5]{0:T(128)S(1)} %stack.23.at_ref, bf16[1,4,512,1152]{3,2,1,0:T(8,128)(2,1)} %decoders_ref.1), custom_call_target="tpu_custom_call" | custom-call | bytes 4718592 | tf_op jit(solution)/shard_map/cut/pallas_call | solution.py:91
  5.5 3.0 %fusion.18 = bf16[512,512]{1,0:T(8,128)(2,1)S(1)} fusion(bf16[1,2304,512]{2,1,0:T(8,128)(2,1)S(1)} %copy-done, bf16[1,512,2304]{2,1,0:T(8,128)(2,1)} %param.6, f32[512]{0:T(512)S(1)} %convert_bitcast_fusion, f32[512]{0:T(512)S(1)} %bitcast.41), kind=kOutput, calls=%fused_computation.6 | convolution fusion | flops 1209008128 | bytes 5246976 | tf_op jit(solution)/shard_map/dot_general | solution.py:219
  9.1 2.3 %collective-permute-start.2 = (bf16[256,512]{1,0:T(8,128)(2,1)S(1)}, bf16[256,512]{1,0:T(8,128)(2,1)S(1)}, u32[]{:S(2)}, u32[]{:S(2)}) collective-permute-start(bf16[256,512]{1,0:T(8,128)(2,1)S(1)} %get-tuple-element.34.refs_2_), channel_id=1, source_target_pairs={{0,32},{32,64},{64,96},{96,0},{1,33},{33,65},{65,97},{97,1},{2,34}... | collective-permute-start | bytes 786440 | tf_op jit(solution)/shard_map/ppermute | solution.py:231
  11.4 6.9 %collective-permute-start.11 = (bf16[256,512]{1,0:T(8,128)(2,1)S(1)}, bf16[256,512]{1,0:T(8,128)(2,1)S(1)}, u32[]{:S(2)}, u32[]{:S(2)}) collective-permute-start(bf16[256,512]{1,0:T(8,128)(2,1)S(1)} %get-tuple-element.34.refs_2_), channel_id=1, source_target_pairs={{0,128},{1,129},{2,130},{3,131},{4,132},{5,133},{6,134},{7,135},{8... | collective-permute-start | bytes 786440 | tf_op jit(solution)/shard_map/ppermute | solution.py:224
  18.4 2.4 %collective-permute-start.12 = (bf16[256,512]{1,0:T(8,128)(2,1)S(1)}, bf16[256,512]{1,0:T(8,128)(2,1)S(1)}, u32[]{:S(2)}, u32[]{:S(2)}) collective-permute-start(bf16[256,512]{1,0:T(8,128)(2,1)S(1)} %get-tuple-element.33), channel_id=1, source_target_pairs={{0,129},{1,128},{2,131},{3,130},{4,133},{5,132},{6,135},{7,134},{8... | collective-permute-start | bytes 786440 | tf_op jit(solution)/shard_map/ppermute | solution.py:225
  21.6 2.4 %collective-permute-start.3 = (bf16[256,512]{1,0:T(8,128)(2,1)S(1)}, bf16[256,512]{1,0:T(8,128)(2,1)S(1)}, u32[]{:S(2)}, u32[]{:S(2)}) collective-permute-start(bf16[256,512]{1,0:T(8,128)(2,1)S(1)} %collective-permute-done.1.refs_3_), channel_id=1, source_target_pairs={{0,32},{32,64},{64,96},{96,0},{1,33},{33,65},{65,97},{97,1},{2,34}... | collective-permute-start | bytes 786440 | tf_op jit(solution)/shard_map/ppermute | solution.py:231
  24.0 2.1 %collective-permute-done.11.refs_2_ = bf16[256,512]{1,0:T(8,128)(2,1)S(1)} collective-permute-done((bf16[256,512]{1,0:T(8,128)(2,1)S(1)}, bf16[256,512]{1,0:T(8,128)(2,1)S(1)}, u32[]{:S(2)}, u32[]{:S(2)}) %collective-permute-start.11) | collective-permute-done | bytes 262176 | tf_op jit(solution)/shard_map/ppermute | solution.py:224
  26.1 1.8 %collective-permute-start.6 = (bf16[256,512]{1,0:T(8,128)(2,1)S(1)}, bf16[256,512]{1,0:T(8,128)(2,1)S(1)}, u32[]{:S(2)}, u32[]{:S(2)}) collective-permute-start(bf16[256,512]{1,0:T(8,128)(2,1)S(1)} %broadcast_maximum_fusion.1), channel_id=1, source_target_pairs={{0,32},{32,64},{64,96},{96,0},{1,33},{33,65},{65,97},{97,1},{2,34}... | collective-permute-start | bytes 786440 | tf_op jit(solution)/shard_map/ppermute | solution.py:231
  27.9 4.2 %collective-permute-done.12.refs_3_ = bf16[256,512]{1,0:T(8,128)(2,1)S(1)} collective-permute-done((bf16[256,512]{1,0:T(8,128)(2,1)S(1)}, bf16[256,512]{1,0:T(8,128)(2,1)S(1)}, u32[]{:S(2)}, u32[]{:S(2)}) %collective-permute-start.12) | collective-permute-done | bytes 262176 | tf_op jit(solution)/shard_map/ppermute | solution.py:225
  32.1 1.8 %collective-permute-start.14 = (bf16[256,512]{1,0:T(8,128)(2,1)S(1)}, bf16[256,512]{1,0:T(8,128)(2,1)S(1)}, u32[]{:S(2)}, u32[]{:S(2)}) collective-permute-start(bf16[256,512]{1,0:T(8,128)(2,1)S(1)} %collective-permute-done.12.refs_3_), channel_id=1, source_target_pairs={{0,32},{32,64},{64,96},{96,0},{1,33},{33,65},{65,97},{97,1},{2,34}... | collective-permute-start | bytes 786440 | tf_op jit(solution)/shard_map/ppermute | solution.py:231
  36.3 3.7 %collective-permute-start.13 = (bf16[256,512]{1,0:T(8,128)(2,1)S(1)}, bf16[256,512]{1,0:T(8,128)(2,1)S(1)}, u32[]{:S(2)}, u32[]{:S(2)}) collective-permute-start(bf16[256,512]{1,0:T(8,128)(2,1)S(1)} %collective-permute-done.11.refs_2_), channel_id=1, source_target_pairs={{0,32},{32,64},{64,96},{96,0},{1,33},{33,65},{65,97},{97,1},{2,34}... | collective-permute-start | bytes 786440 | tf_op jit(solution)/shard_map/ppermute | solution.py:231
  40.0 1.9 %collective-permute-done.14.refs_5_ = bf16[256,512]{1,0:T(8,128)(2,1)S(1)} collective-permute-done((bf16[256,512]{1,0:T(8,128)(2,1)S(1)}, bf16[256,512]{1,0:T(8,128)(2,1)S(1)}, u32[]{:S(2)}, u32[]{:S(2)}) %collective-permute-start.14) | collective-permute-done | bytes 262176 | tf_op jit(solution)/shard_map/ppermute | solution.py:231
  42.2 2.1 %collective-permute-done.15.refs_6_ = bf16[256,512]{1,0:T(8,128)(2,1)S(1)} collective-permute-done((bf16[256,512]{1,0:T(8,128)(2,1)S(1)}, bf16[256,512]{1,0:T(8,128)(2,1)S(1)}, u32[]{:S(2)}, u32[]{:S(2)}) %collective-permute-start.15) | collective-permute-done | bytes 262176 | tf_op jit(solution)/shard_map/ppermute | solution.py:231
  44.3 3.2 %collective-permute-start.18 = (bf16[256,512]{1,0:T(8,128)(2,1)S(1)}, bf16[256,512]{1,0:T(8,128)(2,1)S(1)}, u32[]{:S(2)}, u32[]{:S(2)}) collective-permute-start(bf16[256,512]{1,0:T(8,128)(2,1)S(1)} %collective-permute-done.14.refs_5_), channel_id=1, source_target_pairs={{0,32},{32,64},{64,96},{96,0},{1,33},{33,65},{65,97},{97,1},{2,34}... | collective-permute-start | bytes 786440 | tf_op jit(solution)/shard_map/ppermute | solution.py:231
  47.6 6.0 %shard_map.64.refs_2_ = f32[256,1152]{1,0:T(8,128)S(1)} custom-call(s32[5]{0:T(128)S(1)} %stack.23.at_ref, bf16[4,512,1152]{2,1,0:T(8,128)(2,1)} %cut.1.refs_0_, bf16[4,512,1152]{2,1,0:T(8,128)(2,1)} %collective-permute-done.refs_1_, bf16[256,512]{1,0:T(8,128)(2,1)S(1)} %get-tuple-element.34.refs_2_, bf16[256,512]{1,0:T(8,128)(2,1)S(1)} %collective-permute-done.1.refs_3_, ...), custom_call_target="tpu_custom_call" | custom-call | flops 1811939328 | bytes 11010068 | tf_op jit(solution)/shard_map/pallas_call | solution.py:49
  53.6 4.9 %shard_map.65 = (f32[4,72,256]{2,1,0:T(8,128)S(1)}, bf16[4,72,256]{2,1,0:T(8,128)(2,1)S(1)}, bf16[4,72,256]{2,1,0:T(8,128)(2,1)S(1)}, bf16[4,72,256]{2,1,0:T(8,128)(2,1)S(1)}) custom-call(s32[5]{0:T(128)S(1)} %stack.23.at_ref, bf16[4,512,1152]{2,1,0:T(8,128)(2,1)} %cut.1.refs_0_, bf16[4,512,1152]{2,1,0:T(8,128)(2,1)} %collective-permute-done.refs_1_, ...), custom_call_target="tpu_custom_call" | custom-call | flops 603979776 | bytes 11141140 | tf_op jit(solution)/shard_map/pallas_call | solution.py:49
  58.4 1.6 %collective-permute-start.8 = (bf16[4,72,256]{2,1,0:T(8,128)(2,1)S(1)}, bf16[4,72,256]{2,1,0:T(8,128)(2,1)S(1)}, u32[]{:S(2)}, u32[]{:S(2)}) collective-permute-start(bf16[4,72,256]{2,1,0:T(8,128)(2,1)S(1)} %get-tuple-element.20), channel_id=1, source_target_pairs={{0,2},{1,3},{2,4},{3,5},{4,6},{5,7},{6,0},{7,1},{8,10},{9,11},{10,... | collective-permute-start | bytes 442376 | tf_op jit(solution)/shard_map/ppermute | solution.py:251
  60.0 2.7 %collective-permute-start.9 = (bf16[4,72,256]{2,1,0:T(8,128)(2,1)S(1)}, bf16[4,72,256]{2,1,0:T(8,128)(2,1)S(1)}, u32[]{:S(2)}, u32[]{:S(2)}) collective-permute-start(bf16[4,72,256]{2,1,0:T(8,128)(2,1)S(1)} %get-tuple-element.21), channel_id=1, source_target_pairs={{0,4},{1,5},{2,6},{3,7},{4,0},{5,1},{6,2},{7,3},{8,12},{9,13},{10,... | collective-permute-start | bytes 442376 | tf_op jit(solution)/shard_map/ppermute | solution.py:251
  64.2 6.0 %shard_map.67.refs_2_ = f32[256,1152]{1,0:T(8,128)S(1)} custom-call(s32[5]{0:T(128)S(1)} %stack.23.at_ref, bf16[4,512,1152]{2,1,0:T(8,128)(2,1)} %cut.1.refs_0_, bf16[4,512,1152]{2,1,0:T(8,128)(2,1)} %collective-permute-done.refs_1_, bf16[256,512]{1,0:T(8,128)(2,1)S(1)} %collective-permute-done.11.refs_2_, ...), custom_call_target="tpu_custom_call" | custom-call | flops 1811939328 | bytes 11010068 | tf_op jit(solution)/shard_map/pallas_call | solution.py:49
  70.2 4.9 %shard_map.68 = (f32[4,72,256]{2,1,0:T(8,128)S(1)}, bf16[4,72,256]{2,1,0:T(8,128)(2,1)S(1)}, bf16[4,72,256]{2,1,0:T(8,128)(2,1)S(1)}, bf16[4,72,256]{2,1,0:T(8,128)(2,1)S(1)}) custom-call(s32[5]{0:T(128)S(1)} %stack.23.at_ref, bf16[4,512,1152]{2,1,0:T(8,128)(2,1)} %cut.1.refs_0_, bf16[4,512,1152]{2,1,0:T(8,128)(2,1)} %collective-permute-done.refs_1_, ...), custom_call_target="tpu_custom_call" | custom-call | flops 603979776 | bytes 11141140 | tf_op jit(solution)/shard_map/pallas_call | solution.py:49
  76.6 1.9 %collective-permute-start.21 = (bf16[4,72,256]{2,1,0:T(8,128)(2,1)S(1)}, bf16[4,72,256]{2,1,0:T(8,128)(2,1)S(1)}, u32[]{:S(2)}, u32[]{:S(2)}) collective-permute-start(bf16[4,72,256]{2,1,0:T(8,128)(2,1)S(1)} %get-tuple-element.26), channel_id=1, source_target_pairs={{0,6},{1,7},{2,0},{3,1},{4,2},{5,3},{6,4},{7,5},{8,14},{9,15},{10,... | collective-permute-start | bytes 442376 | tf_op jit(solution)/shard_map/ppermute | solution.py:251
  79.2 4.0 %collective-permute-done.19.refs_1_ = bf16[4,72,256]{2,1,0:T(8,128)(2,1)S(1)} collective-permute-done((bf16[4,72,256]{2,1,0:T(8,128)(2,1)S(1)}, bf16[4,72,256]{2,1,0:T(8,128)(2,1)S(1)}, u32[]{:S(2)}, u32[]{:S(2)}) %collective-permute-start.19) | collective-permute-done | bytes 147488 | tf_op jit(solution)/shard_map/ppermute | solution.py:251
  84.7 10.3 %collective-permute-start.22 = (bf16[2,72,256]{2,1,0:T(8,128)(2,1)S(1)}, bf16[2,72,256]{2,1,0:T(8,128)(2,1)S(1)}, u32[]{:S(2)}, u32[]{:S(2)}) collective-permute-start(bf16[2,72,256]{2,1,0:T(8,128)(2,1)S(1)} %get-tuple-element.28), channel_id=1, source_target_pairs={{0,16},{1,17},{2,18},{3,19},{4,20},{5,21},{6,22},{7,23},{8,24},{9,... | collective-permute-start | bytes 221192 | tf_op jit(solution)/shard_map/ppermute | solution.py:258
  97.3 3.9 %collective-permute-done.23.b_ref = bf16[2,72,256]{2,1,0:T(8,128)(2,1)S(1)} collective-permute-done((bf16[2,72,256]{2,1,0:T(8,128)(2,1)S(1)}, bf16[2,72,256]{2,1,0:T(8,128)(2,1)S(1)}, u32[]{:S(2)}, u32[]{:S(2)}) %collective-permute-start.23) | collective-permute-done | bytes 73760 | tf_op jit(solution)/shard_map/ppermute | solution.py:258
  (52 shorter events, 15.4 us)
Async XLA Ops:
  5.3 39.1 %collective-permute-start = (bf16[4,512,1152]{2,1,0:T(8,128)(2,1)}, bf16[4,512,1152]{2,1,0:T(8,128)(2,1)}, u32[]{:S(2)}, u32[]{:S(2)}) collective-permute-start(bf16[4,512,1152]{2,1,0:T(8,128)(2,1)} %cut.1.refs_0_), channel_id=1, source_target_pairs={{0,1},{1,0},{2,3},{3,2},{4,5},{5,4},{6,7},{7,6},{8,9},{9,8},{10,11... | collective-permute-start | bytes 14155784 | tf_op jit(solution)/shard_map/ppermute | solution.py:228
  8.6 9.8 %collective-permute-start.1 = (bf16[256,512]{1,0:T(8,128)(2,1)S(1)}, bf16[256,512]{1,0:T(8,128)(2,1)S(1)}, u32[]{:S(2)}, u32[]{:S(2)}) collective-permute-start(bf16[256,512]{1,0:T(8,128)(2,1)S(1)} %get-tuple-element.33), channel_id=1, source_target_pairs={{0,1},{1,0},{2,3},{3,2},{4,5},{5,4},{6,7},{7,6},{8,9},{9,8},{10,11... | collective-permute-start | bytes 786440 | tf_op jit(solution)/shard_map/ppermute | solution.py:226
  9.1 11.6 %collective-permute-start.2 = (bf16[256,512]{1,0:T(8,128)(2,1)S(1)}, bf16[256,512]{1,0:T(8,128)(2,1)S(1)}, u32[]{:S(2)}, u32[]{:S(2)}) collective-permute-start(bf16[256,512]{1,0:T(8,128)(2,1)S(1)} %get-tuple-element.34.refs_2_), channel_id=1, source_target_pairs={{0,32},{32,64},{64,96},{96,0},{1,33},{33,65},{65,97},{97,1},{2,34}... | collective-permute-start | bytes 786440 | tf_op jit(solution)/shard_map/ppermute | solution.py:231
  11.4 10.2 %collective-permute-start.4 = (bf16[256,512]{1,0:T(8,128)(2,1)S(1)}, bf16[256,512]{1,0:T(8,128)(2,1)S(1)}, u32[]{:S(2)}, u32[]{:S(2)}) collective-permute-start(bf16[256,512]{1,0:T(8,128)(2,1)S(1)} %get-tuple-element.34.refs_2_), channel_id=1, source_target_pairs={{0,96},{32,0},{64,32},{96,64},{1,97},{33,1},{65,33},{97,65},{2,98}... | collective-permute-start | bytes 786440 | tf_op jit(solution)/shard_map/ppermute | solution.py:231
  11.4 14.7 %collective-permute-start.11 = (bf16[256,512]{1,0:T(8,128)(2,1)S(1)}, bf16[256,512]{1,0:T(8,128)(2,1)S(1)}, u32[]{:S(2)}, u32[]{:S(2)}) collective-permute-start(bf16[256,512]{1,0:T(8,128)(2,1)S(1)} %get-tuple-element.34.refs_2_), channel_id=1, source_target_pairs={{0,128},{1,129},{2,130},{3,131},{4,132},{5,133},{6,134},{7,135},{8... | collective-permute-start | bytes 786440 | tf_op jit(solution)/shard_map/ppermute | solution.py:224
  18.4 13.8 %collective-permute-start.12 = (bf16[256,512]{1,0:T(8,128)(2,1)S(1)}, bf16[256,512]{1,0:T(8,128)(2,1)S(1)}, u32[]{:S(2)}, u32[]{:S(2)}) collective-permute-start(bf16[256,512]{1,0:T(8,128)(2,1)S(1)} %get-tuple-element.33), channel_id=1, source_target_pairs={{0,129},{1,128},{2,131},{3,130},{4,133},{5,132},{6,135},{7,134},{8... | collective-permute-start | bytes 786440 | tf_op jit(solution)/shard_map/ppermute | solution.py:225
  20.8 13.2 %collective-permute-start.5 = (bf16[256,512]{1,0:T(8,128)(2,1)S(1)}, bf16[256,512]{1,0:T(8,128)(2,1)S(1)}, u32[]{:S(2)}, u32[]{:S(2)}) collective-permute-start(bf16[256,512]{1,0:T(8,128)(2,1)S(1)} %collective-permute-done.1.refs_3_), channel_id=1, source_target_pairs={{0,96},{32,0},{64,32},{96,64},{1,97},{33,1},{65,33},{97,65},{2,98}... | collective-permute-start | bytes 786440 | tf_op jit(solution)/shard_map/ppermute | solution.py:231
  21.6 12.6 %collective-permute-start.3 = (bf16[256,512]{1,0:T(8,128)(2,1)S(1)}, bf16[256,512]{1,0:T(8,128)(2,1)S(1)}, u32[]{:S(2)}, u32[]{:S(2)}) collective-permute-start(bf16[256,512]{1,0:T(8,128)(2,1)S(1)} %collective-permute-done.1.refs_3_), channel_id=1, source_target_pairs={{0,32},{32,64},{64,96},{96,0},{1,33},{33,65},{65,97},{97,1},{2,34}... | collective-permute-start | bytes 786440 | tf_op jit(solution)/shard_map/ppermute | solution.py:231
  26.1 10.2 %collective-permute-start.6 = (bf16[256,512]{1,0:T(8,128)(2,1)S(1)}, bf16[256,512]{1,0:T(8,128)(2,1)S(1)}, u32[]{:S(2)}, u32[]{:S(2)}) collective-permute-start(bf16[256,512]{1,0:T(8,128)(2,1)S(1)} %broadcast_maximum_fusion.1), channel_id=1, source_target_pairs={{0,32},{32,64},{64,96},{96,0},{1,33},{33,65},{65,97},{97,1},{2,34}... | collective-permute-start | bytes 786440 | tf_op jit(solution)/shard_map/ppermute | solution.py:231
  32.1 9.8 %collective-permute-start.14 = (bf16[256,512]{1,0:T(8,128)(2,1)S(1)}, bf16[256,512]{1,0:T(8,128)(2,1)S(1)}, u32[]{:S(2)}, u32[]{:S(2)}) collective-permute-start(bf16[256,512]{1,0:T(8,128)(2,1)S(1)} %collective-permute-done.12.refs_3_), channel_id=1, source_target_pairs={{0,32},{32,64},{64,96},{96,0},{1,33},{33,65},{65,97},{97,1},{2,34}... | collective-permute-start | bytes 786440 | tf_op jit(solution)/shard_map/ppermute | solution.py:231
  33.9 10.4 %collective-permute-start.15 = (bf16[256,512]{1,0:T(8,128)(2,1)S(1)}, bf16[256,512]{1,0:T(8,128)(2,1)S(1)}, u32[]{:S(2)}, u32[]{:S(2)}) collective-permute-start(bf16[256,512]{1,0:T(8,128)(2,1)S(1)} %collective-permute-done.11.refs_2_), channel_id=1, source_target_pairs={{0,96},{32,0},{64,32},{96,64},{1,97},{33,1},{65,33},{97,65},{2,98}... | collective-permute-start | bytes 786440 | tf_op jit(solution)/shard_map/ppermute | solution.py:231
  34.2 19.4 %collective-permute-start.7 = (bf16[256,512]{1,0:T(8,128)(2,1)S(1)}, bf16[256,512]{1,0:T(8,128)(2,1)S(1)}, u32[]{:S(2)}, u32[]{:S(2)}) collective-permute-start(bf16[256,512]{1,0:T(8,128)(2,1)S(1)} %broadcast_maximum_fusion), channel_id=1, source_target_pairs={{0,96},{32,0},{64,32},{96,64},{1,97},{33,1},{65,33},{97,65},{2,98}... | collective-permute-start | bytes 786440 | tf_op jit(solution)/shard_map/ppermute | solution.py:231
  36.3 23.7 %collective-permute-start.13 = (bf16[256,512]{1,0:T(8,128)(2,1)S(1)}, bf16[256,512]{1,0:T(8,128)(2,1)S(1)}, u32[]{:S(2)}, u32[]{:S(2)}) collective-permute-start(bf16[256,512]{1,0:T(8,128)(2,1)S(1)} %collective-permute-done.11.refs_2_), channel_id=1, source_target_pairs={{0,32},{32,64},{64,96},{96,0},{1,33},{33,65},{65,97},{97,1},{2,34}... | collective-permute-start | bytes 786440 | tf_op jit(solution)/shard_map/ppermute | solution.py:231
  41.9 20.8 %collective-permute-start.16 = (bf16[256,512]{1,0:T(8,128)(2,1)S(1)}, bf16[256,512]{1,0:T(8,128)(2,1)S(1)}, u32[]{:S(2)}, u32[]{:S(2)}) collective-permute-start(bf16[256,512]{1,0:T(8,128)(2,1)S(1)} %collective-permute-done.12.refs_3_), channel_id=1, source_target_pairs={{0,96},{32,0},{64,32},{96,64},{1,97},{33,1},{65,33},{97,65},{2,98}... | collective-permute-start | bytes 786440 | tf_op jit(solution)/shard_map/ppermute | solution.py:231
  44.3 25.8 %collective-permute-start.17 = (bf16[256,512]{1,0:T(8,128)(2,1)S(1)}, bf16[256,512]{1,0:T(8,128)(2,1)S(1)}, u32[]{:S(2)}, u32[]{:S(2)}) collective-permute-start(bf16[256,512]{1,0:T(8,128)(2,1)S(1)} %collective-permute-done.15.refs_6_), channel_id=1, source_target_pairs={{0,96},{32,0},{64,32},{96,64},{1,97},{33,1},{65,33},{97,65},{2,98}... | collective-permute-start | bytes 786440 | tf_op jit(solution)/shard_map/ppermute | solution.py:231
  44.3 25.9 %collective-permute-start.18 = (bf16[256,512]{1,0:T(8,128)(2,1)S(1)}, bf16[256,512]{1,0:T(8,128)(2,1)S(1)}, u32[]{:S(2)}, u32[]{:S(2)}) collective-permute-start(bf16[256,512]{1,0:T(8,128)(2,1)S(1)} %collective-permute-done.14.refs_5_), channel_id=1, source_target_pairs={{0,32},{32,64},{64,96},{96,0},{1,33},{33,65},{65,97},{97,1},{2,34}... | collective-permute-start | bytes 786440 | tf_op jit(solution)/shard_map/ppermute | solution.py:231
  58.4 18.2 %collective-permute-start.8 = (bf16[4,72,256]{2,1,0:T(8,128)(2,1)S(1)}, bf16[4,72,256]{2,1,0:T(8,128)(2,1)S(1)}, u32[]{:S(2)}, u32[]{:S(2)}) collective-permute-start(bf16[4,72,256]{2,1,0:T(8,128)(2,1)S(1)} %get-tuple-element.20), channel_id=1, source_target_pairs={{0,2},{1,3},{2,4},{3,5},{4,6},{5,7},{6,0},{7,1},{8,10},{9,11},{10,... | collective-permute-start | bytes 442376 | tf_op jit(solution)/shard_map/ppermute | solution.py:251
  60.0 18.5 %collective-permute-start.9 = (bf16[4,72,256]{2,1,0:T(8,128)(2,1)S(1)}, bf16[4,72,256]{2,1,0:T(8,128)(2,1)S(1)}, u32[]{:S(2)}, u32[]{:S(2)}) collective-permute-start(bf16[4,72,256]{2,1,0:T(8,128)(2,1)S(1)} %get-tuple-element.21), channel_id=1, source_target_pairs={{0,4},{1,5},{2,6},{3,7},{4,0},{5,1},{6,2},{7,3},{8,12},{9,13},{10,... | collective-permute-start | bytes 442376 | tf_op jit(solution)/shard_map/ppermute | solution.py:251
  62.8 15.8 %collective-permute-start.10 = (bf16[4,72,256]{2,1,0:T(8,128)(2,1)S(1)}, bf16[4,72,256]{2,1,0:T(8,128)(2,1)S(1)}, u32[]{:S(2)}, u32[]{:S(2)}) collective-permute-start(bf16[4,72,256]{2,1,0:T(8,128)(2,1)S(1)} %get-tuple-element.22), channel_id=1, source_target_pairs={{0,6},{1,7},{2,0},{3,1},{4,2},{5,3},{6,4},{7,5},{8,14},{9,15},{10,... | collective-permute-start | bytes 442376 | tf_op jit(solution)/shard_map/ppermute | solution.py:251
  75.1 8.0 %collective-permute-start.19 = (bf16[4,72,256]{2,1,0:T(8,128)(2,1)S(1)}, bf16[4,72,256]{2,1,0:T(8,128)(2,1)S(1)}, u32[]{:S(2)}, u32[]{:S(2)}) collective-permute-start(bf16[4,72,256]{2,1,0:T(8,128)(2,1)S(1)} %get-tuple-element.24), channel_id=1, source_target_pairs={{0,2},{1,3},{2,4},{3,5},{4,6},{5,7},{6,0},{7,1},{8,10},{9,11},{10,... | collective-permute-start | bytes 442376 | tf_op jit(solution)/shard_map/ppermute | solution.py:251
  75.8 7.3 %collective-permute-start.20 = (bf16[4,72,256]{2,1,0:T(8,128)(2,1)S(1)}, bf16[4,72,256]{2,1,0:T(8,128)(2,1)S(1)}, u32[]{:S(2)}, u32[]{:S(2)}) collective-permute-start(bf16[4,72,256]{2,1,0:T(8,128)(2,1)S(1)} %get-tuple-element.25), channel_id=1, source_target_pairs={{0,4},{1,5},{2,6},{3,7},{4,0},{5,1},{6,2},{7,3},{8,12},{9,13},{10,... | collective-permute-start | bytes 442376 | tf_op jit(solution)/shard_map/ppermute | solution.py:251
  76.6 7.4 %collective-permute-start.21 = (bf16[4,72,256]{2,1,0:T(8,128)(2,1)S(1)}, bf16[4,72,256]{2,1,0:T(8,128)(2,1)S(1)}, u32[]{:S(2)}, u32[]{:S(2)}) collective-permute-start(bf16[4,72,256]{2,1,0:T(8,128)(2,1)S(1)} %get-tuple-element.26), channel_id=1, source_target_pairs={{0,6},{1,7},{2,0},{3,1},{4,2},{5,3},{6,4},{7,5},{8,14},{9,15},{10,... | collective-permute-start | bytes 442376 | tf_op jit(solution)/shard_map/ppermute | solution.py:251
  84.7 12.6 %collective-permute-start.22 = (bf16[2,72,256]{2,1,0:T(8,128)(2,1)S(1)}, bf16[2,72,256]{2,1,0:T(8,128)(2,1)S(1)}, u32[]{:S(2)}, u32[]{:S(2)}) collective-permute-start(bf16[2,72,256]{2,1,0:T(8,128)(2,1)S(1)} %get-tuple-element.28), channel_id=1, source_target_pairs={{0,16},{1,17},{2,18},{3,19},{4,20},{5,21},{6,22},{7,23},{8,24},{9,... | collective-permute-start | bytes 221192 | tf_op jit(solution)/shard_map/ppermute | solution.py:258
  95.0 6.3 %collective-permute-start.23 = (bf16[2,72,256]{2,1,0:T(8,128)(2,1)S(1)}, bf16[2,72,256]{2,1,0:T(8,128)(2,1)S(1)}, u32[]{:S(2)}, u32[]{:S(2)}) collective-permute-start(bf16[2,72,256]{2,1,0:T(8,128)(2,1)S(1)} %get-tuple-element.29), channel_id=1, source_target_pairs={{0,24},{1,25},{2,26},{3,27},{4,28},{5,29},{6,30},{7,31},{8,16},{9,... | collective-permute-start | bytes 221192 | tf_op jit(solution)/shard_map/ppermute | solution.py:258
  (6 other events, 49.8 us)
